TPU v7x, 32 devices: a whole 2x2x4 slice. The times are simulated.
32 devices in a mesh: member: 2 (over y), wave: 4 (over z), level: 2 (over x), fld: 2 (over core).
Axes of the slice: x: 2, y: 2, z: 4, core: 2. Of those that a mesh axis runs over, the one named last changes fastest.
Arguments:
- grid_state: bfloat16 [256, 2, 256, 1536], P(('member', 'level'), 'fld', 'wave'), parts along dimension 0, may hold values from -6 to 6
- legendre: bfloat16 [512, 2, 256, 256], P(('wave', 'level'), 'fld'), may hold values from -0.375 to 0.375
- wave_order: int32 [512], replicated, may hold values from 0 to 511, each once
- lat_order: int32 [256], replicated, may hold values from 0 to 255, each once
- eig_rates: float32 [128], replicated, may hold values from 0.1 to 4
- modes_in: bfloat16 [128, 128], replicated, may hold values from -0.5 to 0.5
- modes_out: bfloat16 [128, 128], replicated, may hold values from -0.5 to 0.5
Outputs:
- new_state: bfloat16 [256, 2, 256, 1536], P(('member', 'level'), 'fld', 'wave'), parts along dimension 0
There are 2 independent parts, one for each index of `member`. A program takes and returns all parts, laid end to end along the dimension named above; an argument that names none is the same for every part. Nothing has to cross between parts.
Inputs may be any that keep to these rules, and one draw needn't show every extreme that they name: Slot s holds zonal wavenumber wave_order[s]; every wavenumber 0 to 511 is held by exactly one slot. Latitude row r lies at Gaussian latitude index lat_order[r] counted from the equator, the same in both hemispheres; every index appears once.
All inputs are finite; a program needn't handle non-finite values.
Results may differ from a plain program's by a relative error of at most 0.0098.
Values may be sent and summed in bfloat16 or wider, within the bound.
No kernel may reach another device: no remote copies, remote signals or barrier semaphores. Data moves between devices by JAX's collectives and lax.ppermute only.
A program may use at most 128 MiB of HBM per device.

v0:
```python
import functools
import math

import jax
import jax.numpy as jnp
from jax import lax
from jax.experimental import pallas as pl
from jax.experimental.pallas import tpu as pltpu
from jax.sharding import PartitionSpec as P


tau_scale = 2.0
LANES = 128
DIRECT_LIMIT = 16
CHUNKS = 4
SPLITS = 4
EXCHANGE_AXES = ("wave", "level")


def partner(value, axis):
    pairs = [(source, source ^ 1) for source in range(lax.axis_size(axis))]
    return lax.ppermute(value, axis, pairs)


def shift_places(value, wave_shift, level_shift):
    if wave_shift == 0 and level_shift == 0:
        return value
    waves, levels = lax.axis_size("wave"), lax.axis_size("level")
    pairs = []
    for wave in range(waves):
        for level in range(levels):
            target = (wave + wave_shift) % waves * levels + (level + level_shift) % levels
            pairs.append((wave * levels + level, target))
    return lax.ppermute(value, EXCHANGE_AXES, pairs)


def rolled(value, start):
    return lax.dynamic_slice_in_dim(
        jnp.concatenate([value, value], axis=0), start, value.shape[0], axis=0
    )


def phase_of(product, period):
    return (product % period).astype(jnp.float32) * (2.0 * math.pi / period)


def table_kernel(scale, high_cos, high_sin, low_cos, low_sin, out):
    for block in range(out.shape[1] // LANES):
        spot = slice(block * LANES, (block + 1) * LANES)
        values = (
            high_cos[:, block : block + 1] * low_cos[...]
            - high_sin[:, block : block + 1] * low_sin[...]
        )
        out[:, spot] = (values * scale).astype(out.dtype)


def fourier_table(ids, quarter, lon_count, chunks):
    rows = ids.shape[0]
    blocks = lon_count // LANES
    high = phase_of(
        ids[:, None] * LANES * jnp.arange(blocks, dtype=jnp.int32)[None, :] + quarter[:, None],
        lon_count,
    )
    low = phase_of(ids[:, None] * jnp.arange(LANES, dtype=jnp.int32)[None, :], lon_count)
    step = rows // chunks
    high_spec = pl.BlockSpec((step, blocks), lambda i: (i, 0))
    low_spec = pl.BlockSpec((step, LANES), lambda i: (i, 0))
    return pl.pallas_call(
        functools.partial(table_kernel, math.sqrt(2.0 / lon_count)),
        out_shape=jax.ShapeDtypeStruct((rows, lon_count), jnp.bfloat16),
        grid=(chunks,),
        in_specs=[high_spec, high_spec, low_spec, low_spec],
        out_specs=pl.BlockSpec((step, lon_count), lambda i: (i, 0)),
        cost_estimate=pl.CostEstimate(
            flops=4 * rows * lon_count, bytes_accessed=2 * rows * lon_count, transcendentals=0
        ),
    )(jnp.cos(high), jnp.sin(high), jnp.cos(low), jnp.sin(low))


def level_block(levels, rows_here):
    return 8 if levels % 8 == 0 and 8 * rows_here % LANES == 0 else levels


def fourier_kernel(grid_ref, coupling, table, *outs):
    levels, rows, lon_count = grid_ref.shape
    field = grid_ref[...].astype(jnp.float32)
    forcing = (field + coupling[...][None] * jnp.tanh(field)).astype(jnp.bfloat16)
    forcing = forcing.reshape(levels * rows, lon_count)
    height = outs[0].shape[0]
    for index, out in enumerate(outs):
        out[...] = lax.dot_general(
            table[index * height : (index + 1) * height],
            forcing,
            (((1,), (1,)), ((), ())),
            preferred_element_type=jnp.float32,
        ).astype(out.dtype)


def fourier(grid_state, coupling, table, pieces, start, levels):
    _, rows_here, lon_count = grid_state.shape
    height = table.shape[0] // pieces
    block = level_block(levels, rows_here)
    first = start // block
    width = levels * rows_here
    return pl.pallas_call(
        fourier_kernel,
        out_shape=[jax.ShapeDtypeStruct((height, width), jnp.bfloat16)] * pieces,
        grid=(levels // block,),
        in_specs=[
            pl.BlockSpec((block, rows_here, lon_count), lambda i: (first + i, 0, 0)),
            pl.BlockSpec((rows_here, 1), lambda i: (0, 0)),
            pl.BlockSpec(table.shape, lambda i: (0, 0), pipeline_mode=pl.Buffered(1)),
        ],
        out_specs=[pl.BlockSpec((height, block * rows_here), lambda i: (0, i))] * pieces,
        compiler_params=pltpu.CompilerParams(vmem_limit_bytes=40 * 2**20),
        cost_estimate=pl.CostEstimate(
            flops=2 * table.shape[0] * width * lon_count,
            bytes_accessed=2 * (width * lon_count + table.shape[0] * (width + lon_count)),
            transcendentals=width * lon_count,
        ),
    )(grid_state, coupling, table)


def column_kernel(sizes, waves, scalars, eig_ref, modes_in, modes_out, table, *refs):
    wave_size, level_size, splits, group, tiles, half_count, wave_count, first = sizes
    places = wave_size * level_size
    pieces, (out, rows_in, rows_out) = refs[: places * splits], refs[places * splits :]
    eights = group // 8
    some = tiles // splits
    rows_here = LANES // 2
    parity = scalars[wave_size].astype(jnp.float32)
    low_half = lax.broadcasted_iota(jnp.int32, (tiles, LANES), 1) < LANES // 2

    for place in range(places):
        for split in range(splits):
            piece = pieces[place * splits + split]

            def spread(part, carry, place=place, split=split, piece=piece):
                for tile in range(some):
                    value = piece[part, :, tile * LANES : (tile + 1) * LANES].astype(jnp.float32)
                    for eight in range(eights):
                        row = ((place * 2 + part) * eights + eight) * tiles + split * some + tile
                        rows_in[pl.ds(pl.multiple_of(row * 8, 8), 8), :] = value[
                            eight * 8 : (eight + 1) * 8
                        ]
                return carry

            lax.fori_loop(0, 2, spread, 0)

    def where_rows(place, part, slot):
        eight, within = slot // 8, slot % 8
        return pl.ds((((place * 2 + part) * eights + eight) * tiles) * 8 + within, tiles, 8)

    def one_slot(slot, carry):
        legendre = jnp.concatenate(
            [
                table[slot, pl.ds(pl.multiple_of(scalars[wave] * rows_here, rows_here), rows_here), :]
                for wave in range(wave_size)
            ],
            axis=0,
        )
        stacked = []
        for part in range(2):
            low_rows, high_rows = [], []
            for level in range(level_size):
                low_pieces, high_pieces = [], []
                for pair in range(wave_size // 2):
                    a = rows_in[where_rows(2 * pair * level_size + level, part, slot), :]
                    b = rows_in[where_rows((2 * pair + 1) * level_size + level, part, slot), :]
                    low_pieces.append(jnp.where(low_half, a, pltpu.roll(b, LANES // 2, 1)))
                    high_pieces.append(jnp.where(low_half, pltpu.roll(a, LANES // 2, 1), b))
                low_rows.append(jnp.concatenate(low_pieces, axis=1))
                high_rows.append(jnp.concatenate(high_pieces, axis=1))
            stacked += low_rows + high_rows
        field = jnp.concatenate(stacked, axis=0).astype(jnp.bfloat16)
        degree = (
            waves[first + slot] + 2 * lax.broadcasted_iota(jnp.int32, (1, half_count), 1)
        ).astype(jnp.float32) + parity
        inside = (degree <= float(wave_count - 1)).astype(jnp.float32)
        ratio = tau_scale * degree * (degree + 1.0) / float(wave_count * (wave_count - 1))
        factor = 1.0 / (1.0 + eig_ref[...] * ratio)
        spectral = jnp.dot(field, legendre, preferred_element_type=jnp.float32)
        spectral = (spectral * inside).astype(jnp.bfloat16)
        levels = modes_in.shape[0]
        solved = []
        for part in range(2):
            column = spectral[part * levels : (part + 1) * levels]
            modal = jnp.dot(modes_in[...], column, preferred_element_type=jnp.float32)
            modal = (modal * factor).astype(jnp.bfloat16)
            solved.append(
                jnp.dot(modes_out[...], modal, preferred_element_type=jnp.float32).astype(
                    jnp.bfloat16
                )
            )
        grid = lax.dot_general(
            jnp.concatenate(solved, axis=0),
            legendre,
            (((1,), (1,)), ((), ())),
            preferred_element_type=jnp.float32,
        )
        for part in range(2):
            for level in range(level_size):
                low_start = part * levels + level * tiles
                high_start = low_start + level_size * tiles
                for pair in range(wave_size // 2):
                    lanes = slice(pair * LANES, (pair + 1) * LANES)
                    low = grid[low_start : low_start + tiles, lanes]
                    high = grid[high_start : high_start + tiles, lanes]
                    a = jnp.where(low_half, low, pltpu.roll(high, LANES // 2, 1))
                    b = jnp.where(low_half, pltpu.roll(low, LANES // 2, 1), high)
                    rows_out[where_rows(2 * pair * level_size + level, part, slot), :] = a
                    rows_out[where_rows((2 * pair + 1) * level_size + level, part, slot), :] = b
        return carry

    lax.fori_loop(0, group, one_slot, 0)

    def gather(index, carry):
        place, part = index // 2, index % 2
        for tile in range(tiles):
            parts = []
            for eight in range(eights):
                start = pl.multiple_of(((index * eights + eight) * tiles + tile) * 8, 8)
                parts.append(rows_out[pl.ds(start, 8), :])
            out[place, part, :, tile * LANES : (tile + 1) * LANES] = jnp.concatenate(
                parts, axis=0
            ).astype(out.dtype)
        return carry

    lax.fori_loop(0, places * 2, gather, 0)


def columns_fused(pieces, legendre, waves, scalars, eig_rates, modes, sizes):
    wave_size, level_size, _, group, tiles, half_count, _, first = sizes
    places = wave_size * level_size
    half_rows = legendre.shape[1]
    width = tiles * LANES
    levels = modes[0].shape[0]
    flat = [piece for place in pieces for piece in place]
    whole = lambda shape: pl.BlockSpec(shape, lambda i: (0,) * len(shape))
    scratch = pltpu.VMEM((places * 2 * group * tiles, LANES), jnp.float32)
    values = places * 2 * group * width
    return pl.pallas_call(
        functools.partial(column_kernel, sizes),
        out_shape=jax.ShapeDtypeStruct((places, 2, group, width), jnp.bfloat16),
        grid=(1,),
        in_specs=[
            pl.BlockSpec(memory_space=pltpu.SMEM),
            pl.BlockSpec(memory_space=pltpu.SMEM),
            whole((levels, 1)),
            whole((levels, levels)),
            whole((levels, levels)),
            pl.BlockSpec((group, half_rows, half_count), lambda i: (first // group, 0, 0)),
        ]
        + [whole(piece.shape) for piece in flat],
        out_specs=whole((places, 2, group, width)),
        scratch_shapes=[scratch, scratch],
        compiler_params=pltpu.CompilerParams(vmem_limit_bytes=40 * 2**20),
        cost_estimate=pl.CostEstimate(
            flops=values * half_rows * 6, bytes_accessed=6 * values, transcendentals=0
        ),
    )(waves, scalars, eig_rates[:, None], *modes, legendre, *flat)


def columns_plain(mirrored, legendre, waves, parity, eig_rates, modes_in, modes_out, sizes):
    wave_size, level_size, count, first, wave_count = sizes
    levels = modes_in.shape[0]
    half_rows, half_count = legendre.shape[1:]
    local_levels, rows_here = levels // level_size, half_rows // wave_size
    shape = mirrored.shape
    mirrored = mirrored.reshape(wave_size, level_size, 2, count, local_levels, rows_here)
    field = mirrored.transpose(3, 2, 1, 4, 0, 5).reshape(count, 2, levels, half_rows)
    table = legendre[first : first + count]
    degree = (
        waves[first : first + count, None] + 2 * jnp.arange(half_count, dtype=jnp.int32)[None, :]
    ).astype(jnp.float32) + parity
    inside = (degree <= float(wave_count - 1)).astype(jnp.float32)
    ratio = tau_scale * degree * (degree + 1.0) / float(wave_count * (wave_count - 1))
    factor = 1.0 / (1.0 + ratio[:, None, :] * eig_rates[None, :, None])
    spectral = jnp.einsum("sclr,srj->sclj", field, table, preferred_element_type=jnp.float32)
    spectral = (spectral * inside[:, None, None, :]).astype(jnp.bfloat16)
    modal = jnp.einsum("kl,sclj->sckj", modes_in, spectral, preferred_element_type=jnp.float32)
    modal = (modal * factor[:, None, :, :]).astype(jnp.bfloat16)
    solved = jnp.einsum(
        "lk,sckj->sclj", modes_out, modal, preferred_element_type=jnp.float32
    ).astype(jnp.bfloat16)
    grid = jnp.einsum("sclj,srj->sclr", solved, table, preferred_element_type=jnp.float32)
    grid = grid.astype(jnp.bfloat16)
    grid = grid.reshape(count, 2, level_size, local_levels, wave_size, rows_here)
    return grid.transpose(4, 2, 1, 0, 3, 5).reshape(shape)


def inverse_kernel(pieces, *refs):
    table, out = refs[pieces], refs[-1]
    coeffs = jnp.concatenate([ref[...] for ref in refs[:pieces]], axis=0)
    current = lax.dot_general(
        coeffs, table[...], (((0,), (0,)), ((), ())), preferred_element_type=jnp.float32
    )
    out[...] = current.astype(out.dtype).reshape(out.shape)


def inverse_fourier(pieces, table, current, shape, start, levels):
    _, rows_here, lon_count = shape
    block = level_block(levels, rows_here)
    width = block * rows_here
    full = shape[0] * rows_here
    first = start // block
    specs = [
        pl.BlockSpec(
            (piece.shape[0], width),
            (lambda i: (0, first + i)) if piece.shape[1] == full else (lambda i: (0, i)),
        )
        for piece in pieces
    ]
    table_spec = pl.BlockSpec(table.shape, lambda i: (0, 0), pipeline_mode=pl.Buffered(1))
    operands = list(pieces) + [table]
    specs.append(table_spec)
    aliases = {}
    if current is not None:
        aliases = {len(operands): 0}
        operands.append(current)
        specs.append(pl.BlockSpec(memory_space=pl.ANY))
    return pl.pallas_call(
        functools.partial(inverse_kernel, len(pieces)),
        out_shape=jax.ShapeDtypeStruct(shape, jnp.bfloat16),
        grid=(levels // block,),
        in_specs=specs,
        out_specs=pl.BlockSpec((block, rows_here, lon_count), lambda i: (first + i, 0, 0)),
        input_output_aliases=aliases,
        compiler_params=pltpu.CompilerParams(vmem_limit_bytes=40 * 2**20),
        cost_estimate=pl.CostEstimate(
            flops=2 * table.shape[0] * levels * rows_here * lon_count,
            bytes_accessed=2 * levels * rows_here * (table.shape[0] + lon_count),
            transcendentals=0,
        ),
    )(*operands)


def shards(grid_state, legendre, wave_order, lat_order, eig_rates, modes_in, modes_out):
    out_shape = grid_state.shape
    local_levels, _, rows_here, lon_count = out_shape
    wave_size = lax.axis_size("wave")
    level_size = lax.axis_size("level")
    places = wave_size * level_size
    half_rows = lat_order.shape[0]
    wave_count = wave_order.shape[0]
    narrow, half_count = legendre.shape[0], legendre.shape[3]
    chunks = min(CHUNKS, narrow)
    count = narrow // chunks
    width = local_levels * rows_here
    fused = (
        places <= DIRECT_LIMIT
        and rows_here * 2 == LANES
        and wave_size % 2 == 0
        and count % 16 == 0
        and local_levels % 8 == 0
    )
    splits = SPLITS if fused else 1
    parity = lax.axis_index("fld")
    wave_place = lax.axis_index("wave")
    level_place = lax.axis_index("level")
    legendre = legendre.reshape(narrow, half_rows, half_count)
    grid_state = grid_state.reshape(local_levels, rows_here, lon_count)
    hemi_sign = 1.0 - 2.0 * parity.astype(jnp.float32)
    lat_rows = lax.dynamic_slice_in_dim(lat_order, wave_place * rows_here, rows_here)
    sine = jnp.sin((lat_rows.astype(jnp.float32) + 0.5) * (math.pi / (2.0 * half_rows)))
    coupling = (0.5 * hemi_sign * sine)[:, None]
    place = wave_place * level_size + level_place
    waves = lax.dynamic_slice_in_dim(wave_order, place * narrow, narrow)

    ids = wave_order.reshape(wave_size, level_size, chunks, count)
    if fused:
        ids = rolled(ids, wave_place)
        ids = jnp.swapaxes(rolled(jnp.swapaxes(ids, 0, 1), level_place), 0, 1)
    ids = ids.reshape(places, chunks, count).transpose(1, 0, 2)
    ids = jnp.broadcast_to(ids[:, :, None, :], (chunks, places, 2, count)).reshape(chunks, -1)
    quarter = jnp.broadcast_to(
        (jnp.arange(2, dtype=jnp.int32) * (lon_count // 4))[None, :, None], (places, 2, count)
    ).reshape(-1)
    tables = [fourier_table(ids[0], quarter, lon_count, 1)]
    if chunks > 1:
        tables.append(
            fourier_table(
                ids[1:].reshape(-1), jnp.tile(quarter, chunks - 1), lon_count, chunks - 1
            )
        )
    table = jnp.concatenate(tables, axis=0)
    places_list = [(wave, level) for wave in range(wave_size) for level in range(level_size)]
    height = 2 * count

    if not fused:
        parts = fourier(grid_state, coupling, table, chunks, 0, local_levels)
        returned = []
        for chunk in range(chunks):
            value = parts[chunk]
            mirrored = (
                partner(value, "fld").astype(jnp.float32) + hemi_sign * value.astype(jnp.float32)
            ).astype(jnp.bfloat16)
            mirrored = lax.all_to_all(
                mirrored.reshape(places, height, width), EXCHANGE_AXES, 0, 0, tiled=True
            )
            grid = columns_plain(
                mirrored.reshape(wave_size, level_size, 2, count, width),
                legendre,
                waves,
                parity.astype(jnp.float32),
                eig_rates,
                modes_in,
                modes_out,
                (wave_size, level_size, count, chunk * count, wave_count),
            ).reshape(places, height, width)
            hemi = (
                0.5
                * (partner(grid, "fld").astype(jnp.float32) + hemi_sign * grid.astype(jnp.float32))
            ).astype(jnp.bfloat16)
            hemi = lax.all_to_all(hemi, EXCHANGE_AXES, 0, 0, tiled=True)
            returned.append(hemi.reshape(places * height, width))
        coeffs = [jnp.concatenate(returned, axis=0)]
        current = inverse_fourier(coeffs, table, None, grid_state.shape, 0, local_levels)
        return current.reshape(out_shape)

    tiles = width // LANES
    level_index = jnp.arange(local_levels, dtype=jnp.int32).reshape(tiles, 2).T
    from_level = (level_place - jnp.arange(level_size, dtype=jnp.int32)) % level_size
    order = (from_level[None, :, None] * local_levels + level_index[:, None, :]).reshape(-1)
    modes = (jnp.take(modes_in, order, axis=1), jnp.take(modes_out, order, axis=0))
    scalars = jnp.concatenate(
        [(wave_place - jnp.arange(wave_size, dtype=jnp.int32)) % wave_size, parity[None]]
    )

    def send(value):
        other = partner(value, "fld")
        arrived = []
        for index, (wave, level) in enumerate(places_list):
            rows = slice(index * height, (index + 1) * height)
            mirrored = (
                other[rows].astype(jnp.float32) + hemi_sign * value[rows].astype(jnp.float32)
            ).astype(jnp.bfloat16)
            moved = shift_places(mirrored, wave, level)
            arrived.append(moved.reshape(2, count, -1))
        return arrived

    some = local_levels // splits
    forward = [[] for _ in range(chunks)]
    for split in range(splits):
        (value,) = fourier(grid_state, coupling, tables[0], 1, split * some, some)
        forward[0].append(send(value))
    rest = fourier(grid_state, coupling, tables[1], chunks - 1, 0, local_levels)
    for chunk in range(1, chunks):
        forward[chunk].append(send(rest[chunk - 1]))

    returned, last = [], []
    for chunk in range(chunks):
        pieces = [list(piece) for piece in zip(*forward[chunk])]
        sizes = (
            wave_size,
            level_size,
            len(pieces[0]),
            count,
            tiles,
            half_count,
            wave_count,
            chunk * count,
        )
        grid = columns_fused(pieces, legendre, waves, scalars, eig_rates, modes, sizes)
        grid = grid.reshape(places, height, width)
        other = partner(grid, "fld")
        cuts = splits if chunk == chunks - 1 else 1
        for cut in range(cuts):
            lanes = slice(cut * (width // cuts), (cut + 1) * (width // cuts))
            back = []
            for index, (wave, level) in enumerate(places_list):
                hemi = (
                    0.5
                    * (
                        other[index, :, lanes].astype(jnp.float32)
                        + hemi_sign * grid[index, :, lanes].astype(jnp.float32)
                    )
                ).astype(jnp.bfloat16)
                back.append(
                    shift_places(
                        hemi, (wave_size - wave) % wave_size, (level_size - level) % level_size
                    )
                )
            (returned if cuts == 1 else last).append(back)
    earlier = [piece for back in returned for piece in back]
    current = None
    for split in range(splits):
        current = inverse_fourier(
            earlier + last[split], table, current, grid_state.shape, split * some, some
        )
    return current.reshape(out_shape)


def solution(mesh):
    placed = (
        P(("member", "level"), "fld", "wave", None),
        P(("wave", "level"), "fld", None, None),
        P(),
        P(),
        P(),
        P(),
        P(),
    )
    return jax.shard_map(
        shards,
        mesh=mesh,
        in_specs=placed,
        out_specs=P(("member", "level"), "fld", "wave", None),
        check_vma=False,
    )
```

profile of v0, /device:TPU:0, one launch (start us, length us, event | category | flops | bytes accessed | tf_op | source)
XLA Modules:
  0.0 543.7 jit_solution(18097353059084607078)
XLA Ops:
  4.7 2.9 shard_map.73.table
  7.6 4.6 copy-done.2
  13.3 2.3 shard_map.74
  16.1 2.3 shard_map.75
  22.4 2.7 fusion.52
  27.5 5.2 shard_map.79.table
  34.4 14.9 %shard_map.80 = (bf16[256,4096]{1,0:T(8,128)(2,1)}, bf16[256,4096]{1,0:T(8,128)(2,1)S(1)}, bf16[256,4096]{1,0:T(8,128)(2,1)S(1)}) custom-call(bf16[64,64,1536]{2,1,0:T(8,128)(2,1)} %bitcast.315, f32[64,1]{1,0:T(8,128)S(1)} %copy.45.coupling, bf16[768,1536]{1,0:T(8,128)(2,1)S(1)} %copy-done.6), custom_call_target="tpu_custom_call" | custom-call | flops 9663676416 | bytes 21233664 | tf_op jit(solution)/shard_map/pallas_call | solution.py:105
  53.2 5.6 %collective-permute-start.28 = (bf16[32,1024]{1,0:T(8,128)(2,1)S(1)}, bf16[32,1024]{1,0:T(8,128)(2,1)S(1)}, u32[]{:S(2)}, u32[]{:S(2)}) collective-permute-start(bf16[32,1024]{1,0:T(8,128)(2,1)S(1)} %get-tuple-element.139), channel_id=1, source_target_pairs={{0,14},{2,12},{4,2},{6,0},{8,6},{10,4},{12,10},{14,8},{1,15},{3,13... | collective-permute-start | bytes 196616 | tf_op jit(solution)/shard_map/ppermute | solution.py:34
  59.4 2.9 collective-permute-start.16
  62.2 2.6 collective-permute-start.12
  67.0 3.3 collective-permute-done.20
  79.1 2.3 collective-permute-start.13
  83.3 3.7 collective-permute-done.21
  89.5 4.5 collective-permute-start.30
  100.9 3.6 collective-permute-start.14
  108.1 2.7 collective-permute-done.10
  119.3 4.6 collective-permute-done.23
  126.5 2.9 add_convert_fusion.16
  135.6 2.6 collective-permute-start.44
  141.9 3.4 collective-permute-done.46
  146.1 28.9 %collective-permute-done.45 = bf16[32,4096]{1,0:T(8,128)(2,1)S(1)} collective-permute-done((bf16[32,4096]{1,0:T(8,128)(2,1)S(1)}, bf16[32,4096]{1,0:T(8,128)(2,1)S(1)}, u32[]{:S(2)}, u32[]{:S(2)}) %collective-permute-start.45) | collective-permute-done | bytes 262176 | tf_op jit(solution)/shard_map/ppermute | solution.py:34
  175.1 6.0 %collective-permute-done.44 = bf16[32,4096]{1,0:T(8,128)(2,1)S(1)} collective-permute-done((bf16[32,4096]{1,0:T(8,128)(2,1)S(1)}, bf16[32,4096]{1,0:T(8,128)(2,1)S(1)}, u32[]{:S(2)}, u32[]{:S(2)}) %collective-permute-start.44) | collective-permute-done | bytes 262176 | tf_op jit(solution)/shard_map/ppermute | solution.py:34
  181.2 3.4 copy-done.3
  184.6 16.6 %shard_map.78 = bf16[8,2,16,4096]{3,2,1,0:T(8,128)(2,1)S(1)} custom-call(s32[64]{0:T(128)S(1)} %dynamic_slice.12.waves, s32[5]{0:T(128)S(1)} %pad_add_fusion.scalars, f32[128,1]{1,0:T(8,128)S(1)} %copy.49.eig_ref, bf16[128,128]{1,0:T(8,128)(2,1)S(1)} %copy.50.modes_in, bf16[128,128]{1,0:T(8,128)(2,1)S(1)} %get-tuple-element.155.modes_out, ...), custom_call_target="tpu_custom_call" | custom-call | flops 1610612736 | bytes 6291456 | tf_op jit(solution)/shard_map/pallas_call | solution.py:242
  201.4 2.5 collective-permute-start.60
  203.9 3.3 collective-permute-start.59
  207.2 3.1 add_convert_fusion
  210.3 24.5 %collective-permute-done.61 = bf16[32,4096]{1,0:T(8,128)(2,1)S(1)} collective-permute-done((bf16[32,4096]{1,0:T(8,128)(2,1)S(1)}, bf16[32,4096]{1,0:T(8,128)(2,1)S(1)}, u32[]{:S(2)}, u32[]{:S(2)}) %collective-permute-start.61) | collective-permute-done | bytes 262176 | tf_op jit(solution)/shard_map/ppermute | solution.py:34
  235.0 3.6 collective-permute-done.60
  238.6 2.3 collective-permute-start.78
  243.5 3.1 collective-permute-done.57
  248.7 7.1 %collective-permute-done.78 = bf16[32,4096]{1,0:T(8,128)(2,1)S(1)} collective-permute-done((bf16[32,4096]{1,0:T(8,128)(2,1)S(1)}, bf16[32,4096]{1,0:T(8,128)(2,1)S(1)}, u32[]{:S(2)}, u32[]{:S(2)}) %collective-permute-start.78) | collective-permute-done | bytes 262176 | tf_op jit(solution)/shard_map/ppermute | solution.py:34
  255.8 24.5 %collective-permute-done.77 = bf16[32,4096]{1,0:T(8,128)(2,1)S(1)} collective-permute-done((bf16[32,4096]{1,0:T(8,128)(2,1)S(1)}, bf16[32,4096]{1,0:T(8,128)(2,1)S(1)}, u32[]{:S(2)}, u32[]{:S(2)}) %collective-permute-start.77) | collective-permute-done | bytes 262176 | tf_op jit(solution)/shard_map/ppermute | solution.py:34
  280.4 15.9 %shard_map.81 = bf16[8,2,16,4096]{3,2,1,0:T(8,128)(2,1)S(1)} custom-call(s32[64]{0:T(128)S(1)} %dynamic_slice.12.waves, s32[5]{0:T(128)S(1)} %pad_add_fusion.scalars, f32[128,1]{1,0:T(8,128)S(1)} %copy.49.eig_ref, bf16[128,128]{1,0:T(8,128)(2,1)S(1)} %copy.50.modes_in, bf16[128,128]{1,0:T(8,128)(2,1)S(1)} %get-tuple-element.155.modes_out, ...), custom_call_target="tpu_custom_call" | custom-call | flops 1610612736 | bytes 6291456 | tf_op jit(solution)/shard_map/pallas_call | solution.py:242
  296.3 15.9 %shard_map.82 = bf16[8,2,16,4096]{3,2,1,0:T(8,128)(2,1)S(1)} custom-call(s32[64]{0:T(128)S(1)} %dynamic_slice.12.waves, s32[5]{0:T(128)S(1)} %pad_add_fusion.scalars, f32[128,1]{1,0:T(8,128)S(1)} %copy.49.eig_ref, bf16[128,128]{1,0:T(8,128)(2,1)S(1)} %copy.50.modes_in, bf16[128,128]{1,0:T(8,128)(2,1)S(1)} %get-tuple-element.155.modes_out, ...), custom_call_target="tpu_custom_call" | custom-call | flops 1610612736 | bytes 6291456 | tf_op jit(solution)/shard_map/pallas_call | solution.py:242
  312.8 15.9 %shard_map.83 = bf16[8,2,16,4096]{3,2,1,0:T(8,128)(2,1)S(1)} custom-call(s32[64]{0:T(128)S(1)} %dynamic_slice.12.waves, s32[5]{0:T(128)S(1)} %pad_add_fusion.scalars, f32[128,1]{1,0:T(8,128)S(1)} %copy.49.eig_ref, bf16[128,128]{1,0:T(8,128)(2,1)S(1)} %copy.50.modes_in, bf16[128,128]{1,0:T(8,128)(2,1)S(1)} %get-tuple-element.155.modes_out, ...), custom_call_target="tpu_custom_call" | custom-call | flops 1610612736 | bytes 6291456 | tf_op jit(solution)/shard_map/pallas_call | solution.py:242
  331.7 11.3 %collective-permute-done.39.refs_7_ = bf16[32,4096]{1,0:T(8,128)(2,1)S(1)} collective-permute-done((bf16[32,4096]{1,0:T(8,128)(2,1)S(1)}, bf16[32,4096]{1,0:T(8,128)(2,1)S(1)}, u32[]{:S(2)}, u32[]{:S(2)}) %collective-permute-start.39) | collective-permute-done | bytes 262176 | tf_op jit(solution)/shard_map/ppermute | solution.py:34
  343.0 6.2 %collective-permute-done.38.refs_6_ = bf16[32,4096]{1,0:T(8,128)(2,1)S(1)} collective-permute-done((bf16[32,4096]{1,0:T(8,128)(2,1)S(1)}, bf16[32,4096]{1,0:T(8,128)(2,1)S(1)}, u32[]{:S(2)}, u32[]{:S(2)}) %collective-permute-start.38) | collective-permute-done | bytes 262176 | tf_op jit(solution)/shard_map/ppermute | solution.py:34
  349.6 15.3 %collective-permute-done.37.refs_5_ = bf16[32,4096]{1,0:T(8,128)(2,1)S(1)} collective-permute-done((bf16[32,4096]{1,0:T(8,128)(2,1)S(1)}, bf16[32,4096]{1,0:T(8,128)(2,1)S(1)}, u32[]{:S(2)}, u32[]{:S(2)}) %collective-permute-start.37) | collective-permute-done | bytes 262176 | tf_op jit(solution)/shard_map/ppermute | solution.py:34
  366.4 4.7 collective-permute-done.36.refs_4_
  371.3 4.9 collective-permute-done.35.refs_3_
  376.3 5.9 %collective-permute-done.34.refs_2_ = bf16[32,4096]{1,0:T(8,128)(2,1)S(1)} collective-permute-done((bf16[32,4096]{1,0:T(8,128)(2,1)S(1)}, bf16[32,4096]{1,0:T(8,128)(2,1)S(1)}, u32[]{:S(2)}, u32[]{:S(2)}) %collective-permute-start.34) | collective-permute-done | bytes 262176 | tf_op jit(solution)/shard_map/ppermute | solution.py:34
  382.6 4.5 collective-permute-start.92
  390.1 5.3 collective-permute-start.106
  398.3 3.8 collective-permute-start.104
  408.5 19.3 %collective-permute-start.70 = (bf16[32,4096]{1,0:T(8,128)(2,1)S(1)}, bf16[32,4096]{1,0:T(8,128)(2,1)S(1)}, u32[]{:S(2)}, u32[]{:S(2)}) collective-permute-start(bf16[32,4096]{1,0:T(8,128)(2,1)S(1)} %get-tuple-element.68), channel_id=1, source_target_pairs={{0,4},{2,6},{4,8},{6,10},{8,12},{10,14},{12,0},{14,2},{1,5},{3,7},... | collective-permute-start | bytes 786440 | tf_op jit(solution)/shard_map/ppermute | solution.py:34
  427.9 2.3 fusion.17
  430.1 3.2 collective-permute-start.67
  436.0 10.7 %collective-permute-done.69.refs_21_ = bf16[32,4096]{1,0:T(8,128)(2,1)S(1)} collective-permute-done((bf16[32,4096]{1,0:T(8,128)(2,1)S(1)}, bf16[32,4096]{1,0:T(8,128)(2,1)S(1)}, u32[]{:S(2)}, u32[]{:S(2)}) %collective-permute-start.69) | collective-permute-done | bytes 262176 | tf_op jit(solution)/shard_map/ppermute | solution.py:34
  446.7 3.6 collective-permute-start.55
  450.3 9.4 %collective-permute-start.54 = (bf16[32,4096]{1,0:T(8,128)(2,1)S(1)}, bf16[32,4096]{1,0:T(8,128)(2,1)S(1)}, u32[]{:S(2)}, u32[]{:S(2)}) collective-permute-start(bf16[32,4096]{1,0:T(8,128)(2,1)S(1)} %get-tuple-element.84), channel_id=1, source_target_pairs={{0,4},{2,6},{4,8},{6,10},{8,12},{10,14},{12,0},{14,2},{1,5},{3,7},... | collective-permute-start | bytes 786440 | tf_op jit(solution)/shard_map/ppermute | solution.py:34
  460.0 10.6 %collective-permute-start.52 = (bf16[32,4096]{1,0:T(8,128)(2,1)S(1)}, bf16[32,4096]{1,0:T(8,128)(2,1)S(1)}, u32[]{:S(2)}, u32[]{:S(2)}) collective-permute-start(bf16[32,4096]{1,0:T(8,128)(2,1)S(1)} %get-tuple-element.86), channel_id=1, source_target_pairs={{0,8},{2,10},{4,12},{6,14},{8,0},{10,2},{12,4},{14,6},{1,9},{3,11}... | collective-permute-start | bytes 786440 | tf_op jit(solution)/shard_map/ppermute | solution.py:34
  470.7 7.5 %collective-permute-start.51 = (bf16[32,4096]{1,0:T(8,128)(2,1)S(1)}, bf16[32,4096]{1,0:T(8,128)(2,1)S(1)}, u32[]{:S(2)}, u32[]{:S(2)}) collective-permute-start(bf16[32,4096]{1,0:T(8,128)(2,1)S(1)} %get-tuple-element.87), channel_id=1, source_target_pairs={{0,14},{2,12},{4,2},{6,0},{8,6},{10,4},{12,10},{14,8},{1,15},{3,13... | collective-permute-start | bytes 786440 | tf_op jit(solution)/shard_map/ppermute | solution.py:34
  479.0 5.5 %collective-permute-done.53.refs_13_ = bf16[32,4096]{1,0:T(8,128)(2,1)S(1)} collective-permute-done((bf16[32,4096]{1,0:T(8,128)(2,1)S(1)}, bf16[32,4096]{1,0:T(8,128)(2,1)S(1)}, u32[]{:S(2)}, u32[]{:S(2)}) %collective-permute-start.53) | collective-permute-done | bytes 262176 | tf_op jit(solution)/shard_map/ppermute | solution.py:34
  484.5 3.6 collective-permute-done.52.refs_12_
  490.2 14.5 %collective-permute-start.97 = (bf16[32,1024]{1,0:T(8,128)(2,1)S(1)}, bf16[32,1024]{1,0:T(8,128)(2,1)S(1)}, u32[]{:S(2)}, u32[]{:S(2)}) collective-permute-start(bf16[32,1024]{1,0:T(8,128)(2,1)S(1)} %get-tuple-element.23), channel_id=1, source_target_pairs={{0,14},{2,12},{4,2},{6,0},{8,6},{10,4},{12,10},{14,8},{1,15},{3,13... | collective-permute-start | bytes 196616 | tf_op jit(solution)/shard_map/ppermute | solution.py:34
  505.3 5.2 shard_map.84.refs_33_
  510.5 4.1 collective-permute-start.90
  515.2 2.9 collective-permute-start.94
  518.1 5.2 shard_map.85.refs_33_
  523.3 3.8 collective-permute-start.82
  528.0 4.9 collective-permute-start.85
  533.0 5.2 shard_map.86.refs_33_
  538.2 5.3 shard_map.87
  (307 shorter events, 97.9 us)
Async XLA Ops:
  15.6 35.4 %collective-permute-start = (bf16[256,1024]{1,0:T(8,128)(2,1)}, bf16[256,1024]{1,0:T(8,128)(2,1)}, u32[]{:S(2)}, u32[]{:S(2)}) collective-permute-start(bf16[256,1024]{1,0:T(8,128)(2,1)} %shard_map.74), channel_id=1, source_target_pairs={{0,1},{1,0},{2,3},{3,2},{4,5},{5,4},{6,7},{7,6},{8,9},{9,8},{10,11... | collective-permute-start | bytes 1572872 | tf_op jit(solution)/shard_map/ppermute | solution.py:22
  18.4 40.5 %collective-permute-start.1 = (bf16[256,1024]{1,0:T(8,128)(2,1)}, bf16[256,1024]{1,0:T(8,128)(2,1)}, u32[]{:S(2)}, u32[]{:S(2)}) collective-permute-start(bf16[256,1024]{1,0:T(8,128)(2,1)} %shard_map.75), channel_id=1, source_target_pairs={{0,1},{1,0},{2,3},{3,2},{4,5},{5,4},{6,7},{7,6},{8,9},{9,8},{10,11... | collective-permute-start | bytes 1572872 | tf_op jit(solution)/shard_map/ppermute | solution.py:22
  20.0 39.4 %collective-permute-start.2 = (bf16[256,1024]{1,0:T(8,128)(2,1)S(1)}, bf16[256,1024]{1,0:T(8,128)(2,1)}, u32[]{:S(2)}, u32[]{:S(2)}) collective-permute-start(bf16[256,1024]{1,0:T(8,128)(2,1)S(1)} %shard_map.76), channel_id=1, source_target_pairs={{0,1},{1,0},{2,3},{3,2},{4,5},{5,4},{6,7},{7,6},{8,9},{9,8},{10,11... | collective-permute-start | bytes 1572872 | tf_op jit(solution)/shard_map/ppermute | solution.py:22
  22.2 37.2 %collective-permute-start.3 = (bf16[256,1024]{1,0:T(8,128)(2,1)S(1)}, bf16[256,1024]{1,0:T(8,128)(2,1)}, u32[]{:S(2)}, u32[]{:S(2)}) collective-permute-start(bf16[256,1024]{1,0:T(8,128)(2,1)S(1)} %shard_map.77), channel_id=1, source_target_pairs={{0,1},{1,0},{2,3},{3,2},{4,5},{5,4},{6,7},{7,6},{8,9},{9,8},{10,11... | collective-permute-start | bytes 1572872 | tf_op jit(solution)/shard_map/ppermute | solution.py:22
  50.6 75.1 %collective-permute-start.40 = (bf16[256,4096]{1,0:T(8,128)(2,1)}, bf16[256,4096]{1,0:T(8,128)(2,1)}, u32[]{:S(2)}, u32[]{:S(2)}) collective-permute-start(bf16[256,4096]{1,0:T(8,128)(2,1)} %get-tuple-element.8), channel_id=1, source_target_pairs={{0,1},{1,0},{2,3},{3,2},{4,5},{5,4},{6,7},{7,6},{8,9},{9,8},{10,11... | collective-permute-start | bytes 6291464 | tf_op jit(solution)/shard_map/ppermute | solution.py:22
  74.7 60.9 %collective-permute-start.56 = (bf16[256,4096]{1,0:T(8,128)(2,1)}, bf16[256,4096]{1,0:T(8,128)(2,1)}, u32[]{:S(2)}, u32[]{:S(2)}) collective-permute-start(bf16[256,4096]{1,0:T(8,128)(2,1)} %copy-done.8), channel_id=1, source_target_pairs={{0,1},{1,0},{2,3},{3,2},{4,5},{5,4},{6,7},{7,6},{8,9},{9,8},{10,11... | collective-permute-start | bytes 6291464 | tf_op jit(solution)/shard_map/ppermute | solution.py:22
  108.1 32.4 %collective-permute-start.72 = (bf16[256,4096]{1,0:T(8,128)(2,1)S(1)}, bf16[256,4096]{1,0:T(8,128)(2,1)}, u32[]{:S(2)}, u32[]{:S(2)}) collective-permute-start(bf16[256,4096]{1,0:T(8,128)(2,1)S(1)} %get-tuple-element.10), channel_id=1, source_target_pairs={{0,1},{1,0},{2,3},{3,2},{4,5},{5,4},{6,7},{7,6},{8,9},{9,8},{10,11... | collective-permute-start | bytes 6291464 | tf_op jit(solution)/shard_map/ppermute | solution.py:22
  132.9 12.4 %collective-permute-start.46 = (bf16[32,4096]{1,0:T(8,128)(2,1)S(1)}, bf16[32,4096]{1,0:T(8,128)(2,1)S(1)}, u32[]{:S(2)}, u32[]{:S(2)}) collective-permute-start(bf16[32,4096]{1,0:T(8,128)(2,1)S(1)} %get-tuple-element.60), channel_id=1, source_target_pairs={{0,12},{2,14},{4,0},{6,2},{8,4},{10,6},{12,8},{14,10},{1,13},{3,15... | collective-permute-start | bytes 786440 | tf_op jit(solution)/shard_map/ppermute | solution.py:34
  134.4 40.6 %collective-permute-start.45 = (bf16[32,4096]{1,0:T(8,128)(2,1)S(1)}, bf16[32,4096]{1,0:T(8,128)(2,1)S(1)}, u32[]{:S(2)}, u32[]{:S(2)}) collective-permute-start(bf16[32,4096]{1,0:T(8,128)(2,1)S(1)} %get-tuple-element.61), channel_id=1, source_target_pairs={{0,10},{2,8},{4,14},{6,12},{8,2},{10,0},{12,6},{14,4},{1,11},{3,9}... | collective-permute-start | bytes 786440 | tf_op jit(solution)/shard_map/ppermute | solution.py:34
  135.6 45.4 %collective-permute-start.44 = (bf16[32,4096]{1,0:T(8,128)(2,1)S(1)}, bf16[32,4096]{1,0:T(8,128)(2,1)S(1)}, u32[]{:S(2)}, u32[]{:S(2)}) collective-permute-start(bf16[32,4096]{1,0:T(8,128)(2,1)S(1)} %get-tuple-element.62), channel_id=1, source_target_pairs={{0,8},{2,10},{4,12},{6,14},{8,0},{10,2},{12,4},{14,6},{1,9},{3,11}... | collective-permute-start | bytes 786440 | tf_op jit(solution)/shard_map/ppermute | solution.py:34
  140.5 60.7 %collective-permute-start.43 = (bf16[32,4096]{1,0:T(8,128)(2,1)S(1)}, bf16[32,4096]{1,0:T(8,128)(2,1)S(1)}, u32[]{:S(2)}, u32[]{:S(2)}) collective-permute-start(bf16[32,4096]{1,0:T(8,128)(2,1)S(1)} %get-tuple-element.63), channel_id=1, source_target_pairs={{0,6},{2,4},{4,10},{6,8},{8,14},{10,12},{12,2},{14,0},{1,7},{3,5},... | collective-permute-start | bytes 786440 | tf_op jit(solution)/shard_map/ppermute | solution.py:34
  141.2 60.1 %collective-permute-start.42 = (bf16[32,4096]{1,0:T(8,128)(2,1)S(1)}, bf16[32,4096]{1,0:T(8,128)(2,1)S(1)}, u32[]{:S(2)}, u32[]{:S(2)}) collective-permute-start(bf16[32,4096]{1,0:T(8,128)(2,1)S(1)} %get-tuple-element.64), channel_id=1, source_target_pairs={{0,4},{2,6},{4,8},{6,10},{8,12},{10,14},{12,0},{14,2},{1,5},{3,7},... | collective-permute-start | bytes 786440 | tf_op jit(solution)/shard_map/ppermute | solution.py:34
  145.2 56.1 %collective-permute-start.41 = (bf16[32,4096]{1,0:T(8,128)(2,1)S(1)}, bf16[32,4096]{1,0:T(8,128)(2,1)S(1)}, u32[]{:S(2)}, u32[]{:S(2)}) collective-permute-start(bf16[32,4096]{1,0:T(8,128)(2,1)S(1)} %get-tuple-element.65), channel_id=1, source_target_pairs={{0,2},{2,0},{4,6},{6,4},{8,10},{10,8},{12,14},{14,12},{1,3},{3,1},... | collective-permute-start | bytes 786440 | tf_op jit(solution)/shard_map/ppermute | solution.py:34
  175.0 28.8 %collective-permute-start.63 = (bf16[32,4096]{1,0:T(8,128)(2,1)S(1)}, bf16[32,4096]{1,0:T(8,128)(2,1)S(1)}, u32[]{:S(2)}, u32[]{:S(2)}) collective-permute-start(bf16[32,4096]{1,0:T(8,128)(2,1)S(1)} %get-tuple-element.51), channel_id=1, source_target_pairs={{0,14},{2,12},{4,2},{6,0},{8,6},{10,4},{12,10},{14,8},{1,15},{3,13... | collective-permute-start | bytes 786440 | tf_op jit(solution)/shard_map/ppermute | solution.py:34
  181.0 26.2 %collective-permute-start.62 = (bf16[32,4096]{1,0:T(8,128)(2,1)S(1)}, bf16[32,4096]{1,0:T(8,128)(2,1)S(1)}, u32[]{:S(2)}, u32[]{:S(2)}) collective-permute-start(bf16[32,4096]{1,0:T(8,128)(2,1)S(1)} %get-tuple-element.52), channel_id=1, source_target_pairs={{0,12},{2,14},{4,0},{6,2},{8,4},{10,6},{12,8},{14,10},{1,13},{3,15... | collective-permute-start | bytes 786440 | tf_op jit(solution)/shard_map/ppermute | solution.py:34
  201.2 127.7 %collective-permute-start.32 = (bf16[8,32,4096]{2,1,0:T(8,128)(2,1)S(1)}, bf16[8,32,4096]{2,1,0:T(8,128)(2,1)}, u32[]{:S(2)}, u32[]{:S(2)}) collective-permute-start(bf16[8,32,4096]{2,1,0:T(8,128)(2,1)S(1)} %bitcast.324), channel_id=1, source_target_pairs={{0,1},{1,0},{2,3},{3,2},{4,5},{5,4},{6,7},{7,6},{8,9},{9,8},{10,11... | collective-permute-start | bytes 6291464 | tf_op jit(solution)/shard_map/ppermute | solution.py:22
  201.3 33.5 %collective-permute-start.61 = (bf16[32,4096]{1,0:T(8,128)(2,1)S(1)}, bf16[32,4096]{1,0:T(8,128)(2,1)S(1)}, u32[]{:S(2)}, u32[]{:S(2)}) collective-permute-start(bf16[32,4096]{1,0:T(8,128)(2,1)S(1)} %get-tuple-element.53), channel_id=1, source_target_pairs={{0,10},{2,8},{4,14},{6,12},{8,2},{10,0},{12,6},{14,4},{1,11},{3,9}... | collective-permute-start | bytes 786440 | tf_op jit(solution)/shard_map/ppermute | solution.py:34
  201.4 37.3 %collective-permute-start.60 = (bf16[32,4096]{1,0:T(8,128)(2,1)S(1)}, bf16[32,4096]{1,0:T(8,128)(2,1)S(1)}, u32[]{:S(2)}, u32[]{:S(2)}) collective-permute-start(bf16[32,4096]{1,0:T(8,128)(2,1)S(1)} %get-tuple-element.54), channel_id=1, source_target_pairs={{0,8},{2,10},{4,12},{6,14},{8,0},{10,2},{12,4},{14,6},{1,9},{3,11}... | collective-permute-start | bytes 786440 | tf_op jit(solution)/shard_map/ppermute | solution.py:34
  203.9 34.7 %collective-permute-start.59 = (bf16[32,4096]{1,0:T(8,128)(2,1)S(1)}, bf16[32,4096]{1,0:T(8,128)(2,1)S(1)}, u32[]{:S(2)}, u32[]{:S(2)}) collective-permute-start(bf16[32,4096]{1,0:T(8,128)(2,1)S(1)} %get-tuple-element.55), channel_id=1, source_target_pairs={{0,6},{2,4},{4,10},{6,8},{8,14},{10,12},{12,2},{14,0},{1,7},{3,5},... | collective-permute-start | bytes 786440 | tf_op jit(solution)/shard_map/ppermute | solution.py:34
  207.2 33.7 %collective-permute-start.58 = (bf16[32,4096]{1,0:T(8,128)(2,1)S(1)}, bf16[32,4096]{1,0:T(8,128)(2,1)S(1)}, u32[]{:S(2)}, u32[]{:S(2)}) collective-permute-start(bf16[32,4096]{1,0:T(8,128)(2,1)S(1)} %get-tuple-element.56), channel_id=1, source_target_pairs={{0,4},{2,6},{4,8},{6,10},{8,12},{10,14},{12,0},{14,2},{1,5},{3,7},... | collective-permute-start | bytes 786440 | tf_op jit(solution)/shard_map/ppermute | solution.py:34
  238.6 17.2 %collective-permute-start.78 = (bf16[32,4096]{1,0:T(8,128)(2,1)S(1)}, bf16[32,4096]{1,0:T(8,128)(2,1)S(1)}, u32[]{:S(2)}, u32[]{:S(2)}) collective-permute-start(bf16[32,4096]{1,0:T(8,128)(2,1)S(1)} %get-tuple-element.44), channel_id=1, source_target_pairs={{0,12},{2,14},{4,0},{6,2},{8,4},{10,6},{12,8},{14,10},{1,13},{3,15... | collective-permute-start | bytes 786440 | tf_op jit(solution)/shard_map/ppermute | solution.py:34
  240.9 39.4 %collective-permute-start.77 = (bf16[32,4096]{1,0:T(8,128)(2,1)S(1)}, bf16[32,4096]{1,0:T(8,128)(2,1)S(1)}, u32[]{:S(2)}, u32[]{:S(2)}) collective-permute-start(bf16[32,4096]{1,0:T(8,128)(2,1)S(1)} %get-tuple-element.45), channel_id=1, source_target_pairs={{0,10},{2,8},{4,14},{6,12},{8,2},{10,0},{12,6},{14,4},{1,11},{3,9}... | collective-permute-start | bytes 786440 | tf_op jit(solution)/shard_map/ppermute | solution.py:34
  246.6 65.6 %collective-permute-start.76 = (bf16[32,4096]{1,0:T(8,128)(2,1)}, bf16[32,4096]{1,0:T(8,128)(2,1)S(1)}, u32[]{:S(2)}, u32[]{:S(2)}) collective-permute-start(bf16[32,4096]{1,0:T(8,128)(2,1)} %get-tuple-element.46), channel_id=1, source_target_pairs={{0,8},{2,10},{4,12},{6,14},{8,0},{10,2},{12,4},{14,6},{1,9},{3,11}... | collective-permute-start | bytes 786440 | tf_op jit(solution)/shard_map/ppermute | solution.py:34
  248.7 63.6 %collective-permute-start.75 = (bf16[32,4096]{1,0:T(8,128)(2,1)}, bf16[32,4096]{1,0:T(8,128)(2,1)S(1)}, u32[]{:S(2)}, u32[]{:S(2)}) collective-permute-start(bf16[32,4096]{1,0:T(8,128)(2,1)} %get-tuple-element.47), channel_id=1, source_target_pairs={{0,6},{2,4},{4,10},{6,8},{8,14},{10,12},{12,2},{14,0},{1,7},{3,5},... | collective-permute-start | bytes 786440 | tf_op jit(solution)/shard_map/ppermute | solution.py:34
  255.8 57.0 %collective-permute-start.74 = (bf16[32,4096]{1,0:T(8,128)(2,1)}, bf16[32,4096]{1,0:T(8,128)(2,1)S(1)}, u32[]{:S(2)}, u32[]{:S(2)}) collective-permute-start(bf16[32,4096]{1,0:T(8,128)(2,1)} %get-tuple-element.48), channel_id=1, source_target_pairs={{0,4},{2,6},{4,8},{6,10},{8,12},{10,14},{12,0},{14,2},{1,5},{3,7},... | collective-permute-start | bytes 786440 | tf_op jit(solution)/shard_map/ppermute | solution.py:34
  280.3 32.5 %collective-permute-start.73 = (bf16[32,4096]{1,0:T(8,128)(2,1)}, bf16[32,4096]{1,0:T(8,128)(2,1)S(1)}, u32[]{:S(2)}, u32[]{:S(2)}) collective-permute-start(bf16[32,4096]{1,0:T(8,128)(2,1)} %get-tuple-element.49), channel_id=1, source_target_pairs={{0,2},{2,0},{4,6},{6,4},{8,10},{10,8},{12,14},{14,12},{1,3},{3,1},... | collective-permute-start | bytes 786440 | tf_op jit(solution)/shard_map/ppermute | solution.py:34
  312.2 74.8 %collective-permute-start.48 = (bf16[8,32,4096]{2,1,0:T(8,128)(2,1)S(1)}, bf16[8,32,4096]{2,1,0:T(8,128)(2,1)}, u32[]{:S(2)}, u32[]{:S(2)}) collective-permute-start(bf16[8,32,4096]{2,1,0:T(8,128)(2,1)S(1)} %bitcast.325), channel_id=1, source_target_pairs={{0,1},{1,0},{2,3},{3,2},{4,5},{5,4},{6,7},{7,6},{8,9},{9,8},{10,11... | collective-permute-start | bytes 6291464 | tf_op jit(solution)/shard_map/ppermute | solution.py:22
  312.3 74.8 %collective-permute-start.64 = (bf16[8,32,4096]{2,1,0:T(8,128)(2,1)S(1)}, bf16[8,32,4096]{2,1,0:T(8,128)(2,1)}, u32[]{:S(2)}, u32[]{:S(2)}) collective-permute-start(bf16[8,32,4096]{2,1,0:T(8,128)(2,1)S(1)} %bitcast.326), channel_id=1, source_target_pairs={{0,1},{1,0},{2,3},{3,2},{4,5},{5,4},{6,7},{7,6},{8,9},{9,8},{10,11... | collective-permute-start | bytes 6291464 | tf_op jit(solution)/shard_map/ppermute | solution.py:22
  328.7 36.3 %collective-permute-start.80 = (bf16[8,32,4096]{2,1,0:T(8,128)(2,1)S(1)}, bf16[8,32,4096]{2,1,0:T(8,128)(2,1)S(1)}, u32[]{:S(2)}, u32[]{:S(2)}) collective-permute-start(bf16[8,32,4096]{2,1,0:T(8,128)(2,1)S(1)} %bitcast.327), channel_id=1, source_target_pairs={{0,1},{1,0},{2,3},{3,2},{4,5},{5,4},{6,7},{7,6},{8,9},{9,8},{10,11... | collective-permute-start | bytes 6291464 | tf_op jit(solution)/shard_map/ppermute | solution.py:22
  331.1 18.1 %collective-permute-start.38 = (bf16[32,4096]{1,0:T(8,128)(2,1)S(1)}, bf16[32,4096]{1,0:T(8,128)(2,1)S(1)}, u32[]{:S(2)}, u32[]{:S(2)}) collective-permute-start(bf16[32,4096]{1,0:T(8,128)(2,1)S(1)} %get-tuple-element.100), channel_id=1, source_target_pairs={{0,4},{2,6},{4,8},{6,10},{8,12},{10,14},{12,0},{14,2},{1,5},{3,7},... | collective-permute-start | bytes 786440 | tf_op jit(solution)/shard_map/ppermute | solution.py:34
  343.0 22.0 %collective-permute-start.37 = (bf16[32,4096]{1,0:T(8,128)(2,1)S(1)}, bf16[32,4096]{1,0:T(8,128)(2,1)S(1)}, u32[]{:S(2)}, u32[]{:S(2)}) collective-permute-start(bf16[32,4096]{1,0:T(8,128)(2,1)S(1)} %get-tuple-element.101), channel_id=1, source_target_pairs={{0,10},{2,8},{4,14},{6,12},{8,2},{10,0},{12,6},{14,4},{1,11},{3,9}... | collective-permute-start | bytes 786440 | tf_op jit(solution)/shard_map/ppermute | solution.py:34
  349.2 22.0 %collective-permute-start.36 = (bf16[32,4096]{1,0:T(8,128)(2,1)S(1)}, bf16[32,4096]{1,0:T(8,128)(2,1)S(1)}, u32[]{:S(2)}, u32[]{:S(2)}) collective-permute-start(bf16[32,4096]{1,0:T(8,128)(2,1)S(1)} %get-tuple-element.102), channel_id=1, source_target_pairs={{0,8},{2,10},{4,12},{6,14},{8,0},{10,2},{12,4},{14,6},{1,9},{3,11}... | collective-permute-start | bytes 786440 | tf_op jit(solution)/shard_map/ppermute | solution.py:34
  365.0 17.3 %collective-permute-start.34 = (bf16[32,4096]{1,0:T(8,128)(2,1)S(1)}, bf16[32,4096]{1,0:T(8,128)(2,1)S(1)}, u32[]{:S(2)}, u32[]{:S(2)}) collective-permute-start(bf16[32,4096]{1,0:T(8,128)(2,1)S(1)} %get-tuple-element.104), channel_id=1, source_target_pairs={{0,12},{2,14},{4,0},{6,2},{8,4},{10,6},{12,8},{14,10},{1,13},{3,15... | collective-permute-start | bytes 786440 | tf_op jit(solution)/shard_map/ppermute | solution.py:34
  376.3 12.3 %collective-permute-start.84 = (bf16[32,1024]{1,0:T(8,128)(2,1)S(1)}, bf16[32,1024]{1,0:T(8,128)(2,1)S(1)}, u32[]{:S(2)}, u32[]{:S(2)}) collective-permute-start(bf16[32,1024]{1,0:T(8,128)(2,1)S(1)} %get-tuple-element.38), channel_id=1, source_target_pairs={{0,8},{2,10},{4,12},{6,14},{8,0},{10,2},{12,4},{14,6},{1,9},{3,11}... | collective-permute-start | bytes 196616 | tf_op jit(solution)/shard_map/ppermute | solution.py:34
  382.6 15.0 %collective-permute-start.92 = (bf16[32,1024]{1,0:T(8,128)(2,1)S(1)}, bf16[32,1024]{1,0:T(8,128)(2,1)S(1)}, u32[]{:S(2)}, u32[]{:S(2)}) collective-permute-start(bf16[32,1024]{1,0:T(8,128)(2,1)S(1)} %get-tuple-element.29), channel_id=1, source_target_pairs={{0,10},{2,8},{4,14},{6,12},{8,2},{10,0},{12,6},{14,4},{1,11},{3,9}... | collective-permute-start | bytes 196616 | tf_op jit(solution)/shard_map/ppermute | solution.py:34
  387.1 15.1 %collective-permute-start.108 = (bf16[32,1024]{1,0:T(8,128)(2,1)S(1)}, bf16[32,1024]{1,0:T(8,128)(2,1)S(1)}, u32[]{:S(2)}, u32[]{:S(2)}) collective-permute-start(bf16[32,1024]{1,0:T(8,128)(2,1)S(1)} %get-tuple-element.11), channel_id=1, source_target_pairs={{0,6},{2,4},{4,10},{6,8},{8,14},{10,12},{12,2},{14,0},{1,7},{3,5},... | collective-permute-start | bytes 196616 | tf_op jit(solution)/shard_map/ppermute | solution.py:34
  388.5 13.6 %collective-permute-start.107 = (bf16[32,1024]{1,0:T(8,128)(2,1)S(1)}, bf16[32,1024]{1,0:T(8,128)(2,1)S(1)}, u32[]{:S(2)}, u32[]{:S(2)}) collective-permute-start(bf16[32,1024]{1,0:T(8,128)(2,1)S(1)} %get-tuple-element.12), channel_id=1, source_target_pairs={{0,4},{2,6},{4,8},{6,10},{8,12},{10,14},{12,0},{14,2},{1,5},{3,7},... | collective-permute-start | bytes 196616 | tf_op jit(solution)/shard_map/ppermute | solution.py:34
  390.1 13.4 %collective-permute-start.106 = (bf16[32,1024]{1,0:T(8,128)(2,1)S(1)}, bf16[32,1024]{1,0:T(8,128)(2,1)S(1)}, u32[]{:S(2)}, u32[]{:S(2)}) collective-permute-start(bf16[32,1024]{1,0:T(8,128)(2,1)S(1)} %get-tuple-element.13), channel_id=1, source_target_pairs={{0,10},{2,8},{4,14},{6,12},{8,2},{10,0},{12,6},{14,4},{1,11},{3,9}... | collective-permute-start | bytes 196616 | tf_op jit(solution)/shard_map/ppermute | solution.py:34
  402.1 25.6 %collective-permute-start.102 = (bf16[32,1024]{1,0:T(8,128)(2,1)S(1)}, bf16[32,1024]{1,0:T(8,128)(2,1)S(1)}, u32[]{:S(2)}, u32[]{:S(2)}) collective-permute-start(bf16[32,1024]{1,0:T(8,128)(2,1)S(1)} %get-tuple-element.17), channel_id=1, source_target_pairs={{0,2},{2,0},{4,6},{6,4},{8,10},{10,8},{12,14},{14,12},{1,3},{3,1},... | collective-permute-start | bytes 196616 | tf_op jit(solution)/shard_map/ppermute | solution.py:34
  403.5 24.2 %collective-permute-start.101 = (bf16[32,1024]{1,0:T(8,128)(2,1)S(1)}, bf16[32,1024]{1,0:T(8,128)(2,1)S(1)}, u32[]{:S(2)}, u32[]{:S(2)}) collective-permute-start(bf16[32,1024]{1,0:T(8,128)(2,1)S(1)} %get-tuple-element.19), channel_id=1, source_target_pairs={{0,6},{2,4},{4,10},{6,8},{8,14},{10,12},{12,2},{14,0},{1,7},{3,5},... | collective-permute-start | bytes 196616 | tf_op jit(solution)/shard_map/ppermute | solution.py:34
  405.9 24.2 %collective-permute-start.100 = (bf16[32,1024]{1,0:T(8,128)(2,1)S(1)}, bf16[32,1024]{1,0:T(8,128)(2,1)S(1)}, u32[]{:S(2)}, u32[]{:S(2)}) collective-permute-start(bf16[32,1024]{1,0:T(8,128)(2,1)S(1)} %get-tuple-element.20), channel_id=1, source_target_pairs={{0,4},{2,6},{4,8},{6,10},{8,12},{10,14},{12,0},{14,2},{1,5},{3,7},... | collective-permute-start | bytes 196616 | tf_op jit(solution)/shard_map/ppermute | solution.py:34
  406.5 26.9 %collective-permute-start.71 = (bf16[32,4096]{1,0:T(8,128)(2,1)S(1)}, bf16[32,4096]{1,0:T(8,128)(2,1)S(1)}, u32[]{:S(2)}, u32[]{:S(2)}) collective-permute-start(bf16[32,4096]{1,0:T(8,128)(2,1)S(1)} %get-tuple-element.67), channel_id=1, source_target_pairs={{0,6},{2,4},{4,10},{6,8},{8,14},{10,12},{12,2},{14,0},{1,7},{3,5},... | collective-permute-start | bytes 786440 | tf_op jit(solution)/shard_map/ppermute | solution.py:34
  408.5 26.9 %collective-permute-start.70 = (bf16[32,4096]{1,0:T(8,128)(2,1)S(1)}, bf16[32,4096]{1,0:T(8,128)(2,1)S(1)}, u32[]{:S(2)}, u32[]{:S(2)}) collective-permute-start(bf16[32,4096]{1,0:T(8,128)(2,1)S(1)} %get-tuple-element.68), channel_id=1, source_target_pairs={{0,4},{2,6},{4,8},{6,10},{8,12},{10,14},{12,0},{14,2},{1,5},{3,7},... | collective-permute-start | bytes 786440 | tf_op jit(solution)/shard_map/ppermute | solution.py:34
  427.7 18.9 %collective-permute-start.69 = (bf16[32,4096]{1,0:T(8,128)(2,1)S(1)}, bf16[32,4096]{1,0:T(8,128)(2,1)S(1)}, u32[]{:S(2)}, u32[]{:S(2)}) collective-permute-start(bf16[32,4096]{1,0:T(8,128)(2,1)S(1)} %get-tuple-element.69), channel_id=1, source_target_pairs={{0,10},{2,8},{4,14},{6,12},{8,2},{10,0},{12,6},{14,4},{1,11},{3,9}... | collective-permute-start | bytes 786440 | tf_op jit(solution)/shard_map/ppermute | solution.py:34
  427.8 22.5 %collective-permute-start.68 = (bf16[32,4096]{1,0:T(8,128)(2,1)S(1)}, bf16[32,4096]{1,0:T(8,128)(2,1)S(1)}, u32[]{:S(2)}, u32[]{:S(2)}) collective-permute-start(bf16[32,4096]{1,0:T(8,128)(2,1)S(1)} %get-tuple-element.70), channel_id=1, source_target_pairs={{0,8},{2,10},{4,12},{6,14},{8,0},{10,2},{12,4},{14,6},{1,9},{3,11}... | collective-permute-start | bytes 786440 | tf_op jit(solution)/shard_map/ppermute | solution.py:34
  430.1 29.6 %collective-permute-start.67 = (bf16[32,4096]{1,0:T(8,128)(2,1)S(1)}, bf16[32,4096]{1,0:T(8,128)(2,1)S(1)}, u32[]{:S(2)}, u32[]{:S(2)}) collective-permute-start(bf16[32,4096]{1,0:T(8,128)(2,1)S(1)} %get-tuple-element.71), channel_id=1, source_target_pairs={{0,14},{2,12},{4,2},{6,0},{8,6},{10,4},{12,10},{14,8},{1,15},{3,13... | collective-permute-start | bytes 786440 | tf_op jit(solution)/shard_map/ppermute | solution.py:34
  433.4 26.6 %collective-permute-start.66 = (bf16[32,4096]{1,0:T(8,128)(2,1)S(1)}, bf16[32,4096]{1,0:T(8,128)(2,1)S(1)}, u32[]{:S(2)}, u32[]{:S(2)}) collective-permute-start(bf16[32,4096]{1,0:T(8,128)(2,1)S(1)} %get-tuple-element.72), channel_id=1, source_target_pairs={{0,12},{2,14},{4,0},{6,2},{8,4},{10,6},{12,8},{14,10},{1,13},{3,15... | collective-permute-start | bytes 786440 | tf_op jit(solution)/shard_map/ppermute | solution.py:34
  435.4 35.3 %collective-permute-start.65 = (bf16[32,4096]{1,0:T(8,128)(2,1)S(1)}, bf16[32,4096]{1,0:T(8,128)(2,1)S(1)}, u32[]{:S(2)}, u32[]{:S(2)}) collective-permute-start(bf16[32,4096]{1,0:T(8,128)(2,1)S(1)} %get-tuple-element.73), channel_id=1, source_target_pairs={{0,2},{2,0},{4,6},{6,4},{8,10},{10,8},{12,14},{14,12},{1,3},{3,1},... | collective-permute-start | bytes 786440 | tf_op jit(solution)/shard_map/ppermute | solution.py:34
  446.7 31.5 %collective-permute-start.55 = (bf16[32,4096]{1,0:T(8,128)(2,1)S(1)}, bf16[32,4096]{1,0:T(8,128)(2,1)S(1)}, u32[]{:S(2)}, u32[]{:S(2)}) collective-permute-start(bf16[32,4096]{1,0:T(8,128)(2,1)S(1)} %get-tuple-element.83), channel_id=1, source_target_pairs={{0,6},{2,4},{4,10},{6,8},{8,14},{10,12},{12,2},{14,0},{1,7},{3,5},... | collective-permute-start | bytes 786440 | tf_op jit(solution)/shard_map/ppermute | solution.py:34
  450.3 27.9 %collective-permute-start.54 = (bf16[32,4096]{1,0:T(8,128)(2,1)S(1)}, bf16[32,4096]{1,0:T(8,128)(2,1)S(1)}, u32[]{:S(2)}, u32[]{:S(2)}) collective-permute-start(bf16[32,4096]{1,0:T(8,128)(2,1)S(1)} %get-tuple-element.84), channel_id=1, source_target_pairs={{0,4},{2,6},{4,8},{6,10},{8,12},{10,14},{12,0},{14,2},{1,5},{3,7},... | collective-permute-start | bytes 786440 | tf_op jit(solution)/shard_map/ppermute | solution.py:34
  459.7 24.8 %collective-permute-start.53 = (bf16[32,4096]{1,0:T(8,128)(2,1)S(1)}, bf16[32,4096]{1,0:T(8,128)(2,1)S(1)}, u32[]{:S(2)}, u32[]{:S(2)}) collective-permute-start(bf16[32,4096]{1,0:T(8,128)(2,1)S(1)} %get-tuple-element.85), channel_id=1, source_target_pairs={{0,10},{2,8},{4,14},{6,12},{8,2},{10,0},{12,6},{14,4},{1,11},{3,9}... | collective-permute-start | bytes 786440 | tf_op jit(solution)/shard_map/ppermute | solution.py:34
  460.0 28.1 %collective-permute-start.52 = (bf16[32,4096]{1,0:T(8,128)(2,1)S(1)}, bf16[32,4096]{1,0:T(8,128)(2,1)S(1)}, u32[]{:S(2)}, u32[]{:S(2)}) collective-permute-start(bf16[32,4096]{1,0:T(8,128)(2,1)S(1)} %get-tuple-element.86), channel_id=1, source_target_pairs={{0,8},{2,10},{4,12},{6,14},{8,0},{10,2},{12,4},{14,6},{1,9},{3,11}... | collective-permute-start | bytes 786440 | tf_op jit(solution)/shard_map/ppermute | solution.py:34
  470.7 19.5 %collective-permute-start.51 = (bf16[32,4096]{1,0:T(8,128)(2,1)S(1)}, bf16[32,4096]{1,0:T(8,128)(2,1)S(1)}, u32[]{:S(2)}, u32[]{:S(2)}) collective-permute-start(bf16[32,4096]{1,0:T(8,128)(2,1)S(1)} %get-tuple-element.87), channel_id=1, source_target_pairs={{0,14},{2,12},{4,2},{6,0},{8,6},{10,4},{12,10},{14,8},{1,15},{3,13... | collective-permute-start | bytes 786440 | tf_op jit(solution)/shard_map/ppermute | solution.py:34
  478.2 26.5 %collective-permute-start.50 = (bf16[32,4096]{1,0:T(8,128)(2,1)S(1)}, bf16[32,4096]{1,0:T(8,128)(2,1)S(1)}, u32[]{:S(2)}, u32[]{:S(2)}) collective-permute-start(bf16[32,4096]{1,0:T(8,128)(2,1)S(1)} %get-tuple-element.88), channel_id=1, source_target_pairs={{0,12},{2,14},{4,0},{6,2},{8,4},{10,6},{12,8},{14,10},{1,13},{3,15... | collective-permute-start | bytes 786440 | tf_op jit(solution)/shard_map/ppermute | solution.py:34
  478.2 26.5 %collective-permute-start.49 = (bf16[32,4096]{1,0:T(8,128)(2,1)S(1)}, bf16[32,4096]{1,0:T(8,128)(2,1)S(1)}, u32[]{:S(2)}, u32[]{:S(2)}) collective-permute-start(bf16[32,4096]{1,0:T(8,128)(2,1)S(1)} %get-tuple-element.89), channel_id=1, source_target_pairs={{0,2},{2,0},{4,6},{6,4},{8,10},{10,8},{12,14},{14,12},{1,3},{3,1},... | collective-permute-start | bytes 786440 | tf_op jit(solution)/shard_map/ppermute | solution.py:34
  484.5 26.0 %collective-permute-start.99 = (bf16[32,1024]{1,0:T(8,128)(2,1)S(1)}, bf16[32,1024]{1,0:T(8,128)(2,1)S(1)}, u32[]{:S(2)}, u32[]{:S(2)}) collective-permute-start(bf16[32,1024]{1,0:T(8,128)(2,1)S(1)} %get-tuple-element.21), channel_id=1, source_target_pairs={{0,10},{2,8},{4,14},{6,12},{8,2},{10,0},{12,6},{14,4},{1,11},{3,9}... | collective-permute-start | bytes 196616 | tf_op jit(solution)/shard_map/ppermute | solution.py:34
  488.1 26.5 %collective-permute-start.98 = (bf16[32,1024]{1,0:T(8,128)(2,1)S(1)}, bf16[32,1024]{1,0:T(8,128)(2,1)S(1)}, u32[]{:S(2)}, u32[]{:S(2)}) collective-permute-start(bf16[32,1024]{1,0:T(8,128)(2,1)S(1)} %get-tuple-element.22), channel_id=1, source_target_pairs={{0,8},{2,10},{4,12},{6,14},{8,0},{10,2},{12,4},{14,6},{1,9},{3,11}... | collective-permute-start | bytes 196616 | tf_op jit(solution)/shard_map/ppermute | solution.py:34
  490.2 24.5 %collective-permute-start.97 = (bf16[32,1024]{1,0:T(8,128)(2,1)S(1)}, bf16[32,1024]{1,0:T(8,128)(2,1)S(1)}, u32[]{:S(2)}, u32[]{:S(2)}) collective-permute-start(bf16[32,1024]{1,0:T(8,128)(2,1)S(1)} %get-tuple-element.23), channel_id=1, source_target_pairs={{0,14},{2,12},{4,2},{6,0},{8,6},{10,4},{12,10},{14,8},{1,15},{3,13... | collective-permute-start | bytes 196616 | tf_op jit(solution)/shard_map/ppermute | solution.py:34
  504.7 13.4 %collective-permute-start.95 = (bf16[32,1024]{1,0:T(8,128)(2,1)S(1)}, bf16[32,1024]{1,0:T(8,128)(2,1)S(1)}, u32[]{:S(2)}, u32[]{:S(2)}) collective-permute-start(bf16[32,1024]{1,0:T(8,128)(2,1)S(1)} %get-tuple-element.25), channel_id=1, source_target_pairs={{0,2},{2,0},{4,6},{6,4},{8,10},{10,8},{12,14},{14,12},{1,3},{3,1},... | collective-permute-start | bytes 196616 | tf_op jit(solution)/shard_map/ppermute | solution.py:34
  510.5 12.8 %collective-permute-start.90 = (bf16[32,1024]{1,0:T(8,128)(2,1)S(1)}, bf16[32,1024]{1,0:T(8,128)(2,1)S(1)}, u32[]{:S(2)}, u32[]{:S(2)}) collective-permute-start(bf16[32,1024]{1,0:T(8,128)(2,1)S(1)} %get-tuple-element.31), channel_id=1, source_target_pairs={{0,14},{2,12},{4,2},{6,0},{8,6},{10,4},{12,10},{14,8},{1,15},{3,13... | collective-permute-start | bytes 196616 | tf_op jit(solution)/shard_map/ppermute | solution.py:34
  514.6 12.5 %collective-permute-start.89 = (bf16[32,1024]{1,0:T(8,128)(2,1)S(1)}, bf16[32,1024]{1,0:T(8,128)(2,1)S(1)}, u32[]{:S(2)}, u32[]{:S(2)}) collective-permute-start(bf16[32,1024]{1,0:T(8,128)(2,1)S(1)} %get-tuple-element.32), channel_id=1, source_target_pairs={{0,12},{2,14},{4,0},{6,2},{8,4},{10,6},{12,8},{14,10},{1,13},{3,15... | collective-permute-start | bytes 196616 | tf_op jit(solution)/shard_map/ppermute | solution.py:34
  514.7 12.8 %collective-permute-start.88 = (bf16[32,1024]{1,0:T(8,128)(2,1)S(1)}, bf16[32,1024]{1,0:T(8,128)(2,1)S(1)}, u32[]{:S(2)}, u32[]{:S(2)}) collective-permute-start(bf16[32,1024]{1,0:T(8,128)(2,1)S(1)} %get-tuple-element.33), channel_id=1, source_target_pairs={{0,2},{2,0},{4,6},{6,4},{8,10},{10,8},{12,14},{14,12},{1,3},{3,1},... | collective-permute-start | bytes 196616 | tf_op jit(solution)/shard_map/ppermute | solution.py:34
  515.2 12.3 %collective-permute-start.94 = (bf16[32,1024]{1,0:T(8,128)(2,1)S(1)}, bf16[32,1024]{1,0:T(8,128)(2,1)S(1)}, u32[]{:S(2)}, u32[]{:S(2)}) collective-permute-start(bf16[32,1024]{1,0:T(8,128)(2,1)S(1)} %get-tuple-element.27), channel_id=1, source_target_pairs={{0,6},{2,4},{4,10},{6,8},{8,14},{10,12},{12,2},{14,0},{1,7},{3,5},... | collective-permute-start | bytes 196616 | tf_op jit(solution)/shard_map/ppermute | solution.py:34
  523.3 14.9 %collective-permute-start.82 = (bf16[32,1024]{1,0:T(8,128)(2,1)S(1)}, bf16[32,1024]{1,0:T(8,128)(2,1)S(1)}, u32[]{:S(2)}, u32[]{:S(2)}) collective-permute-start(bf16[32,1024]{1,0:T(8,128)(2,1)S(1)} %get-tuple-element.40), channel_id=1, source_target_pairs={{0,12},{2,14},{4,0},{6,2},{8,4},{10,6},{12,8},{14,10},{1,13},{3,15... | collective-permute-start | bytes 196616 | tf_op jit(solution)/shard_map/ppermute | solution.py:34
  (83 other events, 1399.7 us)
where the time goes:
time: 553 us; the launch traced here: 544 us
  waiting for transfers between devices  195 us (35%)
  starting transfers between devices  175 us (32%)
  Pallas kernels  116 us (21%)
  other arithmetic  34.7 us (6%)
  local copies, waits for them, and re-layouts  22.6 us (4%)
    ppermute x98, waiting for transfers between devices, shift_places(): return lax.ppermute(value, EXCHANGE_AXES, pairs)  195 us
    ppermute x98, starting transfers between devices, shift_places(): return lax.ppermute(value, EXCHANGE_AXES, pairs)  172 us
    pallas_call x4, Pallas kernels, columns_fused(): pl.pallas_call(functools.partial(column_kernel, sizes), out_shape=jax.Sha...  64.3 us
    pallas_call x5, Pallas kernels, fourier(): pl.pallas_call(fourier_kernel, out_shape=[jax.ShapeDtypeStruct((height, w...  22.7 us
    pallas_call x4, Pallas kernels, inverse_fourier(): pl.pallas_call(functools.partial(inverse_kernel, len(pieces)), out_shape=...  20.8 us
    unnamed x77, local copies, waits for them, and re-layouts  17.9 us
    convert_element_type x7, other arithmetic, send(): mirrored = (other[rows].astype(jnp.float32) + hemi_sign * value[rows].ast...  16.3 us
  transfers between devices with their start and end apart: 109, of which 30 were waited for; matrix products, arithmetic and copies ran while one was open for 6% of the time, Pallas kernels for 19%

commit v1 on v0

v1 whole, which is shorter than its diff:
```python
import functools
import math

import jax
import jax.numpy as jnp
from jax import lax
from jax.experimental import pallas as pl
from jax.experimental.pallas import tpu as pltpu
from jax.sharding import PartitionSpec as P


tau_scale = 2.0
LANES = 128
CHUNKS = 4
WHOLE_SENDS = (0, 2)
WHOLE_BACKS = (0, 2)
DIRECT_LIMIT = 16
EXCHANGE_AXES = ("wave", "level")


def partner(value, axis):
    pairs = [(source, source ^ 1) for source in range(lax.axis_size(axis))]
    return lax.ppermute(value, axis, pairs)


def shift_places(value, wave_shift, level_shift):
    if wave_shift == 0 and level_shift == 0:
        return value
    waves, levels = lax.axis_size("wave"), lax.axis_size("level")
    pairs = []
    for wave in range(waves):
        for level in range(levels):
            target = (wave + wave_shift) % waves * levels + (level + level_shift) % levels
            pairs.append((wave * levels + level, target))
    return lax.ppermute(value, EXCHANGE_AXES, pairs)


def rolled(value, start):
    return lax.dynamic_slice_in_dim(
        jnp.concatenate([value, value], axis=0), start, value.shape[0], axis=0
    )


def phase_of(product, period):
    return (product % period).astype(jnp.float32) * (2.0 * math.pi / period)


def level_block(levels, rows_here):
    return 8 if levels % 8 == 0 and 8 * rows_here % LANES == 0 else levels


def fourier_kernel(scale, grid_ref, coupling, high_cos, high_sin, low_cos, low_sin, out, table):
    levels, rows, lon_count = grid_ref.shape

    @pl.when(pl.program_id(0) == 0)
    def _():
        for block in range(lon_count // LANES):
            values = (
                high_cos[:, block : block + 1] * low_cos[...]
                - high_sin[:, block : block + 1] * low_sin[...]
            )
            table[:, block * LANES : (block + 1) * LANES] = (values * scale).astype(table.dtype)

    field = grid_ref[...].astype(jnp.float32)
    forcing = (field + coupling[...][None] * jnp.tanh(field)).astype(jnp.bfloat16)
    forcing = forcing.reshape(levels * rows, lon_count)
    out[...] = lax.dot_general(
        table[...], forcing, (((1,), (1,)), ((), ())), preferred_element_type=jnp.float32
    ).astype(out.dtype)


def fourier(grid_state, coupling, ids, quarter):
    levels, rows_here, lon_count = grid_state.shape
    height = ids.shape[0]
    blocks = lon_count // LANES
    high = phase_of(
        ids[:, None] * LANES * jnp.arange(blocks, dtype=jnp.int32)[None, :] + quarter[:, None],
        lon_count,
    )
    low = phase_of(ids[:, None] * jnp.arange(LANES, dtype=jnp.int32)[None, :], lon_count)
    block = level_block(levels, rows_here)
    width = levels * rows_here
    whole = lambda *shape: pl.BlockSpec(shape, lambda i: (0,) * len(shape))
    return pl.pallas_call(
        functools.partial(fourier_kernel, math.sqrt(2.0 / lon_count)),
        out_shape=[
            jax.ShapeDtypeStruct((height, width), jnp.bfloat16),
            jax.ShapeDtypeStruct((height, lon_count), jnp.bfloat16),
        ],
        grid=(levels // block,),
        in_specs=[
            pl.BlockSpec((block, rows_here, lon_count), lambda i: (i, 0, 0)),
            whole(rows_here, 1),
            whole(height, blocks),
            whole(height, blocks),
            whole(height, LANES),
            whole(height, LANES),
        ],
        out_specs=[
            pl.BlockSpec((height, block * rows_here), lambda i: (0, i)),
            whole(height, lon_count),
        ],
        compiler_params=pltpu.CompilerParams(vmem_limit_bytes=56 * 2**20),
        cost_estimate=pl.CostEstimate(
            flops=2 * height * width * lon_count,
            bytes_accessed=2 * (width * lon_count + height * (width + lon_count)),
            transcendentals=width * lon_count,
        ),
    )(grid_state, coupling, jnp.cos(high), jnp.sin(high), jnp.cos(low), jnp.sin(low))


def inverse_kernel(pieces, tables, *refs):
    out = refs[-1]
    coeffs = jnp.concatenate([ref[...] for ref in refs[:pieces]], axis=0)
    table = jnp.concatenate([ref[...] for ref in refs[pieces : pieces + tables]], axis=0)
    current = lax.dot_general(
        coeffs, table, (((0,), (0,)), ((), ())), preferred_element_type=jnp.float32
    ).reshape(out.shape)
    if len(refs) > pieces + tables + 1:
        current = current + refs[pieces + tables][...]
    out[...] = current.astype(out.dtype)


def inverse_fourier(pieces, tables, shape, dtype, partial=None):
    levels, rows_here, lon_count = shape
    block = level_block(levels, rows_here)
    height = sum(piece.shape[0] for piece in pieces)
    grid_spec = pl.BlockSpec((block, rows_here, lon_count), lambda i: (i, 0, 0))
    partials = [] if partial is None else [partial]
    return pl.pallas_call(
        functools.partial(inverse_kernel, len(pieces), len(tables)),
        out_shape=jax.ShapeDtypeStruct(shape, dtype),
        grid=(levels // block,),
        in_specs=[
            pl.BlockSpec((piece.shape[0], block * rows_here), lambda i: (0, i)) for piece in pieces
        ]
        + [
            pl.BlockSpec(table.shape, lambda i: (0, 0), pipeline_mode=pl.Buffered(1))
            for table in tables
        ]
        + [grid_spec] * len(partials),
        out_specs=grid_spec,
        compiler_params=pltpu.CompilerParams(vmem_limit_bytes=40 * 2**20),
        cost_estimate=pl.CostEstimate(
            flops=2 * height * levels * rows_here * lon_count,
            bytes_accessed=levels * rows_here * (2 * height + 6 * lon_count),
            transcendentals=0,
        ),
    )(*pieces, *tables, *partials)


def column_kernel(sizes, waves, scalars, eig_ref, modes_in, modes_out, table, *refs):
    wave_size, level_size, group, tiles, half_count, wave_count, first = sizes
    places = wave_size * level_size
    pieces, (out, rows_in, rows_out) = refs[:-3], refs[-3:]
    eights = group // 8
    rows_here = LANES // 2
    parity = scalars[wave_size].astype(jnp.float32)
    low_half = lax.broadcasted_iota(jnp.int32, (tiles, LANES), 1) < LANES // 2

    def spread(start, part, value):
        for tile in range(tiles):
            for eight in range(eights):
                row = ((start * 2 + part) * eights + eight) * tiles + tile
                rows_in[pl.ds(pl.multiple_of(row * 8, 8), 8), :] = value(tile)[
                    eight * 8 : (eight + 1) * 8
                ]

    if len(pieces) == 2:
        own, other = pieces
        sign = 1.0 - 2.0 * parity

        def combined(index, carry):
            place, part = index // 2, index % 2

            def value(tile):
                lanes = slice(tile * LANES, (tile + 1) * LANES)
                both = other[place, part, :, lanes].astype(jnp.float32) + sign * own[
                    place, part, :, lanes
                ].astype(jnp.float32)
                return both.astype(jnp.bfloat16).astype(jnp.float32)

            spread(place, part, value)
            return carry

        lax.fori_loop(0, places * 2, combined, 0)
    else:
        for place, piece in enumerate(pieces):

            def arrived(part, carry, place=place, piece=piece):
                def value(tile):
                    return piece[part, :, tile * LANES : (tile + 1) * LANES].astype(jnp.float32)

                spread(place, part, value)
                return carry

            lax.fori_loop(0, 2, arrived, 0)

    def where_rows(place, part, slot):
        eight, within = slot // 8, slot % 8
        return pl.ds((((place * 2 + part) * eights + eight) * tiles) * 8 + within, tiles, 8)

    def one_slot(slot, carry):
        legendre = jnp.concatenate(
            [
                table[slot, pl.ds(pl.multiple_of(scalars[wave] * rows_here, rows_here), rows_here), :]
                for wave in range(wave_size)
            ],
            axis=0,
        )
        stacked = []
        for part in range(2):
            low_rows, high_rows = [], []
            for level in range(level_size):
                low_pieces, high_pieces = [], []
                for pair in range(wave_size // 2):
                    a = rows_in[where_rows(2 * pair * level_size + level, part, slot), :]
                    b = rows_in[where_rows((2 * pair + 1) * level_size + level, part, slot), :]
                    low_pieces.append(jnp.where(low_half, a, pltpu.roll(b, LANES // 2, 1)))
                    high_pieces.append(jnp.where(low_half, pltpu.roll(a, LANES // 2, 1), b))
                low_rows.append(jnp.concatenate(low_pieces, axis=1))
                high_rows.append(jnp.concatenate(high_pieces, axis=1))
            stacked += low_rows + high_rows
        field = jnp.concatenate(stacked, axis=0).astype(jnp.bfloat16)
        degree = (
            waves[first + slot] + 2 * lax.broadcasted_iota(jnp.int32, (1, half_count), 1)
        ).astype(jnp.float32) + parity
        inside = (degree <= float(wave_count - 1)).astype(jnp.float32)
        ratio = tau_scale * degree * (degree + 1.0) / float(wave_count * (wave_count - 1))
        factor = 1.0 / (1.0 + eig_ref[...] * ratio)
        spectral = jnp.dot(field, legendre, preferred_element_type=jnp.float32)
        spectral = (spectral * inside).astype(jnp.bfloat16)
        levels = modes_in.shape[0]
        solved = []
        for part in range(2):
            column = spectral[part * levels : (part + 1) * levels]
            modal = jnp.dot(modes_in[...], column, preferred_element_type=jnp.float32)
            modal = (modal * factor).astype(jnp.bfloat16)
            solved.append(
                jnp.dot(modes_out[...], modal, preferred_element_type=jnp.float32).astype(
                    jnp.bfloat16
                )
            )
        grid = lax.dot_general(
            jnp.concatenate(solved, axis=0),
            legendre,
            (((1,), (1,)), ((), ())),
            preferred_element_type=jnp.float32,
        )
        for part in range(2):
            for level in range(level_size):
                low_start = part * levels + level * tiles
                high_start = low_start + level_size * tiles
                for pair in range(wave_size // 2):
                    lanes = slice(pair * LANES, (pair + 1) * LANES)
                    low = grid[low_start : low_start + tiles, lanes]
                    high = grid[high_start : high_start + tiles, lanes]
                    a = jnp.where(low_half, low, pltpu.roll(high, LANES // 2, 1))
                    b = jnp.where(low_half, pltpu.roll(low, LANES // 2, 1), high)
                    rows_out[where_rows(2 * pair * level_size + level, part, slot), :] = a
                    rows_out[where_rows((2 * pair + 1) * level_size + level, part, slot), :] = b
        return carry

    lax.fori_loop(0, group, one_slot, 0)

    def gather(index, carry):
        place, part = index // 2, index % 2
        for tile in range(tiles):
            parts = []
            for eight in range(eights):
                start = pl.multiple_of(((index * eights + eight) * tiles + tile) * 8, 8)
                parts.append(rows_out[pl.ds(start, 8), :])
            out[place, part, :, tile * LANES : (tile + 1) * LANES] = jnp.concatenate(
                parts, axis=0
            ).astype(out.dtype)
        return carry

    lax.fori_loop(0, places * 2, gather, 0)


def columns_fused(pieces, legendre, waves, scalars, eig_rates, modes, sizes):
    wave_size, level_size, group, tiles, half_count, _, first = sizes
    places = wave_size * level_size
    half_rows = legendre.shape[1]
    width = tiles * LANES
    levels = modes[0].shape[0]
    whole = lambda shape: pl.BlockSpec(shape, lambda i: (0,) * len(shape))
    scratch = pltpu.VMEM((places * 2 * group * tiles, LANES), jnp.float32)
    values = places * 2 * group * width
    return pl.pallas_call(
        functools.partial(column_kernel, sizes),
        out_shape=jax.ShapeDtypeStruct((places, 2, group, width), jnp.bfloat16),
        grid=(1,),
        in_specs=[
            pl.BlockSpec(memory_space=pltpu.SMEM),
            pl.BlockSpec(memory_space=pltpu.SMEM),
            whole((levels, 1)),
            whole((levels, levels)),
            whole((levels, levels)),
            pl.BlockSpec((group, half_rows, half_count), lambda i: (first // group, 0, 0)),
        ]
        + [whole(piece.shape) for piece in pieces],
        out_specs=whole((places, 2, group, width)),
        scratch_shapes=[scratch, scratch],
        compiler_params=pltpu.CompilerParams(vmem_limit_bytes=40 * 2**20),
        cost_estimate=pl.CostEstimate(
            flops=values * half_rows * 6, bytes_accessed=6 * values, transcendentals=0
        ),
    )(waves, scalars, eig_rates[:, None], *modes, legendre, *pieces)


def columns_plain(mirrored, legendre, waves, parity, eig_rates, modes_in, modes_out, sizes):
    wave_size, level_size, count, first, wave_count = sizes
    levels = modes_in.shape[0]
    half_rows, half_count = legendre.shape[1:]
    local_levels, rows_here = levels // level_size, half_rows // wave_size
    shape = mirrored.shape
    mirrored = mirrored.reshape(wave_size, level_size, 2, count, local_levels, rows_here)
    field = mirrored.transpose(3, 2, 1, 4, 0, 5).reshape(count, 2, levels, half_rows)
    table = legendre[first : first + count]
    degree = (
        waves[first : first + count, None] + 2 * jnp.arange(half_count, dtype=jnp.int32)[None, :]
    ).astype(jnp.float32) + parity
    inside = (degree <= float(wave_count - 1)).astype(jnp.float32)
    ratio = tau_scale * degree * (degree + 1.0) / float(wave_count * (wave_count - 1))
    factor = 1.0 / (1.0 + ratio[:, None, :] * eig_rates[None, :, None])
    spectral = jnp.einsum("sclr,srj->sclj", field, table, preferred_element_type=jnp.float32)
    spectral = (spectral * inside[:, None, None, :]).astype(jnp.bfloat16)
    modal = jnp.einsum("kl,sclj->sckj", modes_in, spectral, preferred_element_type=jnp.float32)
    modal = (modal * factor[:, None, :, :]).astype(jnp.bfloat16)
    solved = jnp.einsum(
        "lk,sckj->sclj", modes_out, modal, preferred_element_type=jnp.float32
    ).astype(jnp.bfloat16)
    grid = jnp.einsum("sclj,srj->sclr", solved, table, preferred_element_type=jnp.float32)
    grid = grid.astype(jnp.bfloat16)
    grid = grid.reshape(count, 2, level_size, local_levels, wave_size, rows_here)
    return grid.transpose(4, 2, 1, 0, 3, 5).reshape(shape)


def shards(grid_state, legendre, wave_order, lat_order, eig_rates, modes_in, modes_out):
    out_shape = grid_state.shape
    local_levels, _, rows_here, lon_count = out_shape
    wave_size = lax.axis_size("wave")
    level_size = lax.axis_size("level")
    places = wave_size * level_size
    half_rows = lat_order.shape[0]
    wave_count = wave_order.shape[0]
    narrow, half_count = legendre.shape[0], legendre.shape[3]
    chunks = min(CHUNKS, narrow)
    count = narrow // chunks
    height = 2 * count
    width = local_levels * rows_here
    direct = (
        places <= DIRECT_LIMIT
        and rows_here * 2 == LANES
        and wave_size % 2 == 0
        and count % 16 == 0
    )
    parity = lax.axis_index("fld")
    wave_place = lax.axis_index("wave")
    level_place = lax.axis_index("level")
    place = wave_place * level_size + level_place
    legendre = legendre.reshape(narrow, half_rows, half_count)
    grid_state = grid_state.reshape(local_levels, rows_here, lon_count)
    hemi_sign = 1.0 - 2.0 * parity.astype(jnp.float32)
    lat_rows = lax.dynamic_slice_in_dim(lat_order, wave_place * rows_here, rows_here)
    sine = jnp.sin((lat_rows.astype(jnp.float32) + 0.5) * (math.pi / (2.0 * half_rows)))
    coupling = (0.5 * hemi_sign * sine)[:, None]
    waves = lax.dynamic_slice_in_dim(wave_order, place * narrow, narrow)
    quarter = jnp.broadcast_to(
        (jnp.arange(2, dtype=jnp.int32) * (lon_count // 4))[None, :, None], (places, 2, count)
    ).reshape(-1)
    fixed = wave_order.reshape(wave_size, level_size, chunks, count)
    turned = rolled(fixed, wave_place)
    turned = jnp.swapaxes(rolled(jnp.swapaxes(turned, 0, 1), level_place), 0, 1)

    def slot_ids(order, chunk):
        ids = order[:, :, chunk].reshape(places, 1, count)
        return jnp.broadcast_to(ids, (places, 2, count)).reshape(-1)

    def exchange(value):
        return lax.all_to_all(value, EXCHANGE_AXES, split_axis=0, concat_axis=0, tiled=True)

    def joined(other, own, scale):
        both = scale * (other.astype(jnp.float32) + hemi_sign * own.astype(jnp.float32))
        return both.astype(jnp.bfloat16)

    if not direct:
        returned, tables = [], []
        for chunk in range(chunks):
            value, table = fourier(grid_state, coupling, slot_ids(fixed, chunk), quarter)
            tables.append(table)
            own = exchange(value.reshape(places, height, width))
            mirrored = joined(partner(own, "fld"), own, 1.0)
            grid = columns_plain(
                mirrored.reshape(wave_size, level_size, 2, count, width),
                legendre,
                waves,
                parity.astype(jnp.float32),
                eig_rates,
                modes_in,
                modes_out,
                (wave_size, level_size, count, chunk * count, wave_count),
            ).reshape(places, height, width)
            hemi = exchange(joined(partner(grid, "fld"), grid, 0.5))
            returned.append(hemi.reshape(places * height, width))
        current = inverse_fourier(returned, tables, grid_state.shape, jnp.bfloat16)
        return current.reshape(out_shape)

    tiles = width // LANES
    level_index = jnp.arange(local_levels, dtype=jnp.int32).reshape(tiles, 2).T
    sources = []
    for is_turned in (0, 1):
        shift = jnp.arange(level_size, dtype=jnp.int32)
        from_level = (level_place - shift) % level_size if is_turned else shift
        order = (from_level[None, :, None] * local_levels + level_index[:, None, :]).reshape(-1)
        shift = jnp.arange(wave_size, dtype=jnp.int32)
        from_wave = (wave_place - shift) % wave_size if is_turned else shift
        sources.append(
            (
                jnp.concatenate([from_wave, parity[None]]),
                (jnp.take(modes_in, order, axis=1), jnp.take(modes_out, order, axis=0)),
            )
        )
    shifts = [(wave, level) for wave in range(wave_size) for level in range(level_size)]

    arrived, tables = [], []
    for chunk in range(chunks):
        is_whole = chunk in WHOLE_SENDS
        value, table = fourier(
            grid_state, coupling, slot_ids(fixed if is_whole else turned, chunk), quarter
        )
        tables.append(table)
        if is_whole:
            arrived.append([exchange(value.reshape(places, 2, count, width))])
            continue
        other = partner(value, "fld")
        pieces = []
        for index, (wave, level) in enumerate(shifts):
            rows = slice(index * height, (index + 1) * height)
            mirrored = joined(other[rows], value[rows], 1.0)
            piece = shift_places(mirrored, wave, level)
            pieces.append(piece.reshape(2, count, width))
        arrived.append(pieces)

    returned = []
    for chunk in range(chunks):
        is_whole = chunk in WHOLE_SENDS
        pieces = arrived[chunk]
        if is_whole:
            pieces = [pieces[0], partner(pieces[0], "fld")]
        scalars, modes = sources[0 if is_whole else 1]
        sizes = (wave_size, level_size, count, tiles, half_count, wave_count, chunk * count)
        grid = columns_fused(pieces, legendre, waves, scalars, eig_rates, modes, sizes)
        grid = grid.reshape(places, height, width)
        other = partner(grid, "fld")
        if chunk in WHOLE_BACKS:
            hemi = exchange(joined(other, grid, 0.5))
            returned.append([hemi.reshape(places * height, width)])
            continue
        pieces = []
        for index, (wave, level) in enumerate(shifts):
            hemi = joined(other[index], grid[index], 0.5)
            pieces.append(
                shift_places(hemi, (wave_size - wave) % wave_size, (level_size - level) % level_size)
            )
        returned.append(pieces)
    half = chunks // 2
    flat = lambda groups: [piece for group in groups for piece in group]
    partial = inverse_fourier(flat(returned[:half]), tables[:half], grid_state.shape, jnp.float32)
    current = inverse_fourier(
        flat(returned[half:]), tables[half:], grid_state.shape, jnp.bfloat16, partial
    )
    return current.reshape(out_shape)


def solution(mesh):
    placed = (
        P(("member", "level"), "fld", "wave", None),
        P(("wave", "level"), "fld", None, None),
        P(),
        P(),
        P(),
        P(),
        P(),
    )
    return jax.shard_map(
        shards,
        mesh=mesh,
        in_specs=placed,
        out_specs=P(("member", "level"), "fld", "wave", None),
        check_vma=False,
    )
```

time: 553 us -> 458 us (0.83)
  starting transfers between devices: 175 us -> 93.6 us
  Pallas kernels: 116 us -> 150 us
  waiting for transfers between devices: 195 us -> 167 us
  local copies, waits for them, and re-layouts: 22.6 us -> 10.4 us
    ppermute x98 -> x28, starting transfers between devices: 172 us -> 70 us  [shift_places(): return lax.ppermute(value, EXCHANGE_AXES, pairs)]
    ppermute x98 -> x28, waiting for transfers between devices: 195 us -> 136 us  [shift_places(): return lax.ppermute(value, EXCHANGE_AXES, pairs)]
    all_to_all x0 -> x4, waiting for transfers between devices: none -> 30.9 us  [exchange(): lax.all_to_all(value, EXCHANGE_AXES, split_axis=0, concat_axis=0, tiled=T...]
    pallas_call x11 -> x6, Pallas kernels: 51.5 us -> 79.1 us  [the longest x4 48.4 us: fourier(): pl.pallas_call(functools.partial(fourier_kernel, math.sqrt(2.0 / lon_coun...]
    all_to_all x0 -> x4, starting transfers between devices: none -> 22.3 us  [exchange(): lax.all_to_all(value, EXCHANGE_AXES, split_axis=0, concat_axis=0, tiled=T...]
    unnamed x77 -> x53, local copies, waits for them, and re-layouts: 17.9 us -> 3.8 us
    pallas_call x4, Pallas kernels: 64.3 us -> 70.5 us  [columns_fused(): pl.pallas_call(functools.partial(column_kernel, sizes), out_shape=jax.Sha...]
    convert_element_type x10 -> x6, other arithmetic: 22.9 us -> 16.9 us  [joined(): return both.astype(jnp.bfloat16)]
  transfers between devices with their start and end apart: 109 -> 40, of which waited for: 30 -> 9; matrix products, arithmetic and copies ran while one was open for 6% -> 7% of each run, Pallas kernels for 19% -> 26%
where the time goes in v1:
time: 458 us; the launch traced here: 453 us
  waiting for transfers between devices  167 us (36%)
  Pallas kernels  150 us (33%)
  starting transfers between devices  93.6 us (20%)
  other arithmetic  32.3 us (7%)
  local copies, waits for them, and re-layouts  10.4 us (2%)
    ppermute x28, waiting for transfers between devices, shift_places(): return lax.ppermute(value, EXCHANGE_AXES, pairs)  136 us
    pallas_call x4, Pallas kernels, columns_fused(): pl.pallas_call(functools.partial(column_kernel, sizes), out_shape=jax.Sha...  70.5 us
    ppermute x28, starting transfers between devices, shift_places(): return lax.ppermute(value, EXCHANGE_AXES, pairs)  70 us
    pallas_call x4, Pallas kernels, fourier(): pl.pallas_call(functools.partial(fourier_kernel, math.sqrt(2.0 / lon_coun...  48.4 us
    all_to_all x4, waiting for transfers between devices, exchange(): lax.all_to_all(value, EXCHANGE_AXES, split_axis=0, concat_axis=0, tiled=T...  30.9 us
    pallas_call x2, Pallas kernels, inverse_fourier(): pl.pallas_call(functools.partial(inverse_kernel, len(pieces), len(tables)...  30.7 us
    all_to_all x4, starting transfers between devices, exchange(): lax.all_to_all(value, EXCHANGE_AXES, split_axis=0, concat_axis=0, tiled=T...  22.3 us
    convert_element_type x6, other arithmetic, joined(): return both.astype(jnp.bfloat16)  16.9 us
  transfers between devices with their start and end apart: 40, of which 9 were waited for; matrix products, arithmetic and copies ran while one was open for 7% of the time, Pallas kernels for 26%

profile of v1, /device:TPU:0, one launch (start us, length us, event | category | flops | bytes accessed | tf_op | source)
XLA Modules:
  0.0 453.1 jit_solution(17165364139324938302)
XLA Ops:
  0.2 0.8 reshape.305
  1.4 1.3 fusion.46
  2.7 0.8 multiply_bitcast_fusion
  4.4 1.2 multiply_sine_fusion.1
  5.6 12.1 %shard_map.77 = (bf16[256,4096]{1,0:T(8,128)(2,1)}, bf16[256,1536]{1,0:T(8,128)(2,1)}) custom-call(bf16[64,64,1536]{2,1,0:T(8,128)(2,1)} %bitcast.184, f32[64,1]{1,0:T(8,128)} %copy.37.coupling, f32[256,12]{1,0:T(8,128)} %get-tuple-element.74.high_cos, f32[256,12]{1,0:T(8,128)} %get-tuple-element.73.high_sin, f32[256,128]{1,0:T(8,128)} %get-tuple-element.90.low_cos, ...), custom_call_target="tpu_custom_call" | custom-call | flops 3221225472 | bytes 15466496 | tf_op jit(solution)/shard_map/pallas_call | solution.py:84
  17.7 7.3 %all-to-all-start.2 = ((bf16[8,2,16,4096]{3,2,1,0:T(8,128)(2,1)}), bf16[8,2,16,4096]{3,2,1,0:T(8,128)(2,1)S(1)}, u32[]{:S(2)}, u32[]{:S(2)}) async-start(bf16[8,2,16,4096]{3,2,1,0:T(8,128)(2,1)} %bitcast.189), calls=%async_computation.2 | async-start | bytes 4194304 | tf_op jit(solution)/shard_map/all_to_all | solution.py:382
  25.2 1.3 fusion.42
  26.5 1.3 fusion.54
  27.8 1.2 multiply_sine_fusion.3
  29.0 1.2 multiply_sine_fusion
  30.2 12.1 %shard_map.73 = (bf16[256,4096]{1,0:T(8,128)(2,1)}, bf16[256,1536]{1,0:T(8,128)(2,1)}) custom-call(bf16[64,64,1536]{2,1,0:T(8,128)(2,1)} %bitcast.185, f32[64,1]{1,0:T(8,128)} %copy.37.coupling, f32[256,12]{1,0:T(8,128)} %get-tuple-element.78.high_cos, f32[256,12]{1,0:T(8,128)} %get-tuple-element.77.high_sin, f32[256,128]{1,0:T(8,128)} %get-tuple-element.96.low_cos, ...), custom_call_target="tpu_custom_call" | custom-call | flops 3221225472 | bytes 15466496 | tf_op jit(solution)/shard_map/pallas_call | solution.py:84
  42.3 30.9 %all-to-all-done.2.refs_0_ = bf16[8,2,16,4096]{3,2,1,0:T(8,128)(2,1)S(1)} async-done(((bf16[8,2,16,4096]{3,2,1,0:T(8,128)(2,1)}), bf16[8,2,16,4096]{3,2,1,0:T(8,128)(2,1)S(1)}, u32[]{:S(2)}, u32[]{:S(2)}) %all-to-all-start.2) | async-done | bytes 2097184 | tf_op jit(solution)/shard_map/all_to_all | solution.py:382
  73.2 4.5 %all-to-all-start = ((bf16[8,2,16,4096]{3,2,1,0:T(8,128)(2,1)}), bf16[8,2,16,4096]{3,2,1,0:T(8,128)(2,1)}, u32[]{:S(2)}, u32[]{:S(2)}) async-start(bf16[8,2,16,4096]{3,2,1,0:T(8,128)(2,1)} %bitcast.188), calls=%async_computation | async-start | bytes 4194304 | tf_op jit(solution)/shard_map/all_to_all | solution.py:382
  77.9 12.1 %shard_map.79 = (bf16[256,4096]{1,0:T(8,128)(2,1)}, bf16[256,1536]{1,0:T(8,128)(2,1)}) custom-call(bf16[64,64,1536]{2,1,0:T(8,128)(2,1)} %bitcast.186, f32[64,1]{1,0:T(8,128)} %copy.37.coupling, f32[256,12]{1,0:T(8,128)} %get-tuple-element.72.high_cos, f32[256,12]{1,0:T(8,128)} %get-tuple-element.71.high_sin, f32[256,128]{1,0:T(8,128)} %get-tuple-element.84.low_cos, ...), custom_call_target="tpu_custom_call" | custom-call | flops 3221225472 | bytes 15466496 | tf_op jit(solution)/shard_map/pallas_call | solution.py:84
  90.9 0.7 gather_fusion
  91.8 0.8 dynamic_slice.12.waves
  93.6 1.2 multiply_sine_fusion.2
  94.8 1.6 copy-done.3
  96.4 18.2 %shard_map.78 = bf16[8,2,16,4096]{3,2,1,0:T(8,128)(2,1)S(1)} custom-call(s32[64]{0:T(128)S(1)} %dynamic_slice.12.waves, s32[5]{0:T(128)S(1)} %pad_add_fusion.scalars, f32[128,1]{1,0:T(8,128)S(1)} %copy.38.eig_ref, bf16[128,128]{1,0:T(8,128)(2,1)S(1)} %select_bitcast_fusion.1.modes_in, bf16[128,128]{1,0:T(8,128)(2,1)S(1)} %broadcast_select_fusion.1.modes_out, ...), custom_call_target="tpu_custom_call" | custom-call | flops 1610612736 | bytes 6291456 | tf_op jit(solution)/shard_map/pallas_call | solution.py:290
  114.7 1.3 fusion.50
  116.1 12.1 %shard_map.75 = (bf16[256,4096]{1,0:T(8,128)(2,1)}, bf16[256,1536]{1,0:T(8,128)(2,1)}) custom-call(bf16[64,64,1536]{2,1,0:T(8,128)(2,1)} %bitcast.187, f32[64,1]{1,0:T(8,128)} %copy.37.coupling, f32[256,12]{1,0:T(8,128)} %get-tuple-element.76.high_cos, f32[256,12]{1,0:T(8,128)} %get-tuple-element.75.high_sin, f32[256,128]{1,0:T(8,128)} %get-tuple-element.92.low_cos, ...), custom_call_target="tpu_custom_call" | custom-call | flops 3221225472 | bytes 15466496 | tf_op jit(solution)/shard_map/pallas_call | solution.py:84
  130.4 3.8 add_convert_fusion
  134.2 4.4 collective-permute-start.27
  139.2 3.9 multiply_convert_fusion
  143.1 6.1 %all-to-all-start.3 = ((bf16[8,32,4096]{2,1,0:T(8,128)(2,1)}), bf16[8,32,4096]{2,1,0:T(8,128)(2,1)}, u32[]{:S(2)}, u32[]{:S(2)}) async-start(bf16[8,32,4096]{2,1,0:T(8,128)(2,1)} %multiply_convert_fusion), calls=%async_computation.3 | async-start | bytes 4194304 | tf_op jit(solution)/shard_map/all_to_all | solution.py:382
  149.4 3.0 collective-permute-start.24
  152.4 19.1 %shard_map.74 = bf16[8,2,16,4096]{3,2,1,0:T(8,128)(2,1)S(1)} custom-call(s32[64]{0:T(128)S(1)} %dynamic_slice.12.waves, s32[5]{0:T(128)S(1)} %pad_add_fusion.scalars, f32[128,1]{1,0:T(8,128)S(1)} %copy.38.eig_ref, bf16[128,128]{1,0:T(8,128)(2,1)S(1)} %select_bitcast_fusion.1.modes_in, bf16[128,128]{1,0:T(8,128)(2,1)S(1)} %broadcast_select_fusion.1.modes_out, ...), custom_call_target="tpu_custom_call" | custom-call | flops 1610612736 | bytes 6291456 | tf_op jit(solution)/shard_map/pallas_call | solution.py:290
  171.5 2.9 collective-permute-start.23
  175.1 2.3 add_convert_fusion.8
  177.3 52.2 %collective-permute-done.24 = bf16[32,4096]{1,0:T(8,128)(2,1)S(1)} collective-permute-done((bf16[32,4096]{1,0:T(8,128)(2,1)S(1)}, bf16[32,4096]{1,0:T(8,128)(2,1)S(1)}, u32[]{:S(2)}, u32[]{:S(2)}) %collective-permute-start.24) | collective-permute-done | bytes 262176 | tf_op jit(solution)/shard_map/ppermute | solution.py:35
  229.5 1.0 collective-permute-start.8
  230.5 3.4 collective-permute-start.7
  234.4 15.9 %shard_map.80 = bf16[8,2,16,4096]{3,2,1,0:T(8,128)(2,1)S(1)} custom-call(s32[64]{0:T(128)S(1)} %dynamic_slice.12.waves, s32[5]{0:T(128)S(1)} %pad_add_fusion.1.scalars, f32[128,1]{1,0:T(8,128)S(1)} %copy.38.eig_ref, bf16[128,128]{1,0:T(8,128)(2,1)S(1)} %select_bitcast_fusion.modes_in, bf16[128,128]{1,0:T(8,128)(2,1)S(1)} %broadcast_select_fusion.modes_out, ...), custom_call_target="tpu_custom_call" | custom-call | flops 1610612736 | bytes 6291456 | tf_op jit(solution)/shard_map/pallas_call | solution.py:290
  250.3 1.1 collective-permute-start.5
  251.5 2.0 collective-permute-start.4
  253.4 16.4 %collective-permute-done.7 = bf16[32,4096]{1,0:T(8,128)(2,1)S(1)} collective-permute-done((bf16[32,4096]{1,0:T(8,128)(2,1)S(1)}, bf16[32,4096]{1,0:T(8,128)(2,1)S(1)}, u32[]{:S(2)}, u32[]{:S(2)}) %collective-permute-start.7) | collective-permute-done | bytes 262176 | tf_op jit(solution)/shard_map/ppermute | solution.py:35
  269.9 1.5 collective-permute-start.3
  271.3 1.9 convert_multiply_fusion
  273.3 1.2 collective-permute-done.6
  274.4 1.8 collective-permute-done.3
  276.2 17.2 %shard_map.76 = bf16[8,2,16,4096]{3,2,1,0:T(8,128)(2,1)} custom-call(s32[64]{0:T(128)S(1)} %dynamic_slice.12.waves, s32[5]{0:T(128)S(1)} %pad_add_fusion.1.scalars, f32[128,1]{1,0:T(8,128)S(1)} %copy.38.eig_ref, bf16[128,128]{1,0:T(8,128)(2,1)S(1)} %select_bitcast_fusion.modes_in, bf16[128,128]{1,0:T(8,128)(2,1)S(1)} %broadcast_select_fusion.modes_out, ...), custom_call_target="tpu_custom_call" | custom-call | flops 1610612736 | bytes 6291456 | tf_op jit(solution)/shard_map/pallas_call | solution.py:290
  293.5 2.5 multiply_convert_fusion.1
  296.0 4.3 all-to-all-start.1
  300.4 2.1 convert_multiply_fusion.8
  302.9 2.2 fusion.1
  305.1 2.9 collective-permute-start.35
  308.0 1.5 collective-permute-start.34
  309.4 1.0 collective-permute-start.33
  310.5 1.9 collective-permute-start.32
  312.4 3.3 collective-permute-start.31
  315.6 2.3 fusion.17
  317.9 28.3 %collective-permute-done.35.refs_8_ = bf16[32,4096]{1,0:T(8,128)(2,1)S(1)} collective-permute-done((bf16[32,4096]{1,0:T(8,128)(2,1)S(1)}, bf16[32,4096]{1,0:T(8,128)(2,1)S(1)}, u32[]{:S(2)}, u32[]{:S(2)}) %collective-permute-start.35) | collective-permute-done | bytes 262176 | tf_op jit(solution)/shard_map/ppermute | solution.py:35
  346.2 4.8 %collective-permute-done.34.refs_7_ = bf16[32,4096]{1,0:T(8,128)(2,1)S(1)} collective-permute-done((bf16[32,4096]{1,0:T(8,128)(2,1)S(1)}, bf16[32,4096]{1,0:T(8,128)(2,1)S(1)}, u32[]{:S(2)}, u32[]{:S(2)}) %collective-permute-start.34) | collective-permute-done | bytes 262176 | tf_op jit(solution)/shard_map/ppermute | solution.py:35
  351.0 1.4 collective-permute-start.29
  352.4 26.6 %collective-permute-done.33.refs_6_ = bf16[32,4096]{1,0:T(8,128)(2,1)S(1)} collective-permute-done((bf16[32,4096]{1,0:T(8,128)(2,1)S(1)}, bf16[32,4096]{1,0:T(8,128)(2,1)S(1)}, u32[]{:S(2)}, u32[]{:S(2)}) %collective-permute-start.33) | collective-permute-done | bytes 262176 | tf_op jit(solution)/shard_map/ppermute | solution.py:35
  378.9 9.3 %collective-permute-start.17 = (bf16[32,4096]{1,0:T(8,128)(2,1)S(1)}, bf16[32,4096]{1,0:T(8,128)(2,1)S(1)}, u32[]{:S(2)}, u32[]{:S(2)}) collective-permute-start(bf16[32,4096]{1,0:T(8,128)(2,1)S(1)} %get-tuple-element.55), channel_id=1, source_target_pairs={{0,6},{2,4},{4,10},{6,8},{8,14},{10,12},{12,2},{14,0},{1,7},{3,5},... | collective-permute-start | bytes 786440 | tf_op jit(solution)/shard_map/ppermute | solution.py:35
  388.3 5.6 %collective-permute-start.16 = (bf16[32,4096]{1,0:T(8,128)(2,1)S(1)}, bf16[32,4096]{1,0:T(8,128)(2,1)S(1)}, u32[]{:S(2)}, u32[]{:S(2)}) collective-permute-start(bf16[32,4096]{1,0:T(8,128)(2,1)S(1)} %get-tuple-element.56), channel_id=1, source_target_pairs={{0,4},{2,6},{4,8},{6,10},{8,12},{10,14},{12,0},{14,2},{1,5},{3,7},... | collective-permute-start | bytes 786440 | tf_op jit(solution)/shard_map/ppermute | solution.py:35
  393.9 3.5 collective-permute-start.15
  397.4 13.9 %collective-permute-start.14 = (bf16[32,4096]{1,0:T(8,128)(2,1)S(1)}, bf16[32,4096]{1,0:T(8,128)(2,1)S(1)}, u32[]{:S(2)}, u32[]{:S(2)}) collective-permute-start(bf16[32,4096]{1,0:T(8,128)(2,1)S(1)} %get-tuple-element.58), channel_id=1, source_target_pairs={{0,8},{2,10},{4,12},{6,14},{8,0},{10,2},{12,4},{14,6},{1,9},{3,11}... | collective-permute-start | bytes 786440 | tf_op jit(solution)/shard_map/ppermute | solution.py:35
  411.3 4.2 collective-permute-start.13
  416.3 13.0 %shard_map.81.refs_11_ = f32[64,64,1536]{2,1,0:T(8,128)} custom-call(bf16[256,4096]{1,0:T(8,128)(2,1)} %bitcast.42.refs_0_, bf16[32,4096]{1,0:T(8,128)(2,1)S(1)} %get-tuple-element.46.refs_1_, bf16[32,4096]{1,0:T(8,128)(2,1)S(1)} %collective-permute-done.29.refs_2_, bf16[32,4096]{1,0:T(8,128)(2,1)S(1)} %collective-permute-done.30.refs_3_, ...), custom_call_target="tpu_custom_call" | custom-call | flops 6442450944 | bytes 41943040 | tf_op jit(solution)/shard_map/pallas_call | solution.py:130
  429.3 4.5 collective-permute-done.12.refs_3_
  434.6 0.9 copy-done.9
  435.5 17.6 %shard_map.82 = bf16[64,64,1536]{2,1,0:T(8,128)(2,1)} custom-call(bf16[256,4096]{1,0:T(8,128)(2,1)} %bitcast.9.refs_0_, bf16[32,4096]{1,0:T(8,128)(2,1)S(1)} %get-tuple-element.62.refs_1_, bf16[32,4096]{1,0:T(8,128)(2,1)S(1)} %copy-done.9, bf16[32,4096]{1,0:T(8,128)(2,1)S(1)} %collective-permute-done.12.refs_3_, ...), custom_call_target="tpu_custom_call" | custom-call | flops 6442450944 | bytes 41943040 | tf_op jit(solution)/shard_map/pallas_call | solution.py:130
  (148 shorter events, 9.8 us)
Async XLA Ops:
  0.0 92.5 %copy-start = (bf16[128,128]{1,0:T(8,128)(2,1)S(1)}, bf16[128,128]{1,0:T(8,128)(2,1)}, u32[]{:S(2)}) copy-start(bf16[128,128]{1,0:T(8,128)(2,1)} %param.17) | copy-start | bytes 98308
  17.7 55.5 %all-to-all-start.2 = ((bf16[8,2,16,4096]{3,2,1,0:T(8,128)(2,1)}), bf16[8,2,16,4096]{3,2,1,0:T(8,128)(2,1)S(1)}, u32[]{:S(2)}, u32[]{:S(2)}) async-start(bf16[8,2,16,4096]{3,2,1,0:T(8,128)(2,1)} %bitcast.189), calls=%async_computation.2 | async-start | bytes 4194304 | tf_op jit(solution)/shard_map/all_to_all | solution.py:382
  73.2 4.5 %copy-start.2 = (bf16[8,2,16,4096]{3,2,1,0:T(8,128)(2,1)}, bf16[8,2,16,4096]{3,2,1,0:T(8,128)(2,1)S(1)}, u32[]{:S(2)}) copy-start(bf16[8,2,16,4096]{3,2,1,0:T(8,128)(2,1)S(1)} %all-to-all-done.2.refs_0_) | copy-start | bytes 6291460
  73.2 57.1 %all-to-all-start = ((bf16[8,2,16,4096]{3,2,1,0:T(8,128)(2,1)}), bf16[8,2,16,4096]{3,2,1,0:T(8,128)(2,1)}, u32[]{:S(2)}, u32[]{:S(2)}) async-start(bf16[8,2,16,4096]{3,2,1,0:T(8,128)(2,1)} %bitcast.188), calls=%async_computation | async-start | bytes 4194304 | tf_op jit(solution)/shard_map/all_to_all | solution.py:382
  77.8 17.0 %collective-permute-start.18 = (bf16[8,2,16,4096]{3,2,1,0:T(8,128)(2,1)S(1)}, bf16[8,2,16,4096]{3,2,1,0:T(8,128)(2,1)}, u32[]{:S(2)}, u32[]{:S(2)}) collective-permute-start(bf16[8,2,16,4096]{3,2,1,0:T(8,128)(2,1)S(1)} %all-to-all-done.2.refs_0_), channel_id=1, source_target_pairs={{0,1},{1,0},{2,3},{3,2},{4,5},{5,4},{6,7},{7,6},{8,9},{9,8},{10,11... | collective-permute-start | bytes 6291464 | tf_op jit(solution)/shard_map/ppermute | solution.py:23
  77.8 12.9 %copy-start.22 = (bf16[128,128]{1,0:T(8,128)(2,1)S(1)}, bf16[128,128]{1,0:T(8,128)(2,1)}, u32[]{:S(2)}) copy-start(bf16[128,128]{1,0:T(8,128)(2,1)} %param.16) | copy-start | bytes 98308
  77.9 15.4 %copy-start.23 = (f32[128]{0:T(128)S(1)}, f32[128]{0:T(128)}, u32[]{:S(2)}) copy-start(f32[128]{0:T(128)} %param.15) | copy-start | bytes 1540
  90.0 40.4 %collective-permute-start.20 = (bf16[256,4096]{1,0:T(8,128)(2,1)}, bf16[256,4096]{1,0:T(8,128)(2,1)}, u32[]{:S(2)}, u32[]{:S(2)}) collective-permute-start(bf16[256,4096]{1,0:T(8,128)(2,1)} %get-tuple-element.20), channel_id=1, source_target_pairs={{0,1},{1,0},{2,3},{3,2},{4,5},{5,4},{6,7},{7,6},{8,9},{9,8},{10,11... | collective-permute-start | bytes 6291464 | tf_op jit(solution)/shard_map/ppermute | solution.py:23
  94.8 1.6 copy-start.3
  114.6 24.6 %collective-permute-start.19 = (bf16[8,32,4096]{2,1,0:T(8,128)(2,1)S(1)}, bf16[8,32,4096]{2,1,0:T(8,128)(2,1)}, u32[]{:S(2)}, u32[]{:S(2)}) collective-permute-start(bf16[8,32,4096]{2,1,0:T(8,128)(2,1)S(1)} %bitcast.167), channel_id=1, source_target_pairs={{0,1},{1,0},{2,3},{3,2},{4,5},{5,4},{6,7},{7,6},{8,9},{9,8},{10,11... | collective-permute-start | bytes 6291464 | tf_op jit(solution)/shard_map/ppermute | solution.py:23
  128.2 43.3 %collective-permute-start.2 = (bf16[256,4096]{1,0:T(8,128)(2,1)}, bf16[256,4096]{1,0:T(8,128)(2,1)}, u32[]{:S(2)}, u32[]{:S(2)}) collective-permute-start(bf16[256,4096]{1,0:T(8,128)(2,1)} %get-tuple-element.16), channel_id=1, source_target_pairs={{0,1},{1,0},{2,3},{3,2},{4,5},{5,4},{6,7},{7,6},{8,9},{9,8},{10,11... | collective-permute-start | bytes 6291464 | tf_op jit(solution)/shard_map/ppermute | solution.py:23
  130.3 19.0 %collective-permute-start = (bf16[8,2,16,4096]{3,2,1,0:T(8,128)(2,1)}, bf16[8,2,16,4096]{3,2,1,0:T(8,128)(2,1)}, u32[]{:S(2)}, u32[]{:S(2)}) collective-permute-start(bf16[8,2,16,4096]{3,2,1,0:T(8,128)(2,1)} %all-to-all-done.refs_0_), channel_id=1, source_target_pairs={{0,1},{1,0},{2,3},{3,2},{4,5},{5,4},{6,7},{7,6},{8,9},{9,8},{10,11... | collective-permute-start | bytes 6291464 | tf_op jit(solution)/shard_map/ppermute | solution.py:23
  134.2 40.2 %collective-permute-start.27 = (bf16[32,4096]{1,0:T(8,128)(2,1)}, bf16[32,4096]{1,0:T(8,128)(2,1)S(1)}, u32[]{:S(2)}, u32[]{:S(2)}) collective-permute-start(bf16[32,4096]{1,0:T(8,128)(2,1)} %get-tuple-element.23), channel_id=1, source_target_pairs={{0,14},{2,12},{4,2},{6,0},{8,6},{10,4},{12,10},{14,8},{1,15},{3,13... | collective-permute-start | bytes 786440 | tf_op jit(solution)/shard_map/ppermute | solution.py:35
  138.6 35.8 %collective-permute-start.26 = (bf16[32,4096]{1,0:T(8,128)(2,1)}, bf16[32,4096]{1,0:T(8,128)(2,1)S(1)}, u32[]{:S(2)}, u32[]{:S(2)}) collective-permute-start(bf16[32,4096]{1,0:T(8,128)(2,1)} %get-tuple-element.24), channel_id=1, source_target_pairs={{0,12},{2,14},{4,0},{6,2},{8,4},{10,6},{12,8},{14,10},{1,13},{3,15... | collective-permute-start | bytes 786440 | tf_op jit(solution)/shard_map/ppermute | solution.py:35
  139.2 35.9 %collective-permute-start.25 = (bf16[32,4096]{1,0:T(8,128)(2,1)}, bf16[32,4096]{1,0:T(8,128)(2,1)S(1)}, u32[]{:S(2)}, u32[]{:S(2)}) collective-permute-start(bf16[32,4096]{1,0:T(8,128)(2,1)} %get-tuple-element.25), channel_id=1, source_target_pairs={{0,10},{2,8},{4,14},{6,12},{8,2},{10,0},{12,6},{14,4},{1,11},{3,9}... | collective-permute-start | bytes 786440 | tf_op jit(solution)/shard_map/ppermute | solution.py:35
  143.1 6.2 %copy-start.21 = (bf16[32,4096]{1,0:T(8,128)(2,1)S(1)}, bf16[32,4096]{1,0:T(8,128)(2,1)}, u32[]{:S(2)}) copy-start(bf16[32,4096]{1,0:T(8,128)(2,1)} %get-tuple-element.26) | copy-start | bytes 786436
  143.1 152.8 %all-to-all-start.3 = ((bf16[8,32,4096]{2,1,0:T(8,128)(2,1)}), bf16[8,32,4096]{2,1,0:T(8,128)(2,1)}, u32[]{:S(2)}, u32[]{:S(2)}) async-start(bf16[8,32,4096]{2,1,0:T(8,128)(2,1)} %multiply_convert_fusion), calls=%async_computation.3 | async-start | bytes 4194304 | tf_op jit(solution)/shard_map/all_to_all | solution.py:382
  149.3 85.1 %slice-start = ((s8[8388608]{0:T(1024)(128)(4,1)}), s8[4194304]{0:T(1024)(128)(4,1)S(1)}, s32[]{:S(2)}) async-start(s8[8388608]{0:T(1024)(128)(4,1)} %bitcast.161), calls=%async_computation.4 | async-start | bytes 8388608
  149.3 22.2 %copy-start.20 = (bf16[32,4096]{1,0:T(8,128)(2,1)S(1)}, bf16[32,4096]{1,0:T(8,128)(2,1)}, u32[]{:S(2)}) copy-start(bf16[32,4096]{1,0:T(8,128)(2,1)} %get-tuple-element.27) | copy-start | bytes 786436
  149.3 25.1 %copy-start.19 = (bf16[32,4096]{1,0:T(8,128)(2,1)S(1)}, bf16[32,4096]{1,0:T(8,128)(2,1)}, u32[]{:S(2)}) copy-start(bf16[32,4096]{1,0:T(8,128)(2,1)} %get-tuple-element.28) | copy-start | bytes 786436
  149.3 25.1 %copy-start.18 = (bf16[32,4096]{1,0:T(8,128)(2,1)S(1)}, bf16[32,4096]{1,0:T(8,128)(2,1)}, u32[]{:S(2)}) copy-start(bf16[32,4096]{1,0:T(8,128)(2,1)} %get-tuple-element.29) | copy-start | bytes 786436
  149.3 25.7 %copy-start.10 = (bf16[256,4096]{1,0:T(8,128)(2,1)S(1)}, bf16[256,4096]{1,0:T(8,128)(2,1)}, u32[]{:S(2)}) copy-start(bf16[256,4096]{1,0:T(8,128)(2,1)} %get-tuple-element.16) | copy-start | bytes 6291460
  149.4 85.0 %slice-start.1 = ((s8[8388608]{0:T(1024)(128)(4,1)}), s8[4194304]{0:T(1024)(128)(4,1)S(1)}, s32[]{:S(2)}) async-start(s8[8388608]{0:T(1024)(128)(4,1)} %bitcast.161), calls=%async_computation.5 | async-start | bytes 8388608
  149.4 80.1 %collective-permute-start.24 = (bf16[32,4096]{1,0:T(8,128)(2,1)S(1)}, bf16[32,4096]{1,0:T(8,128)(2,1)S(1)}, u32[]{:S(2)}, u32[]{:S(2)}) collective-permute-start(bf16[32,4096]{1,0:T(8,128)(2,1)S(1)} %copy-done.21), channel_id=1, source_target_pairs={{0,8},{2,10},{4,12},{6,14},{8,0},{10,2},{12,4},{14,6},{1,9},{3,11}... | collective-permute-start | bytes 786440 | tf_op jit(solution)/shard_map/ppermute | solution.py:35
  171.5 58.0 %collective-permute-start.23 = (bf16[32,4096]{1,0:T(8,128)(2,1)S(1)}, bf16[32,4096]{1,0:T(8,128)(2,1)S(1)}, u32[]{:S(2)}, u32[]{:S(2)}) collective-permute-start(bf16[32,4096]{1,0:T(8,128)(2,1)S(1)} %copy-done.20), channel_id=1, source_target_pairs={{0,6},{2,4},{4,10},{6,8},{8,14},{10,12},{12,2},{14,0},{1,7},{3,5},... | collective-permute-start | bytes 786440 | tf_op jit(solution)/shard_map/ppermute | solution.py:35
  174.4 56.1 %collective-permute-start.22 = (bf16[32,4096]{1,0:T(8,128)(2,1)S(1)}, bf16[32,4096]{1,0:T(8,128)(2,1)S(1)}, u32[]{:S(2)}, u32[]{:S(2)}) collective-permute-start(bf16[32,4096]{1,0:T(8,128)(2,1)S(1)} %copy-done.19), channel_id=1, source_target_pairs={{0,4},{2,6},{4,8},{6,10},{8,12},{10,14},{12,0},{14,2},{1,5},{3,7},... | collective-permute-start | bytes 786440 | tf_op jit(solution)/shard_map/ppermute | solution.py:35
  174.4 59.5 %collective-permute-start.21 = (bf16[32,4096]{1,0:T(8,128)(2,1)S(1)}, bf16[32,4096]{1,0:T(8,128)(2,1)S(1)}, u32[]{:S(2)}, u32[]{:S(2)}) collective-permute-start(bf16[32,4096]{1,0:T(8,128)(2,1)S(1)} %copy-done.18), channel_id=1, source_target_pairs={{0,2},{2,0},{4,6},{6,4},{8,10},{10,8},{12,14},{14,12},{1,3},{3,1},... | collective-permute-start | bytes 786440 | tf_op jit(solution)/shard_map/ppermute | solution.py:35
  175.1 118.4 %collective-permute-start.1 = (bf16[8,32,4096]{2,1,0:T(8,128)(2,1)S(1)}, bf16[8,32,4096]{2,1,0:T(8,128)(2,1)S(1)}, u32[]{:S(2)}, u32[]{:S(2)}) collective-permute-start(bf16[8,32,4096]{2,1,0:T(8,128)(2,1)S(1)} %bitcast.166), channel_id=1, source_target_pairs={{0,1},{1,0},{2,3},{3,2},{4,5},{5,4},{6,7},{7,6},{8,9},{9,8},{10,11... | collective-permute-start | bytes 6291464 | tf_op jit(solution)/shard_map/ppermute | solution.py:23
  229.5 20.9 %collective-permute-start.9 = (bf16[32,4096]{1,0:T(8,128)(2,1)S(1)}, bf16[32,4096]{1,0:T(8,128)(2,1)S(1)}, u32[]{:S(2)}, u32[]{:S(2)}) collective-permute-start(bf16[32,4096]{1,0:T(8,128)(2,1)S(1)} %get-tuple-element.31), channel_id=1, source_target_pairs={{0,14},{2,12},{4,2},{6,0},{8,6},{10,4},{12,10},{14,8},{1,15},{3,13... | collective-permute-start | bytes 786440 | tf_op jit(solution)/shard_map/ppermute | solution.py:35
  229.5 22.0 %collective-permute-start.8 = (bf16[32,4096]{1,0:T(8,128)(2,1)S(1)}, bf16[32,4096]{1,0:T(8,128)(2,1)S(1)}, u32[]{:S(2)}, u32[]{:S(2)}) collective-permute-start(bf16[32,4096]{1,0:T(8,128)(2,1)S(1)} %get-tuple-element.32), channel_id=1, source_target_pairs={{0,12},{2,14},{4,0},{6,2},{8,4},{10,6},{12,8},{14,10},{1,13},{3,15... | collective-permute-start | bytes 786440 | tf_op jit(solution)/shard_map/ppermute | solution.py:35
  230.5 39.4 %collective-permute-start.7 = (bf16[32,4096]{1,0:T(8,128)(2,1)S(1)}, bf16[32,4096]{1,0:T(8,128)(2,1)S(1)}, u32[]{:S(2)}, u32[]{:S(2)}) collective-permute-start(bf16[32,4096]{1,0:T(8,128)(2,1)S(1)} %get-tuple-element.33), channel_id=1, source_target_pairs={{0,10},{2,8},{4,14},{6,12},{8,2},{10,0},{12,6},{14,4},{1,11},{3,9}... | collective-permute-start | bytes 786440 | tf_op jit(solution)/shard_map/ppermute | solution.py:35
  234.0 40.5 %collective-permute-start.6 = (bf16[32,4096]{1,0:T(8,128)(2,1)S(1)}, bf16[32,4096]{1,0:T(8,128)(2,1)S(1)}, u32[]{:S(2)}, u32[]{:S(2)}) collective-permute-start(bf16[32,4096]{1,0:T(8,128)(2,1)S(1)} %get-tuple-element.34), channel_id=1, source_target_pairs={{0,8},{2,10},{4,12},{6,14},{8,0},{10,2},{12,4},{14,6},{1,9},{3,11}... | collective-permute-start | bytes 786440 | tf_op jit(solution)/shard_map/ppermute | solution.py:35
  250.3 24.1 %collective-permute-start.5 = (bf16[32,4096]{1,0:T(8,128)(2,1)S(1)}, bf16[32,4096]{1,0:T(8,128)(2,1)S(1)}, u32[]{:S(2)}, u32[]{:S(2)}) collective-permute-start(bf16[32,4096]{1,0:T(8,128)(2,1)S(1)} %get-tuple-element.35), channel_id=1, source_target_pairs={{0,6},{2,4},{4,10},{6,8},{8,14},{10,12},{12,2},{14,0},{1,7},{3,5},... | collective-permute-start | bytes 786440 | tf_op jit(solution)/shard_map/ppermute | solution.py:35
  251.5 22.9 %collective-permute-start.4 = (bf16[32,4096]{1,0:T(8,128)(2,1)S(1)}, bf16[32,4096]{1,0:T(8,128)(2,1)S(1)}, u32[]{:S(2)}, u32[]{:S(2)}) collective-permute-start(bf16[32,4096]{1,0:T(8,128)(2,1)S(1)} %get-tuple-element.36), channel_id=1, source_target_pairs={{0,4},{2,6},{4,8},{6,10},{8,12},{10,14},{12,0},{14,2},{1,5},{3,7},... | collective-permute-start | bytes 786440 | tf_op jit(solution)/shard_map/ppermute | solution.py:35
  269.9 6.4 %collective-permute-start.3 = (bf16[32,4096]{1,0:T(8,128)(2,1)S(1)}, bf16[32,4096]{1,0:T(8,128)(2,1)S(1)}, u32[]{:S(2)}, u32[]{:S(2)}) collective-permute-start(bf16[32,4096]{1,0:T(8,128)(2,1)S(1)} %get-tuple-element.37), channel_id=1, source_target_pairs={{0,2},{2,0},{4,6},{6,4},{8,10},{10,8},{12,14},{14,12},{1,3},{3,1},... | collective-permute-start | bytes 786440 | tf_op jit(solution)/shard_map/ppermute | solution.py:35
  274.4 28.1 %collective-permute-start.28 = (bf16[8,32,4096]{2,1,0:T(8,128)(2,1)S(1)}, bf16[8,32,4096]{2,1,0:T(8,128)(2,1)}, u32[]{:S(2)}, u32[]{:S(2)}) collective-permute-start(bf16[8,32,4096]{2,1,0:T(8,128)(2,1)S(1)} %bitcast.165), channel_id=1, source_target_pairs={{0,1},{1,0},{2,3},{3,2},{4,5},{5,4},{6,7},{7,6},{8,9},{9,8},{10,11... | collective-permute-start | bytes 6291464 | tf_op jit(solution)/shard_map/ppermute | solution.py:23
  293.5 18.9 %collective-permute-start.10 = (bf16[8,32,4096]{2,1,0:T(8,128)(2,1)}, bf16[8,32,4096]{2,1,0:T(8,128)(2,1)}, u32[]{:S(2)}, u32[]{:S(2)}) collective-permute-start(bf16[8,32,4096]{2,1,0:T(8,128)(2,1)} %bitcast.22), channel_id=1, source_target_pairs={{0,1},{1,0},{2,3},{3,2},{4,5},{5,4},{6,7},{7,6},{8,9},{9,8},{10,11... | collective-permute-start | bytes 6291464 | tf_op jit(solution)/shard_map/ppermute | solution.py:23
  296.0 138.6 %all-to-all-start.1 = ((bf16[8,32,4096]{2,1,0:T(8,128)(2,1)}), bf16[8,32,4096]{2,1,0:T(8,128)(2,1)}, u32[]{:S(2)}, u32[]{:S(2)}) async-start(bf16[8,32,4096]{2,1,0:T(8,128)(2,1)} %multiply_convert_fusion.1), calls=%async_computation.1 | async-start | bytes 4194304 | tf_op jit(solution)/shard_map/all_to_all | solution.py:382
  300.3 2.2 copy-start.11
  300.3 2.2 copy-start.12
  300.3 2.2 copy-start.13
  300.3 2.2 copy-start.14
  300.3 2.3 copy-start.15
  300.4 2.4 copy-start.16
  300.4 2.6 copy-start.17
  305.1 41.1 %collective-permute-start.35 = (bf16[32,4096]{1,0:T(8,128)(2,1)S(1)}, bf16[32,4096]{1,0:T(8,128)(2,1)S(1)}, u32[]{:S(2)}, u32[]{:S(2)}) collective-permute-start(bf16[32,4096]{1,0:T(8,128)(2,1)S(1)} %get-tuple-element.39), channel_id=1, source_target_pairs={{0,6},{2,4},{4,10},{6,8},{8,14},{10,12},{12,2},{14,0},{1,7},{3,5},... | collective-permute-start | bytes 786440 | tf_op jit(solution)/shard_map/ppermute | solution.py:35
  308.0 43.0 %collective-permute-start.34 = (bf16[32,4096]{1,0:T(8,128)(2,1)S(1)}, bf16[32,4096]{1,0:T(8,128)(2,1)S(1)}, u32[]{:S(2)}, u32[]{:S(2)}) collective-permute-start(bf16[32,4096]{1,0:T(8,128)(2,1)S(1)} %get-tuple-element.40), channel_id=1, source_target_pairs={{0,4},{2,6},{4,8},{6,10},{8,12},{10,14},{12,0},{14,2},{1,5},{3,7},... | collective-permute-start | bytes 786440 | tf_op jit(solution)/shard_map/ppermute | solution.py:35
  309.4 69.5 %collective-permute-start.33 = (bf16[32,4096]{1,0:T(8,128)(2,1)S(1)}, bf16[32,4096]{1,0:T(8,128)(2,1)S(1)}, u32[]{:S(2)}, u32[]{:S(2)}) collective-permute-start(bf16[32,4096]{1,0:T(8,128)(2,1)S(1)} %get-tuple-element.41), channel_id=1, source_target_pairs={{0,10},{2,8},{4,14},{6,12},{8,2},{10,0},{12,6},{14,4},{1,11},{3,9}... | collective-permute-start | bytes 786440 | tf_op jit(solution)/shard_map/ppermute | solution.py:35
  310.5 77.8 %collective-permute-start.32 = (bf16[32,4096]{1,0:T(8,128)(2,1)S(1)}, bf16[32,4096]{1,0:T(8,128)(2,1)S(1)}, u32[]{:S(2)}, u32[]{:S(2)}) collective-permute-start(bf16[32,4096]{1,0:T(8,128)(2,1)S(1)} %get-tuple-element.42), channel_id=1, source_target_pairs={{0,8},{2,10},{4,12},{6,14},{8,0},{10,2},{12,4},{14,6},{1,9},{3,11}... | collective-permute-start | bytes 786440 | tf_op jit(solution)/shard_map/ppermute | solution.py:35
  312.4 81.6 %collective-permute-start.31 = (bf16[32,4096]{1,0:T(8,128)(2,1)S(1)}, bf16[32,4096]{1,0:T(8,128)(2,1)S(1)}, u32[]{:S(2)}, u32[]{:S(2)}) collective-permute-start(bf16[32,4096]{1,0:T(8,128)(2,1)S(1)} %get-tuple-element.43), channel_id=1, source_target_pairs={{0,14},{2,12},{4,2},{6,0},{8,6},{10,4},{12,10},{14,8},{1,15},{3,13... | collective-permute-start | bytes 786440 | tf_op jit(solution)/shard_map/ppermute | solution.py:35
  315.6 100.6 %copy-start.6 = (bf16[256,1536]{1,0:T(8,128)(2,1)S(1)}, bf16[256,1536]{1,0:T(8,128)(2,1)}, u32[]{:S(2)}) copy-start(bf16[256,1536]{1,0:T(8,128)(2,1)} %get-tuple-element.21.refs_9_) | copy-start | bytes 2359300
  315.6 100.6 %copy-start.7 = (bf16[256,1536]{1,0:T(8,128)(2,1)S(1)}, bf16[256,1536]{1,0:T(8,128)(2,1)}, u32[]{:S(2)}) copy-start(bf16[256,1536]{1,0:T(8,128)(2,1)} %get-tuple-element.22.refs_10_) | copy-start | bytes 2359300
  346.2 51.2 %collective-permute-start.30 = (bf16[32,4096]{1,0:T(8,128)(2,1)S(1)}, bf16[32,4096]{1,0:T(8,128)(2,1)S(1)}, u32[]{:S(2)}, u32[]{:S(2)}) collective-permute-start(bf16[32,4096]{1,0:T(8,128)(2,1)S(1)} %get-tuple-element.44), channel_id=1, source_target_pairs={{0,12},{2,14},{4,0},{6,2},{8,4},{10,6},{12,8},{14,10},{1,13},{3,15... | collective-permute-start | bytes 786440 | tf_op jit(solution)/shard_map/ppermute | solution.py:35
  351.0 60.4 %collective-permute-start.29 = (bf16[32,4096]{1,0:T(8,128)(2,1)S(1)}, bf16[32,4096]{1,0:T(8,128)(2,1)S(1)}, u32[]{:S(2)}, u32[]{:S(2)}) collective-permute-start(bf16[32,4096]{1,0:T(8,128)(2,1)S(1)} %get-tuple-element.45), channel_id=1, source_target_pairs={{0,2},{2,0},{4,6},{6,4},{8,10},{10,8},{12,14},{14,12},{1,3},{3,1},... | collective-permute-start | bytes 786440 | tf_op jit(solution)/shard_map/ppermute | solution.py:35
  378.9 36.6 %collective-permute-start.17 = (bf16[32,4096]{1,0:T(8,128)(2,1)S(1)}, bf16[32,4096]{1,0:T(8,128)(2,1)S(1)}, u32[]{:S(2)}, u32[]{:S(2)}) collective-permute-start(bf16[32,4096]{1,0:T(8,128)(2,1)S(1)} %get-tuple-element.55), channel_id=1, source_target_pairs={{0,6},{2,4},{4,10},{6,8},{8,14},{10,12},{12,2},{14,0},{1,7},{3,5},... | collective-permute-start | bytes 786440 | tf_op jit(solution)/shard_map/ppermute | solution.py:35
  388.3 27.3 %collective-permute-start.16 = (bf16[32,4096]{1,0:T(8,128)(2,1)S(1)}, bf16[32,4096]{1,0:T(8,128)(2,1)S(1)}, u32[]{:S(2)}, u32[]{:S(2)}) collective-permute-start(bf16[32,4096]{1,0:T(8,128)(2,1)S(1)} %get-tuple-element.56), channel_id=1, source_target_pairs={{0,4},{2,6},{4,8},{6,10},{8,12},{10,14},{12,0},{14,2},{1,5},{3,7},... | collective-permute-start | bytes 786440 | tf_op jit(solution)/shard_map/ppermute | solution.py:35
  393.9 35.4 %collective-permute-start.15 = (bf16[32,4096]{1,0:T(8,128)(2,1)S(1)}, bf16[32,4096]{1,0:T(8,128)(2,1)S(1)}, u32[]{:S(2)}, u32[]{:S(2)}) collective-permute-start(bf16[32,4096]{1,0:T(8,128)(2,1)S(1)} %get-tuple-element.57), channel_id=1, source_target_pairs={{0,10},{2,8},{4,14},{6,12},{8,2},{10,0},{12,6},{14,4},{1,11},{3,9}... | collective-permute-start | bytes 786440 | tf_op jit(solution)/shard_map/ppermute | solution.py:35
  397.4 31.9 %collective-permute-start.14 = (bf16[32,4096]{1,0:T(8,128)(2,1)S(1)}, bf16[32,4096]{1,0:T(8,128)(2,1)S(1)}, u32[]{:S(2)}, u32[]{:S(2)}) collective-permute-start(bf16[32,4096]{1,0:T(8,128)(2,1)S(1)} %get-tuple-element.58), channel_id=1, source_target_pairs={{0,8},{2,10},{4,12},{6,14},{8,0},{10,2},{12,4},{14,6},{1,9},{3,11}... | collective-permute-start | bytes 786440 | tf_op jit(solution)/shard_map/ppermute | solution.py:35
  411.3 18.0 %collective-permute-start.13 = (bf16[32,4096]{1,0:T(8,128)(2,1)S(1)}, bf16[32,4096]{1,0:T(8,128)(2,1)S(1)}, u32[]{:S(2)}, u32[]{:S(2)}) collective-permute-start(bf16[32,4096]{1,0:T(8,128)(2,1)S(1)} %get-tuple-element.59), channel_id=1, source_target_pairs={{0,14},{2,12},{4,2},{6,0},{8,6},{10,4},{12,10},{14,8},{1,15},{3,13... | collective-permute-start | bytes 786440 | tf_op jit(solution)/shard_map/ppermute | solution.py:35
  415.6 18.3 %collective-permute-start.12 = (bf16[32,4096]{1,0:T(8,128)(2,1)S(1)}, bf16[32,4096]{1,0:T(8,128)(2,1)S(1)}, u32[]{:S(2)}, u32[]{:S(2)}) collective-permute-start(bf16[32,4096]{1,0:T(8,128)(2,1)S(1)} %get-tuple-element.60), channel_id=1, source_target_pairs={{0,12},{2,14},{4,0},{6,2},{8,4},{10,6},{12,8},{14,10},{1,13},{3,15... | collective-permute-start | bytes 786440 | tf_op jit(solution)/shard_map/ppermute | solution.py:35
  415.6 18.2 %collective-permute-start.11 = (bf16[32,4096]{1,0:T(8,128)(2,1)S(1)}, bf16[32,4096]{1,0:T(8,128)(2,1)S(1)}, u32[]{:S(2)}, u32[]{:S(2)}) collective-permute-start(bf16[32,4096]{1,0:T(8,128)(2,1)S(1)} %get-tuple-element.61), channel_id=1, source_target_pairs={{0,2},{2,0},{4,6},{6,4},{8,10},{10,8},{12,14},{14,12},{1,3},{3,1},... | collective-permute-start | bytes 786440 | tf_op jit(solution)/shard_map/ppermute | solution.py:35
  416.2 18.3 %copy-start.4 = (bf16[256,1536]{1,0:T(8,128)(2,1)S(1)}, bf16[256,1536]{1,0:T(8,128)(2,1)}, u32[]{:S(2)}) copy-start(bf16[256,1536]{1,0:T(8,128)(2,1)} %get-tuple-element.17.refs_9_) | copy-start | bytes 2359300
  416.2 18.3 %copy-start.5 = (bf16[256,1536]{1,0:T(8,128)(2,1)S(1)}, bf16[256,1536]{1,0:T(8,128)(2,1)}, u32[]{:S(2)}) copy-start(bf16[256,1536]{1,0:T(8,128)(2,1)} %get-tuple-element.18.refs_10_) | copy-start | bytes 2359300
  435.5 17.6 %copy-start.1 = (bf16[128,128]{1,0:T(8,128)(2,1)S(1)}, bf16[128,128]{1,0:T(8,128)(2,1)}, u32[]{:S(2)}) copy-start(bf16[128,128]{1,0:T(8,128)(2,1)} %param.17) | copy-start | bytes 98308
  (2 other events, 1.7 us)

commit v2 on v1

--- a/solution.py
+++ b/solution.py
@@ -12,8 +12,7 @@
 tau_scale = 2.0
 LANES = 128
 CHUNKS = 4
-WHOLE_SENDS = (0, 2)
-WHOLE_BACKS = (0, 2)
+WHOLE_CHUNKS = (0, 2)
 DIRECT_LIMIT = 16
 EXCHANGE_AXES = ("wave", "level")
 
@@ -41,60 +40,68 @@
     )
 
 
-def phase_of(product, period):
-    return (product % period).astype(jnp.float32) * (2.0 * math.pi / period)
-
-
-def level_block(levels, rows_here):
-    return 8 if levels % 8 == 0 and 8 * rows_here % LANES == 0 else levels
-
-
-def fourier_kernel(scale, grid_ref, coupling, high_cos, high_sin, low_cos, low_sin, out, table):
+def level_block(levels, rows_here, most):
+    whole = levels % most == 0 and most * rows_here % LANES == 0
+    return most if whole else levels
+
+
+def write_table(ids, quarter, table):
+    rows, lon_count = table.shape
+    scale = math.sqrt(2.0 / lon_count)
+    wave = ids[...].astype(jnp.float32)
+    lane = lax.broadcasted_iota(jnp.int32, (rows, LANES), 1).astype(jnp.float32)
+
+    def angle(steps):
+        steps = steps - lon_count * jnp.floor(steps * (1.0 / lon_count))
+        return steps * (2.0 * math.pi / lon_count)
+
+    low = angle(wave * lane)
+    high = angle(wave * lane * float(LANES) + quarter[...].astype(jnp.float32))
+    low_cos, low_sin = jnp.cos(low) * scale, jnp.sin(low) * scale
+    high_cos, high_sin = jnp.cos(high), jnp.sin(high)
+    for block in range(lon_count // LANES):
+        values = (
+            high_cos[:, block : block + 1] * low_cos - high_sin[:, block : block + 1] * low_sin
+        )
+        table[:, block * LANES : (block + 1) * LANES] = values.astype(table.dtype)
+
+
+def fourier_kernel(half_rows, sign_ref, grid_ref, lat_rows, ids, quarter, out, table):
     levels, rows, lon_count = grid_ref.shape
 
     @pl.when(pl.program_id(0) == 0)
     def _():
-        for block in range(lon_count // LANES):
-            values = (
-                high_cos[:, block : block + 1] * low_cos[...]
-                - high_sin[:, block : block + 1] * low_sin[...]
-            )
-            table[:, block * LANES : (block + 1) * LANES] = (values * scale).astype(table.dtype)
-
+        write_table(ids, quarter, table)
+
+    latitude = (lat_rows[...].astype(jnp.float32) + 0.5) * (math.pi / (2.0 * half_rows))
+    coupling = 0.5 * sign_ref[0] * jnp.sin(latitude)
     field = grid_ref[...].astype(jnp.float32)
-    forcing = (field + coupling[...][None] * jnp.tanh(field)).astype(jnp.bfloat16)
+    forcing = (field + coupling[None] * jnp.tanh(field)).astype(jnp.bfloat16)
     forcing = forcing.reshape(levels * rows, lon_count)
     out[...] = lax.dot_general(
         table[...], forcing, (((1,), (1,)), ((), ())), preferred_element_type=jnp.float32
     ).astype(out.dtype)
 
 
-def fourier(grid_state, coupling, ids, quarter):
+def fourier(grid_state, sign, lat_rows, half_rows, ids, quarter):
     levels, rows_here, lon_count = grid_state.shape
     height = ids.shape[0]
-    blocks = lon_count // LANES
-    high = phase_of(
-        ids[:, None] * LANES * jnp.arange(blocks, dtype=jnp.int32)[None, :] + quarter[:, None],
-        lon_count,
-    )
-    low = phase_of(ids[:, None] * jnp.arange(LANES, dtype=jnp.int32)[None, :], lon_count)
-    block = level_block(levels, rows_here)
+    block = level_block(levels, rows_here, 16)
     width = levels * rows_here
     whole = lambda *shape: pl.BlockSpec(shape, lambda i: (0,) * len(shape))
     return pl.pallas_call(
-        functools.partial(fourier_kernel, math.sqrt(2.0 / lon_count)),
+        functools.partial(fourier_kernel, half_rows),
         out_shape=[
             jax.ShapeDtypeStruct((height, width), jnp.bfloat16),
             jax.ShapeDtypeStruct((height, lon_count), jnp.bfloat16),
         ],
         grid=(levels // block,),
         in_specs=[
+            pl.BlockSpec(memory_space=pltpu.SMEM),
             pl.BlockSpec((block, rows_here, lon_count), lambda i: (i, 0, 0)),
             whole(rows_here, 1),
-            whole(height, blocks),
-            whole(height, blocks),
-            whole(height, LANES),
-            whole(height, LANES),
+            whole(height, 1),
+            whole(height, 1),
         ],
         out_specs=[
             pl.BlockSpec((height, block * rows_here), lambda i: (0, i)),
@@ -106,7 +113,7 @@
             bytes_accessed=2 * (width * lon_count + height * (width + lon_count)),
             transcendentals=width * lon_count,
         ),
-    )(grid_state, coupling, jnp.cos(high), jnp.sin(high), jnp.cos(low), jnp.sin(low))
+    )(sign[None], grid_state, lat_rows[:, None], ids[:, None], quarter[:, None])
 
 
 def inverse_kernel(pieces, tables, *refs):
@@ -115,38 +122,47 @@
     table = jnp.concatenate([ref[...] for ref in refs[pieces : pieces + tables]], axis=0)
     current = lax.dot_general(
         coeffs, table, (((0,), (0,)), ((), ())), preferred_element_type=jnp.float32
-    ).reshape(out.shape)
-    if len(refs) > pieces + tables + 1:
-        current = current + refs[pieces + tables][...]
-    out[...] = current.astype(out.dtype)
-
-
-def inverse_fourier(pieces, tables, shape, dtype, partial=None):
-    levels, rows_here, lon_count = shape
-    block = level_block(levels, rows_here)
+    )
+    out[...] = current.astype(out.dtype).reshape(out.shape)
+
+
+def inverse_fourier(pieces, tables, current, shape, start, levels):
+    _, rows_here, lon_count = shape
+    block = level_block(levels, rows_here, 8)
+    width = block * rows_here
+    full = shape[0] * rows_here
+    first = start // block
     height = sum(piece.shape[0] for piece in pieces)
-    grid_spec = pl.BlockSpec((block, rows_here, lon_count), lambda i: (i, 0, 0))
-    partials = [] if partial is None else [partial]
+    specs = [
+        pl.BlockSpec(
+            (piece.shape[0], width),
+            (lambda i: (0, first + i)) if piece.shape[1] == full else (lambda i: (0, i)),
+        )
+        for piece in pieces
+    ] + [
+        pl.BlockSpec(table.shape, lambda i: (0, 0), pipeline_mode=pl.Buffered(1))
+        for table in tables
+    ]
+    operands = list(pieces) + list(tables)
+    aliases = {}
+    if current is not None:
+        aliases = {len(operands): 0}
+        operands.append(current)
+        specs.append(pl.BlockSpec(memory_space=pl.ANY))
     return pl.pallas_call(
         functools.partial(inverse_kernel, len(pieces), len(tables)),
-        out_shape=jax.ShapeDtypeStruct(shape, dtype),
+        out_shape=jax.ShapeDtypeStruct(shape, jnp.bfloat16),
         grid=(levels // block,),
-        in_specs=[
-            pl.BlockSpec((piece.shape[0], block * rows_here), lambda i: (0, i)) for piece in pieces
-        ]
-        + [
-            pl.BlockSpec(table.shape, lambda i: (0, 0), pipeline_mode=pl.Buffered(1))
-            for table in tables
-        ]
-        + [grid_spec] * len(partials),
-        out_specs=grid_spec,
+        in_specs=specs,
+        out_specs=pl.BlockSpec((block, rows_here, lon_count), lambda i: (first + i, 0, 0)),
+        input_output_aliases=aliases,
         compiler_params=pltpu.CompilerParams(vmem_limit_bytes=40 * 2**20),
         cost_estimate=pl.CostEstimate(
             flops=2 * height * levels * rows_here * lon_count,
-            bytes_accessed=levels * rows_here * (2 * height + 6 * lon_count),
+            bytes_accessed=2 * levels * rows_here * (height + lon_count),
             transcendentals=0,
         ),
-    )(*pieces, *tables, *partials)
+    )(*operands)
 
 
 def column_kernel(sizes, waves, scalars, eig_ref, modes_in, modes_out, table, *refs):
@@ -355,6 +371,7 @@
         and rows_here * 2 == LANES
         and wave_size % 2 == 0
         and count % 16 == 0
+        and local_levels % 32 == 0
     )
     parity = lax.axis_index("fld")
     wave_place = lax.axis_index("wave")
@@ -364,8 +381,6 @@
     grid_state = grid_state.reshape(local_levels, rows_here, lon_count)
     hemi_sign = 1.0 - 2.0 * parity.astype(jnp.float32)
     lat_rows = lax.dynamic_slice_in_dim(lat_order, wave_place * rows_here, rows_here)
-    sine = jnp.sin((lat_rows.astype(jnp.float32) + 0.5) * (math.pi / (2.0 * half_rows)))
-    coupling = (0.5 * hemi_sign * sine)[:, None]
     waves = lax.dynamic_slice_in_dim(wave_order, place * narrow, narrow)
     quarter = jnp.broadcast_to(
         (jnp.arange(2, dtype=jnp.int32) * (lon_count // 4))[None, :, None], (places, 2, count)
@@ -388,7 +403,9 @@
     if not direct:
         returned, tables = [], []
         for chunk in range(chunks):
-            value, table = fourier(grid_state, coupling, slot_ids(fixed, chunk), quarter)
+            value, table = fourier(
+                grid_state, hemi_sign, lat_rows, half_rows, slot_ids(fixed, chunk), quarter
+            )
             tables.append(table)
             own = exchange(value.reshape(places, height, width))
             mirrored = joined(partner(own, "fld"), own, 1.0)
@@ -404,7 +421,7 @@
             ).reshape(places, height, width)
             hemi = exchange(joined(partner(grid, "fld"), grid, 0.5))
             returned.append(hemi.reshape(places * height, width))
-        current = inverse_fourier(returned, tables, grid_state.shape, jnp.bfloat16)
+        current = inverse_fourier(returned, tables, None, grid_state.shape, 0, local_levels)
         return current.reshape(out_shape)
 
     tiles = width // LANES
@@ -426,10 +443,9 @@
 
     arrived, tables = [], []
     for chunk in range(chunks):
-        is_whole = chunk in WHOLE_SENDS
-        value, table = fourier(
-            grid_state, coupling, slot_ids(fixed if is_whole else turned, chunk), quarter
-        )
+        is_whole = chunk in WHOLE_CHUNKS
+        ids = slot_ids(fixed if is_whole else turned, chunk)
+        value, table = fourier(grid_state, hemi_sign, lat_rows, half_rows, ids, quarter)
         tables.append(table)
         if is_whole:
             arrived.append([exchange(value.reshape(places, 2, count, width))])
@@ -443,9 +459,11 @@
             pieces.append(piece.reshape(2, count, width))
         arrived.append(pieces)
 
-    returned = []
+    cuts = [(0, local_levels // 2)]
+    cuts += [(local_levels // 4 * part, local_levels // 4) for part in (2, 3)]
+    returned, last = [], []
     for chunk in range(chunks):
-        is_whole = chunk in WHOLE_SENDS
+        is_whole = chunk in WHOLE_CHUNKS
         pieces = arrived[chunk]
         if is_whole:
             pieces = [pieces[0], partner(pieces[0], "fld")]
@@ -454,23 +472,27 @@
         grid = columns_fused(pieces, legendre, waves, scalars, eig_rates, modes, sizes)
         grid = grid.reshape(places, height, width)
         other = partner(grid, "fld")
-        if chunk in WHOLE_BACKS:
+        if is_whole:
             hemi = exchange(joined(other, grid, 0.5))
-            returned.append([hemi.reshape(places * height, width)])
+            returned.append(hemi.reshape(places * height, width))
             continue
-        pieces = []
-        for index, (wave, level) in enumerate(shifts):
-            hemi = joined(other[index], grid[index], 0.5)
-            pieces.append(
-                shift_places(hemi, (wave_size - wave) % wave_size, (level_size - level) % level_size)
-            )
-        returned.append(pieces)
-    half = chunks // 2
-    flat = lambda groups: [piece for group in groups for piece in group]
-    partial = inverse_fourier(flat(returned[:half]), tables[:half], grid_state.shape, jnp.float32)
-    current = inverse_fourier(
-        flat(returned[half:]), tables[half:], grid_state.shape, jnp.bfloat16, partial
-    )
+        is_last = chunk == chunks - 1
+        for start, levels in cuts if is_last else [(0, local_levels)]:
+            lanes = slice(start * rows_here, (start + levels) * rows_here)
+            pieces = []
+            for index, (wave, level) in enumerate(shifts):
+                hemi = joined(other[index, :, lanes], grid[index, :, lanes], 0.5)
+                wave, level = (wave_size - wave) % wave_size, (level_size - level) % level_size
+                pieces.append(shift_places(hemi, wave, level))
+            if is_last:
+                last.append(pieces)
+            else:
+                returned += pieces
+    current = None
+    for cut, (start, levels) in enumerate(cuts):
+        current = inverse_fourier(
+            returned + last[cut], tables, current, grid_state.shape, start, levels
+        )
     return current.reshape(out_shape)
 
 

time: 458 us -> 571 us (1.25)
  starting transfers between devices: 93.6 us -> 140 us
  waiting for transfers between devices: 167 us -> 211 us
  local copies, waits for them, and re-layouts: 10.4 us -> 48.7 us
  Pallas kernels: 150 us -> 140 us
    all_to_all x4, waiting for transfers between devices: 30.9 us -> 81 us  [exchange(): lax.all_to_all(value, EXCHANGE_AXES, split_axis=0, concat_axis=0, tiled=T...]
    ppermute x28 -> x42, starting transfers between devices: 70 us -> 119 us  [shift_places(): return lax.ppermute(value, EXCHANGE_AXES, pairs)]
    unnamed x53 -> x117, local copies, waits for them, and re-layouts: 3.8 us -> 37.8 us
    sin x8 -> x0, other arithmetic: 9.97 us -> none  [the longest x4 5.28 us: fourier(): jnp.sin(low)]
    pallas_call x2 -> x3, Pallas kernels: 30.7 us -> 21.7 us  [inverse_fourier(): pl.pallas_call(functools.partial(inverse_kernel, len(pieces), len(tables)...]
    mul x2 -> x3, other arithmetic: 0.01 us -> 6.93 us  [joined(): scale * (other.astype(jnp.float32) + hemi_sign * own.astype(jnp.float32))]
    ppermute x28 -> x42, waiting for transfers between devices: 136 us -> 130 us  [shift_places(): return lax.ppermute(value, EXCHANGE_AXES, pairs)]
    convert_element_type x6 -> x5, other arithmetic: 16.9 us -> 18.3 us  [joined(): return both.astype(jnp.bfloat16)]
  transfers between devices with their start and end apart: 40 -> 54, of which waited for: 9 -> 13; matrix products, arithmetic and copies ran while one was open for 7% -> 6% of each run, Pallas kernels for 26% -> 22%
where the time goes in v2:
time: 571 us; the launch traced here: 569 us
  waiting for transfers between devices  211 us (37%)
  Pallas kernels  140 us (25%)
  starting transfers between devices  140 us (25%)
  local copies, waits for them, and re-layouts  48.7 us (9%)
  other arithmetic  28.5 us (5%)
    ppermute x42, waiting for transfers between devices, shift_places(): return lax.ppermute(value, EXCHANGE_AXES, pairs)  130 us
    ppermute x42, starting transfers between devices, shift_places(): return lax.ppermute(value, EXCHANGE_AXES, pairs)  119 us
    all_to_all x4, waiting for transfers between devices, exchange(): lax.all_to_all(value, EXCHANGE_AXES, split_axis=0, concat_axis=0, tiled=T...  81 us
    pallas_call x4, Pallas kernels, columns_fused(): pl.pallas_call(functools.partial(column_kernel, sizes), out_shape=jax.Sha...  74 us
    pallas_call x4, Pallas kernels, fourier(): pl.pallas_call(functools.partial(fourier_kernel, half_rows), out_shape=[j...  44.4 us
    unnamed x117, local copies, waits for them, and re-layouts  37.8 us
    pallas_call x3, Pallas kernels, inverse_fourier(): pl.pallas_call(functools.partial(inverse_kernel, len(pieces), len(tables)...  21.7 us
    all_to_all x4, starting transfers between devices, exchange(): lax.all_to_all(value, EXCHANGE_AXES, split_axis=0, concat_axis=0, tiled=T...  19.9 us
  transfers between devices with their start and end apart: 54, of which 13 were waited for; matrix products, arithmetic and copies ran while one was open for 6% of the time, Pallas kernels for 22%

profile of v2, /device:TPU:0, one launch (start us, length us, event | category | flops | bytes accessed | tf_op | source)
XLA Modules:
  0.0 568.8 jit_solution(5446842972549798232)
XLA Ops:
  3.9 11.1 %shard_map.73 = (bf16[256,4096]{1,0:T(8,128)(2,1)}, bf16[256,1536]{1,0:T(8,128)(2,1)}) custom-call(f32[1]{0:T(128)} %bitcast.4.sign_ref, bf16[64,64,1536]{2,1,0:T(8,128)(2,1)} %bitcast.172, s32[64,1]{1,0:T(8,128)} %copy.25.lat_rows, s32[256,1]{1,0:T(8,128)} %broadcast_in_dim_reshape.29.ids, s32[256,1]{1,0:T(8,128)} %broadcast_in_dim_reshape.30.quarter), custom_call_target="tpu_custom_call" | custom-call | flops 3221225472 | bytes 15466496 | tf_op jit(solution)/shard_map/pallas_call | solution.py:92
  15.0 7.3 %all-to-all-start = ((bf16[8,2,16,4096]{3,2,1,0:T(8,128)(2,1)}), bf16[8,2,16,4096]{3,2,1,0:T(8,128)(2,1)S(1)}, u32[]{:S(2)}, u32[]{:S(2)}) async-start(bf16[8,2,16,4096]{3,2,1,0:T(8,128)(2,1)} %bitcast.177), calls=%async_computation | async-start | bytes 4194304 | tf_op jit(solution)/shard_map/all_to_all | solution.py:397
  23.0 11.1 %shard_map.77 = (bf16[256,4096]{1,0:T(8,128)(2,1)}, bf16[256,1536]{1,0:T(8,128)(2,1)}) custom-call(f32[1]{0:T(128)} %bitcast.4.sign_ref, bf16[64,64,1536]{2,1,0:T(8,128)(2,1)} %bitcast.173, s32[64,1]{1,0:T(8,128)} %copy.25.lat_rows, s32[256,1]{1,0:T(8,128)} %broadcast_in_dim_reshape.32.ids, s32[256,1]{1,0:T(8,128)} %broadcast_in_dim_reshape.30.quarter), custom_call_target="tpu_custom_call" | custom-call | flops 3221225472 | bytes 15466496 | tf_op jit(solution)/shard_map/pallas_call | solution.py:92
  34.1 36.4 %all-to-all-done.refs_0_ = bf16[8,2,16,4096]{3,2,1,0:T(8,128)(2,1)S(1)} async-done(((bf16[8,2,16,4096]{3,2,1,0:T(8,128)(2,1)}), bf16[8,2,16,4096]{3,2,1,0:T(8,128)(2,1)S(1)}, u32[]{:S(2)}, u32[]{:S(2)}) %all-to-all-start) | async-done | bytes 2097184 | tf_op jit(solution)/shard_map/all_to_all | solution.py:397
  70.5 4.7 all-to-all-start.2
  78.3 44.6 %all-to-all-done.2.refs_0_ = bf16[8,2,16,4096]{3,2,1,0:T(8,128)(2,1)} async-done(((bf16[8,2,16,4096]{3,2,1,0:T(8,128)(2,1)}), bf16[8,2,16,4096]{3,2,1,0:T(8,128)(2,1)}, u32[]{:S(2)}, u32[]{:S(2)}) %all-to-all-start.2) | async-done | bytes 2097184 | tf_op jit(solution)/shard_map/all_to_all | solution.py:397
  122.9 1.6 copy-done.4
  124.5 18.2 %shard_map.74 = bf16[8,2,16,4096]{3,2,1,0:T(8,128)(2,1)S(1)} custom-call(s32[64]{0:T(128)S(1)} %dynamic_slice.12.waves, s32[5]{0:T(128)S(1)} %pad_add_fusion.scalars, f32[128,1]{1,0:T(8,128)S(1)} %copy.28.eig_ref, bf16[128,128]{1,0:T(8,128)(2,1)S(1)} %select_bitcast_fusion.1.modes_in, bf16[128,128]{1,0:T(8,128)(2,1)S(1)} %broadcast_select_fusion.1.modes_out, ...), custom_call_target="tpu_custom_call" | custom-call | flops 1610612736 | bytes 6291456 | tf_op jit(solution)/shard_map/pallas_call | solution.py:306
  144.2 11.1 %shard_map.75 = (bf16[256,4096]{1,0:T(8,128)(2,1)}, bf16[256,1536]{1,0:T(8,128)(2,1)}) custom-call(f32[1]{0:T(128)} %bitcast.4.sign_ref, bf16[64,64,1536]{2,1,0:T(8,128)(2,1)} %bitcast.174, s32[64,1]{1,0:T(8,128)} %copy.25.lat_rows, s32[256,1]{1,0:T(8,128)} %broadcast_in_dim_reshape.31.ids, s32[256,1]{1,0:T(8,128)} %broadcast_in_dim_reshape.30.quarter), custom_call_target="tpu_custom_call" | custom-call | flops 3221225472 | bytes 15466496 | tf_op jit(solution)/shard_map/pallas_call | solution.py:92
  156.0 11.2 %shard_map.79 = (bf16[256,4096]{1,0:T(8,128)(2,1)}, bf16[256,1536]{1,0:T(8,128)(2,1)}) custom-call(f32[1]{0:T(128)} %bitcast.4.sign_ref, bf16[64,64,1536]{2,1,0:T(8,128)(2,1)} %bitcast.175, s32[64,1]{1,0:T(8,128)} %copy.25.lat_rows, s32[256,1]{1,0:T(8,128)} %broadcast_in_dim_reshape.33.ids, s32[256,1]{1,0:T(8,128)} %broadcast_in_dim_reshape.30.quarter), custom_call_target="tpu_custom_call" | custom-call | flops 3221225472 | bytes 15466496 | tf_op jit(solution)/shard_map/pallas_call | solution.py:92
  167.7 20.2 %shard_map.78 = bf16[8,2,16,4096]{3,2,1,0:T(8,128)(2,1)} custom-call(s32[64]{0:T(128)S(1)} %dynamic_slice.12.waves, s32[5]{0:T(128)S(1)} %pad_add_fusion.scalars, f32[128,1]{1,0:T(8,128)S(1)} %copy.28.eig_ref, bf16[128,128]{1,0:T(8,128)(2,1)S(1)} %select_bitcast_fusion.1.modes_in, bf16[128,128]{1,0:T(8,128)(2,1)S(1)} %broadcast_select_fusion.1.modes_out, ...), custom_call_target="tpu_custom_call" | custom-call | flops 1610612736 | bytes 6291456 | tf_op jit(solution)/shard_map/pallas_call | solution.py:306
  187.9 3.9 multiply_convert_fusion.1
  191.8 3.6 all-to-all-start.1
  195.5 3.8 add_convert_fusion.8
  199.3 4.6 collective-permute-start.9
  205.4 2.9 collective-permute-start.6
  208.3 29.1 %collective-permute-done.9 = bf16[32,4096]{1,0:T(8,128)(2,1)S(1)} collective-permute-done((bf16[32,4096]{1,0:T(8,128)(2,1)}, bf16[32,4096]{1,0:T(8,128)(2,1)S(1)}, u32[]{:S(2)}, u32[]{:S(2)}) %collective-permute-start.9) | collective-permute-done | bytes 262176 | tf_op jit(solution)/shard_map/ppermute | solution.py:34
  237.4 31.6 %collective-permute-start.5 = (bf16[32,4096]{1,0:T(8,128)(2,1)}, bf16[32,4096]{1,0:T(8,128)(2,1)S(1)}, u32[]{:S(2)}, u32[]{:S(2)}) collective-permute-start(bf16[32,4096]{1,0:T(8,128)(2,1)} %get-tuple-element.59), channel_id=1, source_target_pairs={{0,6},{2,4},{4,10},{6,8},{8,14},{10,12},{12,2},{14,0},{1,7},{3,5},... | collective-permute-start | bytes 786440 | tf_op jit(solution)/shard_map/ppermute | solution.py:34
  269.0 10.3 %collective-permute-start.4 = (bf16[32,4096]{1,0:T(8,128)(2,1)}, bf16[32,4096]{1,0:T(8,128)(2,1)S(1)}, u32[]{:S(2)}, u32[]{:S(2)}) collective-permute-start(bf16[32,4096]{1,0:T(8,128)(2,1)} %get-tuple-element.60), channel_id=1, source_target_pairs={{0,4},{2,6},{4,8},{6,10},{8,12},{10,14},{12,0},{14,2},{1,5},{3,7},... | collective-permute-start | bytes 786440 | tf_op jit(solution)/shard_map/ppermute | solution.py:34
  279.3 3.8 add_convert_fusion
  283.2 2.1 collective-permute-done.7
  285.9 3.7 collective-permute-done.6
  291.0 2.0 collective-permute-start.26
  293.7 2.4 collective-permute-start.25
  296.1 1.3 gather_fusion.3
  298.9 1.8 collective-permute-done.27
  300.6 6.4 %collective-permute-done.26 = bf16[32,4096]{1,0:T(8,128)(2,1)} collective-permute-done((bf16[32,4096]{1,0:T(8,128)(2,1)}, bf16[32,4096]{1,0:T(8,128)(2,1)}, u32[]{:S(2)}, u32[]{:S(2)}) %collective-permute-start.26) | collective-permute-done | bytes 262176 | tf_op jit(solution)/shard_map/ppermute | solution.py:34
  307.0 24.9 %collective-permute-done.25 = bf16[32,4096]{1,0:T(8,128)(2,1)} collective-permute-done((bf16[32,4096]{1,0:T(8,128)(2,1)}, bf16[32,4096]{1,0:T(8,128)(2,1)}, u32[]{:S(2)}, u32[]{:S(2)}) %collective-permute-start.25) | collective-permute-done | bytes 262176 | tf_op jit(solution)/shard_map/ppermute | solution.py:34
  332.4 3.4 copy-done.2
  338.6 17.7 %shard_map.76 = bf16[8,2,16,4096]{3,2,1,0:T(8,128)(2,1)} custom-call(s32[64]{0:T(128)S(1)} %dynamic_slice.12.waves, s32[5]{0:T(128)S(1)} %pad_add_fusion.1.scalars, f32[128,1]{1,0:T(8,128)S(1)} %copy.28.eig_ref, bf16[128,128]{1,0:T(8,128)(2,1)S(1)} %select_bitcast_fusion.modes_in, bf16[128,128]{1,0:T(8,128)(2,1)S(1)} %broadcast_select_fusion.modes_out, ...), custom_call_target="tpu_custom_call" | custom-call | flops 1610612736 | bytes 6291456 | tf_op jit(solution)/shard_map/pallas_call | solution.py:306
  356.3 17.9 %shard_map.80 = bf16[8,2,16,4096]{3,2,1,0:T(8,128)(2,1)} custom-call(s32[64]{0:T(128)S(1)} %dynamic_slice.12.waves, s32[5]{0:T(128)S(1)} %pad_add_fusion.1.scalars, f32[128,1]{1,0:T(8,128)S(1)} %copy.28.eig_ref, bf16[128,128]{1,0:T(8,128)(2,1)S(1)} %select_bitcast_fusion.modes_in, bf16[128,128]{1,0:T(8,128)(2,1)S(1)} %broadcast_select_fusion.modes_out, ...), custom_call_target="tpu_custom_call" | custom-call | flops 1610612736 | bytes 6291456 | tf_op jit(solution)/shard_map/pallas_call | solution.py:306
  374.7 4.6 multiply_convert_fusion
  379.3 4.4 all-to-all-start.3
  383.6 2.0 convert_multiply_fusion
  385.6 2.1 fusion.30
  387.7 1.9 collective-permute-start.34
  389.6 3.3 collective-permute-start.33
  392.9 2.2 fusion.39
  396.2 2.7 fusion.23
  398.9 2.4 collective-permute-start.49
  401.3 23.1 %collective-permute-done.34.refs_16_ = bf16[32,1024]{1,0:T(8,128)(2,1)S(1)} collective-permute-done((bf16[32,1024]{1,0:T(8,128)(2,1)S(1)}, bf16[32,1024]{1,0:T(8,128)(2,1)S(1)}, u32[]{:S(2)}, u32[]{:S(2)}) %collective-permute-start.34) | collective-permute-done | bytes 65568 | tf_op jit(solution)/shard_map/ppermute | solution.py:34
  425.0 10.2 %collective-permute-start.48 = (bf16[32,2048]{1,0:T(8,128)(2,1)S(1)}, bf16[32,2048]{1,0:T(8,128)(2,1)S(1)}, u32[]{:S(2)}, u32[]{:S(2)}) collective-permute-start(bf16[32,2048]{1,0:T(8,128)(2,1)S(1)} %get-tuple-element.24), channel_id=1, source_target_pairs={{0,4},{2,6},{4,8},{6,10},{8,12},{10,14},{12,0},{14,2},{1,5},{3,7},... | collective-permute-start | bytes 393224 | tf_op jit(solution)/shard_map/ppermute | solution.py:34
  435.2 16.2 %collective-permute-done.33.refs_15_ = bf16[32,1024]{1,0:T(8,128)(2,1)S(1)} collective-permute-done((bf16[32,1024]{1,0:T(8,128)(2,1)S(1)}, bf16[32,1024]{1,0:T(8,128)(2,1)S(1)}, u32[]{:S(2)}, u32[]{:S(2)}) %collective-permute-start.33) | collective-permute-done | bytes 65568 | tf_op jit(solution)/shard_map/ppermute | solution.py:34
  452.6 2.9 collective-permute-start.46
  455.5 2.2 fusion.1
  459.1 1.5 collective-permute-start.16
  461.3 3.3 collective-permute-start.45
  465.2 2.0 collective-permute-start.44
  467.9 1.5 collective-permute-start.43
  469.3 6.8 %collective-permute-done.45.refs_13_ = bf16[32,2048]{1,0:T(8,128)(2,1)S(1)} collective-permute-done((bf16[32,2048]{1,0:T(8,128)(2,1)S(1)}, bf16[32,2048]{1,0:T(8,128)(2,1)S(1)}, u32[]{:S(2)}, u32[]{:S(2)}) %collective-permute-start.45) | collective-permute-done | bytes 131104 | tf_op jit(solution)/shard_map/ppermute | solution.py:34
  476.8 2.9 collective-permute-start.15
  482.1 2.4 collective-permute-start.13
  486.1 1.5 collective-permute-start.11
  487.6 10.6 %collective-permute-done.15.refs_6_ = bf16[32,4096]{1,0:T(8,128)(2,1)S(1)} collective-permute-done((bf16[32,4096]{1,0:T(8,128)(2,1)S(1)}, bf16[32,4096]{1,0:T(8,128)(2,1)S(1)}, u32[]{:S(2)}, u32[]{:S(2)}) %collective-permute-start.15) | collective-permute-done | bytes 262176 | tf_op jit(solution)/shard_map/ppermute | solution.py:34
  498.9 4.9 collective-permute-done.14.refs_5_
  505.2 14.6 %collective-permute-start.38 = (bf16[32,1024]{1,0:T(8,128)(2,1)}, bf16[32,1024]{1,0:T(8,128)(2,1)}, u32[]{:S(2)}, u32[]{:S(2)}) collective-permute-start(bf16[32,1024]{1,0:T(8,128)(2,1)} %get-tuple-element.35), channel_id=1, source_target_pairs={{0,14},{2,12},{4,2},{6,0},{8,6},{10,4},{12,10},{14,8},{1,15},{3,13... | collective-permute-start | bytes 196616 | tf_op jit(solution)/shard_map/ppermute | solution.py:34
  522.1 1.1 copy-done.6
  523.2 1.1 copy-done.7
  538.5 9.9 %shard_map.81.refs_22_ = bf16[64,64,1536]{2,1,0:T(8,128)(2,1)} custom-call(bf16[256,4096]{1,0:T(8,128)(2,1)S(1)} %bitcast.156, bf16[32,4096]{1,0:T(8,128)(2,1)S(1)} %get-tuple-element.70.refs_1_, bf16[32,4096]{1,0:T(8,128)(2,1)S(1)} %copy-done.20, bf16[32,4096]{1,0:T(8,128)(2,1)S(1)} %copy-done.18, bf16[32,4096]{1,0:T(8,128)(2,1)S(1)} %copy-done.16, ...), custom_call_target="tpu_custom_call" | custom-call | flops 6442450944 | bytes 10485760 | tf_op jit(solution)/shard_map/pallas_call | solution.py:152
  548.4 2.0 collective-permute-start.32
  550.4 3.0 collective-permute-start.31
  554.3 2.6 collective-permute-start.35
  556.9 5.9 %shard_map.82.refs_22_ = bf16[64,64,1536]{2,1,0:T(8,128)(2,1)} custom-call(bf16[256,4096]{1,0:T(8,128)(2,1)S(1)} %bitcast.157, bf16[32,4096]{1,0:T(8,128)(2,1)S(1)} %get-tuple-element.70.refs_1_, bf16[32,4096]{1,0:T(8,128)(2,1)S(1)} %copy-done.20, bf16[32,4096]{1,0:T(8,128)(2,1)S(1)} %copy-done.18, ...), custom_call_target="tpu_custom_call", output_to_operand_aliasing={{}: (22, {})} | custom-call | flops 3221225472 | bytes 5242880 | tf_op jit(solution)/shard_map/pallas_call | solution.py:152
  562.9 5.9 %shard_map.83 = bf16[64,64,1536]{2,1,0:T(8,128)(2,1)} custom-call(bf16[256,4096]{1,0:T(8,128)(2,1)S(1)} %bitcast.158, bf16[32,4096]{1,0:T(8,128)(2,1)S(1)} %get-tuple-element.70.refs_1_, bf16[32,4096]{1,0:T(8,128)(2,1)S(1)} %copy-done.20, bf16[32,4096]{1,0:T(8,128)(2,1)S(1)} %copy-done.18, ...), custom_call_target="tpu_custom_call", output_to_operand_aliasing={{}: (22, {})} | custom-call | flops 3221225472 | bytes 5242880 | tf_op jit(solution)/shard_map/pallas_call | solution.py:152
  (226 shorter events, 50.2 us)
Async XLA Ops:
  0.0 77.3 %copy-start = (bf16[128,128]{1,0:T(8,128)(2,1)S(1)}, bf16[128,128]{1,0:T(8,128)(2,1)}, u32[]{:S(2)}) copy-start(bf16[128,128]{1,0:T(8,128)(2,1)} %param.17) | copy-start | bytes 98308
  15.0 55.5 %all-to-all-start = ((bf16[8,2,16,4096]{3,2,1,0:T(8,128)(2,1)}), bf16[8,2,16,4096]{3,2,1,0:T(8,128)(2,1)S(1)}, u32[]{:S(2)}, u32[]{:S(2)}) async-start(bf16[8,2,16,4096]{3,2,1,0:T(8,128)(2,1)} %bitcast.177), calls=%async_computation | async-start | bytes 4194304 | tf_op jit(solution)/shard_map/all_to_all | solution.py:397
  70.5 52.4 %all-to-all-start.2 = ((bf16[8,2,16,4096]{3,2,1,0:T(8,128)(2,1)}), bf16[8,2,16,4096]{3,2,1,0:T(8,128)(2,1)}, u32[]{:S(2)}, u32[]{:S(2)}) async-start(bf16[8,2,16,4096]{3,2,1,0:T(8,128)(2,1)} %bitcast.176), calls=%async_computation.2 | async-start | bytes 4194304 | tf_op jit(solution)/shard_map/all_to_all | solution.py:397
  75.2 47.7 %collective-permute-start = (bf16[8,2,16,4096]{3,2,1,0:T(8,128)(2,1)S(1)}, bf16[8,2,16,4096]{3,2,1,0:T(8,128)(2,1)}, u32[]{:S(2)}, u32[]{:S(2)}) collective-permute-start(bf16[8,2,16,4096]{3,2,1,0:T(8,128)(2,1)S(1)} %all-to-all-done.refs_0_), channel_id=1, source_target_pairs={{0,1},{1,0},{2,3},{3,2},{4,5},{5,4},{6,7},{7,6},{8,9},{9,8},{10,11... | collective-permute-start | bytes 6291464 | tf_op jit(solution)/shard_map/ppermute | solution.py:22
  122.9 44.8 %collective-permute-start.18 = (bf16[8,2,16,4096]{3,2,1,0:T(8,128)(2,1)}, bf16[8,2,16,4096]{3,2,1,0:T(8,128)(2,1)}, u32[]{:S(2)}, u32[]{:S(2)}) collective-permute-start(bf16[8,2,16,4096]{3,2,1,0:T(8,128)(2,1)} %all-to-all-done.2.refs_0_), channel_id=1, source_target_pairs={{0,1},{1,0},{2,3},{3,2},{4,5},{5,4},{6,7},{7,6},{8,9},{9,8},{10,11... | collective-permute-start | bytes 6291464 | tf_op jit(solution)/shard_map/ppermute | solution.py:22
  142.8 45.2 %collective-permute-start.1 = (bf16[8,32,4096]{2,1,0:T(8,128)(2,1)S(1)}, bf16[8,32,4096]{2,1,0:T(8,128)(2,1)}, u32[]{:S(2)}, u32[]{:S(2)}) collective-permute-start(bf16[8,32,4096]{2,1,0:T(8,128)(2,1)S(1)} %bitcast.159), channel_id=1, source_target_pairs={{0,1},{1,0},{2,3},{3,2},{4,5},{5,4},{6,7},{7,6},{8,9},{9,8},{10,11... | collective-permute-start | bytes 6291464 | tf_op jit(solution)/shard_map/ppermute | solution.py:22
  155.2 40.2 %collective-permute-start.2 = (bf16[256,4096]{1,0:T(8,128)(2,1)}, bf16[256,4096]{1,0:T(8,128)(2,1)}, u32[]{:S(2)}, u32[]{:S(2)}) collective-permute-start(bf16[256,4096]{1,0:T(8,128)(2,1)} %get-tuple-element.16), channel_id=1, source_target_pairs={{0,1},{1,0},{2,3},{3,2},{4,5},{5,4},{6,7},{7,6},{8,9},{9,8},{10,11... | collective-permute-start | bytes 6291464 | tf_op jit(solution)/shard_map/ppermute | solution.py:22
  167.2 38.2 %collective-permute-start.20 = (bf16[256,4096]{1,0:T(8,128)(2,1)}, bf16[256,4096]{1,0:T(8,128)(2,1)}, u32[]{:S(2)}, u32[]{:S(2)}) collective-permute-start(bf16[256,4096]{1,0:T(8,128)(2,1)} %get-tuple-element.18), channel_id=1, source_target_pairs={{0,1},{1,0},{2,3},{3,2},{4,5},{5,4},{6,7},{7,6},{8,9},{9,8},{10,11... | collective-permute-start | bytes 6291464 | tf_op jit(solution)/shard_map/ppermute | solution.py:22
  187.9 186.8 %collective-permute-start.19 = (bf16[8,32,4096]{2,1,0:T(8,128)(2,1)}, bf16[8,32,4096]{2,1,0:T(8,128)(2,1)}, u32[]{:S(2)}, u32[]{:S(2)}) collective-permute-start(bf16[8,32,4096]{2,1,0:T(8,128)(2,1)} %bitcast.42), channel_id=1, source_target_pairs={{0,1},{1,0},{2,3},{3,2},{4,5},{5,4},{6,7},{7,6},{8,9},{9,8},{10,11... | collective-permute-start | bytes 6291464 | tf_op jit(solution)/shard_map/ppermute | solution.py:22
  191.8 187.4 %all-to-all-start.1 = ((bf16[8,32,4096]{2,1,0:T(8,128)(2,1)}), bf16[8,32,4096]{2,1,0:T(8,128)(2,1)S(1)}, u32[]{:S(2)}, u32[]{:S(2)}) async-start(bf16[8,32,4096]{2,1,0:T(8,128)(2,1)} %multiply_convert_fusion.1), calls=%async_computation.1 | async-start | bytes 4194304 | tf_op jit(solution)/shard_map/all_to_all | solution.py:397
  199.3 38.1 %collective-permute-start.9 = (bf16[32,4096]{1,0:T(8,128)(2,1)}, bf16[32,4096]{1,0:T(8,128)(2,1)S(1)}, u32[]{:S(2)}, u32[]{:S(2)}) collective-permute-start(bf16[32,4096]{1,0:T(8,128)(2,1)} %get-tuple-element.55), channel_id=1, source_target_pairs={{0,14},{2,12},{4,2},{6,0},{8,6},{10,4},{12,10},{14,8},{1,15},{3,13... | collective-permute-start | bytes 786440 | tf_op jit(solution)/shard_map/ppermute | solution.py:34
  203.9 65.1 %collective-permute-start.8 = (bf16[32,4096]{1,0:T(8,128)(2,1)S(1)}, bf16[32,4096]{1,0:T(8,128)(2,1)S(1)}, u32[]{:S(2)}, u32[]{:S(2)}) collective-permute-start(bf16[32,4096]{1,0:T(8,128)(2,1)S(1)} %get-tuple-element.56), channel_id=1, source_target_pairs={{0,12},{2,14},{4,0},{6,2},{8,4},{10,6},{12,8},{14,10},{1,13},{3,15... | collective-permute-start | bytes 786440 | tf_op jit(solution)/shard_map/ppermute | solution.py:34
  205.3 79.9 %collective-permute-start.7 = (bf16[32,4096]{1,0:T(8,128)(2,1)}, bf16[32,4096]{1,0:T(8,128)(2,1)S(1)}, u32[]{:S(2)}, u32[]{:S(2)}) collective-permute-start(bf16[32,4096]{1,0:T(8,128)(2,1)} %get-tuple-element.57), channel_id=1, source_target_pairs={{0,10},{2,8},{4,14},{6,12},{8,2},{10,0},{12,6},{14,4},{1,11},{3,9}... | collective-permute-start | bytes 786440 | tf_op jit(solution)/shard_map/ppermute | solution.py:34
  205.4 84.1 %collective-permute-start.6 = (bf16[32,4096]{1,0:T(8,128)(2,1)}, bf16[32,4096]{1,0:T(8,128)(2,1)S(1)}, u32[]{:S(2)}, u32[]{:S(2)}) collective-permute-start(bf16[32,4096]{1,0:T(8,128)(2,1)} %get-tuple-element.58), channel_id=1, source_target_pairs={{0,8},{2,10},{4,12},{6,14},{8,0},{10,2},{12,4},{14,6},{1,9},{3,11}... | collective-permute-start | bytes 786440 | tf_op jit(solution)/shard_map/ppermute | solution.py:34
  237.4 52.9 %collective-permute-start.5 = (bf16[32,4096]{1,0:T(8,128)(2,1)}, bf16[32,4096]{1,0:T(8,128)(2,1)S(1)}, u32[]{:S(2)}, u32[]{:S(2)}) collective-permute-start(bf16[32,4096]{1,0:T(8,128)(2,1)} %get-tuple-element.59), channel_id=1, source_target_pairs={{0,6},{2,4},{4,10},{6,8},{8,14},{10,12},{12,2},{14,0},{1,7},{3,5},... | collective-permute-start | bytes 786440 | tf_op jit(solution)/shard_map/ppermute | solution.py:34
  269.0 23.9 %collective-permute-start.4 = (bf16[32,4096]{1,0:T(8,128)(2,1)}, bf16[32,4096]{1,0:T(8,128)(2,1)S(1)}, u32[]{:S(2)}, u32[]{:S(2)}) collective-permute-start(bf16[32,4096]{1,0:T(8,128)(2,1)} %get-tuple-element.60), channel_id=1, source_target_pairs={{0,4},{2,6},{4,8},{6,10},{8,12},{10,14},{12,0},{14,2},{1,5},{3,7},... | collective-permute-start | bytes 786440 | tf_op jit(solution)/shard_map/ppermute | solution.py:34
  285.3 13.0 %collective-permute-start.3 = (bf16[32,4096]{1,0:T(8,128)(2,1)}, bf16[32,4096]{1,0:T(8,128)(2,1)}, u32[]{:S(2)}, u32[]{:S(2)}) collective-permute-start(bf16[32,4096]{1,0:T(8,128)(2,1)} %get-tuple-element.61), channel_id=1, source_target_pairs={{0,2},{2,0},{4,6},{6,4},{8,10},{10,8},{12,14},{14,12},{1,3},{3,1},... | collective-permute-start | bytes 786440 | tf_op jit(solution)/shard_map/ppermute | solution.py:34
  290.3 10.4 %collective-permute-start.27 = (bf16[32,4096]{1,0:T(8,128)(2,1)}, bf16[32,4096]{1,0:T(8,128)(2,1)}, u32[]{:S(2)}, u32[]{:S(2)}) collective-permute-start(bf16[32,4096]{1,0:T(8,128)(2,1)} %get-tuple-element.47), channel_id=1, source_target_pairs={{0,14},{2,12},{4,2},{6,0},{8,6},{10,4},{12,10},{14,8},{1,15},{3,13... | collective-permute-start | bytes 786440 | tf_op jit(solution)/shard_map/ppermute | solution.py:34
  291.0 16.1 %collective-permute-start.26 = (bf16[32,4096]{1,0:T(8,128)(2,1)}, bf16[32,4096]{1,0:T(8,128)(2,1)}, u32[]{:S(2)}, u32[]{:S(2)}) collective-permute-start(bf16[32,4096]{1,0:T(8,128)(2,1)} %get-tuple-element.48), channel_id=1, source_target_pairs={{0,12},{2,14},{4,0},{6,2},{8,4},{10,6},{12,8},{14,10},{1,13},{3,15... | collective-permute-start | bytes 786440 | tf_op jit(solution)/shard_map/ppermute | solution.py:34
  293.7 38.3 %collective-permute-start.25 = (bf16[32,4096]{1,0:T(8,128)(2,1)}, bf16[32,4096]{1,0:T(8,128)(2,1)}, u32[]{:S(2)}, u32[]{:S(2)}) collective-permute-start(bf16[32,4096]{1,0:T(8,128)(2,1)} %get-tuple-element.49), channel_id=1, source_target_pairs={{0,10},{2,8},{4,14},{6,12},{8,2},{10,0},{12,6},{14,4},{1,11},{3,9}... | collective-permute-start | bytes 786440 | tf_op jit(solution)/shard_map/ppermute | solution.py:34
  298.2 58.1 %collective-permute-start.24 = (bf16[32,4096]{1,0:T(8,128)(2,1)}, bf16[32,4096]{1,0:T(8,128)(2,1)S(1)}, u32[]{:S(2)}, u32[]{:S(2)}) collective-permute-start(bf16[32,4096]{1,0:T(8,128)(2,1)} %get-tuple-element.50), channel_id=1, source_target_pairs={{0,8},{2,10},{4,12},{6,14},{8,0},{10,2},{12,4},{14,6},{1,9},{3,11}... | collective-permute-start | bytes 786440 | tf_op jit(solution)/shard_map/ppermute | solution.py:34
  300.6 55.7 %collective-permute-start.23 = (bf16[32,4096]{1,0:T(8,128)(2,1)}, bf16[32,4096]{1,0:T(8,128)(2,1)S(1)}, u32[]{:S(2)}, u32[]{:S(2)}) collective-permute-start(bf16[32,4096]{1,0:T(8,128)(2,1)} %get-tuple-element.51), channel_id=1, source_target_pairs={{0,6},{2,4},{4,10},{6,8},{8,14},{10,12},{12,2},{14,0},{1,7},{3,5},... | collective-permute-start | bytes 786440 | tf_op jit(solution)/shard_map/ppermute | solution.py:34
  307.0 49.3 %collective-permute-start.22 = (bf16[32,4096]{1,0:T(8,128)(2,1)}, bf16[32,4096]{1,0:T(8,128)(2,1)S(1)}, u32[]{:S(2)}, u32[]{:S(2)}) collective-permute-start(bf16[32,4096]{1,0:T(8,128)(2,1)} %get-tuple-element.52), channel_id=1, source_target_pairs={{0,4},{2,6},{4,8},{6,10},{8,12},{10,14},{12,0},{14,2},{1,5},{3,7},... | collective-permute-start | bytes 786440 | tf_op jit(solution)/shard_map/ppermute | solution.py:34
  331.9 24.4 %collective-permute-start.21 = (bf16[32,4096]{1,0:T(8,128)(2,1)}, bf16[32,4096]{1,0:T(8,128)(2,1)S(1)}, u32[]{:S(2)}, u32[]{:S(2)}) collective-permute-start(bf16[32,4096]{1,0:T(8,128)(2,1)} %get-tuple-element.53), channel_id=1, source_target_pairs={{0,2},{2,0},{4,6},{6,4},{8,10},{10,8},{12,14},{14,12},{1,3},{3,1},... | collective-permute-start | bytes 786440 | tf_op jit(solution)/shard_map/ppermute | solution.py:34
  356.3 42.6 %collective-permute-start.10 = (bf16[8,32,4096]{2,1,0:T(8,128)(2,1)}, bf16[8,32,4096]{2,1,0:T(8,128)(2,1)}, u32[]{:S(2)}, u32[]{:S(2)}) collective-permute-start(bf16[8,32,4096]{2,1,0:T(8,128)(2,1)} %bitcast.23), channel_id=1, source_target_pairs={{0,1},{1,0},{2,3},{3,2},{4,5},{5,4},{6,7},{7,6},{8,9},{9,8},{10,11... | collective-permute-start | bytes 6291464 | tf_op jit(solution)/shard_map/ppermute | solution.py:22
  374.2 11.5 %collective-permute-start.28 = (bf16[8,32,4096]{2,1,0:T(8,128)(2,1)}, bf16[8,32,4096]{2,1,0:T(8,128)(2,1)}, u32[]{:S(2)}, u32[]{:S(2)}) collective-permute-start(bf16[8,32,4096]{2,1,0:T(8,128)(2,1)} %bitcast.53), channel_id=1, source_target_pairs={{0,1},{1,0},{2,3},{3,2},{4,5},{5,4},{6,7},{7,6},{8,9},{9,8},{10,11... | collective-permute-start | bytes 6291464 | tf_op jit(solution)/shard_map/ppermute | solution.py:22
  379.3 142.8 %all-to-all-start.3 = ((bf16[8,32,4096]{2,1,0:T(8,128)(2,1)}), bf16[8,32,4096]{2,1,0:T(8,128)(2,1)}, u32[]{:S(2)}, u32[]{:S(2)}) async-start(bf16[8,32,4096]{2,1,0:T(8,128)(2,1)} %multiply_convert_fusion), calls=%async_computation.3 | async-start | bytes 4194304 | tf_op jit(solution)/shard_map/all_to_all | solution.py:397
  387.7 36.7 %collective-permute-start.34 = (bf16[32,1024]{1,0:T(8,128)(2,1)S(1)}, bf16[32,1024]{1,0:T(8,128)(2,1)S(1)}, u32[]{:S(2)}, u32[]{:S(2)}) collective-permute-start(bf16[32,1024]{1,0:T(8,128)(2,1)S(1)} %get-tuple-element.40), channel_id=1, source_target_pairs={{0,4},{2,6},{4,8},{6,10},{8,12},{10,14},{12,0},{14,2},{1,5},{3,7},... | collective-permute-start | bytes 196616 | tf_op jit(solution)/shard_map/ppermute | solution.py:34
  389.6 61.8 %collective-permute-start.33 = (bf16[32,1024]{1,0:T(8,128)(2,1)S(1)}, bf16[32,1024]{1,0:T(8,128)(2,1)S(1)}, u32[]{:S(2)}, u32[]{:S(2)}) collective-permute-start(bf16[32,1024]{1,0:T(8,128)(2,1)S(1)} %get-tuple-element.41), channel_id=1, source_target_pairs={{0,10},{2,8},{4,14},{6,12},{8,2},{10,0},{12,6},{14,4},{1,11},{3,9}... | collective-permute-start | bytes 196616 | tf_op jit(solution)/shard_map/ppermute | solution.py:34
  395.1 56.9 %collective-permute-start.42 = (bf16[32,1024]{1,0:T(8,128)(2,1)S(1)}, bf16[32,1024]{1,0:T(8,128)(2,1)S(1)}, u32[]{:S(2)}, u32[]{:S(2)}) collective-permute-start(bf16[32,1024]{1,0:T(8,128)(2,1)S(1)} %get-tuple-element.31), channel_id=1, source_target_pairs={{0,6},{2,4},{4,10},{6,8},{8,14},{10,12},{12,2},{14,0},{1,7},{3,5},... | collective-permute-start | bytes 196616 | tf_op jit(solution)/shard_map/ppermute | solution.py:34
  395.2 62.6 %collective-permute-start.41 = (bf16[32,1024]{1,0:T(8,128)(2,1)S(1)}, bf16[32,1024]{1,0:T(8,128)(2,1)S(1)}, u32[]{:S(2)}, u32[]{:S(2)}) collective-permute-start(bf16[32,1024]{1,0:T(8,128)(2,1)S(1)} %get-tuple-element.32), channel_id=1, source_target_pairs={{0,4},{2,6},{4,8},{6,10},{8,12},{10,14},{12,0},{14,2},{1,5},{3,7},... | collective-permute-start | bytes 196616 | tf_op jit(solution)/shard_map/ppermute | solution.py:34
  398.9 59.6 %collective-permute-start.49 = (bf16[32,2048]{1,0:T(8,128)(2,1)S(1)}, bf16[32,2048]{1,0:T(8,128)(2,1)S(1)}, u32[]{:S(2)}, u32[]{:S(2)}) collective-permute-start(bf16[32,2048]{1,0:T(8,128)(2,1)S(1)} %get-tuple-element.23), channel_id=1, source_target_pairs={{0,6},{2,4},{4,10},{6,8},{8,14},{10,12},{12,2},{14,0},{1,7},{3,5},... | collective-permute-start | bytes 393224 | tf_op jit(solution)/shard_map/ppermute | solution.py:34
  425.0 35.5 %collective-permute-start.48 = (bf16[32,2048]{1,0:T(8,128)(2,1)S(1)}, bf16[32,2048]{1,0:T(8,128)(2,1)S(1)}, u32[]{:S(2)}, u32[]{:S(2)}) collective-permute-start(bf16[32,2048]{1,0:T(8,128)(2,1)S(1)} %get-tuple-element.24), channel_id=1, source_target_pairs={{0,4},{2,6},{4,8},{6,10},{8,12},{10,14},{12,0},{14,2},{1,5},{3,7},... | collective-permute-start | bytes 393224 | tf_op jit(solution)/shard_map/ppermute | solution.py:34
  452.0 12.5 %collective-permute-start.47 = (bf16[32,2048]{1,0:T(8,128)(2,1)S(1)}, bf16[32,2048]{1,0:T(8,128)(2,1)S(1)}, u32[]{:S(2)}, u32[]{:S(2)}) collective-permute-start(bf16[32,2048]{1,0:T(8,128)(2,1)S(1)} %get-tuple-element.25), channel_id=1, source_target_pairs={{0,10},{2,8},{4,14},{6,12},{8,2},{10,0},{12,6},{14,4},{1,11},{3,9}... | collective-permute-start | bytes 393224 | tf_op jit(solution)/shard_map/ppermute | solution.py:34
  452.6 14.6 %collective-permute-start.46 = (bf16[32,2048]{1,0:T(8,128)(2,1)S(1)}, bf16[32,2048]{1,0:T(8,128)(2,1)S(1)}, u32[]{:S(2)}, u32[]{:S(2)}) collective-permute-start(bf16[32,2048]{1,0:T(8,128)(2,1)S(1)} %get-tuple-element.26), channel_id=1, source_target_pairs={{0,8},{2,10},{4,12},{6,14},{8,0},{10,2},{12,4},{14,6},{1,9},{3,11}... | collective-permute-start | bytes 393224 | tf_op jit(solution)/shard_map/ppermute | solution.py:34
  455.5 66.5 %copy-start.5 = (bf16[256,1536]{1,0:T(8,128)(2,1)S(1)}, bf16[256,1536]{1,0:T(8,128)(2,1)}, u32[]{:S(2)}) copy-start(bf16[256,1536]{1,0:T(8,128)(2,1)} %get-tuple-element.19.refs_18_) | copy-start | bytes 2359300
  458.4 26.1 %collective-permute-start.17 = (bf16[32,4096]{1,0:T(8,128)(2,1)S(1)}, bf16[32,4096]{1,0:T(8,128)(2,1)S(1)}, u32[]{:S(2)}, u32[]{:S(2)}) collective-permute-start(bf16[32,4096]{1,0:T(8,128)(2,1)S(1)} %get-tuple-element.63), channel_id=1, source_target_pairs={{0,6},{2,4},{4,10},{6,8},{8,14},{10,12},{12,2},{14,0},{1,7},{3,5},... | collective-permute-start | bytes 786440 | tf_op jit(solution)/shard_map/ppermute | solution.py:34
  459.1 26.3 %collective-permute-start.16 = (bf16[32,4096]{1,0:T(8,128)(2,1)S(1)}, bf16[32,4096]{1,0:T(8,128)(2,1)S(1)}, u32[]{:S(2)}, u32[]{:S(2)}) collective-permute-start(bf16[32,4096]{1,0:T(8,128)(2,1)S(1)} %get-tuple-element.64), channel_id=1, source_target_pairs={{0,4},{2,6},{4,8},{6,10},{8,12},{10,14},{12,0},{14,2},{1,5},{3,7},... | collective-permute-start | bytes 786440 | tf_op jit(solution)/shard_map/ppermute | solution.py:34
  461.3 14.9 %collective-permute-start.45 = (bf16[32,2048]{1,0:T(8,128)(2,1)S(1)}, bf16[32,2048]{1,0:T(8,128)(2,1)S(1)}, u32[]{:S(2)}, u32[]{:S(2)}) collective-permute-start(bf16[32,2048]{1,0:T(8,128)(2,1)S(1)} %get-tuple-element.27), channel_id=1, source_target_pairs={{0,14},{2,12},{4,2},{6,0},{8,6},{10,4},{12,10},{14,8},{1,15},{3,13... | collective-permute-start | bytes 393224 | tf_op jit(solution)/shard_map/ppermute | solution.py:34
  465.2 14.6 %collective-permute-start.44 = (bf16[32,2048]{1,0:T(8,128)(2,1)S(1)}, bf16[32,2048]{1,0:T(8,128)(2,1)S(1)}, u32[]{:S(2)}, u32[]{:S(2)}) collective-permute-start(bf16[32,2048]{1,0:T(8,128)(2,1)S(1)} %get-tuple-element.28), channel_id=1, source_target_pairs={{0,12},{2,14},{4,0},{6,2},{8,4},{10,6},{12,8},{14,10},{1,13},{3,15... | collective-permute-start | bytes 393224 | tf_op jit(solution)/shard_map/ppermute | solution.py:34
  467.9 13.5 %collective-permute-start.43 = (bf16[32,2048]{1,0:T(8,128)(2,1)S(1)}, bf16[32,2048]{1,0:T(8,128)(2,1)S(1)}, u32[]{:S(2)}, u32[]{:S(2)}) collective-permute-start(bf16[32,2048]{1,0:T(8,128)(2,1)S(1)} %get-tuple-element.29), channel_id=1, source_target_pairs={{0,2},{2,0},{4,6},{6,4},{8,10},{10,8},{12,14},{14,12},{1,3},{3,1},... | collective-permute-start | bytes 393224 | tf_op jit(solution)/shard_map/ppermute | solution.py:34
  476.8 21.4 %collective-permute-start.15 = (bf16[32,4096]{1,0:T(8,128)(2,1)S(1)}, bf16[32,4096]{1,0:T(8,128)(2,1)S(1)}, u32[]{:S(2)}, u32[]{:S(2)}) collective-permute-start(bf16[32,4096]{1,0:T(8,128)(2,1)S(1)} %get-tuple-element.65), channel_id=1, source_target_pairs={{0,10},{2,8},{4,14},{6,12},{8,2},{10,0},{12,6},{14,4},{1,11},{3,9}... | collective-permute-start | bytes 786440 | tf_op jit(solution)/shard_map/ppermute | solution.py:34
  480.4 23.4 %collective-permute-start.14 = (bf16[32,4096]{1,0:T(8,128)(2,1)S(1)}, bf16[32,4096]{1,0:T(8,128)(2,1)S(1)}, u32[]{:S(2)}, u32[]{:S(2)}) collective-permute-start(bf16[32,4096]{1,0:T(8,128)(2,1)S(1)} %get-tuple-element.66), channel_id=1, source_target_pairs={{0,8},{2,10},{4,12},{6,14},{8,0},{10,2},{12,4},{14,6},{1,9},{3,11}... | collective-permute-start | bytes 786440 | tf_op jit(solution)/shard_map/ppermute | solution.py:34
  482.1 22.4 %collective-permute-start.13 = (bf16[32,4096]{1,0:T(8,128)(2,1)S(1)}, bf16[32,4096]{1,0:T(8,128)(2,1)S(1)}, u32[]{:S(2)}, u32[]{:S(2)}) collective-permute-start(bf16[32,4096]{1,0:T(8,128)(2,1)S(1)} %get-tuple-element.67), channel_id=1, source_target_pairs={{0,14},{2,12},{4,2},{6,0},{8,6},{10,4},{12,10},{14,8},{1,15},{3,13... | collective-permute-start | bytes 786440 | tf_op jit(solution)/shard_map/ppermute | solution.py:34
  484.5 35.3 %collective-permute-start.12 = (bf16[32,4096]{1,0:T(8,128)(2,1)S(1)}, bf16[32,4096]{1,0:T(8,128)(2,1)S(1)}, u32[]{:S(2)}, u32[]{:S(2)}) collective-permute-start(bf16[32,4096]{1,0:T(8,128)(2,1)S(1)} %get-tuple-element.68), channel_id=1, source_target_pairs={{0,12},{2,14},{4,0},{6,2},{8,4},{10,6},{12,8},{14,10},{1,13},{3,15... | collective-permute-start | bytes 786440 | tf_op jit(solution)/shard_map/ppermute | solution.py:34
  486.1 34.4 %collective-permute-start.11 = (bf16[32,4096]{1,0:T(8,128)(2,1)S(1)}, bf16[32,4096]{1,0:T(8,128)(2,1)S(1)}, u32[]{:S(2)}, u32[]{:S(2)}) collective-permute-start(bf16[32,4096]{1,0:T(8,128)(2,1)S(1)} %get-tuple-element.69), channel_id=1, source_target_pairs={{0,2},{2,0},{4,6},{6,4},{8,10},{10,8},{12,14},{14,12},{1,3},{3,1},... | collective-permute-start | bytes 786440 | tf_op jit(solution)/shard_map/ppermute | solution.py:34
  498.9 49.5 %collective-permute-start.40 = (bf16[32,1024]{1,0:T(8,128)(2,1)}, bf16[32,1024]{1,0:T(8,128)(2,1)}, u32[]{:S(2)}, u32[]{:S(2)}) collective-permute-start(bf16[32,1024]{1,0:T(8,128)(2,1)} %get-tuple-element.33), channel_id=1, source_target_pairs={{0,10},{2,8},{4,14},{6,12},{8,2},{10,0},{12,6},{14,4},{1,11},{3,9}... | collective-permute-start | bytes 196616 | tf_op jit(solution)/shard_map/ppermute | solution.py:34
  504.5 45.8 %collective-permute-start.39 = (bf16[32,1024]{1,0:T(8,128)(2,1)}, bf16[32,1024]{1,0:T(8,128)(2,1)}, u32[]{:S(2)}, u32[]{:S(2)}) collective-permute-start(bf16[32,1024]{1,0:T(8,128)(2,1)} %get-tuple-element.34), channel_id=1, source_target_pairs={{0,8},{2,10},{4,12},{6,14},{8,0},{10,2},{12,4},{14,6},{1,9},{3,11}... | collective-permute-start | bytes 196616 | tf_op jit(solution)/shard_map/ppermute | solution.py:34
  505.2 48.1 %collective-permute-start.38 = (bf16[32,1024]{1,0:T(8,128)(2,1)}, bf16[32,1024]{1,0:T(8,128)(2,1)}, u32[]{:S(2)}, u32[]{:S(2)}) collective-permute-start(bf16[32,1024]{1,0:T(8,128)(2,1)} %get-tuple-element.35), channel_id=1, source_target_pairs={{0,14},{2,12},{4,2},{6,0},{8,6},{10,4},{12,10},{14,8},{1,15},{3,13... | collective-permute-start | bytes 196616 | tf_op jit(solution)/shard_map/ppermute | solution.py:34
  520.5 32.9 %collective-permute-start.37 = (bf16[32,1024]{1,0:T(8,128)(2,1)}, bf16[32,1024]{1,0:T(8,128)(2,1)}, u32[]{:S(2)}, u32[]{:S(2)}) collective-permute-start(bf16[32,1024]{1,0:T(8,128)(2,1)} %get-tuple-element.36), channel_id=1, source_target_pairs={{0,12},{2,14},{4,0},{6,2},{8,4},{10,6},{12,8},{14,10},{1,13},{3,15... | collective-permute-start | bytes 196616 | tf_op jit(solution)/shard_map/ppermute | solution.py:34
  521.2 33.1 %collective-permute-start.36 = (bf16[32,1024]{1,0:T(8,128)(2,1)}, bf16[32,1024]{1,0:T(8,128)(2,1)}, u32[]{:S(2)}, u32[]{:S(2)}) collective-permute-start(bf16[32,1024]{1,0:T(8,128)(2,1)} %get-tuple-element.37), channel_id=1, source_target_pairs={{0,2},{2,0},{4,6},{6,4},{8,10},{10,8},{12,14},{14,12},{1,3},{3,1},... | collective-permute-start | bytes 196616 | tf_op jit(solution)/shard_map/ppermute | solution.py:34
  538.4 10.0 %copy-start.54 = (bf16[32,1024]{1,0:T(8,128)(2,1)S(1)}, bf16[32,1024]{1,0:T(8,128)(2,1)}, u32[]{:S(2)}) copy-start(bf16[32,1024]{1,0:T(8,128)(2,1)} %get-tuple-element.42) | copy-start | bytes 196612
  538.4 12.0 %copy-start.53 = (bf16[32,1024]{1,0:T(8,128)(2,1)S(1)}, bf16[32,1024]{1,0:T(8,128)(2,1)}, u32[]{:S(2)}) copy-start(bf16[32,1024]{1,0:T(8,128)(2,1)} %get-tuple-element.43) | copy-start | bytes 196612
  538.4 15.0 %copy-start.52 = (bf16[32,1024]{1,0:T(8,128)(2,1)S(1)}, bf16[32,1024]{1,0:T(8,128)(2,1)}, u32[]{:S(2)}) copy-start(bf16[32,1024]{1,0:T(8,128)(2,1)} %get-tuple-element.44) | copy-start | bytes 196612
  538.4 15.0 %copy-start.51 = (bf16[32,1024]{1,0:T(8,128)(2,1)S(1)}, bf16[32,1024]{1,0:T(8,128)(2,1)}, u32[]{:S(2)}) copy-start(bf16[32,1024]{1,0:T(8,128)(2,1)} %get-tuple-element.45) | copy-start | bytes 196612
  538.4 15.9 %copy-start.55 = (bf16[32,1024]{1,0:T(8,128)(2,1)S(1)}, bf16[32,1024]{1,0:T(8,128)(2,1)}, u32[]{:S(2)}) copy-start(bf16[32,1024]{1,0:T(8,128)(2,1)} %get-tuple-element.39) | copy-start | bytes 196612
  538.4 18.5 %copy-start.21 = (bf16[32,1024]{1,0:T(8,128)(2,1)S(1)}, bf16[32,1024]{1,0:T(8,128)(2,1)}, u32[]{:S(2)}) copy-start(bf16[32,1024]{1,0:T(8,128)(2,1)} %get-tuple-element.38.refs_10_) | copy-start | bytes 196612
  538.4 18.5 %copy-start.34 = (bf16[32,1024]{1,0:T(8,128)(2,1)S(1)}, bf16[32,1024]{1,0:T(8,128)(2,1)}, u32[]{:S(2)}) copy-start(bf16[32,1024]{1,0:T(8,128)(2,1)} %copy-done.33) | copy-start | bytes 196612
  538.4 18.5 %copy-start.36 = (bf16[32,1024]{1,0:T(8,128)(2,1)S(1)}, bf16[32,1024]{1,0:T(8,128)(2,1)}, u32[]{:S(2)}) copy-start(bf16[32,1024]{1,0:T(8,128)(2,1)} %copy-done.35) | copy-start | bytes 196612
  548.4 14.5 %collective-permute-start.32 = (bf16[32,1024]{1,0:T(8,128)(2,1)S(1)}, bf16[32,1024]{1,0:T(8,128)(2,1)S(1)}, u32[]{:S(2)}, u32[]{:S(2)}) collective-permute-start(bf16[32,1024]{1,0:T(8,128)(2,1)S(1)} %copy-done.54), channel_id=1, source_target_pairs={{0,8},{2,10},{4,12},{6,14},{8,0},{10,2},{12,4},{14,6},{1,9},{3,11}... | collective-permute-start | bytes 196616 | tf_op jit(solution)/shard_map/ppermute | solution.py:34
  550.4 12.5 %collective-permute-start.31 = (bf16[32,1024]{1,0:T(8,128)(2,1)S(1)}, bf16[32,1024]{1,0:T(8,128)(2,1)S(1)}, u32[]{:S(2)}, u32[]{:S(2)}) collective-permute-start(bf16[32,1024]{1,0:T(8,128)(2,1)S(1)} %copy-done.53), channel_id=1, source_target_pairs={{0,14},{2,12},{4,2},{6,0},{8,6},{10,4},{12,10},{14,8},{1,15},{3,13... | collective-permute-start | bytes 196616 | tf_op jit(solution)/shard_map/ppermute | solution.py:34
  553.4 9.4 %collective-permute-start.30 = (bf16[32,1024]{1,0:T(8,128)(2,1)S(1)}, bf16[32,1024]{1,0:T(8,128)(2,1)S(1)}, u32[]{:S(2)}, u32[]{:S(2)}) collective-permute-start(bf16[32,1024]{1,0:T(8,128)(2,1)S(1)} %copy-done.52), channel_id=1, source_target_pairs={{0,12},{2,14},{4,0},{6,2},{8,4},{10,6},{12,8},{14,10},{1,13},{3,15... | collective-permute-start | bytes 196616 | tf_op jit(solution)/shard_map/ppermute | solution.py:34
  553.4 9.4 %collective-permute-start.29 = (bf16[32,1024]{1,0:T(8,128)(2,1)S(1)}, bf16[32,1024]{1,0:T(8,128)(2,1)S(1)}, u32[]{:S(2)}, u32[]{:S(2)}) collective-permute-start(bf16[32,1024]{1,0:T(8,128)(2,1)S(1)} %copy-done.51), channel_id=1, source_target_pairs={{0,2},{2,0},{4,6},{6,4},{8,10},{10,8},{12,14},{14,12},{1,3},{3,1},... | collective-permute-start | bytes 196616 | tf_op jit(solution)/shard_map/ppermute | solution.py:34
  554.3 8.6 %collective-permute-start.35 = (bf16[32,1024]{1,0:T(8,128)(2,1)S(1)}, bf16[32,1024]{1,0:T(8,128)(2,1)S(1)}, u32[]{:S(2)}, u32[]{:S(2)}) collective-permute-start(bf16[32,1024]{1,0:T(8,128)(2,1)S(1)} %copy-done.55), channel_id=1, source_target_pairs={{0,6},{2,4},{4,10},{6,8},{8,14},{10,12},{12,2},{14,0},{1,7},{3,5},... | collective-permute-start | bytes 196616 | tf_op jit(solution)/shard_map/ppermute | solution.py:34
  (48 other events, 73.5 us)

commit v3 on v2

--- a/solution.py
+++ b/solution.py
@@ -34,21 +34,30 @@
     return lax.ppermute(value, EXCHANGE_AXES, pairs)
 
 
-def rolled(value, start):
-    return lax.dynamic_slice_in_dim(
-        jnp.concatenate([value, value], axis=0), start, value.shape[0], axis=0
-    )
-
-
 def level_block(levels, rows_here, most):
     whole = levels % most == 0 and most * rows_here % LANES == 0
     return most if whole else levels
 
 
-def write_table(ids, quarter, table):
+def pick(values, index):
+    rows, many = index.shape[0], values.shape[1]
+    hit = lax.broadcasted_iota(jnp.int32, (rows, many), 1) == index
+    return jnp.sum(jnp.where(hit, values, 0.0), axis=1, keepdims=True)
+
+
+def write_table(sizes, place_ref, wave_order, table):
+    wave_size, level_size, chunks, chunk, turned, _ = sizes
     rows, lon_count = table.shape
+    places = wave_size * level_size
+    count = rows // (2 * places)
     scale = math.sqrt(2.0 / lon_count)
-    wave = ids[...].astype(jnp.float32)
+    row = lax.broadcasted_iota(jnp.int32, (rows, 1), 0)
+    slot, place = row % count, row // (2 * count)
+    part = (row // count) % 2
+    if turned:
+        wave = (place // level_size + place_ref[0]) % wave_size
+        place = wave * level_size + (place % level_size + place_ref[1]) % level_size
+    wave = pick(wave_order[...].astype(jnp.float32), (place * chunks + chunk) * count + slot)
     lane = lax.broadcasted_iota(jnp.int32, (rows, LANES), 1).astype(jnp.float32)
 
     def angle(steps):
@@ -56,7 +65,7 @@
         return steps * (2.0 * math.pi / lon_count)
 
     low = angle(wave * lane)
-    high = angle(wave * lane * float(LANES) + quarter[...].astype(jnp.float32))
+    high = angle(wave * lane * float(LANES) + part.astype(jnp.float32) * (lon_count / 4))
     low_cos, low_sin = jnp.cos(low) * scale, jnp.sin(low) * scale
     high_cos, high_sin = jnp.cos(high), jnp.sin(high)
     for block in range(lon_count // LANES):
@@ -66,31 +75,34 @@
         table[:, block * LANES : (block + 1) * LANES] = values.astype(table.dtype)
 
 
-def fourier_kernel(half_rows, sign_ref, grid_ref, lat_rows, ids, quarter, out, table):
+def fourier_kernel(sizes, place_ref, grid_ref, wave_order, lat_order, out, table, coupling):
     levels, rows, lon_count = grid_ref.shape
 
     @pl.when(pl.program_id(0) == 0)
     def _():
-        write_table(ids, quarter, table)
-
-    latitude = (lat_rows[...].astype(jnp.float32) + 0.5) * (math.pi / (2.0 * half_rows))
-    coupling = 0.5 * sign_ref[0] * jnp.sin(latitude)
+        write_table(sizes, place_ref, wave_order, table)
+        row = lax.broadcasted_iota(jnp.int32, (rows, 1), 0) + place_ref[0] * rows
+        latitude = pick(lat_order[...].astype(jnp.float32), row) + 0.5
+        sine = jnp.sin(latitude * (math.pi / (2.0 * lat_order.shape[1])))
+        sign = 1.0 - 2.0 * place_ref[2].astype(jnp.float32)
+        coupling[...] = jnp.broadcast_to(0.5 * sign * sine, coupling.shape)
+
     field = grid_ref[...].astype(jnp.float32)
-    forcing = (field + coupling[None] * jnp.tanh(field)).astype(jnp.bfloat16)
+    forcing = (field + coupling[:, :1][None] * jnp.tanh(field)).astype(jnp.bfloat16)
     forcing = forcing.reshape(levels * rows, lon_count)
     out[...] = lax.dot_general(
         table[...], forcing, (((1,), (1,)), ((), ())), preferred_element_type=jnp.float32
     ).astype(out.dtype)
 
 
-def fourier(grid_state, sign, lat_rows, half_rows, ids, quarter):
+def fourier(grid_state, place, wave_order, lat_order, sizes):
     levels, rows_here, lon_count = grid_state.shape
-    height = ids.shape[0]
+    _, _, _, _, _, height = sizes
     block = level_block(levels, rows_here, 16)
     width = levels * rows_here
     whole = lambda *shape: pl.BlockSpec(shape, lambda i: (0,) * len(shape))
     return pl.pallas_call(
-        functools.partial(fourier_kernel, half_rows),
+        functools.partial(fourier_kernel, sizes),
         out_shape=[
             jax.ShapeDtypeStruct((height, width), jnp.bfloat16),
             jax.ShapeDtypeStruct((height, lon_count), jnp.bfloat16),
@@ -99,64 +111,72 @@
         in_specs=[
             pl.BlockSpec(memory_space=pltpu.SMEM),
             pl.BlockSpec((block, rows_here, lon_count), lambda i: (i, 0, 0)),
-            whole(rows_here, 1),
-            whole(height, 1),
-            whole(height, 1),
+            whole(1, wave_order.shape[0]),
+            whole(1, lat_order.shape[0]),
         ],
         out_specs=[
             pl.BlockSpec((height, block * rows_here), lambda i: (0, i)),
             whole(height, lon_count),
         ],
+        scratch_shapes=[pltpu.VMEM((rows_here, LANES), jnp.float32)],
         compiler_params=pltpu.CompilerParams(vmem_limit_bytes=56 * 2**20),
         cost_estimate=pl.CostEstimate(
             flops=2 * height * width * lon_count,
             bytes_accessed=2 * (width * lon_count + height * (width + lon_count)),
             transcendentals=width * lon_count,
         ),
-    )(sign[None], grid_state, lat_rows[:, None], ids[:, None], quarter[:, None])
-
-
-def inverse_kernel(pieces, tables, *refs):
+    )(place, grid_state, wave_order[None], lat_order[None])
+
+
+def inverse_kernel(pieces, tables, has_partial, *refs):
     out = refs[-1]
     coeffs = jnp.concatenate([ref[...] for ref in refs[:pieces]], axis=0)
     table = jnp.concatenate([ref[...] for ref in refs[pieces : pieces + tables]], axis=0)
     current = lax.dot_general(
         coeffs, table, (((0,), (0,)), ((), ())), preferred_element_type=jnp.float32
-    )
-    out[...] = current.astype(out.dtype).reshape(out.shape)
-
-
-def inverse_fourier(pieces, tables, current, shape, start, levels):
+    ).reshape(out.shape)
+    if has_partial:
+        current = current + refs[pieces + tables][...]
+    out[...] = current.astype(out.dtype)
+
+
+def inverse_fourier(pieces, tables, shape, start, levels, current=None, partial=None, dtype=None):
     _, rows_here, lon_count = shape
     block = level_block(levels, rows_here, 8)
     width = block * rows_here
-    full = shape[0] * rows_here
     first = start // block
-    height = sum(piece.shape[0] for piece in pieces)
-    specs = [
-        pl.BlockSpec(
-            (piece.shape[0], width),
-            (lambda i: (0, first + i)) if piece.shape[1] == full else (lambda i: (0, i)),
+    height = sum(table.shape[0] for table in tables)
+    grid_block = (block, rows_here, lon_count)
+
+    def cut(begin):
+        return first - begin // block
+
+    specs, operands, aliases = [], [], {}
+    for piece, begin in pieces:
+        operands.append(piece)
+        specs.append(pl.BlockSpec((piece.shape[0], width), lambda i, skip=cut(begin): (0, skip + i)))
+    for table in tables:
+        operands.append(table)
+        specs.append(
+            pl.BlockSpec(table.shape, lambda i: (0, 0), pipeline_mode=pl.Buffered(1))
         )
-        for piece in pieces
-    ] + [
-        pl.BlockSpec(table.shape, lambda i: (0, 0), pipeline_mode=pl.Buffered(1))
-        for table in tables
-    ]
-    operands = list(pieces) + list(tables)
-    aliases = {}
+    if partial is not None:
+        operands.append(partial[0])
+        specs.append(pl.BlockSpec(grid_block, lambda i, skip=cut(partial[1]): (skip + i, 0, 0)))
     if current is not None:
         aliases = {len(operands): 0}
         operands.append(current)
         specs.append(pl.BlockSpec(memory_space=pl.ANY))
+    out_first = 0 if dtype is not None else first
+    out_shape = (levels, rows_here, lon_count) if dtype is not None else shape
     return pl.pallas_call(
-        functools.partial(inverse_kernel, len(pieces), len(tables)),
-        out_shape=jax.ShapeDtypeStruct(shape, jnp.bfloat16),
+        functools.partial(inverse_kernel, len(pieces), len(tables), partial is not None),
+        out_shape=jax.ShapeDtypeStruct(out_shape, dtype or jnp.bfloat16),
         grid=(levels // block,),
         in_specs=specs,
-        out_specs=pl.BlockSpec((block, rows_here, lon_count), lambda i: (first + i, 0, 0)),
+        out_specs=pl.BlockSpec(grid_block, lambda i: (out_first + i, 0, 0)),
         input_output_aliases=aliases,
-        compiler_params=pltpu.CompilerParams(vmem_limit_bytes=40 * 2**20),
+        compiler_params=pltpu.CompilerParams(vmem_limit_bytes=56 * 2**20),
         cost_estimate=pl.CostEstimate(
             flops=2 * height * levels * rows_here * lon_count,
             bytes_accessed=2 * levels * rows_here * (height + lon_count),
@@ -318,7 +338,7 @@
         + [whole(piece.shape) for piece in pieces],
         out_specs=whole((places, 2, group, width)),
         scratch_shapes=[scratch, scratch],
-        compiler_params=pltpu.CompilerParams(vmem_limit_bytes=40 * 2**20),
+        compiler_params=pltpu.CompilerParams(vmem_limit_bytes=56 * 2**20),
         cost_estimate=pl.CostEstimate(
             flops=values * half_rows * 6, bytes_accessed=6 * values, transcendentals=0
         ),
@@ -380,18 +400,8 @@
     legendre = legendre.reshape(narrow, half_rows, half_count)
     grid_state = grid_state.reshape(local_levels, rows_here, lon_count)
     hemi_sign = 1.0 - 2.0 * parity.astype(jnp.float32)
-    lat_rows = lax.dynamic_slice_in_dim(lat_order, wave_place * rows_here, rows_here)
     waves = lax.dynamic_slice_in_dim(wave_order, place * narrow, narrow)
-    quarter = jnp.broadcast_to(
-        (jnp.arange(2, dtype=jnp.int32) * (lon_count // 4))[None, :, None], (places, 2, count)
-    ).reshape(-1)
-    fixed = wave_order.reshape(wave_size, level_size, chunks, count)
-    turned = rolled(fixed, wave_place)
-    turned = jnp.swapaxes(rolled(jnp.swapaxes(turned, 0, 1), level_place), 0, 1)
-
-    def slot_ids(order, chunk):
-        ids = order[:, :, chunk].reshape(places, 1, count)
-        return jnp.broadcast_to(ids, (places, 2, count)).reshape(-1)
+    where = jnp.stack([wave_place, level_place, parity]).astype(jnp.int32)
 
     def exchange(value):
         return lax.all_to_all(value, EXCHANGE_AXES, split_axis=0, concat_axis=0, tiled=True)
@@ -403,9 +413,8 @@
     if not direct:
         returned, tables = [], []
         for chunk in range(chunks):
-            value, table = fourier(
-                grid_state, hemi_sign, lat_rows, half_rows, slot_ids(fixed, chunk), quarter
-            )
+            sizes = (wave_size, level_size, chunks, chunk, False, places * height)
+            value, table = fourier(grid_state, where, wave_order, lat_order, sizes)
             tables.append(table)
             own = exchange(value.reshape(places, height, width))
             mirrored = joined(partner(own, "fld"), own, 1.0)
@@ -420,8 +429,8 @@
                 (wave_size, level_size, count, chunk * count, wave_count),
             ).reshape(places, height, width)
             hemi = exchange(joined(partner(grid, "fld"), grid, 0.5))
-            returned.append(hemi.reshape(places * height, width))
-        current = inverse_fourier(returned, tables, None, grid_state.shape, 0, local_levels)
+            returned.append((hemi.reshape(places * height, width), 0))
+        current = inverse_fourier(returned, tables, grid_state.shape, 0, local_levels)
         return current.reshape(out_shape)
 
     tiles = width // LANES
@@ -444,8 +453,8 @@
     arrived, tables = [], []
     for chunk in range(chunks):
         is_whole = chunk in WHOLE_CHUNKS
-        ids = slot_ids(fixed if is_whole else turned, chunk)
-        value, table = fourier(grid_state, hemi_sign, lat_rows, half_rows, ids, quarter)
+        sizes = (wave_size, level_size, chunks, chunk, not is_whole, places * height)
+        value, table = fourier(grid_state, where, wave_order, lat_order, sizes)
         tables.append(table)
         if is_whole:
             arrived.append([exchange(value.reshape(places, 2, count, width))])
@@ -459,9 +468,11 @@
             pieces.append(piece.reshape(2, count, width))
         arrived.append(pieces)
 
-    cuts = [(0, local_levels // 2)]
-    cuts += [(local_levels // 4 * part, local_levels // 4) for part in (2, 3)]
-    returned, last = [], []
+    half, fourth = local_levels // 2, local_levels // 4
+    cuts = {chunk: [(0, local_levels)] for chunk in range(chunks)}
+    cuts[1] = [(0, half), (half, half)]
+    cuts[chunks - 1] = [(0, half), (half, fourth), (half + fourth, fourth)]
+    returned = []
     for chunk in range(chunks):
         is_whole = chunk in WHOLE_CHUNKS
         pieces = arrived[chunk]
@@ -474,24 +485,44 @@
         other = partner(grid, "fld")
         if is_whole:
             hemi = exchange(joined(other, grid, 0.5))
-            returned.append(hemi.reshape(places * height, width))
+            returned.append([(0, local_levels, [hemi.reshape(places * height, width)])])
             continue
-        is_last = chunk == chunks - 1
-        for start, levels in cuts if is_last else [(0, local_levels)]:
+        groups = []
+        for start, levels in cuts[chunk]:
             lanes = slice(start * rows_here, (start + levels) * rows_here)
             pieces = []
             for index, (wave, level) in enumerate(shifts):
                 hemi = joined(other[index, :, lanes], grid[index, :, lanes], 0.5)
                 wave, level = (wave_size - wave) % wave_size, (level_size - level) % level_size
                 pieces.append(shift_places(hemi, wave, level))
-            if is_last:
-                last.append(pieces)
-            else:
-                returned += pieces
-    current = None
-    for cut, (start, levels) in enumerate(cuts):
+            groups.append((start, levels, pieces))
+        returned.append(groups)
+
+    def pieces_at(chunk_list, start):
+        return [
+            (piece, begin)
+            for chunk in chunk_list
+            for begin, levels, pieces in returned[chunk]
+            if begin <= start < begin + levels
+            for piece in pieces
+        ]
+
+    shape = grid_state.shape
+    everything = list(range(chunks))
+    partial = inverse_fourier(
+        pieces_at(everything[:2], half), tables[:2], shape, half, half, dtype=jnp.float32
+    )
+    current = inverse_fourier(pieces_at(everything, 0), tables, shape, 0, half)
+    for cut in (1, 2):
+        start = half + (cut - 1) * fourth
         current = inverse_fourier(
-            returned + last[cut], tables, current, grid_state.shape, start, levels
+            pieces_at(everything[2:], start),
+            tables[2:],
+            shape,
+            start,
+            fourth,
+            current=current,
+            partial=(partial, half),
         )
     return current.reshape(out_shape)
 

time: 571 us -> 548 us (0.960)
  local copies, waits for them, and re-layouts: 48.7 us -> 10.9 us
  waiting for transfers between devices: 211 us -> 190 us
  starting transfers between devices: 140 us -> 158 us
  Pallas kernels: 140 us -> 155 us
    unnamed x117 -> x133, local copies, waits for them, and re-layouts: 37.8 us -> 5.69 us
    ppermute x42 -> x49, starting transfers between devices: 119 us -> 137 us  [shift_places(): return lax.ppermute(value, EXCHANGE_AXES, pairs)]
    ppermute x42 -> x49, waiting for transfers between devices: 130 us -> 111 us  [shift_places(): return lax.ppermute(value, EXCHANGE_AXES, pairs)]
    pallas_call x3 -> x4, Pallas kernels: 21.7 us -> 31.4 us  [inverse_fourier(): pl.pallas_call(functools.partial(inverse_kernel, len(pieces), len(tables)...]
    convert_element_type x5 -> x4, other arithmetic: 18.3 us -> 15.4 us  [joined(): return both.astype(jnp.bfloat16)]
  transfers between devices with their start and end apart: 54 -> 61, of which waited for: 13 -> 12; matrix products, arithmetic and copies ran while one was open for 6% -> 7% of each run, Pallas kernels for 22% -> 25%
where the time goes in v3:
time: 548 us; the launch traced here: 547 us
  waiting for transfers between devices  190 us (35%)
  starting transfers between devices  158 us (29%)
  Pallas kernels  155 us (28%)
  other arithmetic  31.4 us (6%)
  local copies, waits for them, and re-layouts  10.9 us (2%)
    ppermute x49, starting transfers between devices, shift_places(): return lax.ppermute(value, EXCHANGE_AXES, pairs)  137 us
    ppermute x49, waiting for transfers between devices, shift_places(): return lax.ppermute(value, EXCHANGE_AXES, pairs)  111 us
    all_to_all x4, waiting for transfers between devices, exchange(): lax.all_to_all(value, EXCHANGE_AXES, split_axis=0, concat_axis=0, tiled=T...  78.9 us
    pallas_call x4, Pallas kernels, columns_fused(): pl.pallas_call(functools.partial(column_kernel, sizes), out_shape=jax.Sha...  78.6 us
    pallas_call x4, Pallas kernels, fourier(): pl.pallas_call(functools.partial(fourier_kernel, sizes), out_shape=[jax.S...  44.8 us
    pallas_call x4, Pallas kernels, inverse_fourier(): pl.pallas_call(functools.partial(inverse_kernel, len(pieces), len(tables)...  31.4 us
    all_to_all x4, starting transfers between devices, exchange(): lax.all_to_all(value, EXCHANGE_AXES, split_axis=0, concat_axis=0, tiled=T...  19.1 us
    convert_element_type x4, other arithmetic, joined(): return both.astype(jnp.bfloat16)  15.4 us
  transfers between devices with their start and end apart: 61, of which 12 were waited for; matrix products, arithmetic and copies ran while one was open for 7% of the time, Pallas kernels for 25%

profile of v3, /device:TPU:0, one launch (start us, length us, event | category | flops | bytes accessed | tf_op | source)
XLA Modules:
  0.0 546.7 jit_solution(8884401813436395906)
XLA Ops:
  0.7 11.1 %shard_map.77 = (bf16[256,4096]{1,0:T(8,128)(2,1)}, bf16[256,1536]{1,0:T(8,128)(2,1)}) custom-call(s32[3]{0:T(128)} %pad_add_fusion.1.place_ref, bf16[64,64,1536]{2,1,0:T(8,128)(2,1)} %bitcast.121, s32[1,512]{1,0:T(1,128)} %bitcast.157, s32[1,256]{1,0:T(1,128)} %bitcast.161), custom_call_target="tpu_custom_call" | custom-call | flops 3221225472 | bytes 15466496 | tf_op jit(solution)/shard_map/pallas_call | solution.py:104
  11.8 7.3 %all-to-all-start.2 = ((bf16[8,2,16,4096]{3,2,1,0:T(8,128)(2,1)}), bf16[8,2,16,4096]{3,2,1,0:T(8,128)(2,1)S(1)}, u32[]{:S(2)}, u32[]{:S(2)}) async-start(bf16[8,2,16,4096]{3,2,1,0:T(8,128)(2,1)} %bitcast.144), calls=%async_computation.2 | async-start | bytes 4194304 | tf_op jit(solution)/shard_map/all_to_all | solution.py:407
  19.1 11.1 %shard_map.73 = (bf16[256,4096]{1,0:T(8,128)(2,1)}, bf16[256,1536]{1,0:T(8,128)(2,1)}) custom-call(s32[3]{0:T(128)} %pad_add_fusion.1.place_ref, bf16[64,64,1536]{2,1,0:T(8,128)(2,1)} %bitcast.122, s32[1,512]{1,0:T(1,128)} %bitcast.158, s32[1,256]{1,0:T(1,128)} %bitcast.162), custom_call_target="tpu_custom_call" | custom-call | flops 3221225472 | bytes 15466496 | tf_op jit(solution)/shard_map/pallas_call | solution.py:104
  30.2 37.1 %all-to-all-done.2.refs_0_ = bf16[8,2,16,4096]{3,2,1,0:T(8,128)(2,1)S(1)} async-done(((bf16[8,2,16,4096]{3,2,1,0:T(8,128)(2,1)}), bf16[8,2,16,4096]{3,2,1,0:T(8,128)(2,1)S(1)}, u32[]{:S(2)}, u32[]{:S(2)}) %all-to-all-start.2) | async-done | bytes 2097184 | tf_op jit(solution)/shard_map/all_to_all | solution.py:407
  67.3 4.7 all-to-all-start
  78.0 41.8 %all-to-all-done.refs_0_ = bf16[8,2,16,4096]{3,2,1,0:T(8,128)(2,1)} async-done(((bf16[8,2,16,4096]{3,2,1,0:T(8,128)(2,1)}), bf16[8,2,16,4096]{3,2,1,0:T(8,128)(2,1)}, u32[]{:S(2)}, u32[]{:S(2)}) %all-to-all-start) | async-done | bytes 2097184 | tf_op jit(solution)/shard_map/all_to_all | solution.py:407
  119.7 20.3 %shard_map.78 = bf16[8,2,16,4096]{3,2,1,0:T(8,128)(2,1)} custom-call(s32[64]{0:T(128)} %dynamic_slice.3.waves, s32[5]{0:T(128)} %pad_add_fusion.scalars, f32[128,1]{1,0:T(8,128)} %copy.12.eig_ref, bf16[128,128]{1,0:T(8,128)(2,1)} %select_bitcast_fusion.1.modes_in, bf16[128,128]{1,0:T(8,128)(2,1)} %broadcast_select_fusion.1.modes_out, ...), custom_call_target="tpu_custom_call" | custom-call | flops 1610612736 | bytes 6291456 | tf_op jit(solution)/shard_map/pallas_call | solution.py:326
  140.5 11.3 %shard_map.79 = (bf16[256,4096]{1,0:T(8,128)(2,1)}, bf16[256,1536]{1,0:T(8,128)(2,1)}) custom-call(s32[3]{0:T(128)} %pad_add_fusion.1.place_ref, bf16[64,64,1536]{2,1,0:T(8,128)(2,1)} %bitcast.123, s32[1,512]{1,0:T(1,128)} %bitcast.159, s32[1,256]{1,0:T(1,128)} %bitcast.163), custom_call_target="tpu_custom_call" | custom-call | flops 3221225472 | bytes 15466496 | tf_op jit(solution)/shard_map/pallas_call | solution.py:104
  151.8 11.3 %shard_map.75 = (bf16[256,4096]{1,0:T(8,128)(2,1)}, bf16[256,1536]{1,0:T(8,128)(2,1)}) custom-call(s32[3]{0:T(128)} %pad_add_fusion.1.place_ref, bf16[64,64,1536]{2,1,0:T(8,128)(2,1)} %bitcast.124, s32[1,512]{1,0:T(1,128)} %bitcast.160, s32[1,256]{1,0:T(1,128)} %bitcast.164), custom_call_target="tpu_custom_call" | custom-call | flops 3221225472 | bytes 15466496 | tf_op jit(solution)/shard_map/pallas_call | solution.py:104
  163.7 20.4 %shard_map.74 = bf16[8,2,16,4096]{3,2,1,0:T(8,128)(2,1)} custom-call(s32[64]{0:T(128)} %dynamic_slice.3.waves, s32[5]{0:T(128)} %pad_add_fusion.scalars, f32[128,1]{1,0:T(8,128)} %copy.12.eig_ref, bf16[128,128]{1,0:T(8,128)(2,1)} %select_bitcast_fusion.1.modes_in, bf16[128,128]{1,0:T(8,128)(2,1)} %broadcast_select_fusion.1.modes_out, ...), custom_call_target="tpu_custom_call" | custom-call | flops 1610612736 | bytes 6291456 | tf_op jit(solution)/shard_map/pallas_call | solution.py:326
  184.1 3.9 multiply_convert_fusion
  188.1 3.6 all-to-all-start.3
  191.7 3.8 add_convert_fusion
  195.5 4.6 collective-permute-start.27
  202.1 2.9 collective-permute-start.24
  205.0 28.6 %collective-permute-done.27 = bf16[32,4096]{1,0:T(8,128)(2,1)S(1)} collective-permute-done((bf16[32,4096]{1,0:T(8,128)(2,1)}, bf16[32,4096]{1,0:T(8,128)(2,1)S(1)}, u32[]{:S(2)}, u32[]{:S(2)}) %collective-permute-start.27) | collective-permute-done | bytes 262176 | tf_op jit(solution)/shard_map/ppermute | solution.py:34
  233.6 31.6 %collective-permute-start.23 = (bf16[32,4096]{1,0:T(8,128)(2,1)}, bf16[32,4096]{1,0:T(8,128)(2,1)}, u32[]{:S(2)}, u32[]{:S(2)}) collective-permute-start(bf16[32,4096]{1,0:T(8,128)(2,1)} %get-tuple-element.60), channel_id=1, source_target_pairs={{0,6},{2,4},{4,10},{6,8},{8,14},{10,12},{12,2},{14,0},{1,7},{3,5},... | collective-permute-start | bytes 786440 | tf_op jit(solution)/shard_map/ppermute | solution.py:34
  265.2 10.3 %collective-permute-start.22 = (bf16[32,4096]{1,0:T(8,128)(2,1)}, bf16[32,4096]{1,0:T(8,128)(2,1)}, u32[]{:S(2)}, u32[]{:S(2)}) collective-permute-start(bf16[32,4096]{1,0:T(8,128)(2,1)} %get-tuple-element.61), channel_id=1, source_target_pairs={{0,4},{2,6},{4,8},{6,10},{8,12},{10,14},{12,0},{14,2},{1,5},{3,7},... | collective-permute-start | bytes 786440 | tf_op jit(solution)/shard_map/ppermute | solution.py:34
  275.6 3.8 add_convert_fusion.8
  279.4 2.1 collective-permute-done.25
  282.1 3.7 collective-permute-done.24
  285.8 2.0 collective-permute-start.8
  287.7 2.4 collective-permute-start.7
  292.1 3.9 collective-permute-done.9
  296.1 6.4 %collective-permute-done.8 = bf16[32,4096]{1,0:T(8,128)(2,1)S(1)} collective-permute-done((bf16[32,4096]{1,0:T(8,128)(2,1)}, bf16[32,4096]{1,0:T(8,128)(2,1)S(1)}, u32[]{:S(2)}, u32[]{:S(2)}) %collective-permute-start.8) | collective-permute-done | bytes 262176 | tf_op jit(solution)/shard_map/ppermute | solution.py:34
  302.5 25.0 %collective-permute-done.7 = bf16[32,4096]{1,0:T(8,128)(2,1)} collective-permute-done((bf16[32,4096]{1,0:T(8,128)(2,1)}, bf16[32,4096]{1,0:T(8,128)(2,1)}, u32[]{:S(2)}, u32[]{:S(2)}) %collective-permute-start.7) | collective-permute-done | bytes 262176 | tf_op jit(solution)/shard_map/ppermute | solution.py:34
  328.6 18.9 %shard_map.80 = bf16[8,2,16,4096]{3,2,1,0:T(8,128)(2,1)} custom-call(s32[64]{0:T(128)} %dynamic_slice.3.waves, s32[5]{0:T(128)} %pad_add_fusion.2.scalars, f32[128,1]{1,0:T(8,128)} %copy.12.eig_ref, bf16[128,128]{1,0:T(8,128)(2,1)} %select_bitcast_fusion.modes_in, bf16[128,128]{1,0:T(8,128)(2,1)} %broadcast_select_fusion.modes_out, ...), custom_call_target="tpu_custom_call" | custom-call | flops 1610612736 | bytes 6291456 | tf_op jit(solution)/shard_map/pallas_call | solution.py:326
  348.6 19.0 %shard_map.76 = bf16[8,2,16,4096]{3,2,1,0:T(8,128)(2,1)} custom-call(s32[64]{0:T(128)} %dynamic_slice.3.waves, s32[5]{0:T(128)} %pad_add_fusion.2.scalars, f32[128,1]{1,0:T(8,128)} %copy.12.eig_ref, bf16[128,128]{1,0:T(8,128)(2,1)} %select_bitcast_fusion.modes_in, bf16[128,128]{1,0:T(8,128)(2,1)} %broadcast_select_fusion.modes_out, ...), custom_call_target="tpu_custom_call" | custom-call | flops 1610612736 | bytes 6291456 | tf_op jit(solution)/shard_map/pallas_call | solution.py:326
  368.2 3.9 multiply_convert_fusion.1
  373.4 3.6 all-to-all-start.1
  377.0 2.7 fusion.6
  379.7 1.9 collective-permute-start.34
  381.7 1.9 fusion.30
  383.5 1.5 collective-permute-start.16
  385.0 2.4 collective-permute-start.15
  387.4 2.0 fusion.39
  389.4 1.4 collective-permute-start.42
  391.4 2.5 fusion.15
  393.9 26.7 %collective-permute-done.16.refs_7_ = bf16[32,1024]{1,0:T(8,128)(2,1)S(1)} collective-permute-done((bf16[32,1024]{1,0:T(8,128)(2,1)S(1)}, bf16[32,1024]{1,0:T(8,128)(2,1)S(1)}, u32[]{:S(2)}, u32[]{:S(2)}) %collective-permute-start.16) | collective-permute-done | bytes 65568 | tf_op jit(solution)/shard_map/ppermute | solution.py:34
  420.6 12.2 %collective-permute-start.33 = (bf16[32,2048]{1,0:T(8,128)(2,1)S(1)}, bf16[32,2048]{1,0:T(8,128)(2,1)S(1)}, u32[]{:S(2)}, u32[]{:S(2)}) collective-permute-start(bf16[32,2048]{1,0:T(8,128)(2,1)S(1)} %get-tuple-element.50), channel_id=1, source_target_pairs={{0,10},{2,8},{4,14},{6,12},{8,2},{10,0},{12,6},{14,4},{1,11},{3,9}... | collective-permute-start | bytes 393224 | tf_op jit(solution)/shard_map/ppermute | solution.py:34
  432.8 7.3 %collective-permute-done.15.refs_6_ = bf16[32,1024]{1,0:T(8,128)(2,1)S(1)} collective-permute-done((bf16[32,1024]{1,0:T(8,128)(2,1)S(1)}, bf16[32,1024]{1,0:T(8,128)(2,1)S(1)}, u32[]{:S(2)}, u32[]{:S(2)}) %collective-permute-start.15) | collective-permute-done | bytes 65568 | tf_op jit(solution)/shard_map/ppermute | solution.py:34
  440.2 5.2 collective-permute-start.47
  445.5 2.3 fusion.23
  447.8 2.5 collective-permute-start.45
  450.3 1.9 collective-permute-start.44
  452.3 1.5 collective-permute-start.43
  453.7 3.8 collective-permute-done.47.refs_6_
  457.5 3.5 collective-permute-start.56
  461.0 2.8 collective-permute-start.55
  463.8 3.4 collective-permute-start.54
  467.2 5.8 %collective-permute-start.53 = (bf16[32,2048]{1,0:T(8,128)(2,1)S(1)}, bf16[32,2048]{1,0:T(8,128)(2,1)S(1)}, u32[]{:S(2)}, u32[]{:S(2)}) collective-permute-start(bf16[32,2048]{1,0:T(8,128)(2,1)S(1)} %get-tuple-element.26), channel_id=1, source_target_pairs={{0,8},{2,10},{4,12},{6,14},{8,0},{10,2},{12,4},{14,6},{1,9},{3,11}... | collective-permute-start | bytes 393224 | tf_op jit(solution)/shard_map/ppermute | solution.py:34
  473.0 4.3 collective-permute-start.52
  478.0 3.9 collective-permute-done.53.refs_14_
  481.9 10.5 %collective-permute-start.31 = (bf16[32,2048]{1,0:T(8,128)(2,1)S(1)}, bf16[32,2048]{1,0:T(8,128)(2,1)S(1)}, u32[]{:S(2)}, u32[]{:S(2)}) collective-permute-start(bf16[32,2048]{1,0:T(8,128)(2,1)S(1)} %get-tuple-element.52), channel_id=1, source_target_pairs={{0,14},{2,12},{4,2},{6,0},{8,6},{10,4},{12,10},{14,8},{1,15},{3,13... | collective-permute-start | bytes 393224 | tf_op jit(solution)/shard_map/ppermute | solution.py:34
  494.3 2.9 collective-permute-start.35
  498.5 11.0 %shard_map.82.refs_12_ = bf16[64,64,1536]{2,1,0:T(8,128)(2,1)} custom-call(bf16[256,4096]{1,0:T(8,128)(2,1)} %bitcast.132, bf16[32,2048]{1,0:T(8,128)(2,1)} %get-tuple-element.38.refs_1_, bf16[32,2048]{1,0:T(8,128)(2,1)} %copy-done.58, bf16[32,2048]{1,0:T(8,128)(2,1)} %copy-done.57, bf16[32,2048]{1,0:T(8,128)(2,1)} %copy-done.56, ...), custom_call_target="tpu_custom_call" | custom-call | flops 6442450944 | bytes 10485760 | tf_op jit(solution)/shard_map/pallas_call | solution.py:172
  509.7 2.9 collective-permute-start.39
  512.6 2.8 collective-permute-start.38
  516.3 8.6 %shard_map.81.refs_11_ = f32[32,64,1536]{2,1,0:T(8,128)} custom-call(bf16[256,4096]{1,0:T(8,128)(2,1)} %bitcast.133, bf16[32,2048]{1,0:T(8,128)(2,1)} %get-tuple-element.55.refs_1_, bf16[32,2048]{1,0:T(8,128)(2,1)} %copy-done.24, bf16[32,2048]{1,0:T(8,128)(2,1)} %copy-done.23, bf16[32,2048]{1,0:T(8,128)(2,1)} %copy-done.22, bf16[32,2048]{1,0:T(8,128)(2,1)} %copy-done.21, ...), custom_call_target="tpu_custom_call" | custom-call | flops 3221225472 | bytes 8388608 | tf_op jit(solution)/shard_map/pallas_call | solution.py:172
  524.9 1.6 collective-permute-start.14
  526.5 3.8 collective-permute-start.13
  531.0 2.9 collective-permute-start.17
  534.0 5.9 %shard_map.83.refs_12_ = bf16[64,64,1536]{2,1,0:T(8,128)(2,1)} custom-call(bf16[256,4096]{1,0:T(8,128)(2,1)} %bitcast.130, bf16[32,1024]{1,0:T(8,128)(2,1)} %get-tuple-element.47.refs_1_, bf16[32,1024]{1,0:T(8,128)(2,1)} %copy-done.36, bf16[32,1024]{1,0:T(8,128)(2,1)} %copy-done.34, bf16[32,1024]{1,0:T(8,128)(2,1)} %copy-done.32, ...), custom_call_target="tpu_custom_call", output_to_operand_aliasing={{}: (12, {})} | custom-call | flops 1610612736 | bytes 4194304 | tf_op jit(solution)/shard_map/pallas_call | solution.py:172
  540.6 5.9 %shard_map.84 = bf16[64,64,1536]{2,1,0:T(8,128)(2,1)} custom-call(bf16[256,4096]{1,0:T(8,128)(2,1)} %bitcast.131, bf16[32,1024]{1,0:T(8,128)(2,1)} %get-tuple-element.70.refs_1_, bf16[32,1024]{1,0:T(8,128)(2,1)} %copy-done.38, bf16[32,1024]{1,0:T(8,128)(2,1)} %copy-done.37, bf16[32,1024]{1,0:T(8,128)(2,1)} %copy-done.35, ...), custom_call_target="tpu_custom_call", output_to_operand_aliasing={{}: (12, {})} | custom-call | flops 1610612736 | bytes 4194304 | tf_op jit(solution)/shard_map/pallas_call | solution.py:172
  (240 shorter events, 23.2 us)
Async XLA Ops:
  0.0 74.5 %copy-start = (bf16[128,128]{1,0:T(8,128)(2,1)S(1)}, bf16[128,128]{1,0:T(8,128)(2,1)}, u32[]{:S(2)}) copy-start(bf16[128,128]{1,0:T(8,128)(2,1)} %param.17) | copy-start | bytes 98308
  11.8 55.5 %all-to-all-start.2 = ((bf16[8,2,16,4096]{3,2,1,0:T(8,128)(2,1)}), bf16[8,2,16,4096]{3,2,1,0:T(8,128)(2,1)S(1)}, u32[]{:S(2)}, u32[]{:S(2)}) async-start(bf16[8,2,16,4096]{3,2,1,0:T(8,128)(2,1)} %bitcast.144), calls=%async_computation.2 | async-start | bytes 4194304 | tf_op jit(solution)/shard_map/all_to_all | solution.py:407
  67.3 52.4 %all-to-all-start = ((bf16[8,2,16,4096]{3,2,1,0:T(8,128)(2,1)}), bf16[8,2,16,4096]{3,2,1,0:T(8,128)(2,1)}, u32[]{:S(2)}, u32[]{:S(2)}) async-start(bf16[8,2,16,4096]{3,2,1,0:T(8,128)(2,1)} %bitcast.143), calls=%async_computation | async-start | bytes 4194304 | tf_op jit(solution)/shard_map/all_to_all | solution.py:407
  72.0 47.7 %collective-permute-start.18 = (bf16[8,2,16,4096]{3,2,1,0:T(8,128)(2,1)S(1)}, bf16[8,2,16,4096]{3,2,1,0:T(8,128)(2,1)}, u32[]{:S(2)}, u32[]{:S(2)}) collective-permute-start(bf16[8,2,16,4096]{3,2,1,0:T(8,128)(2,1)S(1)} %all-to-all-done.2.refs_0_), channel_id=1, source_target_pairs={{0,1},{1,0},{2,3},{3,2},{4,5},{5,4},{6,7},{7,6},{8,9},{9,8},{10,11... | collective-permute-start | bytes 6291464 | tf_op jit(solution)/shard_map/ppermute | solution.py:22
  119.7 44.0 %collective-permute-start = (bf16[8,2,16,4096]{3,2,1,0:T(8,128)(2,1)}, bf16[8,2,16,4096]{3,2,1,0:T(8,128)(2,1)}, u32[]{:S(2)}, u32[]{:S(2)}) collective-permute-start(bf16[8,2,16,4096]{3,2,1,0:T(8,128)(2,1)} %all-to-all-done.refs_0_), channel_id=1, source_target_pairs={{0,1},{1,0},{2,3},{3,2},{4,5},{5,4},{6,7},{7,6},{8,9},{9,8},{10,11... | collective-permute-start | bytes 6291464 | tf_op jit(solution)/shard_map/ppermute | solution.py:22
  140.0 44.1 %collective-permute-start.19 = (bf16[8,32,4096]{2,1,0:T(8,128)(2,1)}, bf16[8,32,4096]{2,1,0:T(8,128)(2,1)}, u32[]{:S(2)}, u32[]{:S(2)}) collective-permute-start(bf16[8,32,4096]{2,1,0:T(8,128)(2,1)} %bitcast.142), channel_id=1, source_target_pairs={{0,1},{1,0},{2,3},{3,2},{4,5},{5,4},{6,7},{7,6},{8,9},{9,8},{10,11... | collective-permute-start | bytes 6291464 | tf_op jit(solution)/shard_map/ppermute | solution.py:22
  151.8 39.9 %collective-permute-start.20 = (bf16[256,4096]{1,0:T(8,128)(2,1)}, bf16[256,4096]{1,0:T(8,128)(2,1)}, u32[]{:S(2)}, u32[]{:S(2)}) collective-permute-start(bf16[256,4096]{1,0:T(8,128)(2,1)} %get-tuple-element.20), channel_id=1, source_target_pairs={{0,1},{1,0},{2,3},{3,2},{4,5},{5,4},{6,7},{7,6},{8,9},{9,8},{10,11... | collective-permute-start | bytes 6291464 | tf_op jit(solution)/shard_map/ppermute | solution.py:22
  163.1 39.0 %collective-permute-start.2 = (bf16[256,4096]{1,0:T(8,128)(2,1)}, bf16[256,4096]{1,0:T(8,128)(2,1)}, u32[]{:S(2)}, u32[]{:S(2)}) collective-permute-start(bf16[256,4096]{1,0:T(8,128)(2,1)} %get-tuple-element.16), channel_id=1, source_target_pairs={{0,1},{1,0},{2,3},{3,2},{4,5},{5,4},{6,7},{7,6},{8,9},{9,8},{10,11... | collective-permute-start | bytes 6291464 | tf_op jit(solution)/shard_map/ppermute | solution.py:22
  184.1 184.1 %collective-permute-start.1 = (bf16[8,32,4096]{2,1,0:T(8,128)(2,1)}, bf16[8,32,4096]{2,1,0:T(8,128)(2,1)}, u32[]{:S(2)}, u32[]{:S(2)}) collective-permute-start(bf16[8,32,4096]{2,1,0:T(8,128)(2,1)} %bitcast.141), channel_id=1, source_target_pairs={{0,1},{1,0},{2,3},{3,2},{4,5},{5,4},{6,7},{7,6},{8,9},{9,8},{10,11... | collective-permute-start | bytes 6291464 | tf_op jit(solution)/shard_map/ppermute | solution.py:22
  188.1 184.0 %all-to-all-start.3 = ((bf16[8,32,4096]{2,1,0:T(8,128)(2,1)}), bf16[8,32,4096]{2,1,0:T(8,128)(2,1)S(1)}, u32[]{:S(2)}, u32[]{:S(2)}) async-start(bf16[8,32,4096]{2,1,0:T(8,128)(2,1)} %multiply_convert_fusion), calls=%async_computation.3 | async-start | bytes 4194304 | tf_op jit(solution)/shard_map/all_to_all | solution.py:407
  195.5 38.2 %collective-permute-start.27 = (bf16[32,4096]{1,0:T(8,128)(2,1)}, bf16[32,4096]{1,0:T(8,128)(2,1)S(1)}, u32[]{:S(2)}, u32[]{:S(2)}) collective-permute-start(bf16[32,4096]{1,0:T(8,128)(2,1)} %get-tuple-element.56), channel_id=1, source_target_pairs={{0,14},{2,12},{4,2},{6,0},{8,6},{10,4},{12,10},{14,8},{1,15},{3,13... | collective-permute-start | bytes 786440 | tf_op jit(solution)/shard_map/ppermute | solution.py:34
  200.1 65.1 %collective-permute-start.26 = (bf16[32,4096]{1,0:T(8,128)(2,1)S(1)}, bf16[32,4096]{1,0:T(8,128)(2,1)S(1)}, u32[]{:S(2)}, u32[]{:S(2)}) collective-permute-start(bf16[32,4096]{1,0:T(8,128)(2,1)S(1)} %get-tuple-element.57), channel_id=1, source_target_pairs={{0,12},{2,14},{4,0},{6,2},{8,4},{10,6},{12,8},{14,10},{1,13},{3,15... | collective-permute-start | bytes 786440 | tf_op jit(solution)/shard_map/ppermute | solution.py:34
  202.1 79.4 %collective-permute-start.25 = (bf16[32,4096]{1,0:T(8,128)(2,1)}, bf16[32,4096]{1,0:T(8,128)(2,1)S(1)}, u32[]{:S(2)}, u32[]{:S(2)}) collective-permute-start(bf16[32,4096]{1,0:T(8,128)(2,1)} %get-tuple-element.58), channel_id=1, source_target_pairs={{0,10},{2,8},{4,14},{6,12},{8,2},{10,0},{12,6},{14,4},{1,11},{3,9}... | collective-permute-start | bytes 786440 | tf_op jit(solution)/shard_map/ppermute | solution.py:34
  202.1 83.6 %collective-permute-start.24 = (bf16[32,4096]{1,0:T(8,128)(2,1)}, bf16[32,4096]{1,0:T(8,128)(2,1)S(1)}, u32[]{:S(2)}, u32[]{:S(2)}) collective-permute-start(bf16[32,4096]{1,0:T(8,128)(2,1)} %get-tuple-element.59), channel_id=1, source_target_pairs={{0,8},{2,10},{4,12},{6,14},{8,0},{10,2},{12,4},{14,6},{1,9},{3,11}... | collective-permute-start | bytes 786440 | tf_op jit(solution)/shard_map/ppermute | solution.py:34
  233.6 52.1 %collective-permute-start.23 = (bf16[32,4096]{1,0:T(8,128)(2,1)}, bf16[32,4096]{1,0:T(8,128)(2,1)}, u32[]{:S(2)}, u32[]{:S(2)}) collective-permute-start(bf16[32,4096]{1,0:T(8,128)(2,1)} %get-tuple-element.60), channel_id=1, source_target_pairs={{0,6},{2,4},{4,10},{6,8},{8,14},{10,12},{12,2},{14,0},{1,7},{3,5},... | collective-permute-start | bytes 786440 | tf_op jit(solution)/shard_map/ppermute | solution.py:34
  265.2 22.5 %collective-permute-start.22 = (bf16[32,4096]{1,0:T(8,128)(2,1)}, bf16[32,4096]{1,0:T(8,128)(2,1)}, u32[]{:S(2)}, u32[]{:S(2)}) collective-permute-start(bf16[32,4096]{1,0:T(8,128)(2,1)} %get-tuple-element.61), channel_id=1, source_target_pairs={{0,4},{2,6},{4,8},{6,10},{8,12},{10,14},{12,0},{14,2},{1,5},{3,7},... | collective-permute-start | bytes 786440 | tf_op jit(solution)/shard_map/ppermute | solution.py:34
  281.5 10.1 %collective-permute-start.21 = (bf16[32,4096]{1,0:T(8,128)(2,1)}, bf16[32,4096]{1,0:T(8,128)(2,1)}, u32[]{:S(2)}, u32[]{:S(2)}) collective-permute-start(bf16[32,4096]{1,0:T(8,128)(2,1)} %get-tuple-element.62), channel_id=1, source_target_pairs={{0,2},{2,0},{4,6},{6,4},{8,10},{10,8},{12,14},{14,12},{1,3},{3,1},... | collective-permute-start | bytes 786440 | tf_op jit(solution)/shard_map/ppermute | solution.py:34
  285.8 10.3 %collective-permute-start.9 = (bf16[32,4096]{1,0:T(8,128)(2,1)}, bf16[32,4096]{1,0:T(8,128)(2,1)S(1)}, u32[]{:S(2)}, u32[]{:S(2)}) collective-permute-start(bf16[32,4096]{1,0:T(8,128)(2,1)} %get-tuple-element.71), channel_id=1, source_target_pairs={{0,14},{2,12},{4,2},{6,0},{8,6},{10,4},{12,10},{14,8},{1,15},{3,13... | collective-permute-start | bytes 786440 | tf_op jit(solution)/shard_map/ppermute | solution.py:34
  285.8 16.7 %collective-permute-start.8 = (bf16[32,4096]{1,0:T(8,128)(2,1)}, bf16[32,4096]{1,0:T(8,128)(2,1)S(1)}, u32[]{:S(2)}, u32[]{:S(2)}) collective-permute-start(bf16[32,4096]{1,0:T(8,128)(2,1)} %get-tuple-element.72), channel_id=1, source_target_pairs={{0,12},{2,14},{4,0},{6,2},{8,4},{10,6},{12,8},{14,10},{1,13},{3,15... | collective-permute-start | bytes 786440 | tf_op jit(solution)/shard_map/ppermute | solution.py:34
  287.7 39.7 %collective-permute-start.7 = (bf16[32,4096]{1,0:T(8,128)(2,1)}, bf16[32,4096]{1,0:T(8,128)(2,1)}, u32[]{:S(2)}, u32[]{:S(2)}) collective-permute-start(bf16[32,4096]{1,0:T(8,128)(2,1)} %get-tuple-element.73), channel_id=1, source_target_pairs={{0,10},{2,8},{4,14},{6,12},{8,2},{10,0},{12,6},{14,4},{1,11},{3,9}... | collective-permute-start | bytes 786440 | tf_op jit(solution)/shard_map/ppermute | solution.py:34
  291.6 56.0 %collective-permute-start.6 = (bf16[32,4096]{1,0:T(8,128)(2,1)}, bf16[32,4096]{1,0:T(8,128)(2,1)S(1)}, u32[]{:S(2)}, u32[]{:S(2)}) collective-permute-start(bf16[32,4096]{1,0:T(8,128)(2,1)} %get-tuple-element.74), channel_id=1, source_target_pairs={{0,8},{2,10},{4,12},{6,14},{8,0},{10,2},{12,4},{14,6},{1,9},{3,11}... | collective-permute-start | bytes 786440 | tf_op jit(solution)/shard_map/ppermute | solution.py:34
  296.1 51.6 %collective-permute-start.5 = (bf16[32,4096]{1,0:T(8,128)(2,1)}, bf16[32,4096]{1,0:T(8,128)(2,1)S(1)}, u32[]{:S(2)}, u32[]{:S(2)}) collective-permute-start(bf16[32,4096]{1,0:T(8,128)(2,1)} %get-tuple-element.75), channel_id=1, source_target_pairs={{0,6},{2,4},{4,10},{6,8},{8,14},{10,12},{12,2},{14,0},{1,7},{3,5},... | collective-permute-start | bytes 786440 | tf_op jit(solution)/shard_map/ppermute | solution.py:34
  302.5 45.2 %collective-permute-start.4 = (bf16[32,4096]{1,0:T(8,128)(2,1)}, bf16[32,4096]{1,0:T(8,128)(2,1)S(1)}, u32[]{:S(2)}, u32[]{:S(2)}) collective-permute-start(bf16[32,4096]{1,0:T(8,128)(2,1)} %get-tuple-element.76), channel_id=1, source_target_pairs={{0,4},{2,6},{4,8},{6,10},{8,12},{10,14},{12,0},{14,2},{1,5},{3,7},... | collective-permute-start | bytes 786440 | tf_op jit(solution)/shard_map/ppermute | solution.py:34
  327.5 20.3 %collective-permute-start.3 = (bf16[32,4096]{1,0:T(8,128)(2,1)S(1)}, bf16[32,4096]{1,0:T(8,128)(2,1)S(1)}, u32[]{:S(2)}, u32[]{:S(2)}) collective-permute-start(bf16[32,4096]{1,0:T(8,128)(2,1)S(1)} %get-tuple-element.77), channel_id=1, source_target_pairs={{0,2},{2,0},{4,6},{6,4},{8,10},{10,8},{12,14},{14,12},{1,3},{3,1},... | collective-permute-start | bytes 786440 | tf_op jit(solution)/shard_map/ppermute | solution.py:34
  347.6 29.4 %collective-permute-start.28 = (bf16[8,32,4096]{2,1,0:T(8,128)(2,1)}, bf16[8,32,4096]{2,1,0:T(8,128)(2,1)}, u32[]{:S(2)}, u32[]{:S(2)}) collective-permute-start(bf16[8,32,4096]{2,1,0:T(8,128)(2,1)} %bitcast.138), channel_id=1, source_target_pairs={{0,1},{1,0},{2,3},{3,2},{4,5},{5,4},{6,7},{7,6},{8,9},{9,8},{10,11... | collective-permute-start | bytes 6291464 | tf_op jit(solution)/shard_map/ppermute | solution.py:22
  367.7 14.0 %collective-permute-start.10 = (bf16[8,32,4096]{2,1,0:T(8,128)(2,1)}, bf16[8,32,4096]{2,1,0:T(8,128)(2,1)}, u32[]{:S(2)}, u32[]{:S(2)}) collective-permute-start(bf16[8,32,4096]{2,1,0:T(8,128)(2,1)} %bitcast.134), channel_id=1, source_target_pairs={{0,1},{1,0},{2,3},{3,2},{4,5},{5,4},{6,7},{7,6},{8,9},{9,8},{10,11... | collective-permute-start | bytes 6291464 | tf_op jit(solution)/shard_map/ppermute | solution.py:22
  373.4 123.8 %all-to-all-start.1 = ((bf16[8,32,4096]{2,1,0:T(8,128)(2,1)}), bf16[8,32,4096]{2,1,0:T(8,128)(2,1)S(1)}, u32[]{:S(2)}, u32[]{:S(2)}) async-start(bf16[8,32,4096]{2,1,0:T(8,128)(2,1)} %multiply_convert_fusion.1), calls=%async_computation.1 | async-start | bytes 4194304 | tf_op jit(solution)/shard_map/all_to_all | solution.py:407
  379.7 65.7 %collective-permute-start.34 = (bf16[32,2048]{1,0:T(8,128)(2,1)S(1)}, bf16[32,2048]{1,0:T(8,128)(2,1)S(1)}, u32[]{:S(2)}, u32[]{:S(2)}) collective-permute-start(bf16[32,2048]{1,0:T(8,128)(2,1)S(1)} %get-tuple-element.49), channel_id=1, source_target_pairs={{0,4},{2,6},{4,8},{6,10},{8,12},{10,14},{12,0},{14,2},{1,5},{3,7},... | collective-permute-start | bytes 393224 | tf_op jit(solution)/shard_map/ppermute | solution.py:34
  383.5 37.1 %collective-permute-start.16 = (bf16[32,1024]{1,0:T(8,128)(2,1)S(1)}, bf16[32,1024]{1,0:T(8,128)(2,1)S(1)}, u32[]{:S(2)}, u32[]{:S(2)}) collective-permute-start(bf16[32,1024]{1,0:T(8,128)(2,1)S(1)} %get-tuple-element.64), channel_id=1, source_target_pairs={{0,4},{2,6},{4,8},{6,10},{8,12},{10,14},{12,0},{14,2},{1,5},{3,7},... | collective-permute-start | bytes 196616 | tf_op jit(solution)/shard_map/ppermute | solution.py:34
  385.0 55.1 %collective-permute-start.15 = (bf16[32,1024]{1,0:T(8,128)(2,1)S(1)}, bf16[32,1024]{1,0:T(8,128)(2,1)S(1)}, u32[]{:S(2)}, u32[]{:S(2)}) collective-permute-start(bf16[32,1024]{1,0:T(8,128)(2,1)S(1)} %get-tuple-element.65), channel_id=1, source_target_pairs={{0,10},{2,8},{4,14},{6,12},{8,2},{10,0},{12,6},{14,4},{1,11},{3,9}... | collective-permute-start | bytes 196616 | tf_op jit(solution)/shard_map/ppermute | solution.py:34
  389.4 50.7 %collective-permute-start.42 = (bf16[32,1024]{1,0:T(8,128)(2,1)S(1)}, bf16[32,1024]{1,0:T(8,128)(2,1)S(1)}, u32[]{:S(2)}, u32[]{:S(2)}) collective-permute-start(bf16[32,1024]{1,0:T(8,128)(2,1)S(1)} %get-tuple-element.40), channel_id=1, source_target_pairs={{0,6},{2,4},{4,10},{6,8},{8,14},{10,12},{12,2},{14,0},{1,7},{3,5},... | collective-permute-start | bytes 196616 | tf_op jit(solution)/shard_map/ppermute | solution.py:34
  390.8 49.4 %collective-permute-start.41 = (bf16[32,1024]{1,0:T(8,128)(2,1)S(1)}, bf16[32,1024]{1,0:T(8,128)(2,1)S(1)}, u32[]{:S(2)}, u32[]{:S(2)}) collective-permute-start(bf16[32,1024]{1,0:T(8,128)(2,1)S(1)} %get-tuple-element.41), channel_id=1, source_target_pairs={{0,4},{2,6},{4,8},{6,10},{8,12},{10,14},{12,0},{14,2},{1,5},{3,7},... | collective-permute-start | bytes 196616 | tf_op jit(solution)/shard_map/ppermute | solution.py:34
  420.6 88.9 %copy-start.26 = (bf16[32,1024]{1,0:T(8,128)(2,1)}, bf16[32,1024]{1,0:T(8,128)(2,1)S(1)}, u32[]{:S(2)}) copy-start(bf16[32,1024]{1,0:T(8,128)(2,1)S(1)} %collective-permute-done.16.refs_7_) | copy-start | bytes 196612
  420.6 27.2 %collective-permute-start.33 = (bf16[32,2048]{1,0:T(8,128)(2,1)S(1)}, bf16[32,2048]{1,0:T(8,128)(2,1)S(1)}, u32[]{:S(2)}, u32[]{:S(2)}) collective-permute-start(bf16[32,2048]{1,0:T(8,128)(2,1)S(1)} %get-tuple-element.50), channel_id=1, source_target_pairs={{0,10},{2,8},{4,14},{6,12},{8,2},{10,0},{12,6},{14,4},{1,11},{3,9}... | collective-permute-start | bytes 393224 | tf_op jit(solution)/shard_map/ppermute | solution.py:34
  440.1 10.2 %collective-permute-start.49 = (bf16[32,2048]{1,0:T(8,128)(2,1)S(1)}, bf16[32,2048]{1,0:T(8,128)(2,1)S(1)}, u32[]{:S(2)}, u32[]{:S(2)}) collective-permute-start(bf16[32,2048]{1,0:T(8,128)(2,1)S(1)} %get-tuple-element.31), channel_id=1, source_target_pairs={{0,6},{2,4},{4,10},{6,8},{8,14},{10,12},{12,2},{14,0},{1,7},{3,5},... | collective-permute-start | bytes 393224 | tf_op jit(solution)/shard_map/ppermute | solution.py:34
  440.1 12.1 %collective-permute-start.48 = (bf16[32,2048]{1,0:T(8,128)(2,1)S(1)}, bf16[32,2048]{1,0:T(8,128)(2,1)S(1)}, u32[]{:S(2)}, u32[]{:S(2)}) collective-permute-start(bf16[32,2048]{1,0:T(8,128)(2,1)S(1)} %get-tuple-element.32), channel_id=1, source_target_pairs={{0,4},{2,6},{4,8},{6,10},{8,12},{10,14},{12,0},{14,2},{1,5},{3,7},... | collective-permute-start | bytes 393224 | tf_op jit(solution)/shard_map/ppermute | solution.py:34
  440.2 17.3 %collective-permute-start.47 = (bf16[32,2048]{1,0:T(8,128)(2,1)S(1)}, bf16[32,2048]{1,0:T(8,128)(2,1)S(1)}, u32[]{:S(2)}, u32[]{:S(2)}) collective-permute-start(bf16[32,2048]{1,0:T(8,128)(2,1)S(1)} %get-tuple-element.33), channel_id=1, source_target_pairs={{0,10},{2,8},{4,14},{6,12},{8,2},{10,0},{12,6},{14,4},{1,11},{3,9}... | collective-permute-start | bytes 393224 | tf_op jit(solution)/shard_map/ppermute | solution.py:34
  445.4 64.1 %copy-start.19 = (bf16[32,2048]{1,0:T(8,128)(2,1)}, bf16[32,2048]{1,0:T(8,128)(2,1)S(1)}, u32[]{:S(2)}) copy-start(bf16[32,2048]{1,0:T(8,128)(2,1)S(1)} %collective-permute-done.34.refs_7_) | copy-start | bytes 393220
  445.4 15.5 %collective-permute-start.46 = (bf16[32,2048]{1,0:T(8,128)(2,1)S(1)}, bf16[32,2048]{1,0:T(8,128)(2,1)S(1)}, u32[]{:S(2)}, u32[]{:S(2)}) collective-permute-start(bf16[32,2048]{1,0:T(8,128)(2,1)S(1)} %get-tuple-element.34), channel_id=1, source_target_pairs={{0,8},{2,10},{4,12},{6,14},{8,0},{10,2},{12,4},{14,6},{1,9},{3,11}... | collective-permute-start | bytes 393224 | tf_op jit(solution)/shard_map/ppermute | solution.py:34
  447.8 15.9 %collective-permute-start.45 = (bf16[32,2048]{1,0:T(8,128)(2,1)S(1)}, bf16[32,2048]{1,0:T(8,128)(2,1)S(1)}, u32[]{:S(2)}, u32[]{:S(2)}) collective-permute-start(bf16[32,2048]{1,0:T(8,128)(2,1)S(1)} %get-tuple-element.35), channel_id=1, source_target_pairs={{0,14},{2,12},{4,2},{6,0},{8,6},{10,4},{12,10},{14,8},{1,15},{3,13... | collective-permute-start | bytes 393224 | tf_op jit(solution)/shard_map/ppermute | solution.py:34
  450.3 16.8 %collective-permute-start.44 = (bf16[32,2048]{1,0:T(8,128)(2,1)S(1)}, bf16[32,2048]{1,0:T(8,128)(2,1)S(1)}, u32[]{:S(2)}, u32[]{:S(2)}) collective-permute-start(bf16[32,2048]{1,0:T(8,128)(2,1)S(1)} %get-tuple-element.36), channel_id=1, source_target_pairs={{0,12},{2,14},{4,0},{6,2},{8,4},{10,6},{12,8},{14,10},{1,13},{3,15... | collective-permute-start | bytes 393224 | tf_op jit(solution)/shard_map/ppermute | solution.py:34
  452.3 20.7 %collective-permute-start.43 = (bf16[32,2048]{1,0:T(8,128)(2,1)S(1)}, bf16[32,2048]{1,0:T(8,128)(2,1)S(1)}, u32[]{:S(2)}, u32[]{:S(2)}) collective-permute-start(bf16[32,2048]{1,0:T(8,128)(2,1)S(1)} %get-tuple-element.37), channel_id=1, source_target_pairs={{0,2},{2,0},{4,6},{6,4},{8,10},{10,8},{12,14},{14,12},{1,3},{3,1},... | collective-permute-start | bytes 393224 | tf_op jit(solution)/shard_map/ppermute | solution.py:34
  457.5 19.8 %collective-permute-start.56 = (bf16[32,2048]{1,0:T(8,128)(2,1)S(1)}, bf16[32,2048]{1,0:T(8,128)(2,1)S(1)}, u32[]{:S(2)}, u32[]{:S(2)}) collective-permute-start(bf16[32,2048]{1,0:T(8,128)(2,1)S(1)} %get-tuple-element.23), channel_id=1, source_target_pairs={{0,6},{2,4},{4,10},{6,8},{8,14},{10,12},{12,2},{14,0},{1,7},{3,5},... | collective-permute-start | bytes 393224 | tf_op jit(solution)/shard_map/ppermute | solution.py:34
  461.0 16.4 %collective-permute-start.55 = (bf16[32,2048]{1,0:T(8,128)(2,1)S(1)}, bf16[32,2048]{1,0:T(8,128)(2,1)S(1)}, u32[]{:S(2)}, u32[]{:S(2)}) collective-permute-start(bf16[32,2048]{1,0:T(8,128)(2,1)S(1)} %get-tuple-element.24), channel_id=1, source_target_pairs={{0,4},{2,6},{4,8},{6,10},{8,12},{10,14},{12,0},{14,2},{1,5},{3,7},... | collective-permute-start | bytes 393224 | tf_op jit(solution)/shard_map/ppermute | solution.py:34
  463.8 14.2 %collective-permute-start.54 = (bf16[32,2048]{1,0:T(8,128)(2,1)S(1)}, bf16[32,2048]{1,0:T(8,128)(2,1)S(1)}, u32[]{:S(2)}, u32[]{:S(2)}) collective-permute-start(bf16[32,2048]{1,0:T(8,128)(2,1)S(1)} %get-tuple-element.25), channel_id=1, source_target_pairs={{0,10},{2,8},{4,14},{6,12},{8,2},{10,0},{12,6},{14,4},{1,11},{3,9}... | collective-permute-start | bytes 393224 | tf_op jit(solution)/shard_map/ppermute | solution.py:34
  467.2 14.8 %collective-permute-start.53 = (bf16[32,2048]{1,0:T(8,128)(2,1)S(1)}, bf16[32,2048]{1,0:T(8,128)(2,1)S(1)}, u32[]{:S(2)}, u32[]{:S(2)}) collective-permute-start(bf16[32,2048]{1,0:T(8,128)(2,1)S(1)} %get-tuple-element.26), channel_id=1, source_target_pairs={{0,8},{2,10},{4,12},{6,14},{8,0},{10,2},{12,4},{14,6},{1,9},{3,11}... | collective-permute-start | bytes 393224 | tf_op jit(solution)/shard_map/ppermute | solution.py:34
  473.0 19.4 %collective-permute-start.52 = (bf16[32,2048]{1,0:T(8,128)(2,1)S(1)}, bf16[32,2048]{1,0:T(8,128)(2,1)S(1)}, u32[]{:S(2)}, u32[]{:S(2)}) collective-permute-start(bf16[32,2048]{1,0:T(8,128)(2,1)S(1)} %get-tuple-element.27), channel_id=1, source_target_pairs={{0,14},{2,12},{4,2},{6,0},{8,6},{10,4},{12,10},{14,8},{1,15},{3,13... | collective-permute-start | bytes 393224 | tf_op jit(solution)/shard_map/ppermute | solution.py:34
  477.3 15.7 %collective-permute-start.51 = (bf16[32,2048]{1,0:T(8,128)(2,1)S(1)}, bf16[32,2048]{1,0:T(8,128)(2,1)S(1)}, u32[]{:S(2)}, u32[]{:S(2)}) collective-permute-start(bf16[32,2048]{1,0:T(8,128)(2,1)S(1)} %get-tuple-element.28), channel_id=1, source_target_pairs={{0,12},{2,14},{4,0},{6,2},{8,4},{10,6},{12,8},{14,10},{1,13},{3,15... | collective-permute-start | bytes 393224 | tf_op jit(solution)/shard_map/ppermute | solution.py:34
  477.3 16.3 %collective-permute-start.50 = (bf16[32,2048]{1,0:T(8,128)(2,1)S(1)}, bf16[32,2048]{1,0:T(8,128)(2,1)S(1)}, u32[]{:S(2)}, u32[]{:S(2)}) collective-permute-start(bf16[32,2048]{1,0:T(8,128)(2,1)S(1)} %get-tuple-element.29), channel_id=1, source_target_pairs={{0,2},{2,0},{4,6},{6,4},{8,10},{10,8},{12,14},{14,12},{1,3},{3,1},... | collective-permute-start | bytes 393224 | tf_op jit(solution)/shard_map/ppermute | solution.py:34
  478.0 31.6 %collective-permute-start.32 = (bf16[32,2048]{1,0:T(8,128)(2,1)}, bf16[32,2048]{1,0:T(8,128)(2,1)S(1)}, u32[]{:S(2)}, u32[]{:S(2)}) collective-permute-start(bf16[32,2048]{1,0:T(8,128)(2,1)} %get-tuple-element.51), channel_id=1, source_target_pairs={{0,8},{2,10},{4,12},{6,14},{8,0},{10,2},{12,4},{14,6},{1,9},{3,11}... | collective-permute-start | bytes 393224 | tf_op jit(solution)/shard_map/ppermute | solution.py:34
  481.9 27.8 %collective-permute-start.31 = (bf16[32,2048]{1,0:T(8,128)(2,1)S(1)}, bf16[32,2048]{1,0:T(8,128)(2,1)S(1)}, u32[]{:S(2)}, u32[]{:S(2)}) collective-permute-start(bf16[32,2048]{1,0:T(8,128)(2,1)S(1)} %get-tuple-element.52), channel_id=1, source_target_pairs={{0,14},{2,12},{4,2},{6,0},{8,6},{10,4},{12,10},{14,8},{1,15},{3,13... | collective-permute-start | bytes 393224 | tf_op jit(solution)/shard_map/ppermute | solution.py:34
  493.0 19.6 %collective-permute-start.30 = (bf16[32,2048]{1,0:T(8,128)(2,1)S(1)}, bf16[32,2048]{1,0:T(8,128)(2,1)S(1)}, u32[]{:S(2)}, u32[]{:S(2)}) collective-permute-start(bf16[32,2048]{1,0:T(8,128)(2,1)S(1)} %get-tuple-element.53), channel_id=1, source_target_pairs={{0,12},{2,14},{4,0},{6,2},{8,4},{10,6},{12,8},{14,10},{1,13},{3,15... | collective-permute-start | bytes 393224 | tf_op jit(solution)/shard_map/ppermute | solution.py:34
  493.0 22.5 %collective-permute-start.29 = (bf16[32,2048]{1,0:T(8,128)(2,1)S(1)}, bf16[32,2048]{1,0:T(8,128)(2,1)S(1)}, u32[]{:S(2)}, u32[]{:S(2)}) collective-permute-start(bf16[32,2048]{1,0:T(8,128)(2,1)S(1)} %get-tuple-element.54), channel_id=1, source_target_pairs={{0,2},{2,0},{4,6},{6,4},{8,10},{10,8},{12,14},{14,12},{1,3},{3,1},... | collective-permute-start | bytes 393224 | tf_op jit(solution)/shard_map/ppermute | solution.py:34
  494.3 21.3 %collective-permute-start.35 = (bf16[32,2048]{1,0:T(8,128)(2,1)}, bf16[32,2048]{1,0:T(8,128)(2,1)S(1)}, u32[]{:S(2)}, u32[]{:S(2)}) collective-permute-start(bf16[32,2048]{1,0:T(8,128)(2,1)} %get-tuple-element.39), channel_id=1, source_target_pairs={{0,6},{2,4},{4,10},{6,8},{8,14},{10,12},{12,2},{14,0},{1,7},{3,5},... | collective-permute-start | bytes 393224 | tf_op jit(solution)/shard_map/ppermute | solution.py:34
  509.6 15.3 %collective-permute-start.40 = (bf16[32,1024]{1,0:T(8,128)(2,1)S(1)}, bf16[32,1024]{1,0:T(8,128)(2,1)S(1)}, u32[]{:S(2)}, u32[]{:S(2)}) collective-permute-start(bf16[32,1024]{1,0:T(8,128)(2,1)S(1)} %copy-done.49), channel_id=1, source_target_pairs={{0,10},{2,8},{4,14},{6,12},{8,2},{10,0},{12,6},{14,4},{1,11},{3,9}... | collective-permute-start | bytes 196616 | tf_op jit(solution)/shard_map/ppermute | solution.py:34
  509.7 16.8 %collective-permute-start.39 = (bf16[32,1024]{1,0:T(8,128)(2,1)S(1)}, bf16[32,1024]{1,0:T(8,128)(2,1)S(1)}, u32[]{:S(2)}, u32[]{:S(2)}) collective-permute-start(bf16[32,1024]{1,0:T(8,128)(2,1)S(1)} %copy-done.48), channel_id=1, source_target_pairs={{0,8},{2,10},{4,12},{6,14},{8,0},{10,2},{12,4},{14,6},{1,9},{3,11}... | collective-permute-start | bytes 196616 | tf_op jit(solution)/shard_map/ppermute | solution.py:34
  512.6 17.7 %collective-permute-start.38 = (bf16[32,1024]{1,0:T(8,128)(2,1)S(1)}, bf16[32,1024]{1,0:T(8,128)(2,1)S(1)}, u32[]{:S(2)}, u32[]{:S(2)}) collective-permute-start(bf16[32,1024]{1,0:T(8,128)(2,1)S(1)} %copy-done.47), channel_id=1, source_target_pairs={{0,14},{2,12},{4,2},{6,0},{8,6},{10,4},{12,10},{14,8},{1,15},{3,13... | collective-permute-start | bytes 196616 | tf_op jit(solution)/shard_map/ppermute | solution.py:34
  515.5 14.9 %collective-permute-start.37 = (bf16[32,1024]{1,0:T(8,128)(2,1)S(1)}, bf16[32,1024]{1,0:T(8,128)(2,1)S(1)}, u32[]{:S(2)}, u32[]{:S(2)}) collective-permute-start(bf16[32,1024]{1,0:T(8,128)(2,1)S(1)} %copy-done.46), channel_id=1, source_target_pairs={{0,12},{2,14},{4,0},{6,2},{8,4},{10,6},{12,8},{14,10},{1,13},{3,15... | collective-permute-start | bytes 196616 | tf_op jit(solution)/shard_map/ppermute | solution.py:34
  515.6 15.5 %collective-permute-start.36 = (bf16[32,1024]{1,0:T(8,128)(2,1)S(1)}, bf16[32,1024]{1,0:T(8,128)(2,1)S(1)}, u32[]{:S(2)}, u32[]{:S(2)}) collective-permute-start(bf16[32,1024]{1,0:T(8,128)(2,1)S(1)} %copy-done.45), channel_id=1, source_target_pairs={{0,2},{2,0},{4,6},{6,4},{8,10},{10,8},{12,14},{14,12},{1,3},{3,1},... | collective-permute-start | bytes 196616 | tf_op jit(solution)/shard_map/ppermute | solution.py:34
  524.9 15.0 %collective-permute-start.14 = (bf16[32,1024]{1,0:T(8,128)(2,1)S(1)}, bf16[32,1024]{1,0:T(8,128)(2,1)S(1)}, u32[]{:S(2)}, u32[]{:S(2)}) collective-permute-start(bf16[32,1024]{1,0:T(8,128)(2,1)S(1)} %copy-done.43), channel_id=1, source_target_pairs={{0,8},{2,10},{4,12},{6,14},{8,0},{10,2},{12,4},{14,6},{1,9},{3,11}... | collective-permute-start | bytes 196616 | tf_op jit(solution)/shard_map/ppermute | solution.py:34
  526.5 13.4 %collective-permute-start.13 = (bf16[32,1024]{1,0:T(8,128)(2,1)S(1)}, bf16[32,1024]{1,0:T(8,128)(2,1)S(1)}, u32[]{:S(2)}, u32[]{:S(2)}) collective-permute-start(bf16[32,1024]{1,0:T(8,128)(2,1)S(1)} %copy-done.42), channel_id=1, source_target_pairs={{0,14},{2,12},{4,2},{6,0},{8,6},{10,4},{12,10},{14,8},{1,15},{3,13... | collective-permute-start | bytes 196616 | tf_op jit(solution)/shard_map/ppermute | solution.py:34
  530.3 9.6 %collective-permute-start.12 = (bf16[32,1024]{1,0:T(8,128)(2,1)S(1)}, bf16[32,1024]{1,0:T(8,128)(2,1)S(1)}, u32[]{:S(2)}, u32[]{:S(2)}) collective-permute-start(bf16[32,1024]{1,0:T(8,128)(2,1)S(1)} %copy-done.41), channel_id=1, source_target_pairs={{0,12},{2,14},{4,0},{6,2},{8,4},{10,6},{12,8},{14,10},{1,13},{3,15... | collective-permute-start | bytes 196616 | tf_op jit(solution)/shard_map/ppermute | solution.py:34
  530.4 9.6 %collective-permute-start.11 = (bf16[32,1024]{1,0:T(8,128)(2,1)S(1)}, bf16[32,1024]{1,0:T(8,128)(2,1)S(1)}, u32[]{:S(2)}, u32[]{:S(2)}) collective-permute-start(bf16[32,1024]{1,0:T(8,128)(2,1)S(1)} %copy-done.40), channel_id=1, source_target_pairs={{0,2},{2,0},{4,6},{6,4},{8,10},{10,8},{12,14},{14,12},{1,3},{3,1},... | collective-permute-start | bytes 196616 | tf_op jit(solution)/shard_map/ppermute | solution.py:34
  531.0 8.9 %collective-permute-start.17 = (bf16[32,1024]{1,0:T(8,128)(2,1)S(1)}, bf16[32,1024]{1,0:T(8,128)(2,1)S(1)}, u32[]{:S(2)}, u32[]{:S(2)}) collective-permute-start(bf16[32,1024]{1,0:T(8,128)(2,1)S(1)} %copy-done.44), channel_id=1, source_target_pairs={{0,6},{2,4},{4,10},{6,8},{8,14},{10,12},{12,2},{14,0},{1,7},{3,5},... | collective-permute-start | bytes 196616 | tf_op jit(solution)/shard_map/ppermute | solution.py:34
  (63 other events, 868.6 us)

commit v4 on v3

--- a/solution.py
+++ b/solution.py
@@ -509,20 +509,29 @@
 
     shape = grid_state.shape
     everything = list(range(chunks))
-    partial = inverse_fourier(
-        pieces_at(everything[:2], half), tables[:2], shape, half, half, dtype=jnp.float32
-    )
-    current = inverse_fourier(pieces_at(everything, 0), tables, shape, 0, half)
-    for cut in (1, 2):
-        start = half + (cut - 1) * fourth
+    partials = []
+    for start in (0, half):
+        partials.append(
+            inverse_fourier(
+                pieces_at(everything[:2], start),
+                tables[:2],
+                shape,
+                start,
+                half,
+                dtype=jnp.bfloat16,
+            )
+        )
+    current = None
+    for start, levels in cuts[chunks - 1]:
+        base = 0 if start < half else half
         current = inverse_fourier(
             pieces_at(everything[2:], start),
             tables[2:],
             shape,
             start,
-            fourth,
+            levels,
             current=current,
-            partial=(partial, half),
+            partial=(partials[0 if base == 0 else 1], base),
         )
     return current.reshape(out_shape)
 

time: 548 us -> 542 us (0.989)
    pallas_call x4 -> x5, Pallas kernels: 31.4 us -> 34.8 us  [inverse_fourier(): pl.pallas_call(functools.partial(inverse_kernel, len(pieces), len(tables)...]
  transfers between devices with their start and end apart: 61 -> 61, of which waited for: 12 -> 12; matrix products, arithmetic and copies ran while one was open for 7% -> 6% of each run, Pallas kernels for 25% -> 26%
where the time goes in v4:
time: 542 us; the launch traced here: 541 us
  waiting for transfers between devices  189 us (35%)
  Pallas kernels  159 us (29%)
  starting transfers between devices  153 us (28%)
  other arithmetic  29.7 us (5%)
  local copies, waits for them, and re-layouts  9.62 us (2%)
    ppermute x49, starting transfers between devices, shift_places(): return lax.ppermute(value, EXCHANGE_AXES, pairs)  132 us
    ppermute x49, waiting for transfers between devices, shift_places(): return lax.ppermute(value, EXCHANGE_AXES, pairs)  110 us
    all_to_all x4, waiting for transfers between devices, exchange(): lax.all_to_all(value, EXCHANGE_AXES, split_axis=0, concat_axis=0, tiled=T...  79.5 us
    pallas_call x4, Pallas kernels, columns_fused(): pl.pallas_call(functools.partial(column_kernel, sizes), out_shape=jax.Sha...  79.3 us
    pallas_call x4, Pallas kernels, fourier(): pl.pallas_call(functools.partial(fourier_kernel, sizes), out_shape=[jax.S...  44.9 us
    pallas_call x5, Pallas kernels, inverse_fourier(): pl.pallas_call(functools.partial(inverse_kernel, len(pieces), len(tables)...  34.8 us
    all_to_all x4, starting transfers between devices, exchange(): lax.all_to_all(value, EXCHANGE_AXES, split_axis=0, concat_axis=0, tiled=T...  19 us
    convert_element_type x4, other arithmetic, joined(): return both.astype(jnp.bfloat16)  13.7 us
  transfers between devices with their start and end apart: 61, of which 12 were waited for; matrix products, arithmetic and copies ran while one was open for 6% of the time, Pallas kernels for 26%

profile of v4, /device:TPU:0, one launch (start us, length us, event | category | flops | bytes accessed | tf_op | source)
XLA Modules:
  0.0 541.0 jit_solution(17260843861236952732)
XLA Ops:
  0.6 11.2 %shard_map.77 = (bf16[256,4096]{1,0:T(8,128)(2,1)}, bf16[256,1536]{1,0:T(8,128)(2,1)}) custom-call(s32[3]{0:T(128)} %pad_add_fusion.1.place_ref, bf16[64,64,1536]{2,1,0:T(8,128)(2,1)} %bitcast.121, s32[1,512]{1,0:T(1,128)} %bitcast.155, s32[1,256]{1,0:T(1,128)} %bitcast.159), custom_call_target="tpu_custom_call" | custom-call | flops 3221225472 | bytes 15466496 | tf_op jit(solution)/shard_map/pallas_call | solution.py:104
  11.8 7.3 %all-to-all-start.2 = ((bf16[8,2,16,4096]{3,2,1,0:T(8,128)(2,1)}), bf16[8,2,16,4096]{3,2,1,0:T(8,128)(2,1)S(1)}, u32[]{:S(2)}, u32[]{:S(2)}) async-start(bf16[8,2,16,4096]{3,2,1,0:T(8,128)(2,1)} %bitcast.142), calls=%async_computation.2 | async-start | bytes 4194304 | tf_op jit(solution)/shard_map/all_to_all | solution.py:407
  19.0 11.1 %shard_map.73 = (bf16[256,4096]{1,0:T(8,128)(2,1)}, bf16[256,1536]{1,0:T(8,128)(2,1)}) custom-call(s32[3]{0:T(128)} %pad_add_fusion.1.place_ref, bf16[64,64,1536]{2,1,0:T(8,128)(2,1)} %bitcast.122, s32[1,512]{1,0:T(1,128)} %bitcast.156, s32[1,256]{1,0:T(1,128)} %bitcast.160), custom_call_target="tpu_custom_call" | custom-call | flops 3221225472 | bytes 15466496 | tf_op jit(solution)/shard_map/pallas_call | solution.py:104
  30.1 37.2 %all-to-all-done.2.refs_0_ = bf16[8,2,16,4096]{3,2,1,0:T(8,128)(2,1)S(1)} async-done(((bf16[8,2,16,4096]{3,2,1,0:T(8,128)(2,1)}), bf16[8,2,16,4096]{3,2,1,0:T(8,128)(2,1)S(1)}, u32[]{:S(2)}, u32[]{:S(2)}) %all-to-all-start.2) | async-done | bytes 2097184 | tf_op jit(solution)/shard_map/all_to_all | solution.py:407
  68.6 3.8 all-to-all-start
  78.4 42.3 %all-to-all-done.refs_0_ = bf16[8,2,16,4096]{3,2,1,0:T(8,128)(2,1)S(1)} async-done(((bf16[8,2,16,4096]{3,2,1,0:T(8,128)(2,1)}), bf16[8,2,16,4096]{3,2,1,0:T(8,128)(2,1)S(1)}, u32[]{:S(2)}, u32[]{:S(2)}) %all-to-all-start) | async-done | bytes 2097184 | tf_op jit(solution)/shard_map/all_to_all | solution.py:407
  120.7 21.0 %shard_map.78 = bf16[8,2,16,4096]{3,2,1,0:T(8,128)(2,1)} custom-call(s32[64]{0:T(128)} %dynamic_slice.3.waves, s32[5]{0:T(128)} %pad_add_fusion.scalars, f32[128,1]{1,0:T(8,128)} %copy.12.eig_ref, bf16[128,128]{1,0:T(8,128)(2,1)} %select_bitcast_fusion.1.modes_in, bf16[128,128]{1,0:T(8,128)(2,1)} %broadcast_select_fusion.1.modes_out, ...), custom_call_target="tpu_custom_call" | custom-call | flops 1610612736 | bytes 6291456 | tf_op jit(solution)/shard_map/pallas_call | solution.py:326
  141.7 11.3 %shard_map.79 = (bf16[256,4096]{1,0:T(8,128)(2,1)}, bf16[256,1536]{1,0:T(8,128)(2,1)}) custom-call(s32[3]{0:T(128)} %pad_add_fusion.1.place_ref, bf16[64,64,1536]{2,1,0:T(8,128)(2,1)} %bitcast.123, s32[1,512]{1,0:T(1,128)} %bitcast.157, s32[1,256]{1,0:T(1,128)} %bitcast.161), custom_call_target="tpu_custom_call" | custom-call | flops 3221225472 | bytes 15466496 | tf_op jit(solution)/shard_map/pallas_call | solution.py:104
  153.5 11.3 %shard_map.75 = (bf16[256,4096]{1,0:T(8,128)(2,1)}, bf16[256,1536]{1,0:T(8,128)(2,1)}) custom-call(s32[3]{0:T(128)} %pad_add_fusion.1.place_ref, bf16[64,64,1536]{2,1,0:T(8,128)(2,1)} %bitcast.124, s32[1,512]{1,0:T(1,128)} %bitcast.158, s32[1,256]{1,0:T(1,128)} %bitcast.162), custom_call_target="tpu_custom_call" | custom-call | flops 3221225472 | bytes 15466496 | tf_op jit(solution)/shard_map/pallas_call | solution.py:104
  165.0 20.4 %shard_map.74 = bf16[8,2,16,4096]{3,2,1,0:T(8,128)(2,1)} custom-call(s32[64]{0:T(128)} %dynamic_slice.3.waves, s32[5]{0:T(128)} %pad_add_fusion.scalars, f32[128,1]{1,0:T(8,128)} %copy.12.eig_ref, bf16[128,128]{1,0:T(8,128)(2,1)} %select_bitcast_fusion.1.modes_in, bf16[128,128]{1,0:T(8,128)(2,1)} %broadcast_select_fusion.1.modes_out, ...), custom_call_target="tpu_custom_call" | custom-call | flops 1610612736 | bytes 6291456 | tf_op jit(solution)/shard_map/pallas_call | solution.py:326
  185.8 3.9 multiply_convert_fusion
  189.7 4.4 all-to-all-start.3
  194.1 3.7 add_convert_fusion
  197.9 4.6 collective-permute-start.27
  204.5 2.9 collective-permute-start.24
  207.4 28.6 %collective-permute-done.27 = bf16[32,4096]{1,0:T(8,128)(2,1)S(1)} collective-permute-done((bf16[32,4096]{1,0:T(8,128)(2,1)}, bf16[32,4096]{1,0:T(8,128)(2,1)S(1)}, u32[]{:S(2)}, u32[]{:S(2)}) %collective-permute-start.27) | collective-permute-done | bytes 262176 | tf_op jit(solution)/shard_map/ppermute | solution.py:34
  236.0 31.6 %collective-permute-start.23 = (bf16[32,4096]{1,0:T(8,128)(2,1)}, bf16[32,4096]{1,0:T(8,128)(2,1)}, u32[]{:S(2)}, u32[]{:S(2)}) collective-permute-start(bf16[32,4096]{1,0:T(8,128)(2,1)} %get-tuple-element.60), channel_id=1, source_target_pairs={{0,6},{2,4},{4,10},{6,8},{8,14},{10,12},{12,2},{14,0},{1,7},{3,5},... | collective-permute-start | bytes 786440 | tf_op jit(solution)/shard_map/ppermute | solution.py:34
  267.6 10.3 %collective-permute-start.22 = (bf16[32,4096]{1,0:T(8,128)(2,1)}, bf16[32,4096]{1,0:T(8,128)(2,1)}, u32[]{:S(2)}, u32[]{:S(2)}) collective-permute-start(bf16[32,4096]{1,0:T(8,128)(2,1)} %get-tuple-element.61), channel_id=1, source_target_pairs={{0,4},{2,6},{4,8},{6,10},{8,12},{10,14},{12,0},{14,2},{1,5},{3,7},... | collective-permute-start | bytes 786440 | tf_op jit(solution)/shard_map/ppermute | solution.py:34
  277.9 3.7 add_convert_fusion.8
  281.7 2.2 collective-permute-done.25
  284.4 3.3 collective-permute-done.24
  287.8 2.0 collective-permute-start.8
  289.8 2.4 collective-permute-start.7
  294.1 3.9 collective-permute-done.9
  298.1 5.8 %collective-permute-done.8 = bf16[32,4096]{1,0:T(8,128)(2,1)S(1)} collective-permute-done((bf16[32,4096]{1,0:T(8,128)(2,1)}, bf16[32,4096]{1,0:T(8,128)(2,1)S(1)}, u32[]{:S(2)}, u32[]{:S(2)}) %collective-permute-start.8) | collective-permute-done | bytes 262176 | tf_op jit(solution)/shard_map/ppermute | solution.py:34
  303.9 25.6 %collective-permute-done.7 = bf16[32,4096]{1,0:T(8,128)(2,1)} collective-permute-done((bf16[32,4096]{1,0:T(8,128)(2,1)}, bf16[32,4096]{1,0:T(8,128)(2,1)}, u32[]{:S(2)}, u32[]{:S(2)}) %collective-permute-start.7) | collective-permute-done | bytes 262176 | tf_op jit(solution)/shard_map/ppermute | solution.py:34
  330.7 18.9 %shard_map.80 = bf16[8,2,16,4096]{3,2,1,0:T(8,128)(2,1)} custom-call(s32[64]{0:T(128)} %dynamic_slice.3.waves, s32[5]{0:T(128)} %pad_add_fusion.2.scalars, f32[128,1]{1,0:T(8,128)} %copy.12.eig_ref, bf16[128,128]{1,0:T(8,128)(2,1)} %select_bitcast_fusion.modes_in, bf16[128,128]{1,0:T(8,128)(2,1)} %broadcast_select_fusion.modes_out, ...), custom_call_target="tpu_custom_call" | custom-call | flops 1610612736 | bytes 6291456 | tf_op jit(solution)/shard_map/pallas_call | solution.py:326
  350.6 19.0 %shard_map.76 = bf16[8,2,16,4096]{3,2,1,0:T(8,128)(2,1)} custom-call(s32[64]{0:T(128)} %dynamic_slice.3.waves, s32[5]{0:T(128)} %pad_add_fusion.2.scalars, f32[128,1]{1,0:T(8,128)} %copy.12.eig_ref, bf16[128,128]{1,0:T(8,128)(2,1)} %select_bitcast_fusion.modes_in, bf16[128,128]{1,0:T(8,128)(2,1)} %broadcast_select_fusion.modes_out, ...), custom_call_target="tpu_custom_call" | custom-call | flops 1610612736 | bytes 6291456 | tf_op jit(solution)/shard_map/pallas_call | solution.py:326
  370.2 2.3 multiply_convert_fusion.1
  372.5 3.6 all-to-all-start.1
  376.1 2.7 fusion.6
  378.8 1.9 collective-permute-start.34
  380.7 1.9 fusion.30
  382.6 1.5 collective-permute-start.16
  384.0 2.4 collective-permute-start.15
  386.5 2.0 fusion.39
  388.5 1.4 collective-permute-start.42
  390.5 29.3 %collective-permute-done.16.refs_7_ = bf16[32,1024]{1,0:T(8,128)(2,1)S(1)} collective-permute-done((bf16[32,1024]{1,0:T(8,128)(2,1)S(1)}, bf16[32,1024]{1,0:T(8,128)(2,1)S(1)}, u32[]{:S(2)}, u32[]{:S(2)}) %collective-permute-start.16) | collective-permute-done | bytes 65568 | tf_op jit(solution)/shard_map/ppermute | solution.py:34
  419.7 12.2 %collective-permute-start.33 = (bf16[32,2048]{1,0:T(8,128)(2,1)S(1)}, bf16[32,2048]{1,0:T(8,128)(2,1)S(1)}, u32[]{:S(2)}, u32[]{:S(2)}) collective-permute-start(bf16[32,2048]{1,0:T(8,128)(2,1)S(1)} %get-tuple-element.50), channel_id=1, source_target_pairs={{0,10},{2,8},{4,14},{6,12},{8,2},{10,0},{12,6},{14,4},{1,11},{3,9}... | collective-permute-start | bytes 393224 | tf_op jit(solution)/shard_map/ppermute | solution.py:34
  431.9 10.1 %collective-permute-done.15.refs_6_ = bf16[32,1024]{1,0:T(8,128)(2,1)S(1)} collective-permute-done((bf16[32,1024]{1,0:T(8,128)(2,1)S(1)}, bf16[32,1024]{1,0:T(8,128)(2,1)S(1)}, u32[]{:S(2)}, u32[]{:S(2)}) %collective-permute-start.15) | collective-permute-done | bytes 65568 | tf_op jit(solution)/shard_map/ppermute | solution.py:34
  442.1 4.3 collective-permute-start.30
  446.4 1.5 collective-permute-start.29
  447.9 2.4 fusion.23
  450.7 5.0 collective-permute-start.54
  455.7 8.0 %collective-permute-start.35 = (bf16[32,2048]{1,0:T(8,128)(2,1)S(1)}, bf16[32,2048]{1,0:T(8,128)(2,1)S(1)}, u32[]{:S(2)}, u32[]{:S(2)}) collective-permute-start(bf16[32,2048]{1,0:T(8,128)(2,1)S(1)} %get-tuple-element.31), channel_id=1, source_target_pairs={{0,6},{2,4},{4,10},{6,8},{8,14},{10,12},{12,2},{14,0},{1,7},{3,5},... | collective-permute-start | bytes 393224 | tf_op jit(solution)/shard_map/ppermute | solution.py:34
  463.7 2.3 fusion.15
  466.1 2.4 collective-permute-start.52
  468.5 3.4 collective-permute-start.50
  473.5 3.3 collective-permute-start.48
  476.8 7.5 %shard_map.81.refs_11_ = bf16[32,64,1536]{2,1,0:T(8,128)(2,1)} custom-call(bf16[256,4096]{1,0:T(8,128)(2,1)} %bitcast.32.refs_0_, bf16[32,2048]{1,0:T(8,128)(2,1)} %get-tuple-element.55.refs_1_, bf16[32,2048]{1,0:T(8,128)(2,1)} %copy-done.53, bf16[32,2048]{1,0:T(8,128)(2,1)} %copy-done.51, bf16[32,2048]{1,0:T(8,128)(2,1)} %copy-done.49, ...), custom_call_target="tpu_custom_call" | custom-call | flops 3221225472 | bytes 8388608 | tf_op jit(solution)/shard_map/pallas_call | solution.py:172
  484.4 3.5 collective-permute-start.47
  488.3 2.9 collective-permute-start.45
  491.1 2.0 collective-permute-start.44
  493.7 7.5 %shard_map.82.refs_11_ = bf16[32,64,1536]{2,1,0:T(8,128)(2,1)} custom-call(bf16[256,4096]{1,0:T(8,128)(2,1)} %bitcast.32.refs_0_, bf16[32,2048]{1,0:T(8,128)(2,1)} %get-tuple-element.30.refs_1_, bf16[32,2048]{1,0:T(8,128)(2,1)} %copy-done.56, bf16[32,2048]{1,0:T(8,128)(2,1)} %copy-done.55, bf16[32,2048]{1,0:T(8,128)(2,1)} %copy-done.54, ...), custom_call_target="tpu_custom_call" | custom-call | flops 3221225472 | bytes 8388608 | tf_op jit(solution)/shard_map/pallas_call | solution.py:172
  502.2 2.9 collective-permute-start.39
  505.1 3.9 collective-permute-start.38
  510.0 1.5 collective-permute-start.36
  512.8 9.1 %shard_map.83.refs_12_ = bf16[64,64,1536]{2,1,0:T(8,128)(2,1)} custom-call(bf16[256,4096]{1,0:T(8,128)(2,1)} %bitcast.129, bf16[32,2048]{1,0:T(8,128)(2,1)} %get-tuple-element.39.refs_1_, bf16[32,2048]{1,0:T(8,128)(2,1)} %copy-done.25, bf16[32,2048]{1,0:T(8,128)(2,1)} %copy-done.24, bf16[32,2048]{1,0:T(8,128)(2,1)} %copy-done.23, ...), custom_call_target="tpu_custom_call" | custom-call | flops 3221225472 | bytes 8388608 | tf_op jit(solution)/shard_map/pallas_call | solution.py:172
  521.9 1.8 collective-permute-start.14
  523.7 2.1 collective-permute-start.13
  526.3 1.5 collective-permute-start.11
  527.8 1.5 collective-permute-start.17
  529.3 5.4 shard_map.84.refs_12_
  535.5 5.4 shard_map.85
  (225 shorter events, 24.5 us)
Async XLA Ops:
  0.0 75.0 %copy-start = (bf16[128,128]{1,0:T(8,128)(2,1)S(1)}, bf16[128,128]{1,0:T(8,128)(2,1)}, u32[]{:S(2)}) copy-start(bf16[128,128]{1,0:T(8,128)(2,1)} %param.17) | copy-start | bytes 98308
  11.8 55.5 %all-to-all-start.2 = ((bf16[8,2,16,4096]{3,2,1,0:T(8,128)(2,1)}), bf16[8,2,16,4096]{3,2,1,0:T(8,128)(2,1)S(1)}, u32[]{:S(2)}, u32[]{:S(2)}) async-start(bf16[8,2,16,4096]{3,2,1,0:T(8,128)(2,1)} %bitcast.142), calls=%async_computation.2 | async-start | bytes 4194304 | tf_op jit(solution)/shard_map/all_to_all | solution.py:407
  68.6 52.1 %all-to-all-start = ((bf16[8,2,16,4096]{3,2,1,0:T(8,128)(2,1)}), bf16[8,2,16,4096]{3,2,1,0:T(8,128)(2,1)S(1)}, u32[]{:S(2)}, u32[]{:S(2)}) async-start(bf16[8,2,16,4096]{3,2,1,0:T(8,128)(2,1)} %bitcast.141), calls=%async_computation | async-start | bytes 4194304 | tf_op jit(solution)/shard_map/all_to_all | solution.py:407
  72.4 48.3 %collective-permute-start.18 = (bf16[8,2,16,4096]{3,2,1,0:T(8,128)(2,1)}, bf16[8,2,16,4096]{3,2,1,0:T(8,128)(2,1)}, u32[]{:S(2)}, u32[]{:S(2)}) collective-permute-start(bf16[8,2,16,4096]{3,2,1,0:T(8,128)(2,1)} %copy-done.8), channel_id=1, source_target_pairs={{0,1},{1,0},{2,3},{3,2},{4,5},{5,4},{6,7},{7,6},{8,9},{9,8},{10,11... | collective-permute-start | bytes 6291464 | tf_op jit(solution)/shard_map/ppermute | solution.py:22
  120.7 44.3 %collective-permute-start = (bf16[8,2,16,4096]{3,2,1,0:T(8,128)(2,1)S(1)}, bf16[8,2,16,4096]{3,2,1,0:T(8,128)(2,1)}, u32[]{:S(2)}, u32[]{:S(2)}) collective-permute-start(bf16[8,2,16,4096]{3,2,1,0:T(8,128)(2,1)S(1)} %all-to-all-done.refs_0_), channel_id=1, source_target_pairs={{0,1},{1,0},{2,3},{3,2},{4,5},{5,4},{6,7},{7,6},{8,9},{9,8},{10,11... | collective-permute-start | bytes 6291464 | tf_op jit(solution)/shard_map/ppermute | solution.py:22
  141.7 44.1 %collective-permute-start.19 = (bf16[8,32,4096]{2,1,0:T(8,128)(2,1)}, bf16[8,32,4096]{2,1,0:T(8,128)(2,1)}, u32[]{:S(2)}, u32[]{:S(2)}) collective-permute-start(bf16[8,32,4096]{2,1,0:T(8,128)(2,1)} %bitcast.140), channel_id=1, source_target_pairs={{0,1},{1,0},{2,3},{3,2},{4,5},{5,4},{6,7},{7,6},{8,9},{9,8},{10,11... | collective-permute-start | bytes 6291464 | tf_op jit(solution)/shard_map/ppermute | solution.py:22
  153.0 41.1 %collective-permute-start.20 = (bf16[256,4096]{1,0:T(8,128)(2,1)}, bf16[256,4096]{1,0:T(8,128)(2,1)}, u32[]{:S(2)}, u32[]{:S(2)}) collective-permute-start(bf16[256,4096]{1,0:T(8,128)(2,1)} %get-tuple-element.20), channel_id=1, source_target_pairs={{0,1},{1,0},{2,3},{3,2},{4,5},{5,4},{6,7},{7,6},{8,9},{9,8},{10,11... | collective-permute-start | bytes 6291464 | tf_op jit(solution)/shard_map/ppermute | solution.py:22
  164.8 39.7 %collective-permute-start.2 = (bf16[256,4096]{1,0:T(8,128)(2,1)}, bf16[256,4096]{1,0:T(8,128)(2,1)}, u32[]{:S(2)}, u32[]{:S(2)}) collective-permute-start(bf16[256,4096]{1,0:T(8,128)(2,1)} %get-tuple-element.16), channel_id=1, source_target_pairs={{0,1},{1,0},{2,3},{3,2},{4,5},{5,4},{6,7},{7,6},{8,9},{9,8},{10,11... | collective-permute-start | bytes 6291464 | tf_op jit(solution)/shard_map/ppermute | solution.py:22
  185.3 184.8 %collective-permute-start.1 = (bf16[8,32,4096]{2,1,0:T(8,128)(2,1)}, bf16[8,32,4096]{2,1,0:T(8,128)(2,1)S(1)}, u32[]{:S(2)}, u32[]{:S(2)}) collective-permute-start(bf16[8,32,4096]{2,1,0:T(8,128)(2,1)} %bitcast.139), channel_id=1, source_target_pairs={{0,1},{1,0},{2,3},{3,2},{4,5},{5,4},{6,7},{7,6},{8,9},{9,8},{10,11... | collective-permute-start | bytes 6291464 | tf_op jit(solution)/shard_map/ppermute | solution.py:22
  189.7 182.8 %all-to-all-start.3 = ((bf16[8,32,4096]{2,1,0:T(8,128)(2,1)}), bf16[8,32,4096]{2,1,0:T(8,128)(2,1)}, u32[]{:S(2)}, u32[]{:S(2)}) async-start(bf16[8,32,4096]{2,1,0:T(8,128)(2,1)} %multiply_convert_fusion), calls=%async_computation.3 | async-start | bytes 4194304 | tf_op jit(solution)/shard_map/all_to_all | solution.py:407
  197.9 38.2 %collective-permute-start.27 = (bf16[32,4096]{1,0:T(8,128)(2,1)}, bf16[32,4096]{1,0:T(8,128)(2,1)S(1)}, u32[]{:S(2)}, u32[]{:S(2)}) collective-permute-start(bf16[32,4096]{1,0:T(8,128)(2,1)} %get-tuple-element.56), channel_id=1, source_target_pairs={{0,14},{2,12},{4,2},{6,0},{8,6},{10,4},{12,10},{14,8},{1,15},{3,13... | collective-permute-start | bytes 786440 | tf_op jit(solution)/shard_map/ppermute | solution.py:34
  202.5 65.1 %collective-permute-start.26 = (bf16[32,4096]{1,0:T(8,128)(2,1)S(1)}, bf16[32,4096]{1,0:T(8,128)(2,1)S(1)}, u32[]{:S(2)}, u32[]{:S(2)}) collective-permute-start(bf16[32,4096]{1,0:T(8,128)(2,1)S(1)} %get-tuple-element.57), channel_id=1, source_target_pairs={{0,12},{2,14},{4,0},{6,2},{8,4},{10,6},{12,8},{14,10},{1,13},{3,15... | collective-permute-start | bytes 786440 | tf_op jit(solution)/shard_map/ppermute | solution.py:34
  204.5 79.4 %collective-permute-start.25 = (bf16[32,4096]{1,0:T(8,128)(2,1)}, bf16[32,4096]{1,0:T(8,128)(2,1)S(1)}, u32[]{:S(2)}, u32[]{:S(2)}) collective-permute-start(bf16[32,4096]{1,0:T(8,128)(2,1)} %get-tuple-element.58), channel_id=1, source_target_pairs={{0,10},{2,8},{4,14},{6,12},{8,2},{10,0},{12,6},{14,4},{1,11},{3,9}... | collective-permute-start | bytes 786440 | tf_op jit(solution)/shard_map/ppermute | solution.py:34
  204.5 83.3 %collective-permute-start.24 = (bf16[32,4096]{1,0:T(8,128)(2,1)}, bf16[32,4096]{1,0:T(8,128)(2,1)S(1)}, u32[]{:S(2)}, u32[]{:S(2)}) collective-permute-start(bf16[32,4096]{1,0:T(8,128)(2,1)} %get-tuple-element.59), channel_id=1, source_target_pairs={{0,8},{2,10},{4,12},{6,14},{8,0},{10,2},{12,4},{14,6},{1,9},{3,11}... | collective-permute-start | bytes 786440 | tf_op jit(solution)/shard_map/ppermute | solution.py:34
  236.0 51.7 %collective-permute-start.23 = (bf16[32,4096]{1,0:T(8,128)(2,1)}, bf16[32,4096]{1,0:T(8,128)(2,1)}, u32[]{:S(2)}, u32[]{:S(2)}) collective-permute-start(bf16[32,4096]{1,0:T(8,128)(2,1)} %get-tuple-element.60), channel_id=1, source_target_pairs={{0,6},{2,4},{4,10},{6,8},{8,14},{10,12},{12,2},{14,0},{1,7},{3,5},... | collective-permute-start | bytes 786440 | tf_op jit(solution)/shard_map/ppermute | solution.py:34
  267.6 22.2 %collective-permute-start.22 = (bf16[32,4096]{1,0:T(8,128)(2,1)}, bf16[32,4096]{1,0:T(8,128)(2,1)}, u32[]{:S(2)}, u32[]{:S(2)}) collective-permute-start(bf16[32,4096]{1,0:T(8,128)(2,1)} %get-tuple-element.61), channel_id=1, source_target_pairs={{0,4},{2,6},{4,8},{6,10},{8,12},{10,14},{12,0},{14,2},{1,5},{3,7},... | collective-permute-start | bytes 786440 | tf_op jit(solution)/shard_map/ppermute | solution.py:34
  283.9 9.7 %collective-permute-start.21 = (bf16[32,4096]{1,0:T(8,128)(2,1)}, bf16[32,4096]{1,0:T(8,128)(2,1)}, u32[]{:S(2)}, u32[]{:S(2)}) collective-permute-start(bf16[32,4096]{1,0:T(8,128)(2,1)} %get-tuple-element.62), channel_id=1, source_target_pairs={{0,2},{2,0},{4,6},{6,4},{8,10},{10,8},{12,14},{14,12},{1,3},{3,1},... | collective-permute-start | bytes 786440 | tf_op jit(solution)/shard_map/ppermute | solution.py:34
  287.8 10.3 %collective-permute-start.9 = (bf16[32,4096]{1,0:T(8,128)(2,1)}, bf16[32,4096]{1,0:T(8,128)(2,1)S(1)}, u32[]{:S(2)}, u32[]{:S(2)}) collective-permute-start(bf16[32,4096]{1,0:T(8,128)(2,1)} %get-tuple-element.71), channel_id=1, source_target_pairs={{0,14},{2,12},{4,2},{6,0},{8,6},{10,4},{12,10},{14,8},{1,15},{3,13... | collective-permute-start | bytes 786440 | tf_op jit(solution)/shard_map/ppermute | solution.py:34
  287.8 16.1 %collective-permute-start.8 = (bf16[32,4096]{1,0:T(8,128)(2,1)}, bf16[32,4096]{1,0:T(8,128)(2,1)S(1)}, u32[]{:S(2)}, u32[]{:S(2)}) collective-permute-start(bf16[32,4096]{1,0:T(8,128)(2,1)} %get-tuple-element.72), channel_id=1, source_target_pairs={{0,12},{2,14},{4,0},{6,2},{8,4},{10,6},{12,8},{14,10},{1,13},{3,15... | collective-permute-start | bytes 786440 | tf_op jit(solution)/shard_map/ppermute | solution.py:34
  289.8 39.7 %collective-permute-start.7 = (bf16[32,4096]{1,0:T(8,128)(2,1)}, bf16[32,4096]{1,0:T(8,128)(2,1)}, u32[]{:S(2)}, u32[]{:S(2)}) collective-permute-start(bf16[32,4096]{1,0:T(8,128)(2,1)} %get-tuple-element.73), channel_id=1, source_target_pairs={{0,10},{2,8},{4,14},{6,12},{8,2},{10,0},{12,6},{14,4},{1,11},{3,9}... | collective-permute-start | bytes 786440 | tf_op jit(solution)/shard_map/ppermute | solution.py:34
  293.6 56.1 %collective-permute-start.6 = (bf16[32,4096]{1,0:T(8,128)(2,1)}, bf16[32,4096]{1,0:T(8,128)(2,1)S(1)}, u32[]{:S(2)}, u32[]{:S(2)}) collective-permute-start(bf16[32,4096]{1,0:T(8,128)(2,1)} %get-tuple-element.74), channel_id=1, source_target_pairs={{0,8},{2,10},{4,12},{6,14},{8,0},{10,2},{12,4},{14,6},{1,9},{3,11}... | collective-permute-start | bytes 786440 | tf_op jit(solution)/shard_map/ppermute | solution.py:34
  298.1 51.6 %copy-start.13 = (bf16[32,4096]{1,0:T(8,128)(2,1)}, bf16[32,4096]{1,0:T(8,128)(2,1)S(1)}, u32[]{:S(2)}) copy-start(bf16[32,4096]{1,0:T(8,128)(2,1)S(1)} %collective-permute-done.9) | copy-start | bytes 786436
  298.1 51.7 %collective-permute-start.5 = (bf16[32,4096]{1,0:T(8,128)(2,1)}, bf16[32,4096]{1,0:T(8,128)(2,1)S(1)}, u32[]{:S(2)}, u32[]{:S(2)}) collective-permute-start(bf16[32,4096]{1,0:T(8,128)(2,1)} %get-tuple-element.75), channel_id=1, source_target_pairs={{0,6},{2,4},{4,10},{6,8},{8,14},{10,12},{12,2},{14,0},{1,7},{3,5},... | collective-permute-start | bytes 786440 | tf_op jit(solution)/shard_map/ppermute | solution.py:34
  303.9 45.9 %collective-permute-start.4 = (bf16[32,4096]{1,0:T(8,128)(2,1)}, bf16[32,4096]{1,0:T(8,128)(2,1)S(1)}, u32[]{:S(2)}, u32[]{:S(2)}) collective-permute-start(bf16[32,4096]{1,0:T(8,128)(2,1)} %get-tuple-element.76), channel_id=1, source_target_pairs={{0,4},{2,6},{4,8},{6,10},{8,12},{10,14},{12,0},{14,2},{1,5},{3,7},... | collective-permute-start | bytes 786440 | tf_op jit(solution)/shard_map/ppermute | solution.py:34
  329.5 20.3 %collective-permute-start.3 = (bf16[32,4096]{1,0:T(8,128)(2,1)S(1)}, bf16[32,4096]{1,0:T(8,128)(2,1)S(1)}, u32[]{:S(2)}, u32[]{:S(2)}) collective-permute-start(bf16[32,4096]{1,0:T(8,128)(2,1)S(1)} %get-tuple-element.77), channel_id=1, source_target_pairs={{0,2},{2,0},{4,6},{6,4},{8,10},{10,8},{12,14},{14,12},{1,3},{3,1},... | collective-permute-start | bytes 786440 | tf_op jit(solution)/shard_map/ppermute | solution.py:34
  349.7 26.5 %collective-permute-start.28 = (bf16[8,32,4096]{2,1,0:T(8,128)(2,1)}, bf16[8,32,4096]{2,1,0:T(8,128)(2,1)}, u32[]{:S(2)}, u32[]{:S(2)}) collective-permute-start(bf16[8,32,4096]{2,1,0:T(8,128)(2,1)} %bitcast.136), channel_id=1, source_target_pairs={{0,1},{1,0},{2,3},{3,2},{4,5},{5,4},{6,7},{7,6},{8,9},{9,8},{10,11... | collective-permute-start | bytes 6291464 | tf_op jit(solution)/shard_map/ppermute | solution.py:22
  369.7 11.0 %collective-permute-start.10 = (bf16[8,32,4096]{2,1,0:T(8,128)(2,1)}, bf16[8,32,4096]{2,1,0:T(8,128)(2,1)}, u32[]{:S(2)}, u32[]{:S(2)}) collective-permute-start(bf16[8,32,4096]{2,1,0:T(8,128)(2,1)} %bitcast.132), channel_id=1, source_target_pairs={{0,1},{1,0},{2,3},{3,2},{4,5},{5,4},{6,7},{7,6},{8,9},{9,8},{10,11... | collective-permute-start | bytes 6291464 | tf_op jit(solution)/shard_map/ppermute | solution.py:22
  372.5 139.0 %all-to-all-start.1 = ((bf16[8,32,4096]{2,1,0:T(8,128)(2,1)}), bf16[8,32,4096]{2,1,0:T(8,128)(2,1)S(1)}, u32[]{:S(2)}, u32[]{:S(2)}) async-start(bf16[8,32,4096]{2,1,0:T(8,128)(2,1)} %multiply_convert_fusion.1), calls=%async_computation.1 | async-start | bytes 4194304 | tf_op jit(solution)/shard_map/all_to_all | solution.py:407
  378.8 69.1 %copy-start.4 = (bf16[8,2,16,4096]{3,2,1,0:T(8,128)(2,1)S(1)}, bf16[8,2,16,4096]{3,2,1,0:T(8,128)(2,1)}, u32[]{:S(2)}) copy-start(bf16[8,2,16,4096]{3,2,1,0:T(8,128)(2,1)} %shard_map.80) | copy-start | bytes 6291460
  378.8 67.6 %collective-permute-start.34 = (bf16[32,2048]{1,0:T(8,128)(2,1)S(1)}, bf16[32,2048]{1,0:T(8,128)(2,1)S(1)}, u32[]{:S(2)}, u32[]{:S(2)}) collective-permute-start(bf16[32,2048]{1,0:T(8,128)(2,1)S(1)} %get-tuple-element.49), channel_id=1, source_target_pairs={{0,4},{2,6},{4,8},{6,10},{8,12},{10,14},{12,0},{14,2},{1,5},{3,7},... | collective-permute-start | bytes 393224 | tf_op jit(solution)/shard_map/ppermute | solution.py:34
  382.6 37.2 %collective-permute-start.16 = (bf16[32,1024]{1,0:T(8,128)(2,1)S(1)}, bf16[32,1024]{1,0:T(8,128)(2,1)S(1)}, u32[]{:S(2)}, u32[]{:S(2)}) collective-permute-start(bf16[32,1024]{1,0:T(8,128)(2,1)S(1)} %get-tuple-element.64), channel_id=1, source_target_pairs={{0,4},{2,6},{4,8},{6,10},{8,12},{10,14},{12,0},{14,2},{1,5},{3,7},... | collective-permute-start | bytes 196616 | tf_op jit(solution)/shard_map/ppermute | solution.py:34
  384.0 58.0 %collective-permute-start.15 = (bf16[32,1024]{1,0:T(8,128)(2,1)S(1)}, bf16[32,1024]{1,0:T(8,128)(2,1)S(1)}, u32[]{:S(2)}, u32[]{:S(2)}) collective-permute-start(bf16[32,1024]{1,0:T(8,128)(2,1)S(1)} %get-tuple-element.65), channel_id=1, source_target_pairs={{0,10},{2,8},{4,14},{6,12},{8,2},{10,0},{12,6},{14,4},{1,11},{3,9}... | collective-permute-start | bytes 196616 | tf_op jit(solution)/shard_map/ppermute | solution.py:34
  388.5 53.5 %collective-permute-start.42 = (bf16[32,1024]{1,0:T(8,128)(2,1)S(1)}, bf16[32,1024]{1,0:T(8,128)(2,1)S(1)}, u32[]{:S(2)}, u32[]{:S(2)}) collective-permute-start(bf16[32,1024]{1,0:T(8,128)(2,1)S(1)} %get-tuple-element.40), channel_id=1, source_target_pairs={{0,6},{2,4},{4,10},{6,8},{8,14},{10,12},{12,2},{14,0},{1,7},{3,5},... | collective-permute-start | bytes 196616 | tf_op jit(solution)/shard_map/ppermute | solution.py:34
  389.9 52.2 %collective-permute-start.41 = (bf16[32,1024]{1,0:T(8,128)(2,1)S(1)}, bf16[32,1024]{1,0:T(8,128)(2,1)S(1)}, u32[]{:S(2)}, u32[]{:S(2)}) collective-permute-start(bf16[32,1024]{1,0:T(8,128)(2,1)S(1)} %get-tuple-element.41), channel_id=1, source_target_pairs={{0,4},{2,6},{4,8},{6,10},{8,12},{10,14},{12,0},{14,2},{1,5},{3,7},... | collective-permute-start | bytes 196616 | tf_op jit(solution)/shard_map/ppermute | solution.py:34
  419.7 30.6 %collective-permute-start.33 = (bf16[32,2048]{1,0:T(8,128)(2,1)S(1)}, bf16[32,2048]{1,0:T(8,128)(2,1)S(1)}, u32[]{:S(2)}, u32[]{:S(2)}) collective-permute-start(bf16[32,2048]{1,0:T(8,128)(2,1)S(1)} %get-tuple-element.50), channel_id=1, source_target_pairs={{0,10},{2,8},{4,14},{6,12},{8,2},{10,0},{12,6},{14,4},{1,11},{3,9}... | collective-permute-start | bytes 393224 | tf_op jit(solution)/shard_map/ppermute | solution.py:34
  442.0 8.4 %collective-permute-start.32 = (bf16[32,2048]{1,0:T(8,128)(2,1)S(1)}, bf16[32,2048]{1,0:T(8,128)(2,1)S(1)}, u32[]{:S(2)}, u32[]{:S(2)}) collective-permute-start(bf16[32,2048]{1,0:T(8,128)(2,1)S(1)} %get-tuple-element.51), channel_id=1, source_target_pairs={{0,8},{2,10},{4,12},{6,14},{8,0},{10,2},{12,4},{14,6},{1,9},{3,11}... | collective-permute-start | bytes 393224 | tf_op jit(solution)/shard_map/ppermute | solution.py:34
  442.0 8.7 %collective-permute-start.31 = (bf16[32,2048]{1,0:T(8,128)(2,1)S(1)}, bf16[32,2048]{1,0:T(8,128)(2,1)S(1)}, u32[]{:S(2)}, u32[]{:S(2)}) collective-permute-start(bf16[32,2048]{1,0:T(8,128)(2,1)S(1)} %get-tuple-element.52), channel_id=1, source_target_pairs={{0,14},{2,12},{4,2},{6,0},{8,6},{10,4},{12,10},{14,8},{1,15},{3,13... | collective-permute-start | bytes 393224 | tf_op jit(solution)/shard_map/ppermute | solution.py:34
  442.1 13.6 %collective-permute-start.30 = (bf16[32,2048]{1,0:T(8,128)(2,1)S(1)}, bf16[32,2048]{1,0:T(8,128)(2,1)S(1)}, u32[]{:S(2)}, u32[]{:S(2)}) collective-permute-start(bf16[32,2048]{1,0:T(8,128)(2,1)S(1)} %get-tuple-element.53), channel_id=1, source_target_pairs={{0,12},{2,14},{4,0},{6,2},{8,4},{10,6},{12,8},{14,10},{1,13},{3,15... | collective-permute-start | bytes 393224 | tf_op jit(solution)/shard_map/ppermute | solution.py:34
  446.4 9.3 %collective-permute-start.29 = (bf16[32,2048]{1,0:T(8,128)(2,1)S(1)}, bf16[32,2048]{1,0:T(8,128)(2,1)S(1)}, u32[]{:S(2)}, u32[]{:S(2)}) collective-permute-start(bf16[32,2048]{1,0:T(8,128)(2,1)S(1)} %get-tuple-element.54), channel_id=1, source_target_pairs={{0,2},{2,0},{4,6},{6,4},{8,10},{10,8},{12,14},{14,12},{1,3},{3,1},... | collective-permute-start | bytes 393224 | tf_op jit(solution)/shard_map/ppermute | solution.py:34
  450.3 15.7 %collective-permute-start.56 = (bf16[32,2048]{1,0:T(8,128)(2,1)S(1)}, bf16[32,2048]{1,0:T(8,128)(2,1)S(1)}, u32[]{:S(2)}, u32[]{:S(2)}) collective-permute-start(bf16[32,2048]{1,0:T(8,128)(2,1)S(1)} %get-tuple-element.23), channel_id=1, source_target_pairs={{0,6},{2,4},{4,10},{6,8},{8,14},{10,12},{12,2},{14,0},{1,7},{3,5},... | collective-permute-start | bytes 393224 | tf_op jit(solution)/shard_map/ppermute | solution.py:34
  450.4 18.0 %collective-permute-start.55 = (bf16[32,2048]{1,0:T(8,128)(2,1)S(1)}, bf16[32,2048]{1,0:T(8,128)(2,1)S(1)}, u32[]{:S(2)}, u32[]{:S(2)}) collective-permute-start(bf16[32,2048]{1,0:T(8,128)(2,1)S(1)} %get-tuple-element.24), channel_id=1, source_target_pairs={{0,4},{2,6},{4,8},{6,10},{8,12},{10,14},{12,0},{14,2},{1,5},{3,7},... | collective-permute-start | bytes 393224 | tf_op jit(solution)/shard_map/ppermute | solution.py:34
  450.7 17.7 %collective-permute-start.54 = (bf16[32,2048]{1,0:T(8,128)(2,1)S(1)}, bf16[32,2048]{1,0:T(8,128)(2,1)S(1)}, u32[]{:S(2)}, u32[]{:S(2)}) collective-permute-start(bf16[32,2048]{1,0:T(8,128)(2,1)S(1)} %get-tuple-element.25), channel_id=1, source_target_pairs={{0,10},{2,8},{4,14},{6,12},{8,2},{10,0},{12,6},{14,4},{1,11},{3,9}... | collective-permute-start | bytes 393224 | tf_op jit(solution)/shard_map/ppermute | solution.py:34
  455.7 16.5 %collective-permute-start.53 = (bf16[32,2048]{1,0:T(8,128)(2,1)S(1)}, bf16[32,2048]{1,0:T(8,128)(2,1)S(1)}, u32[]{:S(2)}, u32[]{:S(2)}) collective-permute-start(bf16[32,2048]{1,0:T(8,128)(2,1)S(1)} %get-tuple-element.26), channel_id=1, source_target_pairs={{0,8},{2,10},{4,12},{6,14},{8,0},{10,2},{12,4},{14,6},{1,9},{3,11}... | collective-permute-start | bytes 393224 | tf_op jit(solution)/shard_map/ppermute | solution.py:34
  455.7 17.7 %collective-permute-start.35 = (bf16[32,2048]{1,0:T(8,128)(2,1)S(1)}, bf16[32,2048]{1,0:T(8,128)(2,1)S(1)}, u32[]{:S(2)}, u32[]{:S(2)}) collective-permute-start(bf16[32,2048]{1,0:T(8,128)(2,1)S(1)} %get-tuple-element.31), channel_id=1, source_target_pairs={{0,6},{2,4},{4,10},{6,8},{8,14},{10,12},{12,2},{14,0},{1,7},{3,5},... | collective-permute-start | bytes 393224 | tf_op jit(solution)/shard_map/ppermute | solution.py:34
  466.1 18.3 %collective-permute-start.52 = (bf16[32,2048]{1,0:T(8,128)(2,1)S(1)}, bf16[32,2048]{1,0:T(8,128)(2,1)S(1)}, u32[]{:S(2)}, u32[]{:S(2)}) collective-permute-start(bf16[32,2048]{1,0:T(8,128)(2,1)S(1)} %get-tuple-element.27), channel_id=1, source_target_pairs={{0,14},{2,12},{4,2},{6,0},{8,6},{10,4},{12,10},{14,8},{1,15},{3,13... | collective-permute-start | bytes 393224 | tf_op jit(solution)/shard_map/ppermute | solution.py:34
  468.5 19.3 %collective-permute-start.51 = (bf16[32,2048]{1,0:T(8,128)(2,1)S(1)}, bf16[32,2048]{1,0:T(8,128)(2,1)S(1)}, u32[]{:S(2)}, u32[]{:S(2)}) collective-permute-start(bf16[32,2048]{1,0:T(8,128)(2,1)S(1)} %get-tuple-element.28), channel_id=1, source_target_pairs={{0,12},{2,14},{4,0},{6,2},{8,4},{10,6},{12,8},{14,10},{1,13},{3,15... | collective-permute-start | bytes 393224 | tf_op jit(solution)/shard_map/ppermute | solution.py:34
  468.5 19.8 %collective-permute-start.50 = (bf16[32,2048]{1,0:T(8,128)(2,1)S(1)}, bf16[32,2048]{1,0:T(8,128)(2,1)S(1)}, u32[]{:S(2)}, u32[]{:S(2)}) collective-permute-start(bf16[32,2048]{1,0:T(8,128)(2,1)S(1)} %get-tuple-element.29), channel_id=1, source_target_pairs={{0,2},{2,0},{4,6},{6,4},{8,10},{10,8},{12,14},{14,12},{1,3},{3,1},... | collective-permute-start | bytes 393224 | tf_op jit(solution)/shard_map/ppermute | solution.py:34
  472.2 18.9 %collective-permute-start.49 = (bf16[32,2048]{1,0:T(8,128)(2,1)S(1)}, bf16[32,2048]{1,0:T(8,128)(2,1)S(1)}, u32[]{:S(2)}, u32[]{:S(2)}) collective-permute-start(bf16[32,2048]{1,0:T(8,128)(2,1)S(1)} %get-tuple-element.32), channel_id=1, source_target_pairs={{0,6},{2,4},{4,10},{6,8},{8,14},{10,12},{12,2},{14,0},{1,7},{3,5},... | collective-permute-start | bytes 393224 | tf_op jit(solution)/shard_map/ppermute | solution.py:34
  473.5 19.7 %collective-permute-start.48 = (bf16[32,2048]{1,0:T(8,128)(2,1)S(1)}, bf16[32,2048]{1,0:T(8,128)(2,1)S(1)}, u32[]{:S(2)}, u32[]{:S(2)}) collective-permute-start(bf16[32,2048]{1,0:T(8,128)(2,1)S(1)} %get-tuple-element.33), channel_id=1, source_target_pairs={{0,4},{2,6},{4,8},{6,10},{8,12},{10,14},{12,0},{14,2},{1,5},{3,7},... | collective-permute-start | bytes 393224 | tf_op jit(solution)/shard_map/ppermute | solution.py:34
  484.4 16.8 %collective-permute-start.47 = (bf16[32,2048]{1,0:T(8,128)(2,1)S(1)}, bf16[32,2048]{1,0:T(8,128)(2,1)S(1)}, u32[]{:S(2)}, u32[]{:S(2)}) collective-permute-start(bf16[32,2048]{1,0:T(8,128)(2,1)S(1)} %get-tuple-element.34), channel_id=1, source_target_pairs={{0,10},{2,8},{4,14},{6,12},{8,2},{10,0},{12,6},{14,4},{1,11},{3,9}... | collective-permute-start | bytes 393224 | tf_op jit(solution)/shard_map/ppermute | solution.py:34
  487.8 14.4 %collective-permute-start.46 = (bf16[32,2048]{1,0:T(8,128)(2,1)S(1)}, bf16[32,2048]{1,0:T(8,128)(2,1)S(1)}, u32[]{:S(2)}, u32[]{:S(2)}) collective-permute-start(bf16[32,2048]{1,0:T(8,128)(2,1)S(1)} %get-tuple-element.35), channel_id=1, source_target_pairs={{0,8},{2,10},{4,12},{6,14},{8,0},{10,2},{12,4},{14,6},{1,9},{3,11}... | collective-permute-start | bytes 393224 | tf_op jit(solution)/shard_map/ppermute | solution.py:34
  488.3 16.8 %collective-permute-start.45 = (bf16[32,2048]{1,0:T(8,128)(2,1)S(1)}, bf16[32,2048]{1,0:T(8,128)(2,1)S(1)}, u32[]{:S(2)}, u32[]{:S(2)}) collective-permute-start(bf16[32,2048]{1,0:T(8,128)(2,1)S(1)} %get-tuple-element.36), channel_id=1, source_target_pairs={{0,14},{2,12},{4,2},{6,0},{8,6},{10,4},{12,10},{14,8},{1,15},{3,13... | collective-permute-start | bytes 393224 | tf_op jit(solution)/shard_map/ppermute | solution.py:34
  491.1 17.9 %collective-permute-start.44 = (bf16[32,2048]{1,0:T(8,128)(2,1)S(1)}, bf16[32,2048]{1,0:T(8,128)(2,1)S(1)}, u32[]{:S(2)}, u32[]{:S(2)}) collective-permute-start(bf16[32,2048]{1,0:T(8,128)(2,1)S(1)} %get-tuple-element.37), channel_id=1, source_target_pairs={{0,12},{2,14},{4,0},{6,2},{8,4},{10,6},{12,8},{14,10},{1,13},{3,15... | collective-permute-start | bytes 393224 | tf_op jit(solution)/shard_map/ppermute | solution.py:34
  493.1 16.9 %collective-permute-start.43 = (bf16[32,2048]{1,0:T(8,128)(2,1)S(1)}, bf16[32,2048]{1,0:T(8,128)(2,1)S(1)}, u32[]{:S(2)}, u32[]{:S(2)}) collective-permute-start(bf16[32,2048]{1,0:T(8,128)(2,1)S(1)} %get-tuple-element.38), channel_id=1, source_target_pairs={{0,2},{2,0},{4,6},{6,4},{8,10},{10,8},{12,14},{14,12},{1,3},{3,1},... | collective-permute-start | bytes 393224 | tf_op jit(solution)/shard_map/ppermute | solution.py:34
  501.2 20.6 %collective-permute-start.40 = (bf16[32,1024]{1,0:T(8,128)(2,1)}, bf16[32,1024]{1,0:T(8,128)(2,1)S(1)}, u32[]{:S(2)}, u32[]{:S(2)}) collective-permute-start(bf16[32,1024]{1,0:T(8,128)(2,1)} %get-tuple-element.42), channel_id=1, source_target_pairs={{0,10},{2,8},{4,14},{6,12},{8,2},{10,0},{12,6},{14,4},{1,11},{3,9}... | collective-permute-start | bytes 196616 | tf_op jit(solution)/shard_map/ppermute | solution.py:34
  502.2 21.4 %collective-permute-start.39 = (bf16[32,1024]{1,0:T(8,128)(2,1)}, bf16[32,1024]{1,0:T(8,128)(2,1)S(1)}, u32[]{:S(2)}, u32[]{:S(2)}) collective-permute-start(bf16[32,1024]{1,0:T(8,128)(2,1)} %get-tuple-element.43), channel_id=1, source_target_pairs={{0,8},{2,10},{4,12},{6,14},{8,0},{10,2},{12,4},{14,6},{1,9},{3,11}... | collective-permute-start | bytes 196616 | tf_op jit(solution)/shard_map/ppermute | solution.py:34
  505.1 20.6 %collective-permute-start.38 = (bf16[32,1024]{1,0:T(8,128)(2,1)}, bf16[32,1024]{1,0:T(8,128)(2,1)S(1)}, u32[]{:S(2)}, u32[]{:S(2)}) collective-permute-start(bf16[32,1024]{1,0:T(8,128)(2,1)} %get-tuple-element.44), channel_id=1, source_target_pairs={{0,14},{2,12},{4,2},{6,0},{8,6},{10,4},{12,10},{14,8},{1,15},{3,13... | collective-permute-start | bytes 196616 | tf_op jit(solution)/shard_map/ppermute | solution.py:34
  509.0 17.4 %collective-permute-start.37 = (bf16[32,1024]{1,0:T(8,128)(2,1)}, bf16[32,1024]{1,0:T(8,128)(2,1)S(1)}, u32[]{:S(2)}, u32[]{:S(2)}) collective-permute-start(bf16[32,1024]{1,0:T(8,128)(2,1)} %get-tuple-element.45), channel_id=1, source_target_pairs={{0,12},{2,14},{4,0},{6,2},{8,4},{10,6},{12,8},{14,10},{1,13},{3,15... | collective-permute-start | bytes 196616 | tf_op jit(solution)/shard_map/ppermute | solution.py:34
  510.0 17.8 %collective-permute-start.36 = (bf16[32,1024]{1,0:T(8,128)(2,1)}, bf16[32,1024]{1,0:T(8,128)(2,1)S(1)}, u32[]{:S(2)}, u32[]{:S(2)}) collective-permute-start(bf16[32,1024]{1,0:T(8,128)(2,1)} %get-tuple-element.46), channel_id=1, source_target_pairs={{0,2},{2,0},{4,6},{6,4},{8,10},{10,8},{12,14},{14,12},{1,3},{3,1},... | collective-permute-start | bytes 196616 | tf_op jit(solution)/shard_map/ppermute | solution.py:34
  521.9 12.8 %collective-permute-start.14 = (bf16[32,1024]{1,0:T(8,128)(2,1)S(1)}, bf16[32,1024]{1,0:T(8,128)(2,1)S(1)}, u32[]{:S(2)}, u32[]{:S(2)}) collective-permute-start(bf16[32,1024]{1,0:T(8,128)(2,1)S(1)} %copy-done.40), channel_id=1, source_target_pairs={{0,8},{2,10},{4,12},{6,14},{8,0},{10,2},{12,4},{14,6},{1,9},{3,11}... | collective-permute-start | bytes 196616 | tf_op jit(solution)/shard_map/ppermute | solution.py:34
  523.7 11.1 %collective-permute-start.13 = (bf16[32,1024]{1,0:T(8,128)(2,1)S(1)}, bf16[32,1024]{1,0:T(8,128)(2,1)S(1)}, u32[]{:S(2)}, u32[]{:S(2)}) collective-permute-start(bf16[32,1024]{1,0:T(8,128)(2,1)S(1)} %get-tuple-element.67), channel_id=1, source_target_pairs={{0,14},{2,12},{4,2},{6,0},{8,6},{10,4},{12,10},{14,8},{1,15},{3,13... | collective-permute-start | bytes 196616 | tf_op jit(solution)/shard_map/ppermute | solution.py:34
  525.7 9.0 %collective-permute-start.12 = (bf16[32,1024]{1,0:T(8,128)(2,1)S(1)}, bf16[32,1024]{1,0:T(8,128)(2,1)S(1)}, u32[]{:S(2)}, u32[]{:S(2)}) collective-permute-start(bf16[32,1024]{1,0:T(8,128)(2,1)S(1)} %get-tuple-element.68), channel_id=1, source_target_pairs={{0,12},{2,14},{4,0},{6,2},{8,4},{10,6},{12,8},{14,10},{1,13},{3,15... | collective-permute-start | bytes 196616 | tf_op jit(solution)/shard_map/ppermute | solution.py:34
  526.3 8.4 %collective-permute-start.11 = (bf16[32,1024]{1,0:T(8,128)(2,1)S(1)}, bf16[32,1024]{1,0:T(8,128)(2,1)S(1)}, u32[]{:S(2)}, u32[]{:S(2)}) collective-permute-start(bf16[32,1024]{1,0:T(8,128)(2,1)S(1)} %get-tuple-element.69), channel_id=1, source_target_pairs={{0,2},{2,0},{4,6},{6,4},{8,10},{10,8},{12,14},{14,12},{1,3},{3,1},... | collective-permute-start | bytes 196616 | tf_op jit(solution)/shard_map/ppermute | solution.py:34
  527.8 7.0 %collective-permute-start.17 = (bf16[32,1024]{1,0:T(8,128)(2,1)S(1)}, bf16[32,1024]{1,0:T(8,128)(2,1)S(1)}, u32[]{:S(2)}, u32[]{:S(2)}) collective-permute-start(bf16[32,1024]{1,0:T(8,128)(2,1)S(1)} %copy-done.41), channel_id=1, source_target_pairs={{0,6},{2,4},{4,10},{6,8},{8,14},{10,12},{12,2},{14,0},{1,7},{3,5},... | collective-permute-start | bytes 196616 | tf_op jit(solution)/shard_map/ppermute | solution.py:34
  (55 other events, 728.6 us)

commit v5 on v4

--- a/solution.py
+++ b/solution.py
@@ -75,11 +75,20 @@
         table[:, block * LANES : (block + 1) * LANES] = values.astype(table.dtype)
 
 
-def fourier_kernel(sizes, place_ref, grid_ref, wave_order, lat_order, out, table, coupling):
-    levels, rows, lon_count = grid_ref.shape
-
-    @pl.when(pl.program_id(0) == 0)
+def fourier_kernel(
+    sizes, place_ref, grid_ref, wave_order, lat_order, out, table, coupling, held, arrived
+):
+    _, levels, rows, lon_count = held.shape
+    step, steps = pl.program_id(0), pl.num_programs(0)
+
+    def fetch(index):
+        slot = index % 2
+        source = grid_ref.at[pl.ds(index * levels, levels)]
+        return pltpu.make_async_copy(source, held.at[slot], arrived.at[slot])
+
+    @pl.when(step == 0)
     def _():
+        fetch(step).start()
         write_table(sizes, place_ref, wave_order, table)
         row = lax.broadcasted_iota(jnp.int32, (rows, 1), 0) + place_ref[0] * rows
         latitude = pick(lat_order[...].astype(jnp.float32), row) + 0.5
@@ -87,7 +96,12 @@
         sign = 1.0 - 2.0 * place_ref[2].astype(jnp.float32)
         coupling[...] = jnp.broadcast_to(0.5 * sign * sine, coupling.shape)
 
-    field = grid_ref[...].astype(jnp.float32)
+    @pl.when(step + 1 < steps)
+    def _():
+        fetch(step + 1).start()
+
+    fetch(step).wait()
+    field = held[step % 2].astype(jnp.float32)
     forcing = (field + coupling[:, :1][None] * jnp.tanh(field)).astype(jnp.bfloat16)
     forcing = forcing.reshape(levels * rows, lon_count)
     out[...] = lax.dot_general(
@@ -110,7 +124,7 @@
         grid=(levels // block,),
         in_specs=[
             pl.BlockSpec(memory_space=pltpu.SMEM),
-            pl.BlockSpec((block, rows_here, lon_count), lambda i: (i, 0, 0)),
+            pl.BlockSpec(memory_space=pl.ANY),
             whole(1, wave_order.shape[0]),
             whole(1, lat_order.shape[0]),
         ],
@@ -118,7 +132,11 @@
             pl.BlockSpec((height, block * rows_here), lambda i: (0, i)),
             whole(height, lon_count),
         ],
-        scratch_shapes=[pltpu.VMEM((rows_here, LANES), jnp.float32)],
+        scratch_shapes=[
+            pltpu.VMEM((rows_here, LANES), jnp.float32),
+            pltpu.VMEM((2, block, rows_here, lon_count), jnp.bfloat16),
+            pltpu.SemaphoreType.DMA((2,)),
+        ],
         compiler_params=pltpu.CompilerParams(vmem_limit_bytes=56 * 2**20),
         cost_estimate=pl.CostEstimate(
             flops=2 * height * width * lon_count,
@@ -131,18 +149,30 @@
 def inverse_kernel(pieces, tables, has_partial, *refs):
     out = refs[-1]
     coeffs = jnp.concatenate([ref[...] for ref in refs[:pieces]], axis=0)
-    table = jnp.concatenate([ref[...] for ref in refs[pieces : pieces + tables]], axis=0)
-    current = lax.dot_general(
-        coeffs, table, (((0,), (0,)), ((), ())), preferred_element_type=jnp.float32
-    ).reshape(out.shape)
-    if has_partial:
-        current = current + refs[pieces + tables][...]
-    out[...] = current.astype(out.dtype)
+    levels, rows, lon_count = out.shape
+    loops = 3 if not has_partial and lon_count % (3 * LANES) == 0 else 1
+    some = lon_count // loops
+
+    def longitudes(index, carry):
+        lanes = pl.ds(pl.multiple_of(index * some, some), some)
+        table = jnp.concatenate([ref[:, lanes] for ref in refs[pieces : pieces + tables]], axis=0)
+        current = lax.dot_general(
+            coeffs, table, (((0,), (0,)), ((), ())), preferred_element_type=jnp.float32
+        ).reshape(levels, rows, some)
+        if has_partial:
+            current = current + refs[pieces + tables][:, :, lanes]
+        out[:, :, lanes] = current.astype(out.dtype)
+        return carry
+
+    if loops == 1:
+        longitudes(0, 0)
+    else:
+        lax.fori_loop(0, loops, longitudes, 0)
 
 
 def inverse_fourier(pieces, tables, shape, start, levels, current=None, partial=None, dtype=None):
     _, rows_here, lon_count = shape
-    block = level_block(levels, rows_here, 8)
+    block = level_block(levels, rows_here, 8 if partial is None else levels // 2)
     width = block * rows_here
     first = start // block
     height = sum(table.shape[0] for table in tables)
@@ -469,9 +499,8 @@
         arrived.append(pieces)
 
     half, fourth = local_levels // 2, local_levels // 4
-    cuts = {chunk: [(0, local_levels)] for chunk in range(chunks)}
-    cuts[1] = [(0, half), (half, half)]
-    cuts[chunks - 1] = [(0, half), (half, fourth), (half + fourth, fourth)]
+    groups = [(0, half), (half, fourth), (half + fourth, fourth)]
+    cuts = {chunk: groups if chunk in (1, chunks - 1) else [(0, local_levels)] for chunk in range(chunks)}
     returned = []
     for chunk in range(chunks):
         is_whole = chunk in WHOLE_CHUNKS
@@ -487,7 +516,7 @@
             hemi = exchange(joined(other, grid, 0.5))
             returned.append([(0, local_levels, [hemi.reshape(places * height, width)])])
             continue
-        groups = []
+        sent = []
         for start, levels in cuts[chunk]:
             lanes = slice(start * rows_here, (start + levels) * rows_here)
             pieces = []
@@ -495,8 +524,8 @@
                 hemi = joined(other[index, :, lanes], grid[index, :, lanes], 0.5)
                 wave, level = (wave_size - wave) % wave_size, (level_size - level) % level_size
                 pieces.append(shift_places(hemi, wave, level))
-            groups.append((start, levels, pieces))
-        returned.append(groups)
+            sent.append((start, levels, pieces))
+        returned.append(sent)
 
     def pieces_at(chunk_list, start):
         return [
@@ -510,20 +539,19 @@
     shape = grid_state.shape
     everything = list(range(chunks))
     partials = []
-    for start in (0, half):
+    for start, levels in groups:
         partials.append(
             inverse_fourier(
                 pieces_at(everything[:2], start),
                 tables[:2],
                 shape,
                 start,
-                half,
+                levels,
                 dtype=jnp.bfloat16,
             )
         )
     current = None
-    for start, levels in cuts[chunks - 1]:
-        base = 0 if start < half else half
+    for cut, (start, levels) in enumerate(groups):
         current = inverse_fourier(
             pieces_at(everything[2:], start),
             tables[2:],
@@ -531,7 +559,7 @@
             start,
             levels,
             current=current,
-            partial=(partials[0 if base == 0 else 1], base),
+            partial=(partials[cut], start),
         )
     return current.reshape(out_shape)
 

time: 542 us -> 467 us (0.86)
  waiting for transfers between devices: 189 us -> 103 us
  starting transfers between devices: 153 us -> 163 us
    ppermute x49 -> x56, waiting for transfers between devices: 110 us -> 54.3 us  [shift_places(): return lax.ppermute(value, EXCHANGE_AXES, pairs)]
    all_to_all x4, waiting for transfers between devices: 79.5 us -> 48.6 us  [exchange(): lax.all_to_all(value, EXCHANGE_AXES, split_axis=0, concat_axis=0, tiled=T...]
    ppermute x49 -> x56, starting transfers between devices: 132 us -> 142 us  [shift_places(): return lax.ppermute(value, EXCHANGE_AXES, pairs)]
    pallas_call x5 -> x6, Pallas kernels: 34.8 us -> 39.6 us  [inverse_fourier(): pl.pallas_call(functools.partial(inverse_kernel, len(pieces), len(tables)...]
    mul x5 -> x6, other arithmetic: 11.3 us -> 9.18 us  [joined(): scale * (other.astype(jnp.float32) + hemi_sign * own.astype(jnp.float32))]
  transfers between devices with their start and end apart: 61 -> 68, of which waited for: 12 -> 10; matrix products, arithmetic and copies ran while one was open for 6% -> 7% of each run, Pallas kernels for 26% -> 31%
where the time goes in v5:
time: 467 us; the launch traced here: 466 us
  starting transfers between devices  163 us (35%)
  Pallas kernels  160 us (34%)
  waiting for transfers between devices  103 us (22%)
  other arithmetic  28.4 us (6%)
  local copies, waits for them, and re-layouts  10.6 us (2%)
    ppermute x56, starting transfers between devices, shift_places(): return lax.ppermute(value, EXCHANGE_AXES, pairs)  142 us
    pallas_call x4, Pallas kernels, columns_fused(): pl.pallas_call(functools.partial(column_kernel, sizes), out_shape=jax.Sha...  78.8 us
    ppermute x56, waiting for transfers between devices, shift_places(): return lax.ppermute(value, EXCHANGE_AXES, pairs)  54.3 us
    all_to_all x4, waiting for transfers between devices, exchange(): lax.all_to_all(value, EXCHANGE_AXES, split_axis=0, concat_axis=0, tiled=T...  48.6 us
    pallas_call x4, Pallas kernels, fourier(): pl.pallas_call(functools.partial(fourier_kernel, sizes), out_shape=[jax.S...  41.3 us
    pallas_call x6, Pallas kernels, inverse_fourier(): pl.pallas_call(functools.partial(inverse_kernel, len(pieces), len(tables)...  39.6 us
    all_to_all x4, starting transfers between devices, exchange(): lax.all_to_all(value, EXCHANGE_AXES, split_axis=0, concat_axis=0, tiled=T...  19.2 us
    convert_element_type x4, other arithmetic, joined(): return both.astype(jnp.bfloat16)  14.7 us
  transfers between devices with their start and end apart: 68, of which 10 were waited for; matrix products, arithmetic and copies ran while one was open for 7% of the time, Pallas kernels for 31%

profile of v5, /device:TPU:0, one launch (start us, length us, event | category | flops | bytes accessed | tf_op | source)
XLA Modules:
  0.0 465.5 jit_solution(16983797371332107392)
XLA Ops:
  0.6 10.3 %shard_map.77 = (bf16[256,4096]{1,0:T(8,128)(2,1)}, bf16[256,1536]{1,0:T(8,128)(2,1)}) custom-call(s32[3]{0:T(128)} %pad_add_fusion.1.place_ref, bf16[64,64,1536]{2,1,0:T(8,128)(2,1)} %bitcast.137, s32[1,512]{1,0:T(1,128)} %bitcast.175, s32[1,256]{1,0:T(1,128)} %bitcast.179), custom_call_target="tpu_custom_call" | custom-call | flops 3221225472 | bytes 15466496 | tf_op jit(solution)/shard_map/pallas_call | solution.py:118
  10.9 7.3 %all-to-all-start.2 = ((bf16[8,2,16,4096]{3,2,1,0:T(8,128)(2,1)}), bf16[8,2,16,4096]{3,2,1,0:T(8,128)(2,1)S(1)}, u32[]{:S(2)}, u32[]{:S(2)}) async-start(bf16[8,2,16,4096]{3,2,1,0:T(8,128)(2,1)} %bitcast.162), calls=%async_computation.2 | async-start | bytes 4194304 | tf_op jit(solution)/shard_map/all_to_all | solution.py:437
  18.2 10.2 %shard_map.73 = (bf16[256,4096]{1,0:T(8,128)(2,1)}, bf16[256,1536]{1,0:T(8,128)(2,1)}) custom-call(s32[3]{0:T(128)} %pad_add_fusion.1.place_ref, bf16[64,64,1536]{2,1,0:T(8,128)(2,1)} %bitcast.138, s32[1,512]{1,0:T(1,128)} %bitcast.176, s32[1,256]{1,0:T(1,128)} %bitcast.180), custom_call_target="tpu_custom_call" | custom-call | flops 3221225472 | bytes 15466496 | tf_op jit(solution)/shard_map/pallas_call | solution.py:118
  28.4 38.0 %all-to-all-done.2.refs_0_ = bf16[8,2,16,4096]{3,2,1,0:T(8,128)(2,1)S(1)} async-done(((bf16[8,2,16,4096]{3,2,1,0:T(8,128)(2,1)}), bf16[8,2,16,4096]{3,2,1,0:T(8,128)(2,1)S(1)}, u32[]{:S(2)}, u32[]{:S(2)}) %all-to-all-start.2) | async-done | bytes 2097184 | tf_op jit(solution)/shard_map/all_to_all | solution.py:437
  66.4 4.7 %all-to-all-start = ((bf16[8,2,16,4096]{3,2,1,0:T(8,128)(2,1)}), bf16[8,2,16,4096]{3,2,1,0:T(8,128)(2,1)}, u32[]{:S(2)}, u32[]{:S(2)}) async-start(bf16[8,2,16,4096]{3,2,1,0:T(8,128)(2,1)} %bitcast.161), calls=%async_computation | async-start | bytes 4194304 | tf_op jit(solution)/shard_map/all_to_all | solution.py:437
  77.0 20.2 %shard_map.78 = bf16[8,2,16,4096]{3,2,1,0:T(8,128)(2,1)} custom-call(s32[64]{0:T(128)} %dynamic_slice.3.waves, s32[5]{0:T(128)} %pad_add_fusion.scalars, f32[128,1]{1,0:T(8,128)} %copy.12.eig_ref, bf16[128,128]{1,0:T(8,128)(2,1)} %select_bitcast_fusion.1.modes_in, bf16[128,128]{1,0:T(8,128)(2,1)} %broadcast_select_fusion.1.modes_out, ...), custom_call_target="tpu_custom_call" | custom-call | flops 1610612736 | bytes 6291456 | tf_op jit(solution)/shard_map/pallas_call | solution.py:356
  97.7 10.4 %shard_map.79 = (bf16[256,4096]{1,0:T(8,128)(2,1)}, bf16[256,1536]{1,0:T(8,128)(2,1)}) custom-call(s32[3]{0:T(128)} %pad_add_fusion.1.place_ref, bf16[64,64,1536]{2,1,0:T(8,128)(2,1)} %bitcast.139, s32[1,512]{1,0:T(1,128)} %bitcast.177, s32[1,256]{1,0:T(1,128)} %bitcast.181), custom_call_target="tpu_custom_call" | custom-call | flops 3221225472 | bytes 15466496 | tf_op jit(solution)/shard_map/pallas_call | solution.py:118
  108.2 10.6 %all-to-all-done.refs_0_ = bf16[8,2,16,4096]{3,2,1,0:T(8,128)(2,1)} async-done(((bf16[8,2,16,4096]{3,2,1,0:T(8,128)(2,1)}), bf16[8,2,16,4096]{3,2,1,0:T(8,128)(2,1)}, u32[]{:S(2)}, u32[]{:S(2)}) %all-to-all-start) | async-done | bytes 2097184 | tf_op jit(solution)/shard_map/all_to_all | solution.py:437
  118.8 10.4 %shard_map.75 = (bf16[256,4096]{1,0:T(8,128)(2,1)}, bf16[256,1536]{1,0:T(8,128)(2,1)}) custom-call(s32[3]{0:T(128)} %pad_add_fusion.1.place_ref, bf16[64,64,1536]{2,1,0:T(8,128)(2,1)} %bitcast.140, s32[1,512]{1,0:T(1,128)} %bitcast.178, s32[1,256]{1,0:T(1,128)} %bitcast.182), custom_call_target="tpu_custom_call" | custom-call | flops 3221225472 | bytes 15466496 | tf_op jit(solution)/shard_map/pallas_call | solution.py:118
  131.4 3.9 multiply_convert_fusion
  135.3 3.6 all-to-all-start.3
  138.9 20.4 %shard_map.74 = bf16[8,2,16,4096]{3,2,1,0:T(8,128)(2,1)} custom-call(s32[64]{0:T(128)} %dynamic_slice.3.waves, s32[5]{0:T(128)} %pad_add_fusion.scalars, f32[128,1]{1,0:T(8,128)} %copy.12.eig_ref, bf16[128,128]{1,0:T(8,128)(2,1)} %select_bitcast_fusion.1.modes_in, bf16[128,128]{1,0:T(8,128)(2,1)} %broadcast_select_fusion.1.modes_out, ...), custom_call_target="tpu_custom_call" | custom-call | flops 1610612736 | bytes 6291456 | tf_op jit(solution)/shard_map/pallas_call | solution.py:356
  159.3 3.1 add_convert_fusion
  162.5 4.6 collective-permute-start.27
  169.1 2.9 collective-permute-start.24
  172.0 8.8 %collective-permute-done.27 = bf16[32,4096]{1,0:T(8,128)(2,1)S(1)} collective-permute-done((bf16[32,4096]{1,0:T(8,128)(2,1)}, bf16[32,4096]{1,0:T(8,128)(2,1)S(1)}, u32[]{:S(2)}, u32[]{:S(2)}) %collective-permute-start.27) | collective-permute-done | bytes 262176 | tf_op jit(solution)/shard_map/ppermute | solution.py:34
  180.9 31.6 %collective-permute-start.23 = (bf16[32,4096]{1,0:T(8,128)(2,1)S(1)}, bf16[32,4096]{1,0:T(8,128)(2,1)S(1)}, u32[]{:S(2)}, u32[]{:S(2)}) collective-permute-start(bf16[32,4096]{1,0:T(8,128)(2,1)S(1)} %get-tuple-element.68), channel_id=1, source_target_pairs={{0,6},{2,4},{4,10},{6,8},{8,14},{10,12},{12,2},{14,0},{1,7},{3,5},... | collective-permute-start | bytes 786440 | tf_op jit(solution)/shard_map/ppermute | solution.py:34
  212.5 10.3 %collective-permute-start.22 = (bf16[32,4096]{1,0:T(8,128)(2,1)}, bf16[32,4096]{1,0:T(8,128)(2,1)S(1)}, u32[]{:S(2)}, u32[]{:S(2)}) collective-permute-start(bf16[32,4096]{1,0:T(8,128)(2,1)} %get-tuple-element.69), channel_id=1, source_target_pairs={{0,4},{2,6},{4,8},{6,10},{8,12},{10,14},{12,0},{14,2},{1,5},{3,7},... | collective-permute-start | bytes 786440 | tf_op jit(solution)/shard_map/ppermute | solution.py:34
  222.8 6.0 %collective-permute-done.25 = bf16[32,4096]{1,0:T(8,128)(2,1)S(1)} collective-permute-done((bf16[32,4096]{1,0:T(8,128)(2,1)S(1)}, bf16[32,4096]{1,0:T(8,128)(2,1)S(1)}, u32[]{:S(2)}, u32[]{:S(2)}) %collective-permute-start.25) | collective-permute-done | bytes 262176 | tf_op jit(solution)/shard_map/ppermute | solution.py:34
  230.0 3.7 add_convert_fusion.8
  234.9 3.3 collective-permute-start.7
  240.2 19.1 %shard_map.80 = bf16[8,2,16,4096]{3,2,1,0:T(8,128)(2,1)} custom-call(s32[64]{0:T(128)} %dynamic_slice.3.waves, s32[5]{0:T(128)} %pad_add_fusion.2.scalars, f32[128,1]{1,0:T(8,128)} %copy.12.eig_ref, bf16[128,128]{1,0:T(8,128)(2,1)} %select_bitcast_fusion.modes_in, bf16[128,128]{1,0:T(8,128)(2,1)} %broadcast_select_fusion.modes_out, ...), custom_call_target="tpu_custom_call" | custom-call | flops 1610612736 | bytes 6291456 | tf_op jit(solution)/shard_map/pallas_call | solution.py:356
  260.5 1.9 collective-permute-start.4
  262.4 11.8 %collective-permute-done.7 = bf16[32,4096]{1,0:T(8,128)(2,1)S(1)} collective-permute-done((bf16[32,4096]{1,0:T(8,128)(2,1)S(1)}, bf16[32,4096]{1,0:T(8,128)(2,1)S(1)}, u32[]{:S(2)}, u32[]{:S(2)}) %collective-permute-start.7) | collective-permute-done | bytes 262176 | tf_op jit(solution)/shard_map/ppermute | solution.py:34
  275.0 3.9 multiply_convert_fusion.1
  280.3 3.6 all-to-all-start.1
  284.0 19.0 %shard_map.76 = bf16[8,2,16,4096]{3,2,1,0:T(8,128)(2,1)} custom-call(s32[64]{0:T(128)} %dynamic_slice.3.waves, s32[5]{0:T(128)} %pad_add_fusion.2.scalars, f32[128,1]{1,0:T(8,128)} %copy.12.eig_ref, bf16[128,128]{1,0:T(8,128)(2,1)} %select_bitcast_fusion.modes_in, bf16[128,128]{1,0:T(8,128)(2,1)} %broadcast_select_fusion.modes_out, ...), custom_call_target="tpu_custom_call" | custom-call | flops 1610612736 | bytes 6291456 | tf_op jit(solution)/shard_map/pallas_call | solution.py:356
  303.5 1.8 fusion.30
  305.4 1.6 collective-permute-start.34
  307.0 3.3 collective-permute-start.33
  310.8 2.2 collective-permute-start.31
  313.0 2.3 fusion.15
  315.4 2.0 fusion.47
  317.4 1.7 collective-permute-start.30
  319.1 5.6 %collective-permute-done.34.refs_7_ = bf16[32,1024]{1,0:T(8,128)(2,1)S(1)} collective-permute-done((bf16[32,1024]{1,0:T(8,128)(2,1)S(1)}, bf16[32,1024]{1,0:T(8,128)(2,1)S(1)}, u32[]{:S(2)}, u32[]{:S(2)}) %collective-permute-start.34) | collective-permute-done | bytes 65568 | tf_op jit(solution)/shard_map/ppermute | solution.py:34
  324.8 1.5 collective-permute-start.29
  326.3 13.8 %collective-permute-done.33.refs_6_ = bf16[32,1024]{1,0:T(8,128)(2,1)S(1)} collective-permute-done((bf16[32,1024]{1,0:T(8,128)(2,1)S(1)}, bf16[32,1024]{1,0:T(8,128)(2,1)S(1)}, u32[]{:S(2)}, u32[]{:S(2)}) %collective-permute-start.33) | collective-permute-done | bytes 65568 | tf_op jit(solution)/shard_map/ppermute | solution.py:34
  342.2 2.5 collective-permute-start.48
  344.7 2.4 collective-permute-start.63
  347.1 2.9 collective-permute-start.61
  351.9 3.8 collective-permute-start.59
  355.8 1.5 collective-permute-start.57
  357.2 6.5 %collective-permute-done.61.refs_6_ = bf16[32,2048]{1,0:T(8,128)(2,1)S(1)} collective-permute-done((bf16[32,2048]{1,0:T(8,128)(2,1)S(1)}, bf16[32,2048]{1,0:T(8,128)(2,1)S(1)}, u32[]{:S(2)}, u32[]{:S(2)}) %collective-permute-start.61) | collective-permute-done | bytes 131104 | tf_op jit(solution)/shard_map/ppermute | solution.py:34
  363.8 5.4 %collective-permute-start.56 = (bf16[32,2048]{1,0:T(8,128)(2,1)S(1)}, bf16[32,2048]{1,0:T(8,128)(2,1)S(1)}, u32[]{:S(2)}, u32[]{:S(2)}) collective-permute-start(bf16[32,2048]{1,0:T(8,128)(2,1)S(1)} %get-tuple-element.31), channel_id=1, source_target_pairs={{0,6},{2,4},{4,10},{6,8},{8,14},{10,12},{12,2},{14,0},{1,7},{3,5},... | collective-permute-start | bytes 393224 | tf_op jit(solution)/shard_map/ppermute | solution.py:34
  369.2 2.7 collective-permute-start.55
  372.8 3.5 collective-permute-start.54
  376.3 3.2 collective-permute-start.52
  379.5 2.0 collective-permute-start.51
  382.2 8.8 %shard_map.83.refs_11_ = bf16[32,64,1536]{2,1,0:T(8,128)(2,1)} custom-call(bf16[256,4096]{1,0:T(8,128)(2,1)} %bitcast.148, bf16[32,2048]{1,0:T(8,128)(2,1)} %get-tuple-element.30.refs_1_, bf16[32,2048]{1,0:T(8,128)(2,1)} %copy-done.77, bf16[32,2048]{1,0:T(8,128)(2,1)} %copy-done.76, bf16[32,2048]{1,0:T(8,128)(2,1)} %copy-done.75, ...), custom_call_target="tpu_custom_call" | custom-call | flops 3221225472 | bytes 8388608 | tf_op jit(solution)/shard_map/pallas_call | solution.py:202
  391.1 10.4 %collective-permute-start.47 = (bf16[32,1024]{1,0:T(8,128)(2,1)}, bf16[32,1024]{1,0:T(8,128)(2,1)S(1)}, u32[]{:S(2)}, u32[]{:S(2)}) collective-permute-start(bf16[32,1024]{1,0:T(8,128)(2,1)} %get-tuple-element.41), channel_id=1, source_target_pairs={{0,10},{2,8},{4,14},{6,12},{8,2},{10,0},{12,6},{14,4},{1,11},{3,9}... | collective-permute-start | bytes 196616 | tf_op jit(solution)/shard_map/ppermute | solution.py:34
  402.1 3.9 collective-permute-start.44
  406.0 1.4 collective-permute-start.43
  408.7 8.3 %shard_map.84.refs_12_ = bf16[64,64,1536]{2,1,0:T(8,128)(2,1)} custom-call(bf16[256,4096]{1,0:T(8,128)(2,1)} %bitcast.145, bf16[32,2048]{1,0:T(8,128)(2,1)} %get-tuple-element.38.refs_1_, bf16[32,2048]{1,0:T(8,128)(2,1)} %copy-done.26, bf16[32,2048]{1,0:T(8,128)(2,1)} %copy-done.25, bf16[32,2048]{1,0:T(8,128)(2,1)} %copy-done.24, ...), custom_call_target="tpu_custom_call" | custom-call | flops 3221225472 | bytes 8388608 | tf_op jit(solution)/shard_map/pallas_call | solution.py:202
  417.2 5.3 %collective-permute-start.15 = (bf16[32,1024]{1,0:T(8,128)(2,1)S(1)}, bf16[32,1024]{1,0:T(8,128)(2,1)S(1)}, u32[]{:S(2)}, u32[]{:S(2)}) collective-permute-start(bf16[32,1024]{1,0:T(8,128)(2,1)S(1)} %copy-done.58), channel_id=1, source_target_pairs={{0,10},{2,8},{4,14},{6,12},{8,2},{10,0},{12,6},{14,4},{1,11},{3,9}... | collective-permute-start | bytes 196616 | tf_op jit(solution)/shard_map/ppermute | solution.py:34
  423.6 5.9 %shard_map.82.refs_11_ = bf16[16,64,1536]{2,1,0:T(8,128)(2,1)} custom-call(bf16[256,4096]{1,0:T(8,128)(2,1)} %bitcast.149, bf16[32,1024]{1,0:T(8,128)(2,1)} %get-tuple-element.46.refs_1_, bf16[32,1024]{1,0:T(8,128)(2,1)} %copy-done.49, bf16[32,1024]{1,0:T(8,128)(2,1)} %copy-done.46, bf16[32,1024]{1,0:T(8,128)(2,1)} %copy-done.44, ...), custom_call_target="tpu_custom_call" | custom-call | flops 1610612736 | bytes 4194304 | tf_op jit(solution)/shard_map/pallas_call | solution.py:202
  429.5 4.7 %collective-permute-start.40 = (bf16[32,1024]{1,0:T(8,128)(2,1)S(1)}, bf16[32,1024]{1,0:T(8,128)(2,1)S(1)}, u32[]{:S(2)}, u32[]{:S(2)}) collective-permute-start(bf16[32,1024]{1,0:T(8,128)(2,1)S(1)} %copy-done.66), channel_id=1, source_target_pairs={{0,10},{2,8},{4,14},{6,12},{8,2},{10,0},{12,6},{14,4},{1,11},{3,9}... | collective-permute-start | bytes 196616 | tf_op jit(solution)/shard_map/ppermute | solution.py:34
  434.3 2.7 collective-permute-start.38
  437.0 1.8 collective-permute-start.37
  438.9 1.5 collective-permute-start.36
  440.3 5.9 %shard_map.81.refs_11_ = bf16[16,64,1536]{2,1,0:T(8,128)(2,1)} custom-call(bf16[256,4096]{1,0:T(8,128)(2,1)} %bitcast.150, bf16[32,1024]{1,0:T(8,128)(2,1)} %get-tuple-element.63.refs_1_, bf16[32,1024]{1,0:T(8,128)(2,1)} %copy-done.32, bf16[32,1024]{1,0:T(8,128)(2,1)} %copy-done.31, bf16[32,1024]{1,0:T(8,128)(2,1)} %copy-done.30, ...), custom_call_target="tpu_custom_call" | custom-call | flops 1610612736 | bytes 4194304 | tf_op jit(solution)/shard_map/pallas_call | solution.py:202
  446.4 2.7 collective-permute-start.13
  449.1 1.8 collective-permute-start.12
  452.9 5.4 %shard_map.85.refs_12_ = bf16[64,64,1536]{2,1,0:T(8,128)(2,1)} custom-call(bf16[256,4096]{1,0:T(8,128)(2,1)} %bitcast.146, bf16[32,1024]{1,0:T(8,128)(2,1)} %get-tuple-element.55.refs_1_, bf16[32,1024]{1,0:T(8,128)(2,1)} %copy-done.51, bf16[32,1024]{1,0:T(8,128)(2,1)} %copy-done.48, bf16[32,1024]{1,0:T(8,128)(2,1)} %copy-done.45, ...), custom_call_target="tpu_custom_call", output_to_operand_aliasing={{}: (12, {})} | custom-call | flops 1610612736 | bytes 4194304 | tf_op jit(solution)/shard_map/pallas_call | solution.py:202
  459.9 5.4 %shard_map.86 = bf16[64,64,1536]{2,1,0:T(8,128)(2,1)} custom-call(bf16[256,4096]{1,0:T(8,128)(2,1)} %bitcast.147, bf16[32,1024]{1,0:T(8,128)(2,1)} %get-tuple-element.78.refs_1_, bf16[32,1024]{1,0:T(8,128)(2,1)} %copy-done.53, bf16[32,1024]{1,0:T(8,128)(2,1)} %copy-done.52, bf16[32,1024]{1,0:T(8,128)(2,1)} %copy-done.50, ...), custom_call_target="tpu_custom_call", output_to_operand_aliasing={{}: (12, {})} | custom-call | flops 1610612736 | bytes 4194304 | tf_op jit(solution)/shard_map/pallas_call | solution.py:202
  (281 shorter events, 32.4 us)
Async XLA Ops:
  10.9 55.6 %all-to-all-start.2 = ((bf16[8,2,16,4096]{3,2,1,0:T(8,128)(2,1)}), bf16[8,2,16,4096]{3,2,1,0:T(8,128)(2,1)S(1)}, u32[]{:S(2)}, u32[]{:S(2)}) async-start(bf16[8,2,16,4096]{3,2,1,0:T(8,128)(2,1)} %bitcast.162), calls=%async_computation.2 | async-start | bytes 4194304 | tf_op jit(solution)/shard_map/all_to_all | solution.py:437
  66.4 52.4 %all-to-all-start = ((bf16[8,2,16,4096]{3,2,1,0:T(8,128)(2,1)}), bf16[8,2,16,4096]{3,2,1,0:T(8,128)(2,1)}, u32[]{:S(2)}, u32[]{:S(2)}) async-start(bf16[8,2,16,4096]{3,2,1,0:T(8,128)(2,1)} %bitcast.161), calls=%async_computation | async-start | bytes 4194304 | tf_op jit(solution)/shard_map/all_to_all | solution.py:437
  97.3 34.1 %collective-permute-start.19 = (bf16[8,32,4096]{2,1,0:T(8,128)(2,1)}, bf16[8,32,4096]{2,1,0:T(8,128)(2,1)}, u32[]{:S(2)}, u32[]{:S(2)}) collective-permute-start(bf16[8,32,4096]{2,1,0:T(8,128)(2,1)} %bitcast.160), channel_id=1, source_target_pairs={{0,1},{1,0},{2,3},{3,2},{4,5},{5,4},{6,7},{7,6},{8,9},{9,8},{10,11... | collective-permute-start | bytes 6291464 | tf_op jit(solution)/shard_map/ppermute | solution.py:22
  108.1 51.2 %collective-permute-start.20 = (bf16[256,4096]{1,0:T(8,128)(2,1)}, bf16[256,4096]{1,0:T(8,128)(2,1)}, u32[]{:S(2)}, u32[]{:S(2)}) collective-permute-start(bf16[256,4096]{1,0:T(8,128)(2,1)} %get-tuple-element.20), channel_id=1, source_target_pairs={{0,1},{1,0},{2,3},{3,2},{4,5},{5,4},{6,7},{7,6},{8,9},{9,8},{10,11... | collective-permute-start | bytes 6291464 | tf_op jit(solution)/shard_map/ppermute | solution.py:22
  118.8 20.1 %collective-permute-start = (bf16[8,2,16,4096]{3,2,1,0:T(8,128)(2,1)}, bf16[8,2,16,4096]{3,2,1,0:T(8,128)(2,1)}, u32[]{:S(2)}, u32[]{:S(2)}) collective-permute-start(bf16[8,2,16,4096]{3,2,1,0:T(8,128)(2,1)} %all-to-all-done.refs_0_), channel_id=1, source_target_pairs={{0,1},{1,0},{2,3},{3,2},{4,5},{5,4},{6,7},{7,6},{8,9},{9,8},{10,11... | collective-permute-start | bytes 6291464 | tf_op jit(solution)/shard_map/ppermute | solution.py:22
  129.3 39.8 %collective-permute-start.2 = (bf16[256,4096]{1,0:T(8,128)(2,1)}, bf16[256,4096]{1,0:T(8,128)(2,1)}, u32[]{:S(2)}, u32[]{:S(2)}) collective-permute-start(bf16[256,4096]{1,0:T(8,128)(2,1)} %get-tuple-element.16), channel_id=1, source_target_pairs={{0,1},{1,0},{2,3},{3,2},{4,5},{5,4},{6,7},{7,6},{8,9},{9,8},{10,11... | collective-permute-start | bytes 6291464 | tf_op jit(solution)/shard_map/ppermute | solution.py:22
  135.3 143.7 %all-to-all-start.3 = ((bf16[8,32,4096]{2,1,0:T(8,128)(2,1)}), bf16[8,32,4096]{2,1,0:T(8,128)(2,1)S(1)}, u32[]{:S(2)}, u32[]{:S(2)}) async-start(bf16[8,32,4096]{2,1,0:T(8,128)(2,1)} %multiply_convert_fusion), calls=%async_computation.3 | async-start | bytes 4194304 | tf_op jit(solution)/shard_map/all_to_all | solution.py:437
  159.3 115.7 %collective-permute-start.1 = (bf16[8,32,4096]{2,1,0:T(8,128)(2,1)}, bf16[8,32,4096]{2,1,0:T(8,128)(2,1)}, u32[]{:S(2)}, u32[]{:S(2)}) collective-permute-start(bf16[8,32,4096]{2,1,0:T(8,128)(2,1)} %bitcast.159), channel_id=1, source_target_pairs={{0,1},{1,0},{2,3},{3,2},{4,5},{5,4},{6,7},{7,6},{8,9},{9,8},{10,11... | collective-permute-start | bytes 6291464 | tf_op jit(solution)/shard_map/ppermute | solution.py:22
  162.5 18.4 %collective-permute-start.27 = (bf16[32,4096]{1,0:T(8,128)(2,1)}, bf16[32,4096]{1,0:T(8,128)(2,1)S(1)}, u32[]{:S(2)}, u32[]{:S(2)}) collective-permute-start(bf16[32,4096]{1,0:T(8,128)(2,1)} %get-tuple-element.64), channel_id=1, source_target_pairs={{0,14},{2,12},{4,2},{6,0},{8,6},{10,4},{12,10},{14,8},{1,15},{3,13... | collective-permute-start | bytes 786440 | tf_op jit(solution)/shard_map/ppermute | solution.py:34
  167.1 45.3 %collective-permute-start.26 = (bf16[32,4096]{1,0:T(8,128)(2,1)}, bf16[32,4096]{1,0:T(8,128)(2,1)S(1)}, u32[]{:S(2)}, u32[]{:S(2)}) collective-permute-start(bf16[32,4096]{1,0:T(8,128)(2,1)} %get-tuple-element.65), channel_id=1, source_target_pairs={{0,12},{2,14},{4,0},{6,2},{8,4},{10,6},{12,8},{14,10},{1,13},{3,15... | collective-permute-start | bytes 786440 | tf_op jit(solution)/shard_map/ppermute | solution.py:34
  167.7 61.1 %collective-permute-start.25 = (bf16[32,4096]{1,0:T(8,128)(2,1)S(1)}, bf16[32,4096]{1,0:T(8,128)(2,1)S(1)}, u32[]{:S(2)}, u32[]{:S(2)}) collective-permute-start(bf16[32,4096]{1,0:T(8,128)(2,1)S(1)} %get-tuple-element.66), channel_id=1, source_target_pairs={{0,10},{2,8},{4,14},{6,12},{8,2},{10,0},{12,6},{14,4},{1,11},{3,9}... | collective-permute-start | bytes 786440 | tf_op jit(solution)/shard_map/ppermute | solution.py:34
  169.1 64.7 %collective-permute-start.24 = (bf16[32,4096]{1,0:T(8,128)(2,1)}, bf16[32,4096]{1,0:T(8,128)(2,1)S(1)}, u32[]{:S(2)}, u32[]{:S(2)}) collective-permute-start(bf16[32,4096]{1,0:T(8,128)(2,1)} %get-tuple-element.67), channel_id=1, source_target_pairs={{0,8},{2,10},{4,12},{6,14},{8,0},{10,2},{12,4},{14,6},{1,9},{3,11}... | collective-permute-start | bytes 786440 | tf_op jit(solution)/shard_map/ppermute | solution.py:34
  180.9 53.0 %collective-permute-start.23 = (bf16[32,4096]{1,0:T(8,128)(2,1)S(1)}, bf16[32,4096]{1,0:T(8,128)(2,1)S(1)}, u32[]{:S(2)}, u32[]{:S(2)}) collective-permute-start(bf16[32,4096]{1,0:T(8,128)(2,1)S(1)} %get-tuple-element.68), channel_id=1, source_target_pairs={{0,6},{2,4},{4,10},{6,8},{8,14},{10,12},{12,2},{14,0},{1,7},{3,5},... | collective-permute-start | bytes 786440 | tf_op jit(solution)/shard_map/ppermute | solution.py:34
  212.5 22.4 %collective-permute-start.22 = (bf16[32,4096]{1,0:T(8,128)(2,1)}, bf16[32,4096]{1,0:T(8,128)(2,1)S(1)}, u32[]{:S(2)}, u32[]{:S(2)}) collective-permute-start(bf16[32,4096]{1,0:T(8,128)(2,1)} %get-tuple-element.69), channel_id=1, source_target_pairs={{0,4},{2,6},{4,8},{6,10},{8,12},{10,14},{12,0},{14,2},{1,5},{3,7},... | collective-permute-start | bytes 786440 | tf_op jit(solution)/shard_map/ppermute | solution.py:34
  229.4 10.1 %collective-permute-start.21 = (bf16[32,4096]{1,0:T(8,128)(2,1)}, bf16[32,4096]{1,0:T(8,128)(2,1)S(1)}, u32[]{:S(2)}, u32[]{:S(2)}) collective-permute-start(bf16[32,4096]{1,0:T(8,128)(2,1)} %get-tuple-element.70), channel_id=1, source_target_pairs={{0,2},{2,0},{4,6},{6,4},{8,10},{10,8},{12,14},{14,12},{1,3},{3,1},... | collective-permute-start | bytes 786440 | tf_op jit(solution)/shard_map/ppermute | solution.py:34
  233.8 25.6 %collective-permute-start.9 = (bf16[32,4096]{1,0:T(8,128)(2,1)S(1)}, bf16[32,4096]{1,0:T(8,128)(2,1)S(1)}, u32[]{:S(2)}, u32[]{:S(2)}) collective-permute-start(bf16[32,4096]{1,0:T(8,128)(2,1)S(1)} %get-tuple-element.79), channel_id=1, source_target_pairs={{0,14},{2,12},{4,2},{6,0},{8,6},{10,4},{12,10},{14,8},{1,15},{3,13... | collective-permute-start | bytes 786440 | tf_op jit(solution)/shard_map/ppermute | solution.py:34
  233.9 26.6 %collective-permute-start.8 = (bf16[32,4096]{1,0:T(8,128)(2,1)S(1)}, bf16[32,4096]{1,0:T(8,128)(2,1)S(1)}, u32[]{:S(2)}, u32[]{:S(2)}) collective-permute-start(bf16[32,4096]{1,0:T(8,128)(2,1)S(1)} %get-tuple-element.80), channel_id=1, source_target_pairs={{0,12},{2,14},{4,0},{6,2},{8,4},{10,6},{12,8},{14,10},{1,13},{3,15... | collective-permute-start | bytes 786440 | tf_op jit(solution)/shard_map/ppermute | solution.py:34
  234.9 39.4 %collective-permute-start.7 = (bf16[32,4096]{1,0:T(8,128)(2,1)S(1)}, bf16[32,4096]{1,0:T(8,128)(2,1)S(1)}, u32[]{:S(2)}, u32[]{:S(2)}) collective-permute-start(bf16[32,4096]{1,0:T(8,128)(2,1)S(1)} %get-tuple-element.81), channel_id=1, source_target_pairs={{0,10},{2,8},{4,14},{6,12},{8,2},{10,0},{12,6},{14,4},{1,11},{3,9}... | collective-permute-start | bytes 786440 | tf_op jit(solution)/shard_map/ppermute | solution.py:34
  239.5 44.4 %collective-permute-start.6 = (bf16[32,4096]{1,0:T(8,128)(2,1)}, bf16[32,4096]{1,0:T(8,128)(2,1)}, u32[]{:S(2)}, u32[]{:S(2)}) collective-permute-start(bf16[32,4096]{1,0:T(8,128)(2,1)} %get-tuple-element.82), channel_id=1, source_target_pairs={{0,8},{2,10},{4,12},{6,14},{8,0},{10,2},{12,4},{14,6},{1,9},{3,11}... | collective-permute-start | bytes 786440 | tf_op jit(solution)/shard_map/ppermute | solution.py:34
  259.3 24.6 %collective-permute-start.5 = (bf16[32,4096]{1,0:T(8,128)(2,1)S(1)}, bf16[32,4096]{1,0:T(8,128)(2,1)}, u32[]{:S(2)}, u32[]{:S(2)}) collective-permute-start(bf16[32,4096]{1,0:T(8,128)(2,1)S(1)} %get-tuple-element.83), channel_id=1, source_target_pairs={{0,6},{2,4},{4,10},{6,8},{8,14},{10,12},{12,2},{14,0},{1,7},{3,5},... | collective-permute-start | bytes 786440 | tf_op jit(solution)/shard_map/ppermute | solution.py:34
  260.5 23.5 %collective-permute-start.4 = (bf16[32,4096]{1,0:T(8,128)(2,1)S(1)}, bf16[32,4096]{1,0:T(8,128)(2,1)}, u32[]{:S(2)}, u32[]{:S(2)}) collective-permute-start(bf16[32,4096]{1,0:T(8,128)(2,1)S(1)} %get-tuple-element.84), channel_id=1, source_target_pairs={{0,4},{2,6},{4,8},{6,10},{8,12},{10,14},{12,0},{14,2},{1,5},{3,7},... | collective-permute-start | bytes 786440 | tf_op jit(solution)/shard_map/ppermute | solution.py:34
  274.3 9.7 %collective-permute-start.3 = (bf16[32,4096]{1,0:T(8,128)(2,1)S(1)}, bf16[32,4096]{1,0:T(8,128)(2,1)}, u32[]{:S(2)}, u32[]{:S(2)}) collective-permute-start(bf16[32,4096]{1,0:T(8,128)(2,1)S(1)} %get-tuple-element.85), channel_id=1, source_target_pairs={{0,2},{2,0},{4,6},{6,4},{8,10},{10,8},{12,14},{14,12},{1,3},{3,1},... | collective-permute-start | bytes 786440 | tf_op jit(solution)/shard_map/ppermute | solution.py:34
  275.0 28.5 %collective-permute-start.28 = (bf16[8,32,4096]{2,1,0:T(8,128)(2,1)}, bf16[8,32,4096]{2,1,0:T(8,128)(2,1)}, u32[]{:S(2)}, u32[]{:S(2)}) collective-permute-start(bf16[8,32,4096]{2,1,0:T(8,128)(2,1)} %bitcast.155), channel_id=1, source_target_pairs={{0,1},{1,0},{2,3},{3,2},{4,5},{5,4},{6,7},{7,6},{8,9},{9,8},{10,11... | collective-permute-start | bytes 6291464 | tf_op jit(solution)/shard_map/ppermute | solution.py:22
  280.3 127.0 %all-to-all-start.1 = ((bf16[8,32,4096]{2,1,0:T(8,128)(2,1)}), bf16[8,32,4096]{2,1,0:T(8,128)(2,1)S(1)}, u32[]{:S(2)}, u32[]{:S(2)}) async-start(bf16[8,32,4096]{2,1,0:T(8,128)(2,1)} %multiply_convert_fusion.1), calls=%async_computation.1 | async-start | bytes 4194304 | tf_op jit(solution)/shard_map/all_to_all | solution.py:437
  303.0 14.4 %collective-permute-start.10 = (bf16[8,32,4096]{2,1,0:T(8,128)(2,1)}, bf16[8,32,4096]{2,1,0:T(8,128)(2,1)S(1)}, u32[]{:S(2)}, u32[]{:S(2)}) collective-permute-start(bf16[8,32,4096]{2,1,0:T(8,128)(2,1)} %bitcast.151), channel_id=1, source_target_pairs={{0,1},{1,0},{2,3},{3,2},{4,5},{5,4},{6,7},{7,6},{8,9},{9,8},{10,11... | collective-permute-start | bytes 6291464 | tf_op jit(solution)/shard_map/ppermute | solution.py:22
  305.4 19.4 %collective-permute-start.34 = (bf16[32,1024]{1,0:T(8,128)(2,1)S(1)}, bf16[32,1024]{1,0:T(8,128)(2,1)S(1)}, u32[]{:S(2)}, u32[]{:S(2)}) collective-permute-start(bf16[32,1024]{1,0:T(8,128)(2,1)S(1)} %get-tuple-element.57), channel_id=1, source_target_pairs={{0,4},{2,6},{4,8},{6,10},{8,12},{10,14},{12,0},{14,2},{1,5},{3,7},... | collective-permute-start | bytes 196616 | tf_op jit(solution)/shard_map/ppermute | solution.py:34
  307.0 33.0 %collective-permute-start.33 = (bf16[32,1024]{1,0:T(8,128)(2,1)S(1)}, bf16[32,1024]{1,0:T(8,128)(2,1)S(1)}, u32[]{:S(2)}, u32[]{:S(2)}) collective-permute-start(bf16[32,1024]{1,0:T(8,128)(2,1)S(1)} %get-tuple-element.58), channel_id=1, source_target_pairs={{0,10},{2,8},{4,14},{6,12},{8,2},{10,0},{12,6},{14,4},{1,11},{3,9}... | collective-permute-start | bytes 196616 | tf_op jit(solution)/shard_map/ppermute | solution.py:34
  310.3 31.9 %collective-permute-start.32 = (bf16[32,1024]{1,0:T(8,128)(2,1)S(1)}, bf16[32,1024]{1,0:T(8,128)(2,1)S(1)}, u32[]{:S(2)}, u32[]{:S(2)}) collective-permute-start(bf16[32,1024]{1,0:T(8,128)(2,1)S(1)} %get-tuple-element.59), channel_id=1, source_target_pairs={{0,8},{2,10},{4,12},{6,14},{8,0},{10,2},{12,4},{14,6},{1,9},{3,11}... | collective-permute-start | bytes 196616 | tf_op jit(solution)/shard_map/ppermute | solution.py:34
  310.8 33.8 %collective-permute-start.31 = (bf16[32,1024]{1,0:T(8,128)(2,1)S(1)}, bf16[32,1024]{1,0:T(8,128)(2,1)S(1)}, u32[]{:S(2)}, u32[]{:S(2)}) collective-permute-start(bf16[32,1024]{1,0:T(8,128)(2,1)S(1)} %get-tuple-element.60), channel_id=1, source_target_pairs={{0,14},{2,12},{4,2},{6,0},{8,6},{10,4},{12,10},{14,8},{1,15},{3,13... | collective-permute-start | bytes 196616 | tf_op jit(solution)/shard_map/ppermute | solution.py:34
  317.4 29.6 %collective-permute-start.30 = (bf16[32,1024]{1,0:T(8,128)(2,1)S(1)}, bf16[32,1024]{1,0:T(8,128)(2,1)S(1)}, u32[]{:S(2)}, u32[]{:S(2)}) collective-permute-start(bf16[32,1024]{1,0:T(8,128)(2,1)S(1)} %get-tuple-element.61), channel_id=1, source_target_pairs={{0,12},{2,14},{4,0},{6,2},{8,4},{10,6},{12,8},{14,10},{1,13},{3,15... | collective-permute-start | bytes 196616 | tf_op jit(solution)/shard_map/ppermute | solution.py:34
  324.8 22.3 %collective-permute-start.29 = (bf16[32,1024]{1,0:T(8,128)(2,1)S(1)}, bf16[32,1024]{1,0:T(8,128)(2,1)S(1)}, u32[]{:S(2)}, u32[]{:S(2)}) collective-permute-start(bf16[32,1024]{1,0:T(8,128)(2,1)S(1)} %get-tuple-element.62), channel_id=1, source_target_pairs={{0,2},{2,0},{4,6},{6,4},{8,10},{10,8},{12,14},{14,12},{1,3},{3,1},... | collective-permute-start | bytes 196616 | tf_op jit(solution)/shard_map/ppermute | solution.py:34
  340.0 9.9 %collective-permute-start.49 = (bf16[32,1024]{1,0:T(8,128)(2,1)S(1)}, bf16[32,1024]{1,0:T(8,128)(2,1)S(1)}, u32[]{:S(2)}, u32[]{:S(2)}) collective-permute-start(bf16[32,1024]{1,0:T(8,128)(2,1)S(1)} %get-tuple-element.39), channel_id=1, source_target_pairs={{0,6},{2,4},{4,10},{6,8},{8,14},{10,12},{12,2},{14,0},{1,7},{3,5},... | collective-permute-start | bytes 196616 | tf_op jit(solution)/shard_map/ppermute | solution.py:34
  342.2 9.7 %collective-permute-start.48 = (bf16[32,1024]{1,0:T(8,128)(2,1)S(1)}, bf16[32,1024]{1,0:T(8,128)(2,1)S(1)}, u32[]{:S(2)}, u32[]{:S(2)}) collective-permute-start(bf16[32,1024]{1,0:T(8,128)(2,1)S(1)} %get-tuple-element.40), channel_id=1, source_target_pairs={{0,4},{2,6},{4,8},{6,10},{8,12},{10,14},{12,0},{14,2},{1,5},{3,7},... | collective-permute-start | bytes 196616 | tf_op jit(solution)/shard_map/ppermute | solution.py:34
  344.7 11.1 %collective-permute-start.63 = (bf16[32,2048]{1,0:T(8,128)(2,1)S(1)}, bf16[32,2048]{1,0:T(8,128)(2,1)S(1)}, u32[]{:S(2)}, u32[]{:S(2)}) collective-permute-start(bf16[32,2048]{1,0:T(8,128)(2,1)S(1)} %get-tuple-element.23), channel_id=1, source_target_pairs={{0,6},{2,4},{4,10},{6,8},{8,14},{10,12},{12,2},{14,0},{1,7},{3,5},... | collective-permute-start | bytes 393224 | tf_op jit(solution)/shard_map/ppermute | solution.py:34
  347.1 16.7 %collective-permute-start.61 = (bf16[32,2048]{1,0:T(8,128)(2,1)S(1)}, bf16[32,2048]{1,0:T(8,128)(2,1)S(1)}, u32[]{:S(2)}, u32[]{:S(2)}) collective-permute-start(bf16[32,2048]{1,0:T(8,128)(2,1)S(1)} %get-tuple-element.25), channel_id=1, source_target_pairs={{0,10},{2,8},{4,14},{6,12},{8,2},{10,0},{12,6},{14,4},{1,11},{3,9}... | collective-permute-start | bytes 393224 | tf_op jit(solution)/shard_map/ppermute | solution.py:34
  350.0 19.2 %collective-permute-start.60 = (bf16[32,2048]{1,0:T(8,128)(2,1)S(1)}, bf16[32,2048]{1,0:T(8,128)(2,1)S(1)}, u32[]{:S(2)}, u32[]{:S(2)}) collective-permute-start(bf16[32,2048]{1,0:T(8,128)(2,1)S(1)} %get-tuple-element.26), channel_id=1, source_target_pairs={{0,8},{2,10},{4,12},{6,14},{8,0},{10,2},{12,4},{14,6},{1,9},{3,11}... | collective-permute-start | bytes 393224 | tf_op jit(solution)/shard_map/ppermute | solution.py:34
  351.9 20.9 %collective-permute-start.59 = (bf16[32,2048]{1,0:T(8,128)(2,1)S(1)}, bf16[32,2048]{1,0:T(8,128)(2,1)S(1)}, u32[]{:S(2)}, u32[]{:S(2)}) collective-permute-start(bf16[32,2048]{1,0:T(8,128)(2,1)S(1)} %get-tuple-element.27), channel_id=1, source_target_pairs={{0,14},{2,12},{4,2},{6,0},{8,6},{10,4},{12,10},{14,8},{1,15},{3,13... | collective-permute-start | bytes 393224 | tf_op jit(solution)/shard_map/ppermute | solution.py:34
  355.7 20.6 %collective-permute-start.58 = (bf16[32,2048]{1,0:T(8,128)(2,1)S(1)}, bf16[32,2048]{1,0:T(8,128)(2,1)S(1)}, u32[]{:S(2)}, u32[]{:S(2)}) collective-permute-start(bf16[32,2048]{1,0:T(8,128)(2,1)S(1)} %get-tuple-element.28), channel_id=1, source_target_pairs={{0,12},{2,14},{4,0},{6,2},{8,4},{10,6},{12,8},{14,10},{1,13},{3,15... | collective-permute-start | bytes 393224 | tf_op jit(solution)/shard_map/ppermute | solution.py:34
  355.8 20.6 %collective-permute-start.57 = (bf16[32,2048]{1,0:T(8,128)(2,1)S(1)}, bf16[32,2048]{1,0:T(8,128)(2,1)S(1)}, u32[]{:S(2)}, u32[]{:S(2)}) collective-permute-start(bf16[32,2048]{1,0:T(8,128)(2,1)S(1)} %get-tuple-element.29), channel_id=1, source_target_pairs={{0,2},{2,0},{4,6},{6,4},{8,10},{10,8},{12,14},{14,12},{1,3},{3,1},... | collective-permute-start | bytes 393224 | tf_op jit(solution)/shard_map/ppermute | solution.py:34
  363.8 15.8 %collective-permute-start.56 = (bf16[32,2048]{1,0:T(8,128)(2,1)S(1)}, bf16[32,2048]{1,0:T(8,128)(2,1)S(1)}, u32[]{:S(2)}, u32[]{:S(2)}) collective-permute-start(bf16[32,2048]{1,0:T(8,128)(2,1)S(1)} %get-tuple-element.31), channel_id=1, source_target_pairs={{0,6},{2,4},{4,10},{6,8},{8,14},{10,12},{12,2},{14,0},{1,7},{3,5},... | collective-permute-start | bytes 393224 | tf_op jit(solution)/shard_map/ppermute | solution.py:34
  369.2 12.4 %collective-permute-start.55 = (bf16[32,2048]{1,0:T(8,128)(2,1)S(1)}, bf16[32,2048]{1,0:T(8,128)(2,1)S(1)}, u32[]{:S(2)}, u32[]{:S(2)}) collective-permute-start(bf16[32,2048]{1,0:T(8,128)(2,1)S(1)} %get-tuple-element.32), channel_id=1, source_target_pairs={{0,4},{2,6},{4,8},{6,10},{8,12},{10,14},{12,0},{14,2},{1,5},{3,7},... | collective-permute-start | bytes 393224 | tf_op jit(solution)/shard_map/ppermute | solution.py:34
  372.8 18.3 %collective-permute-start.54 = (bf16[32,2048]{1,0:T(8,128)(2,1)S(1)}, bf16[32,2048]{1,0:T(8,128)(2,1)S(1)}, u32[]{:S(2)}, u32[]{:S(2)}) collective-permute-start(bf16[32,2048]{1,0:T(8,128)(2,1)S(1)} %get-tuple-element.33), channel_id=1, source_target_pairs={{0,10},{2,8},{4,14},{6,12},{8,2},{10,0},{12,6},{14,4},{1,11},{3,9}... | collective-permute-start | bytes 393224 | tf_op jit(solution)/shard_map/ppermute | solution.py:34
  376.3 25.2 %collective-permute-start.53 = (bf16[32,2048]{1,0:T(8,128)(2,1)S(1)}, bf16[32,2048]{1,0:T(8,128)(2,1)S(1)}, u32[]{:S(2)}, u32[]{:S(2)}) collective-permute-start(bf16[32,2048]{1,0:T(8,128)(2,1)S(1)} %get-tuple-element.34), channel_id=1, source_target_pairs={{0,8},{2,10},{4,12},{6,14},{8,0},{10,2},{12,4},{14,6},{1,9},{3,11}... | collective-permute-start | bytes 393224 | tf_op jit(solution)/shard_map/ppermute | solution.py:34
  376.3 25.1 %collective-permute-start.52 = (bf16[32,2048]{1,0:T(8,128)(2,1)S(1)}, bf16[32,2048]{1,0:T(8,128)(2,1)S(1)}, u32[]{:S(2)}, u32[]{:S(2)}) collective-permute-start(bf16[32,2048]{1,0:T(8,128)(2,1)S(1)} %get-tuple-element.35), channel_id=1, source_target_pairs={{0,14},{2,12},{4,2},{6,0},{8,6},{10,4},{12,10},{14,8},{1,15},{3,13... | collective-permute-start | bytes 393224 | tf_op jit(solution)/shard_map/ppermute | solution.py:34
  379.5 22.5 %collective-permute-start.51 = (bf16[32,2048]{1,0:T(8,128)(2,1)S(1)}, bf16[32,2048]{1,0:T(8,128)(2,1)S(1)}, u32[]{:S(2)}, u32[]{:S(2)}) collective-permute-start(bf16[32,2048]{1,0:T(8,128)(2,1)S(1)} %get-tuple-element.36), channel_id=1, source_target_pairs={{0,12},{2,14},{4,0},{6,2},{8,4},{10,6},{12,8},{14,10},{1,13},{3,15... | collective-permute-start | bytes 393224 | tf_op jit(solution)/shard_map/ppermute | solution.py:34
  381.6 24.4 %collective-permute-start.50 = (bf16[32,2048]{1,0:T(8,128)(2,1)S(1)}, bf16[32,2048]{1,0:T(8,128)(2,1)S(1)}, u32[]{:S(2)}, u32[]{:S(2)}) collective-permute-start(bf16[32,2048]{1,0:T(8,128)(2,1)S(1)} %get-tuple-element.37), channel_id=1, source_target_pairs={{0,2},{2,0},{4,6},{6,4},{8,10},{10,8},{12,14},{14,12},{1,3},{3,1},... | collective-permute-start | bytes 393224 | tf_op jit(solution)/shard_map/ppermute | solution.py:34
  391.1 25.9 %collective-permute-start.47 = (bf16[32,1024]{1,0:T(8,128)(2,1)}, bf16[32,1024]{1,0:T(8,128)(2,1)S(1)}, u32[]{:S(2)}, u32[]{:S(2)}) collective-permute-start(bf16[32,1024]{1,0:T(8,128)(2,1)} %get-tuple-element.41), channel_id=1, source_target_pairs={{0,10},{2,8},{4,14},{6,12},{8,2},{10,0},{12,6},{14,4},{1,11},{3,9}... | collective-permute-start | bytes 196616 | tf_op jit(solution)/shard_map/ppermute | solution.py:34
  401.5 15.6 %collective-permute-start.46 = (bf16[32,1024]{1,0:T(8,128)(2,1)}, bf16[32,1024]{1,0:T(8,128)(2,1)S(1)}, u32[]{:S(2)}, u32[]{:S(2)}) collective-permute-start(bf16[32,1024]{1,0:T(8,128)(2,1)} %get-tuple-element.42), channel_id=1, source_target_pairs={{0,8},{2,10},{4,12},{6,14},{8,0},{10,2},{12,4},{14,6},{1,9},{3,11}... | collective-permute-start | bytes 196616 | tf_op jit(solution)/shard_map/ppermute | solution.py:34
  401.5 15.7 %collective-permute-start.45 = (bf16[32,1024]{1,0:T(8,128)(2,1)}, bf16[32,1024]{1,0:T(8,128)(2,1)S(1)}, u32[]{:S(2)}, u32[]{:S(2)}) collective-permute-start(bf16[32,1024]{1,0:T(8,128)(2,1)} %get-tuple-element.43), channel_id=1, source_target_pairs={{0,14},{2,12},{4,2},{6,0},{8,6},{10,4},{12,10},{14,8},{1,15},{3,13... | collective-permute-start | bytes 196616 | tf_op jit(solution)/shard_map/ppermute | solution.py:34
  402.1 20.4 %collective-permute-start.44 = (bf16[32,1024]{1,0:T(8,128)(2,1)}, bf16[32,1024]{1,0:T(8,128)(2,1)S(1)}, u32[]{:S(2)}, u32[]{:S(2)}) collective-permute-start(bf16[32,1024]{1,0:T(8,128)(2,1)} %get-tuple-element.44), channel_id=1, source_target_pairs={{0,12},{2,14},{4,0},{6,2},{8,4},{10,6},{12,8},{14,10},{1,13},{3,15... | collective-permute-start | bytes 196616 | tf_op jit(solution)/shard_map/ppermute | solution.py:34
  406.0 16.7 %collective-permute-start.43 = (bf16[32,1024]{1,0:T(8,128)(2,1)}, bf16[32,1024]{1,0:T(8,128)(2,1)S(1)}, u32[]{:S(2)}, u32[]{:S(2)}) collective-permute-start(bf16[32,1024]{1,0:T(8,128)(2,1)} %get-tuple-element.45), channel_id=1, source_target_pairs={{0,2},{2,0},{4,6},{6,4},{8,10},{10,8},{12,14},{14,12},{1,3},{3,1},... | collective-permute-start | bytes 196616 | tf_op jit(solution)/shard_map/ppermute | solution.py:34
  417.0 12.4 %collective-permute-start.35 = (bf16[32,1024]{1,0:T(8,128)(2,1)S(1)}, bf16[32,1024]{1,0:T(8,128)(2,1)S(1)}, u32[]{:S(2)}, u32[]{:S(2)}) collective-permute-start(bf16[32,1024]{1,0:T(8,128)(2,1)S(1)} %copy-done.62), channel_id=1, source_target_pairs={{0,6},{2,4},{4,10},{6,8},{8,14},{10,12},{12,2},{14,0},{1,7},{3,5},... | collective-permute-start | bytes 196616 | tf_op jit(solution)/shard_map/ppermute | solution.py:34
  417.1 17.1 %collective-permute-start.16 = (bf16[32,1024]{1,0:T(8,128)(2,1)S(1)}, bf16[32,1024]{1,0:T(8,128)(2,1)S(1)}, u32[]{:S(2)}, u32[]{:S(2)}) collective-permute-start(bf16[32,1024]{1,0:T(8,128)(2,1)S(1)} %copy-done.59), channel_id=1, source_target_pairs={{0,4},{2,6},{4,8},{6,10},{8,12},{10,14},{12,0},{14,2},{1,5},{3,7},... | collective-permute-start | bytes 196616 | tf_op jit(solution)/shard_map/ppermute | solution.py:34
  417.2 17.1 %collective-permute-start.15 = (bf16[32,1024]{1,0:T(8,128)(2,1)S(1)}, bf16[32,1024]{1,0:T(8,128)(2,1)S(1)}, u32[]{:S(2)}, u32[]{:S(2)}) collective-permute-start(bf16[32,1024]{1,0:T(8,128)(2,1)S(1)} %copy-done.58), channel_id=1, source_target_pairs={{0,10},{2,8},{4,14},{6,12},{8,2},{10,0},{12,6},{14,4},{1,11},{3,9}... | collective-permute-start | bytes 196616 | tf_op jit(solution)/shard_map/ppermute | solution.py:34
  422.5 14.5 %collective-permute-start.42 = (bf16[32,1024]{1,0:T(8,128)(2,1)S(1)}, bf16[32,1024]{1,0:T(8,128)(2,1)S(1)}, u32[]{:S(2)}, u32[]{:S(2)}) collective-permute-start(bf16[32,1024]{1,0:T(8,128)(2,1)S(1)} %copy-done.68), channel_id=1, source_target_pairs={{0,6},{2,4},{4,10},{6,8},{8,14},{10,12},{12,2},{14,0},{1,7},{3,5},... | collective-permute-start | bytes 196616 | tf_op jit(solution)/shard_map/ppermute | solution.py:34
  422.7 16.2 %collective-permute-start.41 = (bf16[32,1024]{1,0:T(8,128)(2,1)S(1)}, bf16[32,1024]{1,0:T(8,128)(2,1)S(1)}, u32[]{:S(2)}, u32[]{:S(2)}) collective-permute-start(bf16[32,1024]{1,0:T(8,128)(2,1)S(1)} %copy-done.67), channel_id=1, source_target_pairs={{0,4},{2,6},{4,8},{6,10},{8,12},{10,14},{12,0},{14,2},{1,5},{3,7},... | collective-permute-start | bytes 196616 | tf_op jit(solution)/shard_map/ppermute | solution.py:34
  429.5 16.8 %collective-permute-start.40 = (bf16[32,1024]{1,0:T(8,128)(2,1)S(1)}, bf16[32,1024]{1,0:T(8,128)(2,1)S(1)}, u32[]{:S(2)}, u32[]{:S(2)}) collective-permute-start(bf16[32,1024]{1,0:T(8,128)(2,1)S(1)} %copy-done.66), channel_id=1, source_target_pairs={{0,10},{2,8},{4,14},{6,12},{8,2},{10,0},{12,6},{14,4},{1,11},{3,9}... | collective-permute-start | bytes 196616 | tf_op jit(solution)/shard_map/ppermute | solution.py:34
  434.2 12.1 %collective-permute-start.39 = (bf16[32,1024]{1,0:T(8,128)(2,1)S(1)}, bf16[32,1024]{1,0:T(8,128)(2,1)S(1)}, u32[]{:S(2)}, u32[]{:S(2)}) collective-permute-start(bf16[32,1024]{1,0:T(8,128)(2,1)S(1)} %copy-done.65), channel_id=1, source_target_pairs={{0,8},{2,10},{4,12},{6,14},{8,0},{10,2},{12,4},{14,6},{1,9},{3,11}... | collective-permute-start | bytes 196616 | tf_op jit(solution)/shard_map/ppermute | solution.py:34
  434.3 14.7 %collective-permute-start.38 = (bf16[32,1024]{1,0:T(8,128)(2,1)S(1)}, bf16[32,1024]{1,0:T(8,128)(2,1)S(1)}, u32[]{:S(2)}, u32[]{:S(2)}) collective-permute-start(bf16[32,1024]{1,0:T(8,128)(2,1)S(1)} %copy-done.64), channel_id=1, source_target_pairs={{0,14},{2,12},{4,2},{6,0},{8,6},{10,4},{12,10},{14,8},{1,15},{3,13... | collective-permute-start | bytes 196616 | tf_op jit(solution)/shard_map/ppermute | solution.py:34
  437.0 13.9 %collective-permute-start.37 = (bf16[32,1024]{1,0:T(8,128)(2,1)S(1)}, bf16[32,1024]{1,0:T(8,128)(2,1)S(1)}, u32[]{:S(2)}, u32[]{:S(2)}) collective-permute-start(bf16[32,1024]{1,0:T(8,128)(2,1)S(1)} %copy-done.63), channel_id=1, source_target_pairs={{0,12},{2,14},{4,0},{6,2},{8,4},{10,6},{12,8},{14,10},{1,13},{3,15... | collective-permute-start | bytes 196616 | tf_op jit(solution)/shard_map/ppermute | solution.py:34
  438.9 13.4 %collective-permute-start.36 = (bf16[32,1024]{1,0:T(8,128)(2,1)S(1)}, bf16[32,1024]{1,0:T(8,128)(2,1)S(1)}, u32[]{:S(2)}, u32[]{:S(2)}) collective-permute-start(bf16[32,1024]{1,0:T(8,128)(2,1)S(1)} %copy-done.61), channel_id=1, source_target_pairs={{0,2},{2,0},{4,6},{6,4},{8,10},{10,8},{12,14},{14,12},{1,3},{3,1},... | collective-permute-start | bytes 196616 | tf_op jit(solution)/shard_map/ppermute | solution.py:34
  446.3 12.0 %collective-permute-start.14 = (bf16[32,1024]{1,0:T(8,128)(2,1)S(1)}, bf16[32,1024]{1,0:T(8,128)(2,1)S(1)}, u32[]{:S(2)}, u32[]{:S(2)}) collective-permute-start(bf16[32,1024]{1,0:T(8,128)(2,1)S(1)} %copy-done.57), channel_id=1, source_target_pairs={{0,8},{2,10},{4,12},{6,14},{8,0},{10,2},{12,4},{14,6},{1,9},{3,11}... | collective-permute-start | bytes 196616 | tf_op jit(solution)/shard_map/ppermute | solution.py:34
  446.4 12.0 %collective-permute-start.13 = (bf16[32,1024]{1,0:T(8,128)(2,1)S(1)}, bf16[32,1024]{1,0:T(8,128)(2,1)S(1)}, u32[]{:S(2)}, u32[]{:S(2)}) collective-permute-start(bf16[32,1024]{1,0:T(8,128)(2,1)S(1)} %copy-done.56), channel_id=1, source_target_pairs={{0,14},{2,12},{4,2},{6,0},{8,6},{10,4},{12,10},{14,8},{1,15},{3,13... | collective-permute-start | bytes 196616 | tf_op jit(solution)/shard_map/ppermute | solution.py:34
  449.1 9.3 %collective-permute-start.12 = (bf16[32,1024]{1,0:T(8,128)(2,1)S(1)}, bf16[32,1024]{1,0:T(8,128)(2,1)S(1)}, u32[]{:S(2)}, u32[]{:S(2)}) collective-permute-start(bf16[32,1024]{1,0:T(8,128)(2,1)S(1)} %copy-done.55), channel_id=1, source_target_pairs={{0,12},{2,14},{4,0},{6,2},{8,4},{10,6},{12,8},{14,10},{1,13},{3,15... | collective-permute-start | bytes 196616 | tf_op jit(solution)/shard_map/ppermute | solution.py:34
  (82 other events, 1057.4 us)

commit v6 on v5

--- a/solution.py
+++ b/solution.py
@@ -500,7 +500,9 @@
 
     half, fourth = local_levels // 2, local_levels // 4
     groups = [(0, half), (half, fourth), (half + fourth, fourth)]
-    cuts = {chunk: groups if chunk in (1, chunks - 1) else [(0, local_levels)] for chunk in range(chunks)}
+    cuts = {chunk: [(0, local_levels)] for chunk in range(chunks)}
+    cuts[1] = [(0, half), (half, half)]
+    cuts[chunks - 1] = groups
     returned = []
     for chunk in range(chunks):
         is_whole = chunk in WHOLE_CHUNKS
@@ -539,7 +541,7 @@
     shape = grid_state.shape
     everything = list(range(chunks))
     partials = []
-    for start, levels in groups:
+    for start, levels in cuts[1]:
         partials.append(
             inverse_fourier(
                 pieces_at(everything[:2], start),
@@ -551,7 +553,7 @@
             )
         )
     current = None
-    for cut, (start, levels) in enumerate(groups):
+    for start, levels in groups:
         current = inverse_fourier(
             pieces_at(everything[2:], start),
             tables[2:],
@@ -559,7 +561,7 @@
             start,
             levels,
             current=current,
-            partial=(partials[cut], start),
+            partial=(partials[0], 0) if start < half else (partials[1], half),
         )
     return current.reshape(out_shape)
 

time: 467 us -> 540 us (1.16)
  waiting for transfers between devices: 103 us -> 190 us
  starting transfers between devices: 163 us -> 152 us
    ppermute x56 -> x49, waiting for transfers between devices: 54.3 us -> 110 us  [shift_places(): return lax.ppermute(value, EXCHANGE_AXES, pairs)]
    all_to_all x4, waiting for transfers between devices: 48.6 us -> 80.4 us  [exchange(): lax.all_to_all(value, EXCHANGE_AXES, split_axis=0, concat_axis=0, tiled=T...]
    ppermute x56 -> x49, starting transfers between devices: 142 us -> 131 us  [shift_places(): return lax.ppermute(value, EXCHANGE_AXES, pairs)]
    pallas_call x6 -> x5, Pallas kernels: 39.6 us -> 36.5 us  [inverse_fourier(): pl.pallas_call(functools.partial(inverse_kernel, len(pieces), len(tables)...]
    mul x6 -> x5, other arithmetic: 9.18 us -> 11.3 us  [joined(): scale * (other.astype(jnp.float32) + hemi_sign * own.astype(jnp.float32))]
  transfers between devices with their start and end apart: 68 -> 61, of which waited for: 10 -> 12; matrix products, arithmetic and copies ran while one was open for 7% -> 6% of each run, Pallas kernels for 31% -> 26%
where the time goes in v6:
time: 540 us; the launch traced here: 539 us
  waiting for transfers between devices  190 us (35%)
  Pallas kernels  157 us (29%)
  starting transfers between devices  152 us (28%)
  other arithmetic  29.7 us (6%)
  local copies, waits for them, and re-layouts  9.62 us (2%)
    ppermute x49, starting transfers between devices, shift_places(): return lax.ppermute(value, EXCHANGE_AXES, pairs)  131 us
    ppermute x49, waiting for transfers between devices, shift_places(): return lax.ppermute(value, EXCHANGE_AXES, pairs)  110 us
    all_to_all x4, waiting for transfers between devices, exchange(): lax.all_to_all(value, EXCHANGE_AXES, split_axis=0, concat_axis=0, tiled=T...  80.4 us
    pallas_call x4, Pallas kernels, columns_fused(): pl.pallas_call(functools.partial(column_kernel, sizes), out_shape=jax.Sha...  79.3 us
    pallas_call x4, Pallas kernels, fourier(): pl.pallas_call(functools.partial(fourier_kernel, sizes), out_shape=[jax.S...  41.4 us
    pallas_call x5, Pallas kernels, inverse_fourier(): pl.pallas_call(functools.partial(inverse_kernel, len(pieces), len(tables)...  36.5 us
    all_to_all x4, starting transfers between devices, exchange(): lax.all_to_all(value, EXCHANGE_AXES, split_axis=0, concat_axis=0, tiled=T...  19 us
    convert_element_type x4, other arithmetic, joined(): return both.astype(jnp.bfloat16)  13.7 us
  transfers between devices with their start and end apart: 61, of which 12 were waited for; matrix products, arithmetic and copies ran while one was open for 6% of the time, Pallas kernels for 26%

profile of v6, /device:TPU:0, one launch (start us, length us, event | category | flops | bytes accessed | tf_op | source)
XLA Modules:
  0.0 539.0 jit_solution(14241268546179316635)
XLA Ops:
  0.6 10.3 %shard_map.77 = (bf16[256,4096]{1,0:T(8,128)(2,1)}, bf16[256,1536]{1,0:T(8,128)(2,1)}) custom-call(s32[3]{0:T(128)} %pad_add_fusion.1.place_ref, bf16[64,64,1536]{2,1,0:T(8,128)(2,1)} %bitcast.121, s32[1,512]{1,0:T(1,128)} %bitcast.155, s32[1,256]{1,0:T(1,128)} %bitcast.159), custom_call_target="tpu_custom_call" | custom-call | flops 3221225472 | bytes 15466496 | tf_op jit(solution)/shard_map/pallas_call | solution.py:118
  10.9 7.3 %all-to-all-start.2 = ((bf16[8,2,16,4096]{3,2,1,0:T(8,128)(2,1)}), bf16[8,2,16,4096]{3,2,1,0:T(8,128)(2,1)S(1)}, u32[]{:S(2)}, u32[]{:S(2)}) async-start(bf16[8,2,16,4096]{3,2,1,0:T(8,128)(2,1)} %bitcast.142), calls=%async_computation.2 | async-start | bytes 4194304 | tf_op jit(solution)/shard_map/all_to_all | solution.py:437
  18.2 10.2 %shard_map.73 = (bf16[256,4096]{1,0:T(8,128)(2,1)}, bf16[256,1536]{1,0:T(8,128)(2,1)}) custom-call(s32[3]{0:T(128)} %pad_add_fusion.1.place_ref, bf16[64,64,1536]{2,1,0:T(8,128)(2,1)} %bitcast.122, s32[1,512]{1,0:T(1,128)} %bitcast.156, s32[1,256]{1,0:T(1,128)} %bitcast.160), custom_call_target="tpu_custom_call" | custom-call | flops 3221225472 | bytes 15466496 | tf_op jit(solution)/shard_map/pallas_call | solution.py:118
  28.4 38.0 %all-to-all-done.2.refs_0_ = bf16[8,2,16,4096]{3,2,1,0:T(8,128)(2,1)S(1)} async-done(((bf16[8,2,16,4096]{3,2,1,0:T(8,128)(2,1)}), bf16[8,2,16,4096]{3,2,1,0:T(8,128)(2,1)S(1)}, u32[]{:S(2)}, u32[]{:S(2)}) %all-to-all-start.2) | async-done | bytes 2097184 | tf_op jit(solution)/shard_map/all_to_all | solution.py:437
  67.7 3.8 all-to-all-start
  77.5 42.3 %all-to-all-done.refs_0_ = bf16[8,2,16,4096]{3,2,1,0:T(8,128)(2,1)S(1)} async-done(((bf16[8,2,16,4096]{3,2,1,0:T(8,128)(2,1)}), bf16[8,2,16,4096]{3,2,1,0:T(8,128)(2,1)S(1)}, u32[]{:S(2)}, u32[]{:S(2)}) %all-to-all-start) | async-done | bytes 2097184 | tf_op jit(solution)/shard_map/all_to_all | solution.py:437
  119.9 21.0 %shard_map.78 = bf16[8,2,16,4096]{3,2,1,0:T(8,128)(2,1)} custom-call(s32[64]{0:T(128)} %dynamic_slice.3.waves, s32[5]{0:T(128)} %pad_add_fusion.scalars, f32[128,1]{1,0:T(8,128)} %copy.12.eig_ref, bf16[128,128]{1,0:T(8,128)(2,1)} %select_bitcast_fusion.1.modes_in, bf16[128,128]{1,0:T(8,128)(2,1)} %broadcast_select_fusion.1.modes_out, ...), custom_call_target="tpu_custom_call" | custom-call | flops 1610612736 | bytes 6291456 | tf_op jit(solution)/shard_map/pallas_call | solution.py:356
  140.8 10.4 %shard_map.79 = (bf16[256,4096]{1,0:T(8,128)(2,1)}, bf16[256,1536]{1,0:T(8,128)(2,1)}) custom-call(s32[3]{0:T(128)} %pad_add_fusion.1.place_ref, bf16[64,64,1536]{2,1,0:T(8,128)(2,1)} %bitcast.123, s32[1,512]{1,0:T(1,128)} %bitcast.157, s32[1,256]{1,0:T(1,128)} %bitcast.161), custom_call_target="tpu_custom_call" | custom-call | flops 3221225472 | bytes 15466496 | tf_op jit(solution)/shard_map/pallas_call | solution.py:118
  151.8 10.4 %shard_map.75 = (bf16[256,4096]{1,0:T(8,128)(2,1)}, bf16[256,1536]{1,0:T(8,128)(2,1)}) custom-call(s32[3]{0:T(128)} %pad_add_fusion.1.place_ref, bf16[64,64,1536]{2,1,0:T(8,128)(2,1)} %bitcast.124, s32[1,512]{1,0:T(1,128)} %bitcast.158, s32[1,256]{1,0:T(1,128)} %bitcast.162), custom_call_target="tpu_custom_call" | custom-call | flops 3221225472 | bytes 15466496 | tf_op jit(solution)/shard_map/pallas_call | solution.py:118
  162.5 20.4 %shard_map.74 = bf16[8,2,16,4096]{3,2,1,0:T(8,128)(2,1)} custom-call(s32[64]{0:T(128)} %dynamic_slice.3.waves, s32[5]{0:T(128)} %pad_add_fusion.scalars, f32[128,1]{1,0:T(8,128)} %copy.12.eig_ref, bf16[128,128]{1,0:T(8,128)(2,1)} %select_bitcast_fusion.1.modes_in, bf16[128,128]{1,0:T(8,128)(2,1)} %broadcast_select_fusion.1.modes_out, ...), custom_call_target="tpu_custom_call" | custom-call | flops 1610612736 | bytes 6291456 | tf_op jit(solution)/shard_map/pallas_call | solution.py:356
  183.3 3.9 multiply_convert_fusion
  187.3 4.4 all-to-all-start.3
  191.7 3.7 add_convert_fusion
  195.4 4.6 collective-permute-start.27
  202.0 2.9 collective-permute-start.24
  204.9 28.6 %collective-permute-done.27 = bf16[32,4096]{1,0:T(8,128)(2,1)S(1)} collective-permute-done((bf16[32,4096]{1,0:T(8,128)(2,1)}, bf16[32,4096]{1,0:T(8,128)(2,1)S(1)}, u32[]{:S(2)}, u32[]{:S(2)}) %collective-permute-start.27) | collective-permute-done | bytes 262176 | tf_op jit(solution)/shard_map/ppermute | solution.py:34
  233.6 31.6 %collective-permute-start.23 = (bf16[32,4096]{1,0:T(8,128)(2,1)}, bf16[32,4096]{1,0:T(8,128)(2,1)}, u32[]{:S(2)}, u32[]{:S(2)}) collective-permute-start(bf16[32,4096]{1,0:T(8,128)(2,1)} %get-tuple-element.60), channel_id=1, source_target_pairs={{0,6},{2,4},{4,10},{6,8},{8,14},{10,12},{12,2},{14,0},{1,7},{3,5},... | collective-permute-start | bytes 786440 | tf_op jit(solution)/shard_map/ppermute | solution.py:34
  265.1 10.3 %collective-permute-start.22 = (bf16[32,4096]{1,0:T(8,128)(2,1)}, bf16[32,4096]{1,0:T(8,128)(2,1)}, u32[]{:S(2)}, u32[]{:S(2)}) collective-permute-start(bf16[32,4096]{1,0:T(8,128)(2,1)} %get-tuple-element.61), channel_id=1, source_target_pairs={{0,4},{2,6},{4,8},{6,10},{8,12},{10,14},{12,0},{14,2},{1,5},{3,7},... | collective-permute-start | bytes 786440 | tf_op jit(solution)/shard_map/ppermute | solution.py:34
  275.5 3.7 add_convert_fusion.8
  279.2 2.2 collective-permute-done.25
  282.0 3.3 collective-permute-done.24
  285.3 2.0 collective-permute-start.8
  287.3 2.4 collective-permute-start.7
  291.7 3.9 collective-permute-done.9
  295.6 5.8 %collective-permute-done.8 = bf16[32,4096]{1,0:T(8,128)(2,1)S(1)} collective-permute-done((bf16[32,4096]{1,0:T(8,128)(2,1)}, bf16[32,4096]{1,0:T(8,128)(2,1)S(1)}, u32[]{:S(2)}, u32[]{:S(2)}) %collective-permute-start.8) | collective-permute-done | bytes 262176 | tf_op jit(solution)/shard_map/ppermute | solution.py:34
  301.4 25.6 %collective-permute-done.7 = bf16[32,4096]{1,0:T(8,128)(2,1)} collective-permute-done((bf16[32,4096]{1,0:T(8,128)(2,1)}, bf16[32,4096]{1,0:T(8,128)(2,1)}, u32[]{:S(2)}, u32[]{:S(2)}) %collective-permute-start.7) | collective-permute-done | bytes 262176 | tf_op jit(solution)/shard_map/ppermute | solution.py:34
  328.2 18.9 %shard_map.80 = bf16[8,2,16,4096]{3,2,1,0:T(8,128)(2,1)} custom-call(s32[64]{0:T(128)} %dynamic_slice.3.waves, s32[5]{0:T(128)} %pad_add_fusion.2.scalars, f32[128,1]{1,0:T(8,128)} %copy.12.eig_ref, bf16[128,128]{1,0:T(8,128)(2,1)} %select_bitcast_fusion.modes_in, bf16[128,128]{1,0:T(8,128)(2,1)} %broadcast_select_fusion.modes_out, ...), custom_call_target="tpu_custom_call" | custom-call | flops 1610612736 | bytes 6291456 | tf_op jit(solution)/shard_map/pallas_call | solution.py:356
  348.2 19.0 %shard_map.76 = bf16[8,2,16,4096]{3,2,1,0:T(8,128)(2,1)} custom-call(s32[64]{0:T(128)} %dynamic_slice.3.waves, s32[5]{0:T(128)} %pad_add_fusion.2.scalars, f32[128,1]{1,0:T(8,128)} %copy.12.eig_ref, bf16[128,128]{1,0:T(8,128)(2,1)} %select_bitcast_fusion.modes_in, bf16[128,128]{1,0:T(8,128)(2,1)} %broadcast_select_fusion.modes_out, ...), custom_call_target="tpu_custom_call" | custom-call | flops 1610612736 | bytes 6291456 | tf_op jit(solution)/shard_map/pallas_call | solution.py:356
  367.7 2.3 multiply_convert_fusion.1
  370.0 3.6 all-to-all-start.1
  373.7 2.7 fusion.6
  376.3 1.9 collective-permute-start.34
  378.2 1.9 fusion.30
  380.1 1.5 collective-permute-start.16
  381.6 2.4 collective-permute-start.15
  384.0 2.0 fusion.39
  386.0 1.4 collective-permute-start.42
  388.0 29.3 %collective-permute-done.16.refs_7_ = bf16[32,1024]{1,0:T(8,128)(2,1)S(1)} collective-permute-done((bf16[32,1024]{1,0:T(8,128)(2,1)S(1)}, bf16[32,1024]{1,0:T(8,128)(2,1)S(1)}, u32[]{:S(2)}, u32[]{:S(2)}) %collective-permute-start.16) | collective-permute-done | bytes 65568 | tf_op jit(solution)/shard_map/ppermute | solution.py:34
  417.3 12.2 %collective-permute-start.33 = (bf16[32,2048]{1,0:T(8,128)(2,1)S(1)}, bf16[32,2048]{1,0:T(8,128)(2,1)S(1)}, u32[]{:S(2)}, u32[]{:S(2)}) collective-permute-start(bf16[32,2048]{1,0:T(8,128)(2,1)S(1)} %get-tuple-element.50), channel_id=1, source_target_pairs={{0,10},{2,8},{4,14},{6,12},{8,2},{10,0},{12,6},{14,4},{1,11},{3,9}... | collective-permute-start | bytes 393224 | tf_op jit(solution)/shard_map/ppermute | solution.py:34
  429.4 10.1 %collective-permute-done.15.refs_6_ = bf16[32,1024]{1,0:T(8,128)(2,1)S(1)} collective-permute-done((bf16[32,1024]{1,0:T(8,128)(2,1)S(1)}, bf16[32,1024]{1,0:T(8,128)(2,1)S(1)}, u32[]{:S(2)}, u32[]{:S(2)}) %collective-permute-start.15) | collective-permute-done | bytes 65568 | tf_op jit(solution)/shard_map/ppermute | solution.py:34
  439.7 4.3 collective-permute-start.30
  444.0 1.5 collective-permute-start.29
  445.4 2.4 fusion.23
  448.3 5.0 collective-permute-start.54
  453.2 8.0 %collective-permute-start.35 = (bf16[32,2048]{1,0:T(8,128)(2,1)S(1)}, bf16[32,2048]{1,0:T(8,128)(2,1)S(1)}, u32[]{:S(2)}, u32[]{:S(2)}) collective-permute-start(bf16[32,2048]{1,0:T(8,128)(2,1)S(1)} %get-tuple-element.31), channel_id=1, source_target_pairs={{0,6},{2,4},{4,10},{6,8},{8,14},{10,12},{12,2},{14,0},{1,7},{3,5},... | collective-permute-start | bytes 393224 | tf_op jit(solution)/shard_map/ppermute | solution.py:34
  461.2 2.3 fusion.15
  463.6 2.4 collective-permute-start.52
  466.0 3.4 collective-permute-start.50
  471.0 3.3 collective-permute-start.48
  474.3 8.8 %shard_map.81.refs_11_ = bf16[32,64,1536]{2,1,0:T(8,128)(2,1)} custom-call(bf16[256,4096]{1,0:T(8,128)(2,1)} %bitcast.32.refs_0_, bf16[32,2048]{1,0:T(8,128)(2,1)} %get-tuple-element.55.refs_1_, bf16[32,2048]{1,0:T(8,128)(2,1)} %copy-done.53, bf16[32,2048]{1,0:T(8,128)(2,1)} %copy-done.51, bf16[32,2048]{1,0:T(8,128)(2,1)} %copy-done.49, ...), custom_call_target="tpu_custom_call" | custom-call | flops 3221225472 | bytes 8388608 | tf_op jit(solution)/shard_map/pallas_call | solution.py:202
  483.1 3.5 collective-permute-start.47
  487.0 2.9 collective-permute-start.45
  489.9 2.0 collective-permute-start.44
  492.5 8.7 %shard_map.82.refs_11_ = bf16[32,64,1536]{2,1,0:T(8,128)(2,1)} custom-call(bf16[256,4096]{1,0:T(8,128)(2,1)} %bitcast.32.refs_0_, bf16[32,2048]{1,0:T(8,128)(2,1)} %get-tuple-element.30.refs_1_, bf16[32,2048]{1,0:T(8,128)(2,1)} %copy-done.56, bf16[32,2048]{1,0:T(8,128)(2,1)} %copy-done.55, bf16[32,2048]{1,0:T(8,128)(2,1)} %copy-done.54, ...), custom_call_target="tpu_custom_call" | custom-call | flops 3221225472 | bytes 8388608 | tf_op jit(solution)/shard_map/pallas_call | solution.py:202
  502.3 2.9 collective-permute-start.39
  505.1 1.6 collective-permute-start.38
  506.8 2.0 collective-permute-start.37
  508.8 1.5 collective-permute-start.36
  511.6 8.2 %shard_map.83.refs_12_ = bf16[64,64,1536]{2,1,0:T(8,128)(2,1)} custom-call(bf16[256,4096]{1,0:T(8,128)(2,1)} %bitcast.129, bf16[32,2048]{1,0:T(8,128)(2,1)} %get-tuple-element.39.refs_1_, bf16[32,2048]{1,0:T(8,128)(2,1)} %copy-done.25, bf16[32,2048]{1,0:T(8,128)(2,1)} %copy-done.24, bf16[32,2048]{1,0:T(8,128)(2,1)} %copy-done.23, ...), custom_call_target="tpu_custom_call" | custom-call | flops 3221225472 | bytes 8388608 | tf_op jit(solution)/shard_map/pallas_call | solution.py:202
  520.9 2.8 collective-permute-start.13
  524.3 1.5 collective-permute-start.11
  525.8 1.5 collective-permute-start.17
  527.2 5.4 %shard_map.84.refs_12_ = bf16[64,64,1536]{2,1,0:T(8,128)(2,1)} custom-call(bf16[256,4096]{1,0:T(8,128)(2,1)} %bitcast.130, bf16[32,1024]{1,0:T(8,128)(2,1)} %get-tuple-element.47.refs_1_, bf16[32,1024]{1,0:T(8,128)(2,1)} %copy-done.35, bf16[32,1024]{1,0:T(8,128)(2,1)} %copy-done.33, bf16[32,1024]{1,0:T(8,128)(2,1)} %copy-done.32, ...), custom_call_target="tpu_custom_call", output_to_operand_aliasing={{}: (12, {})} | custom-call | flops 1610612736 | bytes 4194304 | tf_op jit(solution)/shard_map/pallas_call | solution.py:202
  533.4 5.4 shard_map.85
  (225 shorter events, 24.6 us)
Async XLA Ops:
  0.0 74.1 %copy-start = (bf16[128,128]{1,0:T(8,128)(2,1)S(1)}, bf16[128,128]{1,0:T(8,128)(2,1)}, u32[]{:S(2)}) copy-start(bf16[128,128]{1,0:T(8,128)(2,1)} %param.17) | copy-start | bytes 98308
  10.9 55.5 %all-to-all-start.2 = ((bf16[8,2,16,4096]{3,2,1,0:T(8,128)(2,1)}), bf16[8,2,16,4096]{3,2,1,0:T(8,128)(2,1)S(1)}, u32[]{:S(2)}, u32[]{:S(2)}) async-start(bf16[8,2,16,4096]{3,2,1,0:T(8,128)(2,1)} %bitcast.142), calls=%async_computation.2 | async-start | bytes 4194304 | tf_op jit(solution)/shard_map/all_to_all | solution.py:437
  67.7 52.1 %all-to-all-start = ((bf16[8,2,16,4096]{3,2,1,0:T(8,128)(2,1)}), bf16[8,2,16,4096]{3,2,1,0:T(8,128)(2,1)S(1)}, u32[]{:S(2)}, u32[]{:S(2)}) async-start(bf16[8,2,16,4096]{3,2,1,0:T(8,128)(2,1)} %bitcast.141), calls=%async_computation | async-start | bytes 4194304 | tf_op jit(solution)/shard_map/all_to_all | solution.py:437
  71.5 48.3 %collective-permute-start.18 = (bf16[8,2,16,4096]{3,2,1,0:T(8,128)(2,1)}, bf16[8,2,16,4096]{3,2,1,0:T(8,128)(2,1)}, u32[]{:S(2)}, u32[]{:S(2)}) collective-permute-start(bf16[8,2,16,4096]{3,2,1,0:T(8,128)(2,1)} %copy-done.8), channel_id=1, source_target_pairs={{0,1},{1,0},{2,3},{3,2},{4,5},{5,4},{6,7},{7,6},{8,9},{9,8},{10,11... | collective-permute-start | bytes 6291464 | tf_op jit(solution)/shard_map/ppermute | solution.py:22
  119.8 42.7 %collective-permute-start = (bf16[8,2,16,4096]{3,2,1,0:T(8,128)(2,1)S(1)}, bf16[8,2,16,4096]{3,2,1,0:T(8,128)(2,1)}, u32[]{:S(2)}, u32[]{:S(2)}) collective-permute-start(bf16[8,2,16,4096]{3,2,1,0:T(8,128)(2,1)S(1)} %all-to-all-done.refs_0_), channel_id=1, source_target_pairs={{0,1},{1,0},{2,3},{3,2},{4,5},{5,4},{6,7},{7,6},{8,9},{9,8},{10,11... | collective-permute-start | bytes 6291464 | tf_op jit(solution)/shard_map/ppermute | solution.py:22
  140.8 42.5 %collective-permute-start.19 = (bf16[8,32,4096]{2,1,0:T(8,128)(2,1)}, bf16[8,32,4096]{2,1,0:T(8,128)(2,1)}, u32[]{:S(2)}, u32[]{:S(2)}) collective-permute-start(bf16[8,32,4096]{2,1,0:T(8,128)(2,1)} %bitcast.140), channel_id=1, source_target_pairs={{0,1},{1,0},{2,3},{3,2},{4,5},{5,4},{6,7},{7,6},{8,9},{9,8},{10,11... | collective-permute-start | bytes 6291464 | tf_op jit(solution)/shard_map/ppermute | solution.py:22
  151.3 40.3 %collective-permute-start.20 = (bf16[256,4096]{1,0:T(8,128)(2,1)}, bf16[256,4096]{1,0:T(8,128)(2,1)}, u32[]{:S(2)}, u32[]{:S(2)}) collective-permute-start(bf16[256,4096]{1,0:T(8,128)(2,1)} %get-tuple-element.20), channel_id=1, source_target_pairs={{0,1},{1,0},{2,3},{3,2},{4,5},{5,4},{6,7},{7,6},{8,9},{9,8},{10,11... | collective-permute-start | bytes 6291464 | tf_op jit(solution)/shard_map/ppermute | solution.py:22
  162.3 39.7 %collective-permute-start.2 = (bf16[256,4096]{1,0:T(8,128)(2,1)}, bf16[256,4096]{1,0:T(8,128)(2,1)}, u32[]{:S(2)}, u32[]{:S(2)}) collective-permute-start(bf16[256,4096]{1,0:T(8,128)(2,1)} %get-tuple-element.16), channel_id=1, source_target_pairs={{0,1},{1,0},{2,3},{3,2},{4,5},{5,4},{6,7},{7,6},{8,9},{9,8},{10,11... | collective-permute-start | bytes 6291464 | tf_op jit(solution)/shard_map/ppermute | solution.py:22
  182.9 184.8 %collective-permute-start.1 = (bf16[8,32,4096]{2,1,0:T(8,128)(2,1)}, bf16[8,32,4096]{2,1,0:T(8,128)(2,1)S(1)}, u32[]{:S(2)}, u32[]{:S(2)}) collective-permute-start(bf16[8,32,4096]{2,1,0:T(8,128)(2,1)} %bitcast.139), channel_id=1, source_target_pairs={{0,1},{1,0},{2,3},{3,2},{4,5},{5,4},{6,7},{7,6},{8,9},{9,8},{10,11... | collective-permute-start | bytes 6291464 | tf_op jit(solution)/shard_map/ppermute | solution.py:22
  187.3 182.8 %all-to-all-start.3 = ((bf16[8,32,4096]{2,1,0:T(8,128)(2,1)}), bf16[8,32,4096]{2,1,0:T(8,128)(2,1)}, u32[]{:S(2)}, u32[]{:S(2)}) async-start(bf16[8,32,4096]{2,1,0:T(8,128)(2,1)} %multiply_convert_fusion), calls=%async_computation.3 | async-start | bytes 4194304 | tf_op jit(solution)/shard_map/all_to_all | solution.py:437
  195.4 38.2 %collective-permute-start.27 = (bf16[32,4096]{1,0:T(8,128)(2,1)}, bf16[32,4096]{1,0:T(8,128)(2,1)S(1)}, u32[]{:S(2)}, u32[]{:S(2)}) collective-permute-start(bf16[32,4096]{1,0:T(8,128)(2,1)} %get-tuple-element.56), channel_id=1, source_target_pairs={{0,14},{2,12},{4,2},{6,0},{8,6},{10,4},{12,10},{14,8},{1,15},{3,13... | collective-permute-start | bytes 786440 | tf_op jit(solution)/shard_map/ppermute | solution.py:34
  200.0 65.1 %collective-permute-start.26 = (bf16[32,4096]{1,0:T(8,128)(2,1)S(1)}, bf16[32,4096]{1,0:T(8,128)(2,1)S(1)}, u32[]{:S(2)}, u32[]{:S(2)}) collective-permute-start(bf16[32,4096]{1,0:T(8,128)(2,1)S(1)} %get-tuple-element.57), channel_id=1, source_target_pairs={{0,12},{2,14},{4,0},{6,2},{8,4},{10,6},{12,8},{14,10},{1,13},{3,15... | collective-permute-start | bytes 786440 | tf_op jit(solution)/shard_map/ppermute | solution.py:34
  202.0 79.4 %collective-permute-start.25 = (bf16[32,4096]{1,0:T(8,128)(2,1)}, bf16[32,4096]{1,0:T(8,128)(2,1)S(1)}, u32[]{:S(2)}, u32[]{:S(2)}) collective-permute-start(bf16[32,4096]{1,0:T(8,128)(2,1)} %get-tuple-element.58), channel_id=1, source_target_pairs={{0,10},{2,8},{4,14},{6,12},{8,2},{10,0},{12,6},{14,4},{1,11},{3,9}... | collective-permute-start | bytes 786440 | tf_op jit(solution)/shard_map/ppermute | solution.py:34
  202.0 83.3 %collective-permute-start.24 = (bf16[32,4096]{1,0:T(8,128)(2,1)}, bf16[32,4096]{1,0:T(8,128)(2,1)S(1)}, u32[]{:S(2)}, u32[]{:S(2)}) collective-permute-start(bf16[32,4096]{1,0:T(8,128)(2,1)} %get-tuple-element.59), channel_id=1, source_target_pairs={{0,8},{2,10},{4,12},{6,14},{8,0},{10,2},{12,4},{14,6},{1,9},{3,11}... | collective-permute-start | bytes 786440 | tf_op jit(solution)/shard_map/ppermute | solution.py:34
  233.6 51.7 %collective-permute-start.23 = (bf16[32,4096]{1,0:T(8,128)(2,1)}, bf16[32,4096]{1,0:T(8,128)(2,1)}, u32[]{:S(2)}, u32[]{:S(2)}) collective-permute-start(bf16[32,4096]{1,0:T(8,128)(2,1)} %get-tuple-element.60), channel_id=1, source_target_pairs={{0,6},{2,4},{4,10},{6,8},{8,14},{10,12},{12,2},{14,0},{1,7},{3,5},... | collective-permute-start | bytes 786440 | tf_op jit(solution)/shard_map/ppermute | solution.py:34
  265.1 22.2 %collective-permute-start.22 = (bf16[32,4096]{1,0:T(8,128)(2,1)}, bf16[32,4096]{1,0:T(8,128)(2,1)}, u32[]{:S(2)}, u32[]{:S(2)}) collective-permute-start(bf16[32,4096]{1,0:T(8,128)(2,1)} %get-tuple-element.61), channel_id=1, source_target_pairs={{0,4},{2,6},{4,8},{6,10},{8,12},{10,14},{12,0},{14,2},{1,5},{3,7},... | collective-permute-start | bytes 786440 | tf_op jit(solution)/shard_map/ppermute | solution.py:34
  281.4 9.7 %collective-permute-start.21 = (bf16[32,4096]{1,0:T(8,128)(2,1)}, bf16[32,4096]{1,0:T(8,128)(2,1)}, u32[]{:S(2)}, u32[]{:S(2)}) collective-permute-start(bf16[32,4096]{1,0:T(8,128)(2,1)} %get-tuple-element.62), channel_id=1, source_target_pairs={{0,2},{2,0},{4,6},{6,4},{8,10},{10,8},{12,14},{14,12},{1,3},{3,1},... | collective-permute-start | bytes 786440 | tf_op jit(solution)/shard_map/ppermute | solution.py:34
  285.3 10.3 %collective-permute-start.9 = (bf16[32,4096]{1,0:T(8,128)(2,1)}, bf16[32,4096]{1,0:T(8,128)(2,1)S(1)}, u32[]{:S(2)}, u32[]{:S(2)}) collective-permute-start(bf16[32,4096]{1,0:T(8,128)(2,1)} %get-tuple-element.71), channel_id=1, source_target_pairs={{0,14},{2,12},{4,2},{6,0},{8,6},{10,4},{12,10},{14,8},{1,15},{3,13... | collective-permute-start | bytes 786440 | tf_op jit(solution)/shard_map/ppermute | solution.py:34
  285.3 16.1 %collective-permute-start.8 = (bf16[32,4096]{1,0:T(8,128)(2,1)}, bf16[32,4096]{1,0:T(8,128)(2,1)S(1)}, u32[]{:S(2)}, u32[]{:S(2)}) collective-permute-start(bf16[32,4096]{1,0:T(8,128)(2,1)} %get-tuple-element.72), channel_id=1, source_target_pairs={{0,12},{2,14},{4,0},{6,2},{8,4},{10,6},{12,8},{14,10},{1,13},{3,15... | collective-permute-start | bytes 786440 | tf_op jit(solution)/shard_map/ppermute | solution.py:34
  287.3 39.7 %collective-permute-start.7 = (bf16[32,4096]{1,0:T(8,128)(2,1)}, bf16[32,4096]{1,0:T(8,128)(2,1)}, u32[]{:S(2)}, u32[]{:S(2)}) collective-permute-start(bf16[32,4096]{1,0:T(8,128)(2,1)} %get-tuple-element.73), channel_id=1, source_target_pairs={{0,10},{2,8},{4,14},{6,12},{8,2},{10,0},{12,6},{14,4},{1,11},{3,9}... | collective-permute-start | bytes 786440 | tf_op jit(solution)/shard_map/ppermute | solution.py:34
  291.1 56.1 %collective-permute-start.6 = (bf16[32,4096]{1,0:T(8,128)(2,1)}, bf16[32,4096]{1,0:T(8,128)(2,1)S(1)}, u32[]{:S(2)}, u32[]{:S(2)}) collective-permute-start(bf16[32,4096]{1,0:T(8,128)(2,1)} %get-tuple-element.74), channel_id=1, source_target_pairs={{0,8},{2,10},{4,12},{6,14},{8,0},{10,2},{12,4},{14,6},{1,9},{3,11}... | collective-permute-start | bytes 786440 | tf_op jit(solution)/shard_map/ppermute | solution.py:34
  295.6 51.6 %copy-start.13 = (bf16[32,4096]{1,0:T(8,128)(2,1)}, bf16[32,4096]{1,0:T(8,128)(2,1)S(1)}, u32[]{:S(2)}) copy-start(bf16[32,4096]{1,0:T(8,128)(2,1)S(1)} %collective-permute-done.9) | copy-start | bytes 786436
  295.6 51.7 %collective-permute-start.5 = (bf16[32,4096]{1,0:T(8,128)(2,1)}, bf16[32,4096]{1,0:T(8,128)(2,1)S(1)}, u32[]{:S(2)}, u32[]{:S(2)}) collective-permute-start(bf16[32,4096]{1,0:T(8,128)(2,1)} %get-tuple-element.75), channel_id=1, source_target_pairs={{0,6},{2,4},{4,10},{6,8},{8,14},{10,12},{12,2},{14,0},{1,7},{3,5},... | collective-permute-start | bytes 786440 | tf_op jit(solution)/shard_map/ppermute | solution.py:34
  301.4 45.9 %collective-permute-start.4 = (bf16[32,4096]{1,0:T(8,128)(2,1)}, bf16[32,4096]{1,0:T(8,128)(2,1)S(1)}, u32[]{:S(2)}, u32[]{:S(2)}) collective-permute-start(bf16[32,4096]{1,0:T(8,128)(2,1)} %get-tuple-element.76), channel_id=1, source_target_pairs={{0,4},{2,6},{4,8},{6,10},{8,12},{10,14},{12,0},{14,2},{1,5},{3,7},... | collective-permute-start | bytes 786440 | tf_op jit(solution)/shard_map/ppermute | solution.py:34
  327.0 20.3 %collective-permute-start.3 = (bf16[32,4096]{1,0:T(8,128)(2,1)S(1)}, bf16[32,4096]{1,0:T(8,128)(2,1)S(1)}, u32[]{:S(2)}, u32[]{:S(2)}) collective-permute-start(bf16[32,4096]{1,0:T(8,128)(2,1)S(1)} %get-tuple-element.77), channel_id=1, source_target_pairs={{0,2},{2,0},{4,6},{6,4},{8,10},{10,8},{12,14},{14,12},{1,3},{3,1},... | collective-permute-start | bytes 786440 | tf_op jit(solution)/shard_map/ppermute | solution.py:34
  347.2 26.5 %collective-permute-start.28 = (bf16[8,32,4096]{2,1,0:T(8,128)(2,1)}, bf16[8,32,4096]{2,1,0:T(8,128)(2,1)}, u32[]{:S(2)}, u32[]{:S(2)}) collective-permute-start(bf16[8,32,4096]{2,1,0:T(8,128)(2,1)} %bitcast.136), channel_id=1, source_target_pairs={{0,1},{1,0},{2,3},{3,2},{4,5},{5,4},{6,7},{7,6},{8,9},{9,8},{10,11... | collective-permute-start | bytes 6291464 | tf_op jit(solution)/shard_map/ppermute | solution.py:22
  367.2 11.0 %collective-permute-start.10 = (bf16[8,32,4096]{2,1,0:T(8,128)(2,1)}, bf16[8,32,4096]{2,1,0:T(8,128)(2,1)}, u32[]{:S(2)}, u32[]{:S(2)}) collective-permute-start(bf16[8,32,4096]{2,1,0:T(8,128)(2,1)} %bitcast.132), channel_id=1, source_target_pairs={{0,1},{1,0},{2,3},{3,2},{4,5},{5,4},{6,7},{7,6},{8,9},{9,8},{10,11... | collective-permute-start | bytes 6291464 | tf_op jit(solution)/shard_map/ppermute | solution.py:22
  370.0 140.2 %all-to-all-start.1 = ((bf16[8,32,4096]{2,1,0:T(8,128)(2,1)}), bf16[8,32,4096]{2,1,0:T(8,128)(2,1)S(1)}, u32[]{:S(2)}, u32[]{:S(2)}) async-start(bf16[8,32,4096]{2,1,0:T(8,128)(2,1)} %multiply_convert_fusion.1), calls=%async_computation.1 | async-start | bytes 4194304 | tf_op jit(solution)/shard_map/all_to_all | solution.py:437
  376.3 69.1 %copy-start.4 = (bf16[8,2,16,4096]{3,2,1,0:T(8,128)(2,1)S(1)}, bf16[8,2,16,4096]{3,2,1,0:T(8,128)(2,1)}, u32[]{:S(2)}) copy-start(bf16[8,2,16,4096]{3,2,1,0:T(8,128)(2,1)} %shard_map.80) | copy-start | bytes 6291460
  376.3 67.6 %collective-permute-start.34 = (bf16[32,2048]{1,0:T(8,128)(2,1)S(1)}, bf16[32,2048]{1,0:T(8,128)(2,1)S(1)}, u32[]{:S(2)}, u32[]{:S(2)}) collective-permute-start(bf16[32,2048]{1,0:T(8,128)(2,1)S(1)} %get-tuple-element.49), channel_id=1, source_target_pairs={{0,4},{2,6},{4,8},{6,10},{8,12},{10,14},{12,0},{14,2},{1,5},{3,7},... | collective-permute-start | bytes 393224 | tf_op jit(solution)/shard_map/ppermute | solution.py:34
  380.1 37.2 %collective-permute-start.16 = (bf16[32,1024]{1,0:T(8,128)(2,1)S(1)}, bf16[32,1024]{1,0:T(8,128)(2,1)S(1)}, u32[]{:S(2)}, u32[]{:S(2)}) collective-permute-start(bf16[32,1024]{1,0:T(8,128)(2,1)S(1)} %get-tuple-element.64), channel_id=1, source_target_pairs={{0,4},{2,6},{4,8},{6,10},{8,12},{10,14},{12,0},{14,2},{1,5},{3,7},... | collective-permute-start | bytes 196616 | tf_op jit(solution)/shard_map/ppermute | solution.py:34
  381.6 58.0 %collective-permute-start.15 = (bf16[32,1024]{1,0:T(8,128)(2,1)S(1)}, bf16[32,1024]{1,0:T(8,128)(2,1)S(1)}, u32[]{:S(2)}, u32[]{:S(2)}) collective-permute-start(bf16[32,1024]{1,0:T(8,128)(2,1)S(1)} %get-tuple-element.65), channel_id=1, source_target_pairs={{0,10},{2,8},{4,14},{6,12},{8,2},{10,0},{12,6},{14,4},{1,11},{3,9}... | collective-permute-start | bytes 196616 | tf_op jit(solution)/shard_map/ppermute | solution.py:34
  386.0 53.5 %collective-permute-start.42 = (bf16[32,1024]{1,0:T(8,128)(2,1)S(1)}, bf16[32,1024]{1,0:T(8,128)(2,1)S(1)}, u32[]{:S(2)}, u32[]{:S(2)}) collective-permute-start(bf16[32,1024]{1,0:T(8,128)(2,1)S(1)} %get-tuple-element.40), channel_id=1, source_target_pairs={{0,6},{2,4},{4,10},{6,8},{8,14},{10,12},{12,2},{14,0},{1,7},{3,5},... | collective-permute-start | bytes 196616 | tf_op jit(solution)/shard_map/ppermute | solution.py:34
  387.4 52.2 %collective-permute-start.41 = (bf16[32,1024]{1,0:T(8,128)(2,1)S(1)}, bf16[32,1024]{1,0:T(8,128)(2,1)S(1)}, u32[]{:S(2)}, u32[]{:S(2)}) collective-permute-start(bf16[32,1024]{1,0:T(8,128)(2,1)S(1)} %get-tuple-element.41), channel_id=1, source_target_pairs={{0,4},{2,6},{4,8},{6,10},{8,12},{10,14},{12,0},{14,2},{1,5},{3,7},... | collective-permute-start | bytes 196616 | tf_op jit(solution)/shard_map/ppermute | solution.py:34
  417.3 30.6 %collective-permute-start.33 = (bf16[32,2048]{1,0:T(8,128)(2,1)S(1)}, bf16[32,2048]{1,0:T(8,128)(2,1)S(1)}, u32[]{:S(2)}, u32[]{:S(2)}) collective-permute-start(bf16[32,2048]{1,0:T(8,128)(2,1)S(1)} %get-tuple-element.50), channel_id=1, source_target_pairs={{0,10},{2,8},{4,14},{6,12},{8,2},{10,0},{12,6},{14,4},{1,11},{3,9}... | collective-permute-start | bytes 393224 | tf_op jit(solution)/shard_map/ppermute | solution.py:34
  439.6 8.4 %collective-permute-start.32 = (bf16[32,2048]{1,0:T(8,128)(2,1)S(1)}, bf16[32,2048]{1,0:T(8,128)(2,1)S(1)}, u32[]{:S(2)}, u32[]{:S(2)}) collective-permute-start(bf16[32,2048]{1,0:T(8,128)(2,1)S(1)} %get-tuple-element.51), channel_id=1, source_target_pairs={{0,8},{2,10},{4,12},{6,14},{8,0},{10,2},{12,4},{14,6},{1,9},{3,11}... | collective-permute-start | bytes 393224 | tf_op jit(solution)/shard_map/ppermute | solution.py:34
  439.6 8.7 %collective-permute-start.31 = (bf16[32,2048]{1,0:T(8,128)(2,1)S(1)}, bf16[32,2048]{1,0:T(8,128)(2,1)S(1)}, u32[]{:S(2)}, u32[]{:S(2)}) collective-permute-start(bf16[32,2048]{1,0:T(8,128)(2,1)S(1)} %get-tuple-element.52), channel_id=1, source_target_pairs={{0,14},{2,12},{4,2},{6,0},{8,6},{10,4},{12,10},{14,8},{1,15},{3,13... | collective-permute-start | bytes 393224 | tf_op jit(solution)/shard_map/ppermute | solution.py:34
  439.7 13.6 %collective-permute-start.30 = (bf16[32,2048]{1,0:T(8,128)(2,1)S(1)}, bf16[32,2048]{1,0:T(8,128)(2,1)S(1)}, u32[]{:S(2)}, u32[]{:S(2)}) collective-permute-start(bf16[32,2048]{1,0:T(8,128)(2,1)S(1)} %get-tuple-element.53), channel_id=1, source_target_pairs={{0,12},{2,14},{4,0},{6,2},{8,4},{10,6},{12,8},{14,10},{1,13},{3,15... | collective-permute-start | bytes 393224 | tf_op jit(solution)/shard_map/ppermute | solution.py:34
  444.0 9.3 %collective-permute-start.29 = (bf16[32,2048]{1,0:T(8,128)(2,1)S(1)}, bf16[32,2048]{1,0:T(8,128)(2,1)S(1)}, u32[]{:S(2)}, u32[]{:S(2)}) collective-permute-start(bf16[32,2048]{1,0:T(8,128)(2,1)S(1)} %get-tuple-element.54), channel_id=1, source_target_pairs={{0,2},{2,0},{4,6},{6,4},{8,10},{10,8},{12,14},{14,12},{1,3},{3,1},... | collective-permute-start | bytes 393224 | tf_op jit(solution)/shard_map/ppermute | solution.py:34
  447.9 15.7 %collective-permute-start.56 = (bf16[32,2048]{1,0:T(8,128)(2,1)S(1)}, bf16[32,2048]{1,0:T(8,128)(2,1)S(1)}, u32[]{:S(2)}, u32[]{:S(2)}) collective-permute-start(bf16[32,2048]{1,0:T(8,128)(2,1)S(1)} %get-tuple-element.23), channel_id=1, source_target_pairs={{0,6},{2,4},{4,10},{6,8},{8,14},{10,12},{12,2},{14,0},{1,7},{3,5},... | collective-permute-start | bytes 393224 | tf_op jit(solution)/shard_map/ppermute | solution.py:34
  448.0 18.0 %collective-permute-start.55 = (bf16[32,2048]{1,0:T(8,128)(2,1)S(1)}, bf16[32,2048]{1,0:T(8,128)(2,1)S(1)}, u32[]{:S(2)}, u32[]{:S(2)}) collective-permute-start(bf16[32,2048]{1,0:T(8,128)(2,1)S(1)} %get-tuple-element.24), channel_id=1, source_target_pairs={{0,4},{2,6},{4,8},{6,10},{8,12},{10,14},{12,0},{14,2},{1,5},{3,7},... | collective-permute-start | bytes 393224 | tf_op jit(solution)/shard_map/ppermute | solution.py:34
  448.3 17.7 %collective-permute-start.54 = (bf16[32,2048]{1,0:T(8,128)(2,1)S(1)}, bf16[32,2048]{1,0:T(8,128)(2,1)S(1)}, u32[]{:S(2)}, u32[]{:S(2)}) collective-permute-start(bf16[32,2048]{1,0:T(8,128)(2,1)S(1)} %get-tuple-element.25), channel_id=1, source_target_pairs={{0,10},{2,8},{4,14},{6,12},{8,2},{10,0},{12,6},{14,4},{1,11},{3,9}... | collective-permute-start | bytes 393224 | tf_op jit(solution)/shard_map/ppermute | solution.py:34
  453.2 16.5 %collective-permute-start.53 = (bf16[32,2048]{1,0:T(8,128)(2,1)S(1)}, bf16[32,2048]{1,0:T(8,128)(2,1)S(1)}, u32[]{:S(2)}, u32[]{:S(2)}) collective-permute-start(bf16[32,2048]{1,0:T(8,128)(2,1)S(1)} %get-tuple-element.26), channel_id=1, source_target_pairs={{0,8},{2,10},{4,12},{6,14},{8,0},{10,2},{12,4},{14,6},{1,9},{3,11}... | collective-permute-start | bytes 393224 | tf_op jit(solution)/shard_map/ppermute | solution.py:34
  453.2 17.7 %collective-permute-start.35 = (bf16[32,2048]{1,0:T(8,128)(2,1)S(1)}, bf16[32,2048]{1,0:T(8,128)(2,1)S(1)}, u32[]{:S(2)}, u32[]{:S(2)}) collective-permute-start(bf16[32,2048]{1,0:T(8,128)(2,1)S(1)} %get-tuple-element.31), channel_id=1, source_target_pairs={{0,6},{2,4},{4,10},{6,8},{8,14},{10,12},{12,2},{14,0},{1,7},{3,5},... | collective-permute-start | bytes 393224 | tf_op jit(solution)/shard_map/ppermute | solution.py:34
  463.6 19.5 %collective-permute-start.52 = (bf16[32,2048]{1,0:T(8,128)(2,1)S(1)}, bf16[32,2048]{1,0:T(8,128)(2,1)S(1)}, u32[]{:S(2)}, u32[]{:S(2)}) collective-permute-start(bf16[32,2048]{1,0:T(8,128)(2,1)S(1)} %get-tuple-element.27), channel_id=1, source_target_pairs={{0,14},{2,12},{4,2},{6,0},{8,6},{10,4},{12,10},{14,8},{1,15},{3,13... | collective-permute-start | bytes 393224 | tf_op jit(solution)/shard_map/ppermute | solution.py:34
  466.0 20.6 %collective-permute-start.51 = (bf16[32,2048]{1,0:T(8,128)(2,1)S(1)}, bf16[32,2048]{1,0:T(8,128)(2,1)S(1)}, u32[]{:S(2)}, u32[]{:S(2)}) collective-permute-start(bf16[32,2048]{1,0:T(8,128)(2,1)S(1)} %get-tuple-element.28), channel_id=1, source_target_pairs={{0,12},{2,14},{4,0},{6,2},{8,4},{10,6},{12,8},{14,10},{1,13},{3,15... | collective-permute-start | bytes 393224 | tf_op jit(solution)/shard_map/ppermute | solution.py:34
  466.0 21.0 %collective-permute-start.50 = (bf16[32,2048]{1,0:T(8,128)(2,1)S(1)}, bf16[32,2048]{1,0:T(8,128)(2,1)S(1)}, u32[]{:S(2)}, u32[]{:S(2)}) collective-permute-start(bf16[32,2048]{1,0:T(8,128)(2,1)S(1)} %get-tuple-element.29), channel_id=1, source_target_pairs={{0,2},{2,0},{4,6},{6,4},{8,10},{10,8},{12,14},{14,12},{1,3},{3,1},... | collective-permute-start | bytes 393224 | tf_op jit(solution)/shard_map/ppermute | solution.py:34
  469.7 20.2 %collective-permute-start.49 = (bf16[32,2048]{1,0:T(8,128)(2,1)S(1)}, bf16[32,2048]{1,0:T(8,128)(2,1)S(1)}, u32[]{:S(2)}, u32[]{:S(2)}) collective-permute-start(bf16[32,2048]{1,0:T(8,128)(2,1)S(1)} %get-tuple-element.32), channel_id=1, source_target_pairs={{0,6},{2,4},{4,10},{6,8},{8,14},{10,12},{12,2},{14,0},{1,7},{3,5},... | collective-permute-start | bytes 393224 | tf_op jit(solution)/shard_map/ppermute | solution.py:34
  471.0 20.9 %collective-permute-start.48 = (bf16[32,2048]{1,0:T(8,128)(2,1)S(1)}, bf16[32,2048]{1,0:T(8,128)(2,1)S(1)}, u32[]{:S(2)}, u32[]{:S(2)}) collective-permute-start(bf16[32,2048]{1,0:T(8,128)(2,1)S(1)} %get-tuple-element.33), channel_id=1, source_target_pairs={{0,4},{2,6},{4,8},{6,10},{8,12},{10,14},{12,0},{14,2},{1,5},{3,7},... | collective-permute-start | bytes 393224 | tf_op jit(solution)/shard_map/ppermute | solution.py:34
  483.1 18.1 %collective-permute-start.47 = (bf16[32,2048]{1,0:T(8,128)(2,1)S(1)}, bf16[32,2048]{1,0:T(8,128)(2,1)S(1)}, u32[]{:S(2)}, u32[]{:S(2)}) collective-permute-start(bf16[32,2048]{1,0:T(8,128)(2,1)S(1)} %get-tuple-element.34), channel_id=1, source_target_pairs={{0,10},{2,8},{4,14},{6,12},{8,2},{10,0},{12,6},{14,4},{1,11},{3,9}... | collective-permute-start | bytes 393224 | tf_op jit(solution)/shard_map/ppermute | solution.py:34
  486.6 15.7 %collective-permute-start.46 = (bf16[32,2048]{1,0:T(8,128)(2,1)S(1)}, bf16[32,2048]{1,0:T(8,128)(2,1)S(1)}, u32[]{:S(2)}, u32[]{:S(2)}) collective-permute-start(bf16[32,2048]{1,0:T(8,128)(2,1)S(1)} %get-tuple-element.35), channel_id=1, source_target_pairs={{0,8},{2,10},{4,12},{6,14},{8,0},{10,2},{12,4},{14,6},{1,9},{3,11}... | collective-permute-start | bytes 393224 | tf_op jit(solution)/shard_map/ppermute | solution.py:34
  487.0 18.1 %collective-permute-start.45 = (bf16[32,2048]{1,0:T(8,128)(2,1)S(1)}, bf16[32,2048]{1,0:T(8,128)(2,1)S(1)}, u32[]{:S(2)}, u32[]{:S(2)}) collective-permute-start(bf16[32,2048]{1,0:T(8,128)(2,1)S(1)} %get-tuple-element.36), channel_id=1, source_target_pairs={{0,14},{2,12},{4,2},{6,0},{8,6},{10,4},{12,10},{14,8},{1,15},{3,13... | collective-permute-start | bytes 393224 | tf_op jit(solution)/shard_map/ppermute | solution.py:34
  489.9 16.9 %collective-permute-start.44 = (bf16[32,2048]{1,0:T(8,128)(2,1)S(1)}, bf16[32,2048]{1,0:T(8,128)(2,1)S(1)}, u32[]{:S(2)}, u32[]{:S(2)}) collective-permute-start(bf16[32,2048]{1,0:T(8,128)(2,1)S(1)} %get-tuple-element.37), channel_id=1, source_target_pairs={{0,12},{2,14},{4,0},{6,2},{8,4},{10,6},{12,8},{14,10},{1,13},{3,15... | collective-permute-start | bytes 393224 | tf_op jit(solution)/shard_map/ppermute | solution.py:34
  491.9 16.9 %collective-permute-start.43 = (bf16[32,2048]{1,0:T(8,128)(2,1)S(1)}, bf16[32,2048]{1,0:T(8,128)(2,1)S(1)}, u32[]{:S(2)}, u32[]{:S(2)}) collective-permute-start(bf16[32,2048]{1,0:T(8,128)(2,1)S(1)} %get-tuple-element.38), channel_id=1, source_target_pairs={{0,2},{2,0},{4,6},{6,4},{8,10},{10,8},{12,14},{14,12},{1,3},{3,1},... | collective-permute-start | bytes 393224 | tf_op jit(solution)/shard_map/ppermute | solution.py:34
  501.2 18.5 %collective-permute-start.40 = (bf16[32,1024]{1,0:T(8,128)(2,1)}, bf16[32,1024]{1,0:T(8,128)(2,1)S(1)}, u32[]{:S(2)}, u32[]{:S(2)}) collective-permute-start(bf16[32,1024]{1,0:T(8,128)(2,1)} %get-tuple-element.42), channel_id=1, source_target_pairs={{0,10},{2,8},{4,14},{6,12},{8,2},{10,0},{12,6},{14,4},{1,11},{3,9}... | collective-permute-start | bytes 196616 | tf_op jit(solution)/shard_map/ppermute | solution.py:34
  502.3 18.6 %collective-permute-start.39 = (bf16[32,1024]{1,0:T(8,128)(2,1)}, bf16[32,1024]{1,0:T(8,128)(2,1)S(1)}, u32[]{:S(2)}, u32[]{:S(2)}) collective-permute-start(bf16[32,1024]{1,0:T(8,128)(2,1)} %get-tuple-element.43), channel_id=1, source_target_pairs={{0,8},{2,10},{4,12},{6,14},{8,0},{10,2},{12,4},{14,6},{1,9},{3,11}... | collective-permute-start | bytes 196616 | tf_op jit(solution)/shard_map/ppermute | solution.py:34
  505.1 18.5 %collective-permute-start.38 = (bf16[32,1024]{1,0:T(8,128)(2,1)}, bf16[32,1024]{1,0:T(8,128)(2,1)S(1)}, u32[]{:S(2)}, u32[]{:S(2)}) collective-permute-start(bf16[32,1024]{1,0:T(8,128)(2,1)} %get-tuple-element.44), channel_id=1, source_target_pairs={{0,14},{2,12},{4,2},{6,0},{8,6},{10,4},{12,10},{14,8},{1,15},{3,13... | collective-permute-start | bytes 196616 | tf_op jit(solution)/shard_map/ppermute | solution.py:34
  506.8 17.5 %collective-permute-start.37 = (bf16[32,1024]{1,0:T(8,128)(2,1)}, bf16[32,1024]{1,0:T(8,128)(2,1)S(1)}, u32[]{:S(2)}, u32[]{:S(2)}) collective-permute-start(bf16[32,1024]{1,0:T(8,128)(2,1)} %get-tuple-element.45), channel_id=1, source_target_pairs={{0,12},{2,14},{4,0},{6,2},{8,4},{10,6},{12,8},{14,10},{1,13},{3,15... | collective-permute-start | bytes 196616 | tf_op jit(solution)/shard_map/ppermute | solution.py:34
  508.8 17.0 %collective-permute-start.36 = (bf16[32,1024]{1,0:T(8,128)(2,1)}, bf16[32,1024]{1,0:T(8,128)(2,1)S(1)}, u32[]{:S(2)}, u32[]{:S(2)}) collective-permute-start(bf16[32,1024]{1,0:T(8,128)(2,1)} %get-tuple-element.46), channel_id=1, source_target_pairs={{0,2},{2,0},{4,6},{6,4},{8,10},{10,8},{12,14},{14,12},{1,3},{3,1},... | collective-permute-start | bytes 196616 | tf_op jit(solution)/shard_map/ppermute | solution.py:34
  519.8 12.8 %collective-permute-start.14 = (bf16[32,1024]{1,0:T(8,128)(2,1)S(1)}, bf16[32,1024]{1,0:T(8,128)(2,1)S(1)}, u32[]{:S(2)}, u32[]{:S(2)}) collective-permute-start(bf16[32,1024]{1,0:T(8,128)(2,1)S(1)} %copy-done.40), channel_id=1, source_target_pairs={{0,8},{2,10},{4,12},{6,14},{8,0},{10,2},{12,4},{14,6},{1,9},{3,11}... | collective-permute-start | bytes 196616 | tf_op jit(solution)/shard_map/ppermute | solution.py:34
  520.9 11.8 %collective-permute-start.13 = (bf16[32,1024]{1,0:T(8,128)(2,1)S(1)}, bf16[32,1024]{1,0:T(8,128)(2,1)S(1)}, u32[]{:S(2)}, u32[]{:S(2)}) collective-permute-start(bf16[32,1024]{1,0:T(8,128)(2,1)S(1)} %get-tuple-element.67), channel_id=1, source_target_pairs={{0,14},{2,12},{4,2},{6,0},{8,6},{10,4},{12,10},{14,8},{1,15},{3,13... | collective-permute-start | bytes 196616 | tf_op jit(solution)/shard_map/ppermute | solution.py:34
  523.7 9.0 %collective-permute-start.12 = (bf16[32,1024]{1,0:T(8,128)(2,1)S(1)}, bf16[32,1024]{1,0:T(8,128)(2,1)S(1)}, u32[]{:S(2)}, u32[]{:S(2)}) collective-permute-start(bf16[32,1024]{1,0:T(8,128)(2,1)S(1)} %get-tuple-element.68), channel_id=1, source_target_pairs={{0,12},{2,14},{4,0},{6,2},{8,4},{10,6},{12,8},{14,10},{1,13},{3,15... | collective-permute-start | bytes 196616 | tf_op jit(solution)/shard_map/ppermute | solution.py:34
  524.3 8.4 %collective-permute-start.11 = (bf16[32,1024]{1,0:T(8,128)(2,1)S(1)}, bf16[32,1024]{1,0:T(8,128)(2,1)S(1)}, u32[]{:S(2)}, u32[]{:S(2)}) collective-permute-start(bf16[32,1024]{1,0:T(8,128)(2,1)S(1)} %get-tuple-element.69), channel_id=1, source_target_pairs={{0,2},{2,0},{4,6},{6,4},{8,10},{10,8},{12,14},{14,12},{1,3},{3,1},... | collective-permute-start | bytes 196616 | tf_op jit(solution)/shard_map/ppermute | solution.py:34
  525.8 7.0 %collective-permute-start.17 = (bf16[32,1024]{1,0:T(8,128)(2,1)S(1)}, bf16[32,1024]{1,0:T(8,128)(2,1)S(1)}, u32[]{:S(2)}, u32[]{:S(2)}) collective-permute-start(bf16[32,1024]{1,0:T(8,128)(2,1)S(1)} %copy-done.41), channel_id=1, source_target_pairs={{0,6},{2,4},{4,10},{6,8},{8,14},{10,12},{12,2},{14,0},{1,7},{3,5},... | collective-permute-start | bytes 196616 | tf_op jit(solution)/shard_map/ppermute | solution.py:34
  (55 other events, 732.2 us)

commit v7 on v6

--- a/solution.py
+++ b/solution.py
@@ -12,7 +12,8 @@
 tau_scale = 2.0
 LANES = 128
 CHUNKS = 4
-WHOLE_CHUNKS = (0, 2)
+WHOLE_SENDS = (0, 2)
+WHOLE_BACKS = (0,)
 DIRECT_LIMIT = 16
 EXCHANGE_AXES = ("wave", "level")
 
@@ -440,6 +441,10 @@
         both = scale * (other.astype(jnp.float32) + hemi_sign * own.astype(jnp.float32))
         return both.astype(jnp.bfloat16)
 
+    def block_at(value, wave, level):
+        place = (wave_place + wave) % wave_size * level_size + (level_place + level) % level_size
+        return lax.dynamic_index_in_dim(value, place, 0, keepdims=False)
+
     if not direct:
         returned, tables = [], []
         for chunk in range(chunks):
@@ -482,7 +487,7 @@
 
     arrived, tables = [], []
     for chunk in range(chunks):
-        is_whole = chunk in WHOLE_CHUNKS
+        is_whole = chunk in WHOLE_SENDS
         sizes = (wave_size, level_size, chunks, chunk, not is_whole, places * height)
         value, table = fourier(grid_state, where, wave_order, lat_order, sizes)
         tables.append(table)
@@ -505,7 +510,7 @@
     cuts[chunks - 1] = groups
     returned = []
     for chunk in range(chunks):
-        is_whole = chunk in WHOLE_CHUNKS
+        is_whole = chunk in WHOLE_SENDS
         pieces = arrived[chunk]
         if is_whole:
             pieces = [pieces[0], partner(pieces[0], "fld")]
@@ -514,16 +519,24 @@
         grid = columns_fused(pieces, legendre, waves, scalars, eig_rates, modes, sizes)
         grid = grid.reshape(places, height, width)
         other = partner(grid, "fld")
-        if is_whole:
+        if chunk in WHOLE_BACKS:
             hemi = exchange(joined(other, grid, 0.5))
             returned.append([(0, local_levels, [hemi.reshape(places * height, width)])])
             continue
         sent = []
+        if is_whole:
+            blocks = tables[chunk].reshape(places, height, lon_count)
+            blocks = [block_at(blocks, wave, level) for wave, level in shifts]
+            tables[chunk] = jnp.concatenate(blocks, axis=0)
         for start, levels in cuts[chunk]:
             lanes = slice(start * rows_here, (start + levels) * rows_here)
             pieces = []
             for index, (wave, level) in enumerate(shifts):
-                hemi = joined(other[index, :, lanes], grid[index, :, lanes], 0.5)
+                if is_whole:
+                    pair = block_at(other, -wave, -level), block_at(grid, -wave, -level)
+                else:
+                    pair = other[index, :, lanes], grid[index, :, lanes]
+                hemi = joined(*pair, 0.5)
                 wave, level = (wave_size - wave) % wave_size, (level_size - level) % level_size
                 pieces.append(shift_places(hemi, wave, level))
             sent.append((start, levels, pieces))

time: 540 us -> 464 us (0.86)
  waiting for transfers between devices: 190 us -> 82.4 us
  starting transfers between devices: 152 us -> 175 us
  local copies, waits for them, and re-layouts: 9.62 us -> 19.7 us
    all_to_all x4 -> x3, waiting for transfers between devices: 80.4 us -> 11 us  [exchange(): lax.all_to_all(value, EXCHANGE_AXES, split_axis=0, concat_axis=0, tiled=T...]
    ppermute x49 -> x56, waiting for transfers between devices: 110 us -> 71.4 us  [shift_places(): return lax.ppermute(value, EXCHANGE_AXES, pairs)]
    ppermute x49 -> x56, starting transfers between devices: 131 us -> 157 us  [shift_places(): return lax.ppermute(value, EXCHANGE_AXES, pairs)]
    unnamed x117 -> x134, local copies, waits for them, and re-layouts: 4.34 us -> 13.5 us
    convert_element_type x4 -> x3, other arithmetic: 13.7 us -> 9.39 us  [joined(): return both.astype(jnp.bfloat16)]
    mul x5 -> x6, other arithmetic: 11.3 us -> 14.3 us  [joined(): scale * (other.astype(jnp.float32) + hemi_sign * own.astype(jnp.float32))]
    all_to_all x4 -> x3, starting transfers between devices: 19 us -> 16.2 us  [exchange(): lax.all_to_all(value, EXCHANGE_AXES, split_axis=0, concat_axis=0, tiled=T...]
  transfers between devices with their start and end apart: 61 -> 67, of which waited for: 12 -> 16; matrix products, arithmetic and copies ran while one was open for 6% -> 9% of each run, Pallas kernels for 26% -> 30%
where the time goes in v7:
time: 464 us; the launch traced here: 463 us
  starting transfers between devices  175 us (38%)
  Pallas kernels  157 us (34%)
  waiting for transfers between devices  82.4 us (18%)
  other arithmetic  28.3 us (6%)
  local copies, waits for them, and re-layouts  19.7 us (4%)
    ppermute x56, starting transfers between devices, shift_places(): return lax.ppermute(value, EXCHANGE_AXES, pairs)  157 us
    pallas_call x4, Pallas kernels, columns_fused(): pl.pallas_call(functools.partial(column_kernel, sizes), out_shape=jax.Sha...  78.8 us
    ppermute x56, waiting for transfers between devices, shift_places(): return lax.ppermute(value, EXCHANGE_AXES, pairs)  71.4 us
    pallas_call x4, Pallas kernels, fourier(): pl.pallas_call(functools.partial(fourier_kernel, sizes), out_shape=[jax.S...  41.2 us
    pallas_call x5, Pallas kernels, inverse_fourier(): pl.pallas_call(functools.partial(inverse_kernel, len(pieces), len(tables)...  36.7 us
    all_to_all x3, starting transfers between devices, exchange(): lax.all_to_all(value, EXCHANGE_AXES, split_axis=0, concat_axis=0, tiled=T...  16.2 us
    mul x6, other arithmetic, joined(): scale * (other.astype(jnp.float32) + hemi_sign * own.astype(jnp.float32))  14.3 us
    unnamed x134, local copies, waits for them, and re-layouts  13.5 us
  transfers between devices with their start and end apart: 67, of which 16 were waited for; matrix products, arithmetic and copies ran while one was open for 9% of the time, Pallas kernels for 30%

profile of v7, /device:TPU:0, one launch (start us, length us, event | category | flops | bytes accessed | tf_op | source)
XLA Modules:
  0.0 463.0 jit_solution(15369847430507814678)
XLA Ops:
  0.6 10.2 %shard_map.77 = (bf16[256,4096]{1,0:T(8,128)(2,1)}, bf16[256,1536]{1,0:T(8,128)(2,1)}) custom-call(s32[3]{0:T(128)} %pad_add_fusion.1.place_ref, bf16[64,64,1536]{2,1,0:T(8,128)(2,1)} %bitcast.152, s32[1,512]{1,0:T(1,128)} %bitcast.185, s32[1,256]{1,0:T(1,128)} %bitcast.189), custom_call_target="tpu_custom_call" | custom-call | flops 3221225472 | bytes 15466496 | tf_op jit(solution)/shard_map/pallas_call | solution.py:119
  10.8 7.3 %all-to-all-start.1 = ((bf16[8,2,16,4096]{3,2,1,0:T(8,128)(2,1)}), bf16[8,2,16,4096]{3,2,1,0:T(8,128)(2,1)S(1)}, u32[]{:S(2)}, u32[]{:S(2)}) async-start(bf16[8,2,16,4096]{3,2,1,0:T(8,128)(2,1)} %bitcast.171), calls=%async_computation.1 | async-start | bytes 4194304 | tf_op jit(solution)/shard_map/all_to_all | solution.py:438
  18.1 10.4 %shard_map.79 = (bf16[256,4096]{1,0:T(8,128)(2,1)}, bf16[256,1536]{1,0:T(8,128)(2,1)}) custom-call(s32[3]{0:T(128)} %pad_add_fusion.1.place_ref, bf16[64,64,1536]{2,1,0:T(8,128)(2,1)} %bitcast.153, s32[1,512]{1,0:T(1,128)} %bitcast.186, s32[1,256]{1,0:T(1,128)} %bitcast.190), custom_call_target="tpu_custom_call" | custom-call | flops 3221225472 | bytes 15466496 | tf_op jit(solution)/shard_map/pallas_call | solution.py:119
  28.7 10.4 %shard_map.75 = (bf16[256,4096]{1,0:T(8,128)(2,1)}, bf16[256,1536]{1,0:T(8,128)(2,1)}) custom-call(s32[3]{0:T(128)} %pad_add_fusion.1.place_ref, bf16[64,64,1536]{2,1,0:T(8,128)(2,1)} %bitcast.154, s32[1,512]{1,0:T(1,128)} %bitcast.187, s32[1,256]{1,0:T(1,128)} %bitcast.191), custom_call_target="tpu_custom_call" | custom-call | flops 3221225472 | bytes 15466496 | tf_op jit(solution)/shard_map/pallas_call | solution.py:119
  45.2 10.2 %shard_map.73 = (bf16[256,4096]{1,0:T(8,128)(2,1)}, bf16[256,1536]{1,0:T(8,128)(2,1)}) custom-call(s32[3]{0:T(128)} %pad_add_fusion.1.place_ref, bf16[64,64,1536]{2,1,0:T(8,128)(2,1)} %bitcast.155, s32[1,512]{1,0:T(1,128)} %bitcast.188, s32[1,256]{1,0:T(1,128)} %bitcast.192), custom_call_target="tpu_custom_call" | custom-call | flops 3221225472 | bytes 15466496 | tf_op jit(solution)/shard_map/pallas_call | solution.py:119
  55.4 11.0 %all-to-all-done.1.refs_0_ = bf16[8,2,16,4096]{3,2,1,0:T(8,128)(2,1)S(1)} async-done(((bf16[8,2,16,4096]{3,2,1,0:T(8,128)(2,1)}), bf16[8,2,16,4096]{3,2,1,0:T(8,128)(2,1)S(1)}, u32[]{:S(2)}, u32[]{:S(2)}) %all-to-all-start.1) | async-done | bytes 2097184 | tf_op jit(solution)/shard_map/all_to_all | solution.py:438
  66.4 4.6 all-to-all-start
  74.8 3.8 add_convert_fusion
  78.6 4.3 collective-permute-start.34
  84.8 20.4 %shard_map.78 = bf16[8,2,16,4096]{3,2,1,0:T(8,128)(2,1)} custom-call(s32[64]{0:T(128)} %dynamic_slice.77.waves, s32[5]{0:T(128)} %pad_add_fusion.scalars, f32[128,1]{1,0:T(8,128)} %copy.12.eig_ref, bf16[128,128]{1,0:T(8,128)(2,1)} %select_bitcast_fusion.1.modes_in, bf16[128,128]{1,0:T(8,128)(2,1)} %broadcast_select_fusion.1.modes_out, ...), custom_call_target="tpu_custom_call" | custom-call | flops 1610612736 | bytes 6291456 | tf_op jit(solution)/shard_map/pallas_call | solution.py:357
  105.9 2.9 collective-permute-start.31
  108.8 3.3 collective-permute-done.34
  112.1 32.2 %collective-permute-start.30 = (bf16[32,4096]{1,0:T(8,128)(2,1)}, bf16[32,4096]{1,0:T(8,128)(2,1)}, u32[]{:S(2)}, u32[]{:S(2)}) collective-permute-start(bf16[32,4096]{1,0:T(8,128)(2,1)} %get-tuple-element.60), channel_id=1, source_target_pairs={{0,6},{2,4},{4,10},{6,8},{8,14},{10,12},{12,2},{14,0},{1,7},{3,5},... | collective-permute-start | bytes 786440 | tf_op jit(solution)/shard_map/ppermute | solution.py:35
  144.3 10.3 %collective-permute-start.29 = (bf16[32,4096]{1,0:T(8,128)(2,1)}, bf16[32,4096]{1,0:T(8,128)(2,1)}, u32[]{:S(2)}, u32[]{:S(2)}) collective-permute-start(bf16[32,4096]{1,0:T(8,128)(2,1)} %get-tuple-element.61), channel_id=1, source_target_pairs={{0,4},{2,6},{4,8},{6,10},{8,12},{10,14},{12,0},{14,2},{1,5},{3,7},... | collective-permute-start | bytes 786440 | tf_op jit(solution)/shard_map/ppermute | solution.py:35
  154.6 3.2 add_convert_fusion.8
  157.9 1.8 collective-permute-done.32
  161.9 2.7 collective-permute-done.31
  165.6 3.4 collective-permute-start.14
  170.4 3.8 collective-permute-done.16
  174.9 4.7 %collective-permute-done.15 = bf16[32,4096]{1,0:T(8,128)(2,1)} collective-permute-done((bf16[32,4096]{1,0:T(8,128)(2,1)}, bf16[32,4096]{1,0:T(8,128)(2,1)}, u32[]{:S(2)}, u32[]{:S(2)}) %collective-permute-start.15) | collective-permute-done | bytes 262176 | tf_op jit(solution)/shard_map/ppermute | solution.py:35
  179.5 25.8 %collective-permute-done.14 = bf16[32,4096]{1,0:T(8,128)(2,1)} collective-permute-done((bf16[32,4096]{1,0:T(8,128)(2,1)}, bf16[32,4096]{1,0:T(8,128)(2,1)}, u32[]{:S(2)}, u32[]{:S(2)}) %collective-permute-start.14) | collective-permute-done | bytes 262176 | tf_op jit(solution)/shard_map/ppermute | solution.py:35
  206.1 18.9 %shard_map.80 = bf16[8,2,16,4096]{3,2,1,0:T(8,128)(2,1)} custom-call(s32[64]{0:T(128)} %dynamic_slice.77.waves, s32[5]{0:T(128)} %pad_add_fusion.2.scalars, f32[128,1]{1,0:T(8,128)} %copy.12.eig_ref, bf16[128,128]{1,0:T(8,128)(2,1)} %select_bitcast_fusion.modes_in, bf16[128,128]{1,0:T(8,128)(2,1)} %broadcast_select_fusion.modes_out, ...), custom_call_target="tpu_custom_call" | custom-call | flops 1610612736 | bytes 6291456 | tf_op jit(solution)/shard_map/pallas_call | solution.py:357
  226.5 19.1 %shard_map.76 = bf16[8,2,16,4096]{3,2,1,0:T(8,128)(2,1)} custom-call(s32[64]{0:T(128)} %dynamic_slice.77.waves, s32[5]{0:T(128)} %pad_add_fusion.2.scalars, f32[128,1]{1,0:T(8,128)} %copy.12.eig_ref, bf16[128,128]{1,0:T(8,128)(2,1)} %select_bitcast_fusion.modes_in, bf16[128,128]{1,0:T(8,128)(2,1)} %broadcast_select_fusion.modes_out, ...), custom_call_target="tpu_custom_call" | custom-call | flops 1610612736 | bytes 6291456 | tf_op jit(solution)/shard_map/pallas_call | solution.py:357
  245.7 2.4 multiply_convert_fusion
  248.1 4.4 all-to-all-start.2
  255.2 20.4 %shard_map.74 = bf16[8,2,16,4096]{3,2,1,0:T(8,128)(2,1)} custom-call(s32[64]{0:T(128)} %dynamic_slice.77.waves, s32[5]{0:T(128)} %pad_add_fusion.scalars, f32[128,1]{1,0:T(8,128)} %copy.12.eig_ref, bf16[128,128]{1,0:T(8,128)(2,1)} %select_bitcast_fusion.1.modes_in, bf16[128,128]{1,0:T(8,128)(2,1)} %broadcast_select_fusion.1.modes_out, ...), custom_call_target="tpu_custom_call" | custom-call | flops 1610612736 | bytes 6291456 | tf_op jit(solution)/shard_map/pallas_call | solution.py:357
  276.0 2.5 fusion.14
  278.5 1.5 collective-permute-start.41
  280.0 1.9 fusion.38
  283.4 2.3 collective-permute-start.22
  285.8 2.1 fusion.47
  289.3 6.8 %collective-permute-done.23.refs_14_ = bf16[32,1024]{1,0:T(8,128)(2,1)S(1)} collective-permute-done((bf16[32,1024]{1,0:T(8,128)(2,1)S(1)}, bf16[32,1024]{1,0:T(8,128)(2,1)S(1)}, u32[]{:S(2)}, u32[]{:S(2)}) %collective-permute-start.23) | collective-permute-done | bytes 65568 | tf_op jit(solution)/shard_map/ppermute | solution.py:35
  296.7 10.6 %collective-permute-start.48 = (bf16[32,1024]{1,0:T(8,128)(2,1)}, bf16[32,1024]{1,0:T(8,128)(2,1)}, u32[]{:S(2)}, u32[]{:S(2)}) collective-permute-start(bf16[32,1024]{1,0:T(8,128)(2,1)} %get-tuple-element.41), channel_id=1, source_target_pairs={{0,4},{2,6},{4,8},{6,10},{8,12},{10,14},{12,0},{14,2},{1,5},{3,7},... | collective-permute-start | bytes 196616 | tf_op jit(solution)/shard_map/ppermute | solution.py:35
  308.2 4.1 collective-permute-done.22.refs_13_
  312.3 2.9 collective-permute-start.39
  315.2 2.4 collective-permute-start.37
  317.7 2.4 fusion.31
  320.1 2.8 collective-permute-done.40.refs_6_
  325.4 4.6 collective-permute-start.63
  331.4 4.3 collective-permute-start.61
  337.3 3.4 collective-permute-start.59
  341.7 5.5 %collective-permute-done.61.refs_6_ = bf16[32,2048]{1,0:T(8,128)(2,1)S(1)} collective-permute-done((bf16[32,2048]{1,0:T(8,128)(2,1)S(1)}, bf16[32,2048]{1,0:T(8,128)(2,1)S(1)}, u32[]{:S(2)}, u32[]{:S(2)}) %collective-permute-start.61) | collective-permute-done | bytes 131104 | tf_op jit(solution)/shard_map/ppermute | solution.py:35
  348.5 2.4 fusion.23
  350.9 5.3 %collective-permute-start.42 = (bf16[32,2048]{1,0:T(8,128)(2,1)S(1)}, bf16[32,2048]{1,0:T(8,128)(2,1)S(1)}, u32[]{:S(2)}, u32[]{:S(2)}) collective-permute-start(bf16[32,2048]{1,0:T(8,128)(2,1)S(1)} %get-tuple-element.31), channel_id=1, source_target_pairs={{0,6},{2,4},{4,10},{6,8},{8,14},{10,12},{12,2},{14,0},{1,7},{3,5},... | collective-permute-start | bytes 393224 | tf_op jit(solution)/shard_map/ppermute | solution.py:35
  356.9 4.2 collective-permute-start.55
  361.8 3.0 collective-permute-start.53
  364.8 3.0 fusion.7
  367.8 2.3 collective-permute-start.52
  371.3 2.6 collective-permute-done.54.refs_13_
  373.8 7.9 %collective-permute-start.8 = (bf16[32,4096]{1,0:T(8,128)(2,1)S(1)}, bf16[32,4096]{1,0:T(8,128)(2,1)S(1)}, u32[]{:S(2)}, u32[]{:S(2)}) collective-permute-start(bf16[32,4096]{1,0:T(8,128)(2,1)S(1)} %get-tuple-element.79), channel_id=1, source_target_pairs={{0,6},{2,4},{4,10},{6,8},{8,14},{10,12},{12,2},{14,0},{1,7},{3,5},... | collective-permute-start | bytes 786440 | tf_op jit(solution)/shard_map/ppermute | solution.py:35
  381.7 2.3 collective-permute-start.7
  384.1 8.8 %shard_map.81.refs_18_ = bf16[32,64,1536]{2,1,0:T(8,128)(2,1)} custom-call(bf16[256,4096]{1,0:T(8,128)(2,1)} %bitcast.48.refs_0_, bf16[32,2048]{1,0:T(8,128)(2,1)} %get-tuple-element.55.refs_1_, bf16[32,2048]{1,0:T(8,128)(2,1)} %copy-done.60, bf16[32,2048]{1,0:T(8,128)(2,1)} %copy-done.56, bf16[32,2048]{1,0:T(8,128)(2,1)} %copy-done.54, ...), custom_call_target="tpu_custom_call" | custom-call | flops 3221225472 | bytes 8388608 | tf_op jit(solution)/shard_map/pallas_call | solution.py:203
  392.9 3.9 collective-permute-start.6
  397.5 2.8 collective-permute-start.4
  400.3 2.0 collective-permute-start.3
  403.4 8.8 %shard_map.82.refs_18_ = bf16[32,64,1536]{2,1,0:T(8,128)(2,1)} custom-call(bf16[256,4096]{1,0:T(8,128)(2,1)} %bitcast.48.refs_0_, bf16[32,2048]{1,0:T(8,128)(2,1)} %get-tuple-element.30.refs_1_, bf16[32,2048]{1,0:T(8,128)(2,1)} %copy-done.61, bf16[32,2048]{1,0:T(8,128)(2,1)} %copy-done.59, bf16[32,2048]{1,0:T(8,128)(2,1)} %copy-done.58, ...), custom_call_target="tpu_custom_call" | custom-call | flops 3221225472 | bytes 8388608 | tf_op jit(solution)/shard_map/pallas_call | solution.py:203
  412.5 5.1 %collective-permute-done.5.refs_4_ = bf16[32,4096]{1,0:T(8,128)(2,1)S(1)} collective-permute-done((bf16[32,4096]{1,0:T(8,128)(2,1)S(1)}, bf16[32,4096]{1,0:T(8,128)(2,1)S(1)}, u32[]{:S(2)}, u32[]{:S(2)}) %collective-permute-start.5) | collective-permute-done | bytes 262176 | tf_op jit(solution)/shard_map/ppermute | solution.py:35
  417.7 15.3 %collective-permute-start.45 = (bf16[32,1024]{1,0:T(8,128)(2,1)S(1)}, bf16[32,1024]{1,0:T(8,128)(2,1)S(1)}, u32[]{:S(2)}, u32[]{:S(2)}) collective-permute-start(bf16[32,1024]{1,0:T(8,128)(2,1)S(1)} %copy-done.45), channel_id=1, source_target_pairs={{0,14},{2,12},{4,2},{6,0},{8,6},{10,4},{12,10},{14,8},{1,15},{3,13... | collective-permute-start | bytes 196616 | tf_op jit(solution)/shard_map/ppermute | solution.py:35
  434.2 8.2 %shard_map.83.refs_19_ = bf16[64,64,1536]{2,1,0:T(8,128)(2,1)} custom-call(bf16[32,4096]{1,0:T(8,128)(2,1)} %get-tuple-element.86.refs_0_, bf16[32,4096]{1,0:T(8,128)(2,1)} %copy-done.15, bf16[32,4096]{1,0:T(8,128)(2,1)} %copy-done.14, bf16[32,4096]{1,0:T(8,128)(2,1)} %copy-done.13, bf16[32,4096]{1,0:T(8,128)(2,1)} %copy-done.12, ...), custom_call_target="tpu_custom_call" | custom-call | flops 3221225472 | bytes 8388608 | tf_op jit(solution)/shard_map/pallas_call | solution.py:203
  442.5 2.1 collective-permute-start.21
  444.5 2.9 collective-permute-start.20
  448.6 2.5 collective-permute-start.24
  451.1 5.4 %shard_map.84.refs_19_ = bf16[64,64,1536]{2,1,0:T(8,128)(2,1)} custom-call(bf16[32,4096]{1,0:T(8,128)(2,1)} %get-tuple-element.86.refs_0_, bf16[32,4096]{1,0:T(8,128)(2,1)} %copy-done.15, bf16[32,4096]{1,0:T(8,128)(2,1)} %copy-done.14, bf16[32,4096]{1,0:T(8,128)(2,1)} %copy-done.13, bf16[32,4096]{1,0:T(8,128)(2,1)} %copy-done.12, ...), custom_call_target="tpu_custom_call", output_to_operand_aliasing={{}: (19, {})} | custom-call | flops 1610612736 | bytes 4194304 | tf_op jit(solution)/shard_map/pallas_call | solution.py:203
  457.3 5.4 %shard_map.85 = bf16[64,64,1536]{2,1,0:T(8,128)(2,1)} custom-call(bf16[32,4096]{1,0:T(8,128)(2,1)} %get-tuple-element.86.refs_0_, bf16[32,4096]{1,0:T(8,128)(2,1)} %copy-done.15, bf16[32,4096]{1,0:T(8,128)(2,1)} %copy-done.14, bf16[32,4096]{1,0:T(8,128)(2,1)} %copy-done.13, bf16[32,4096]{1,0:T(8,128)(2,1)} %copy-done.12, ...), custom_call_target="tpu_custom_call", output_to_operand_aliasing={{}: (19, {})} | custom-call | flops 1610612736 | bytes 4194304 | tf_op jit(solution)/shard_map/pallas_call | solution.py:203
  (255 shorter events, 43.7 us)
Async XLA Ops:
  10.8 55.5 %all-to-all-start.1 = ((bf16[8,2,16,4096]{3,2,1,0:T(8,128)(2,1)}), bf16[8,2,16,4096]{3,2,1,0:T(8,128)(2,1)S(1)}, u32[]{:S(2)}, u32[]{:S(2)}) async-start(bf16[8,2,16,4096]{3,2,1,0:T(8,128)(2,1)} %bitcast.171), calls=%async_computation.1 | async-start | bytes 4194304 | tf_op jit(solution)/shard_map/all_to_all | solution.py:438
  28.6 46.2 %collective-permute-start.27 = (bf16[256,4096]{1,0:T(8,128)(2,1)}, bf16[256,4096]{1,0:T(8,128)(2,1)}, u32[]{:S(2)}, u32[]{:S(2)}) collective-permute-start(bf16[256,4096]{1,0:T(8,128)(2,1)} %get-tuple-element.20), channel_id=1, source_target_pairs={{0,1},{1,0},{2,3},{3,2},{4,5},{5,4},{6,7},{7,6},{8,9},{9,8},{10,11... | collective-permute-start | bytes 6291464 | tf_op jit(solution)/shard_map/ppermute | solution.py:23
  39.1 66.8 %collective-permute-start.9 = (bf16[256,4096]{1,0:T(8,128)(2,1)}, bf16[256,4096]{1,0:T(8,128)(2,1)}, u32[]{:S(2)}, u32[]{:S(2)}) collective-permute-start(bf16[256,4096]{1,0:T(8,128)(2,1)} %get-tuple-element.16), channel_id=1, source_target_pairs={{0,1},{1,0},{2,3},{3,2},{4,5},{5,4},{6,7},{7,6},{8,9},{9,8},{10,11... | collective-permute-start | bytes 6291464 | tf_op jit(solution)/shard_map/ppermute | solution.py:23
  66.4 158.7 %all-to-all-start = ((bf16[8,2,16,4096]{3,2,1,0:T(8,128)(2,1)}), bf16[8,2,16,4096]{3,2,1,0:T(8,128)(2,1)}, u32[]{:S(2)}, u32[]{:S(2)}) async-start(bf16[8,2,16,4096]{3,2,1,0:T(8,128)(2,1)} %bitcast.170), calls=%async_computation | async-start | bytes 4194304 | tf_op jit(solution)/shard_map/all_to_all | solution.py:438
  71.0 12.5 %collective-permute-start.25 = (bf16[8,2,16,4096]{3,2,1,0:T(8,128)(2,1)S(1)}, bf16[8,2,16,4096]{3,2,1,0:T(8,128)(2,1)S(1)}, u32[]{:S(2)}, u32[]{:S(2)}) collective-permute-start(bf16[8,2,16,4096]{3,2,1,0:T(8,128)(2,1)S(1)} %all-to-all-done.1.refs_0_), channel_id=1, source_target_pairs={{0,1},{1,0},{2,3},{3,2},{4,5},{5,4},{6,7},{7,6},{8,9},{9,8},{10,11... | collective-permute-start | bytes 6291464 | tf_op jit(solution)/shard_map/ppermute | solution.py:23
  78.6 33.5 %collective-permute-start.34 = (bf16[32,4096]{1,0:T(8,128)(2,1)S(1)}, bf16[32,4096]{1,0:T(8,128)(2,1)S(1)}, u32[]{:S(2)}, u32[]{:S(2)}) collective-permute-start(bf16[32,4096]{1,0:T(8,128)(2,1)S(1)} %get-tuple-element.56), channel_id=1, source_target_pairs={{0,14},{2,12},{4,2},{6,0},{8,6},{10,4},{12,10},{14,8},{1,15},{3,13... | collective-permute-start | bytes 786440 | tf_op jit(solution)/shard_map/ppermute | solution.py:35
  83.0 61.4 %collective-permute-start.33 = (bf16[32,4096]{1,0:T(8,128)(2,1)S(1)}, bf16[32,4096]{1,0:T(8,128)(2,1)S(1)}, u32[]{:S(2)}, u32[]{:S(2)}) collective-permute-start(bf16[32,4096]{1,0:T(8,128)(2,1)S(1)} %get-tuple-element.57), channel_id=1, source_target_pairs={{0,12},{2,14},{4,0},{6,2},{8,4},{10,6},{12,8},{14,10},{1,13},{3,15... | collective-permute-start | bytes 786440 | tf_op jit(solution)/shard_map/ppermute | solution.py:35
  105.3 140.4 %collective-permute-start.26 = (bf16[8,32,4096]{2,1,0:T(8,128)(2,1)}, bf16[8,32,4096]{2,1,0:T(8,128)(2,1)S(1)}, u32[]{:S(2)}, u32[]{:S(2)}) collective-permute-start(bf16[8,32,4096]{2,1,0:T(8,128)(2,1)} %bitcast.167), channel_id=1, source_target_pairs={{0,1},{1,0},{2,3},{3,2},{4,5},{5,4},{6,7},{7,6},{8,9},{9,8},{10,11... | collective-permute-start | bytes 6291464 | tf_op jit(solution)/shard_map/ppermute | solution.py:23
  105.9 53.8 %collective-permute-start.32 = (bf16[32,4096]{1,0:T(8,128)(2,1)}, bf16[32,4096]{1,0:T(8,128)(2,1)S(1)}, u32[]{:S(2)}, u32[]{:S(2)}) collective-permute-start(bf16[32,4096]{1,0:T(8,128)(2,1)} %get-tuple-element.58), channel_id=1, source_target_pairs={{0,10},{2,8},{4,14},{6,12},{8,2},{10,0},{12,6},{14,4},{1,11},{3,9}... | collective-permute-start | bytes 786440 | tf_op jit(solution)/shard_map/ppermute | solution.py:35
  105.9 58.7 %collective-permute-start.31 = (bf16[32,4096]{1,0:T(8,128)(2,1)}, bf16[32,4096]{1,0:T(8,128)(2,1)}, u32[]{:S(2)}, u32[]{:S(2)}) collective-permute-start(bf16[32,4096]{1,0:T(8,128)(2,1)} %get-tuple-element.59), channel_id=1, source_target_pairs={{0,8},{2,10},{4,12},{6,14},{8,0},{10,2},{12,4},{14,6},{1,9},{3,11}... | collective-permute-start | bytes 786440 | tf_op jit(solution)/shard_map/ppermute | solution.py:35
  112.1 52.5 %collective-permute-start.30 = (bf16[32,4096]{1,0:T(8,128)(2,1)}, bf16[32,4096]{1,0:T(8,128)(2,1)}, u32[]{:S(2)}, u32[]{:S(2)}) collective-permute-start(bf16[32,4096]{1,0:T(8,128)(2,1)} %get-tuple-element.60), channel_id=1, source_target_pairs={{0,6},{2,4},{4,10},{6,8},{8,14},{10,12},{12,2},{14,0},{1,7},{3,5},... | collective-permute-start | bytes 786440 | tf_op jit(solution)/shard_map/ppermute | solution.py:35
  144.3 21.3 %collective-permute-start.29 = (bf16[32,4096]{1,0:T(8,128)(2,1)}, bf16[32,4096]{1,0:T(8,128)(2,1)}, u32[]{:S(2)}, u32[]{:S(2)}) collective-permute-start(bf16[32,4096]{1,0:T(8,128)(2,1)} %get-tuple-element.61), channel_id=1, source_target_pairs={{0,4},{2,6},{4,8},{6,10},{8,12},{10,14},{12,0},{14,2},{1,5},{3,7},... | collective-permute-start | bytes 786440 | tf_op jit(solution)/shard_map/ppermute | solution.py:35
  160.4 10.0 %collective-permute-start.28 = (bf16[32,4096]{1,0:T(8,128)(2,1)}, bf16[32,4096]{1,0:T(8,128)(2,1)}, u32[]{:S(2)}, u32[]{:S(2)}) collective-permute-start(bf16[32,4096]{1,0:T(8,128)(2,1)} %get-tuple-element.62), channel_id=1, source_target_pairs={{0,2},{2,0},{4,6},{6,4},{8,10},{10,8},{12,14},{14,12},{1,3},{3,1},... | collective-permute-start | bytes 786440 | tf_op jit(solution)/shard_map/ppermute | solution.py:35
  164.6 9.6 %collective-permute-start.16 = (bf16[32,4096]{1,0:T(8,128)(2,1)}, bf16[32,4096]{1,0:T(8,128)(2,1)}, u32[]{:S(2)}, u32[]{:S(2)}) collective-permute-start(bf16[32,4096]{1,0:T(8,128)(2,1)} %get-tuple-element.71), channel_id=1, source_target_pairs={{0,14},{2,12},{4,2},{6,0},{8,6},{10,4},{12,10},{14,8},{1,15},{3,13... | collective-permute-start | bytes 786440 | tf_op jit(solution)/shard_map/ppermute | solution.py:35
  164.6 14.9 %collective-permute-start.15 = (bf16[32,4096]{1,0:T(8,128)(2,1)}, bf16[32,4096]{1,0:T(8,128)(2,1)}, u32[]{:S(2)}, u32[]{:S(2)}) collective-permute-start(bf16[32,4096]{1,0:T(8,128)(2,1)} %get-tuple-element.72), channel_id=1, source_target_pairs={{0,12},{2,14},{4,0},{6,2},{8,4},{10,6},{12,8},{14,10},{1,13},{3,15... | collective-permute-start | bytes 786440 | tf_op jit(solution)/shard_map/ppermute | solution.py:35
  165.6 39.7 %collective-permute-start.14 = (bf16[32,4096]{1,0:T(8,128)(2,1)}, bf16[32,4096]{1,0:T(8,128)(2,1)}, u32[]{:S(2)}, u32[]{:S(2)}) collective-permute-start(bf16[32,4096]{1,0:T(8,128)(2,1)} %get-tuple-element.73), channel_id=1, source_target_pairs={{0,10},{2,8},{4,14},{6,12},{8,2},{10,0},{12,6},{14,4},{1,11},{3,9}... | collective-permute-start | bytes 786440 | tf_op jit(solution)/shard_map/ppermute | solution.py:35
  170.4 54.7 %collective-permute-start.13 = (bf16[32,4096]{1,0:T(8,128)(2,1)}, bf16[32,4096]{1,0:T(8,128)(2,1)}, u32[]{:S(2)}, u32[]{:S(2)}) collective-permute-start(bf16[32,4096]{1,0:T(8,128)(2,1)} %get-tuple-element.74), channel_id=1, source_target_pairs={{0,8},{2,10},{4,12},{6,14},{8,0},{10,2},{12,4},{14,6},{1,9},{3,11}... | collective-permute-start | bytes 786440 | tf_op jit(solution)/shard_map/ppermute | solution.py:35
  174.2 50.9 %collective-permute-start.12 = (bf16[32,4096]{1,0:T(8,128)(2,1)}, bf16[32,4096]{1,0:T(8,128)(2,1)}, u32[]{:S(2)}, u32[]{:S(2)}) collective-permute-start(bf16[32,4096]{1,0:T(8,128)(2,1)} %get-tuple-element.75), channel_id=1, source_target_pairs={{0,6},{2,4},{4,10},{6,8},{8,14},{10,12},{12,2},{14,0},{1,7},{3,5},... | collective-permute-start | bytes 786440 | tf_op jit(solution)/shard_map/ppermute | solution.py:35
  179.5 47.0 %collective-permute-start.11 = (bf16[32,4096]{1,0:T(8,128)(2,1)S(1)}, bf16[32,4096]{1,0:T(8,128)(2,1)}, u32[]{:S(2)}, u32[]{:S(2)}) collective-permute-start(bf16[32,4096]{1,0:T(8,128)(2,1)S(1)} %get-tuple-element.76), channel_id=1, source_target_pairs={{0,4},{2,6},{4,8},{6,10},{8,12},{10,14},{12,0},{14,2},{1,5},{3,7},... | collective-permute-start | bytes 786440 | tf_op jit(solution)/shard_map/ppermute | solution.py:35
  205.3 21.2 %collective-permute-start.10 = (bf16[32,4096]{1,0:T(8,128)(2,1)S(1)}, bf16[32,4096]{1,0:T(8,128)(2,1)}, u32[]{:S(2)}, u32[]{:S(2)}) collective-permute-start(bf16[32,4096]{1,0:T(8,128)(2,1)S(1)} %get-tuple-element.77), channel_id=1, source_target_pairs={{0,2},{2,0},{4,6},{6,4},{8,10},{10,8},{12,14},{14,12},{1,3},{3,1},... | collective-permute-start | bytes 786440 | tf_op jit(solution)/shard_map/ppermute | solution.py:35
  225.0 51.0 %collective-permute-start.35 = (bf16[8,32,4096]{2,1,0:T(8,128)(2,1)}, bf16[8,32,4096]{2,1,0:T(8,128)(2,1)}, u32[]{:S(2)}, u32[]{:S(2)}) collective-permute-start(bf16[8,32,4096]{2,1,0:T(8,128)(2,1)} %bitcast.160), channel_id=1, source_target_pairs={{0,1},{1,0},{2,3},{3,2},{4,5},{5,4},{6,7},{7,6},{8,9},{9,8},{10,11... | collective-permute-start | bytes 6291464 | tf_op jit(solution)/shard_map/ppermute | solution.py:23
  225.1 30.0 %collective-permute-start = (bf16[8,2,16,4096]{3,2,1,0:T(8,128)(2,1)}, bf16[8,2,16,4096]{3,2,1,0:T(8,128)(2,1)}, u32[]{:S(2)}, u32[]{:S(2)}) collective-permute-start(bf16[8,2,16,4096]{3,2,1,0:T(8,128)(2,1)} %all-to-all-done.refs_0_), channel_id=1, source_target_pairs={{0,1},{1,0},{2,3},{3,2},{4,5},{5,4},{6,7},{7,6},{8,9},{9,8},{10,11... | collective-permute-start | bytes 6291464 | tf_op jit(solution)/shard_map/ppermute | solution.py:23
  245.6 34.4 %collective-permute-start.17 = (bf16[8,32,4096]{2,1,0:T(8,128)(2,1)}, bf16[8,32,4096]{2,1,0:T(8,128)(2,1)}, u32[]{:S(2)}, u32[]{:S(2)}) collective-permute-start(bf16[8,32,4096]{2,1,0:T(8,128)(2,1)} %bitcast.163), channel_id=1, source_target_pairs={{0,1},{1,0},{2,3},{3,2},{4,5},{5,4},{6,7},{7,6},{8,9},{9,8},{10,11... | collective-permute-start | bytes 6291464 | tf_op jit(solution)/shard_map/ppermute | solution.py:23
  248.1 136.0 %all-to-all-start.2 = ((bf16[8,32,4096]{2,1,0:T(8,128)(2,1)}), bf16[8,32,4096]{2,1,0:T(8,128)(2,1)}, u32[]{:S(2)}, u32[]{:S(2)}) async-start(bf16[8,32,4096]{2,1,0:T(8,128)(2,1)} %multiply_convert_fusion), calls=%async_computation.2 | async-start | bytes 4194304 | tf_op jit(solution)/shard_map/all_to_all | solution.py:438
  275.6 85.9 %collective-permute-start.1 = (bf16[8,32,4096]{2,1,0:T(8,128)(2,1)}, bf16[8,32,4096]{2,1,0:T(8,128)(2,1)}, u32[]{:S(2)}, u32[]{:S(2)}) collective-permute-start(bf16[8,32,4096]{2,1,0:T(8,128)(2,1)} %bitcast.168), channel_id=1, source_target_pairs={{0,1},{1,0},{2,3},{3,2},{4,5},{5,4},{6,7},{7,6},{8,9},{9,8},{10,11... | collective-permute-start | bytes 6291464 | tf_op jit(solution)/shard_map/ppermute | solution.py:23
  278.5 36.7 %collective-permute-start.41 = (bf16[32,2048]{1,0:T(8,128)(2,1)}, bf16[32,2048]{1,0:T(8,128)(2,1)}, u32[]{:S(2)}, u32[]{:S(2)}) collective-permute-start(bf16[32,2048]{1,0:T(8,128)(2,1)} %get-tuple-element.49), channel_id=1, source_target_pairs={{0,4},{2,6},{4,8},{6,10},{8,12},{10,14},{12,0},{14,2},{1,5},{3,7},... | collective-permute-start | bytes 393224 | tf_op jit(solution)/shard_map/ppermute | solution.py:35
  281.9 14.1 %collective-permute-start.23 = (bf16[32,1024]{1,0:T(8,128)(2,1)S(1)}, bf16[32,1024]{1,0:T(8,128)(2,1)S(1)}, u32[]{:S(2)}, u32[]{:S(2)}) collective-permute-start(bf16[32,1024]{1,0:T(8,128)(2,1)S(1)} %get-tuple-element.64), channel_id=1, source_target_pairs={{0,4},{2,6},{4,8},{6,10},{8,12},{10,14},{12,0},{14,2},{1,5},{3,7},... | collective-permute-start | bytes 196616 | tf_op jit(solution)/shard_map/ppermute | solution.py:35
  283.4 28.9 %collective-permute-start.22 = (bf16[32,1024]{1,0:T(8,128)(2,1)}, bf16[32,1024]{1,0:T(8,128)(2,1)}, u32[]{:S(2)}, u32[]{:S(2)}) collective-permute-start(bf16[32,1024]{1,0:T(8,128)(2,1)} %get-tuple-element.65), channel_id=1, source_target_pairs={{0,10},{2,8},{4,14},{6,12},{8,2},{10,0},{12,6},{14,4},{1,11},{3,9}... | collective-permute-start | bytes 196616 | tf_op jit(solution)/shard_map/ppermute | solution.py:35
  287.8 24.5 %collective-permute-start.49 = (bf16[32,1024]{1,0:T(8,128)(2,1)}, bf16[32,1024]{1,0:T(8,128)(2,1)}, u32[]{:S(2)}, u32[]{:S(2)}) collective-permute-start(bf16[32,1024]{1,0:T(8,128)(2,1)} %get-tuple-element.40), channel_id=1, source_target_pairs={{0,6},{2,4},{4,10},{6,8},{8,14},{10,12},{12,2},{14,0},{1,7},{3,5},... | collective-permute-start | bytes 196616 | tf_op jit(solution)/shard_map/ppermute | solution.py:35
  296.7 18.5 %collective-permute-start.48 = (bf16[32,1024]{1,0:T(8,128)(2,1)}, bf16[32,1024]{1,0:T(8,128)(2,1)}, u32[]{:S(2)}, u32[]{:S(2)}) collective-permute-start(bf16[32,1024]{1,0:T(8,128)(2,1)} %get-tuple-element.41), channel_id=1, source_target_pairs={{0,4},{2,6},{4,8},{6,10},{8,12},{10,14},{12,0},{14,2},{1,5},{3,7},... | collective-permute-start | bytes 196616 | tf_op jit(solution)/shard_map/ppermute | solution.py:35
  312.3 10.6 %collective-permute-start.40 = (bf16[32,2048]{1,0:T(8,128)(2,1)S(1)}, bf16[32,2048]{1,0:T(8,128)(2,1)S(1)}, u32[]{:S(2)}, u32[]{:S(2)}) collective-permute-start(bf16[32,2048]{1,0:T(8,128)(2,1)S(1)} %get-tuple-element.50), channel_id=1, source_target_pairs={{0,10},{2,8},{4,14},{6,12},{8,2},{10,0},{12,6},{14,4},{1,11},{3,9}... | collective-permute-start | bytes 393224 | tf_op jit(solution)/shard_map/ppermute | solution.py:35
  312.3 12.5 %collective-permute-start.39 = (bf16[32,2048]{1,0:T(8,128)(2,1)S(1)}, bf16[32,2048]{1,0:T(8,128)(2,1)S(1)}, u32[]{:S(2)}, u32[]{:S(2)}) collective-permute-start(bf16[32,2048]{1,0:T(8,128)(2,1)S(1)} %get-tuple-element.51), channel_id=1, source_target_pairs={{0,8},{2,10},{4,12},{6,14},{8,0},{10,2},{12,4},{14,6},{1,9},{3,11}... | collective-permute-start | bytes 393224 | tf_op jit(solution)/shard_map/ppermute | solution.py:35
  315.2 14.8 %collective-permute-start.38 = (bf16[32,2048]{1,0:T(8,128)(2,1)S(1)}, bf16[32,2048]{1,0:T(8,128)(2,1)S(1)}, u32[]{:S(2)}, u32[]{:S(2)}) collective-permute-start(bf16[32,2048]{1,0:T(8,128)(2,1)S(1)} %get-tuple-element.52), channel_id=1, source_target_pairs={{0,14},{2,12},{4,2},{6,0},{8,6},{10,4},{12,10},{14,8},{1,15},{3,13... | collective-permute-start | bytes 393224 | tf_op jit(solution)/shard_map/ppermute | solution.py:35
  315.2 15.5 %collective-permute-start.37 = (bf16[32,2048]{1,0:T(8,128)(2,1)S(1)}, bf16[32,2048]{1,0:T(8,128)(2,1)S(1)}, u32[]{:S(2)}, u32[]{:S(2)}) collective-permute-start(bf16[32,2048]{1,0:T(8,128)(2,1)S(1)} %get-tuple-element.53), channel_id=1, source_target_pairs={{0,12},{2,14},{4,0},{6,2},{8,4},{10,6},{12,8},{14,10},{1,13},{3,15... | collective-permute-start | bytes 393224 | tf_op jit(solution)/shard_map/ppermute | solution.py:35
  322.9 13.6 %collective-permute-start.36 = (bf16[32,2048]{1,0:T(8,128)(2,1)S(1)}, bf16[32,2048]{1,0:T(8,128)(2,1)S(1)}, u32[]{:S(2)}, u32[]{:S(2)}) collective-permute-start(bf16[32,2048]{1,0:T(8,128)(2,1)S(1)} %get-tuple-element.54), channel_id=1, source_target_pairs={{0,2},{2,0},{4,6},{6,4},{8,10},{10,8},{12,14},{14,12},{1,3},{3,1},... | collective-permute-start | bytes 393224 | tf_op jit(solution)/shard_map/ppermute | solution.py:35
  325.4 11.9 %collective-permute-start.63 = (bf16[32,2048]{1,0:T(8,128)(2,1)S(1)}, bf16[32,2048]{1,0:T(8,128)(2,1)S(1)}, u32[]{:S(2)}, u32[]{:S(2)}) collective-permute-start(bf16[32,2048]{1,0:T(8,128)(2,1)S(1)} %get-tuple-element.23), channel_id=1, source_target_pairs={{0,6},{2,4},{4,10},{6,8},{8,14},{10,12},{12,2},{14,0},{1,7},{3,5},... | collective-permute-start | bytes 393224 | tf_op jit(solution)/shard_map/ppermute | solution.py:35
  330.7 10.0 %collective-permute-start.62 = (bf16[32,2048]{1,0:T(8,128)(2,1)S(1)}, bf16[32,2048]{1,0:T(8,128)(2,1)S(1)}, u32[]{:S(2)}, u32[]{:S(2)}) collective-permute-start(bf16[32,2048]{1,0:T(8,128)(2,1)S(1)} %get-tuple-element.24), channel_id=1, source_target_pairs={{0,4},{2,6},{4,8},{6,10},{8,12},{10,14},{12,0},{14,2},{1,5},{3,7},... | collective-permute-start | bytes 393224 | tf_op jit(solution)/shard_map/ppermute | solution.py:35
  331.4 15.9 %collective-permute-start.61 = (bf16[32,2048]{1,0:T(8,128)(2,1)S(1)}, bf16[32,2048]{1,0:T(8,128)(2,1)S(1)}, u32[]{:S(2)}, u32[]{:S(2)}) collective-permute-start(bf16[32,2048]{1,0:T(8,128)(2,1)S(1)} %get-tuple-element.25), channel_id=1, source_target_pairs={{0,10},{2,8},{4,14},{6,12},{8,2},{10,0},{12,6},{14,4},{1,11},{3,9}... | collective-permute-start | bytes 393224 | tf_op jit(solution)/shard_map/ppermute | solution.py:35
  337.3 13.6 %collective-permute-start.60 = (bf16[32,2048]{1,0:T(8,128)(2,1)S(1)}, bf16[32,2048]{1,0:T(8,128)(2,1)S(1)}, u32[]{:S(2)}, u32[]{:S(2)}) collective-permute-start(bf16[32,2048]{1,0:T(8,128)(2,1)S(1)} %get-tuple-element.26), channel_id=1, source_target_pairs={{0,8},{2,10},{4,12},{6,14},{8,0},{10,2},{12,4},{14,6},{1,9},{3,11}... | collective-permute-start | bytes 393224 | tf_op jit(solution)/shard_map/ppermute | solution.py:35
  337.3 18.9 %collective-permute-start.59 = (bf16[32,2048]{1,0:T(8,128)(2,1)S(1)}, bf16[32,2048]{1,0:T(8,128)(2,1)S(1)}, u32[]{:S(2)}, u32[]{:S(2)}) collective-permute-start(bf16[32,2048]{1,0:T(8,128)(2,1)S(1)} %get-tuple-element.27), channel_id=1, source_target_pairs={{0,14},{2,12},{4,2},{6,0},{8,6},{10,4},{12,10},{14,8},{1,15},{3,13... | collective-permute-start | bytes 393224 | tf_op jit(solution)/shard_map/ppermute | solution.py:35
  340.7 16.2 %collective-permute-start.58 = (bf16[32,2048]{1,0:T(8,128)(2,1)S(1)}, bf16[32,2048]{1,0:T(8,128)(2,1)S(1)}, u32[]{:S(2)}, u32[]{:S(2)}) collective-permute-start(bf16[32,2048]{1,0:T(8,128)(2,1)S(1)} %get-tuple-element.28), channel_id=1, source_target_pairs={{0,12},{2,14},{4,0},{6,2},{8,4},{10,6},{12,8},{14,10},{1,13},{3,15... | collective-permute-start | bytes 393224 | tf_op jit(solution)/shard_map/ppermute | solution.py:35
  347.3 13.9 %collective-permute-start.57 = (bf16[32,2048]{1,0:T(8,128)(2,1)S(1)}, bf16[32,2048]{1,0:T(8,128)(2,1)S(1)}, u32[]{:S(2)}, u32[]{:S(2)}) collective-permute-start(bf16[32,2048]{1,0:T(8,128)(2,1)S(1)} %get-tuple-element.29), channel_id=1, source_target_pairs={{0,2},{2,0},{4,6},{6,4},{8,10},{10,8},{12,14},{14,12},{1,3},{3,1},... | collective-permute-start | bytes 393224 | tf_op jit(solution)/shard_map/ppermute | solution.py:35
  350.9 16.8 %collective-permute-start.42 = (bf16[32,2048]{1,0:T(8,128)(2,1)S(1)}, bf16[32,2048]{1,0:T(8,128)(2,1)S(1)}, u32[]{:S(2)}, u32[]{:S(2)}) collective-permute-start(bf16[32,2048]{1,0:T(8,128)(2,1)S(1)} %get-tuple-element.31), channel_id=1, source_target_pairs={{0,6},{2,4},{4,10},{6,8},{8,14},{10,12},{12,2},{14,0},{1,7},{3,5},... | collective-permute-start | bytes 393224 | tf_op jit(solution)/shard_map/ppermute | solution.py:35
  356.2 13.9 %collective-permute-start.56 = (bf16[32,2048]{1,0:T(8,128)(2,1)S(1)}, bf16[32,2048]{1,0:T(8,128)(2,1)S(1)}, u32[]{:S(2)}, u32[]{:S(2)}) collective-permute-start(bf16[32,2048]{1,0:T(8,128)(2,1)S(1)} %get-tuple-element.32), channel_id=1, source_target_pairs={{0,6},{2,4},{4,10},{6,8},{8,14},{10,12},{12,2},{14,0},{1,7},{3,5},... | collective-permute-start | bytes 393224 | tf_op jit(solution)/shard_map/ppermute | solution.py:35
  356.9 13.1 %collective-permute-start.55 = (bf16[32,2048]{1,0:T(8,128)(2,1)S(1)}, bf16[32,2048]{1,0:T(8,128)(2,1)S(1)}, u32[]{:S(2)}, u32[]{:S(2)}) collective-permute-start(bf16[32,2048]{1,0:T(8,128)(2,1)S(1)} %get-tuple-element.33), channel_id=1, source_target_pairs={{0,4},{2,6},{4,8},{6,10},{8,12},{10,14},{12,0},{14,2},{1,5},{3,7},... | collective-permute-start | bytes 393224 | tf_op jit(solution)/shard_map/ppermute | solution.py:35
  361.1 12.7 %collective-permute-start.54 = (bf16[32,2048]{1,0:T(8,128)(2,1)S(1)}, bf16[32,2048]{1,0:T(8,128)(2,1)S(1)}, u32[]{:S(2)}, u32[]{:S(2)}) collective-permute-start(bf16[32,2048]{1,0:T(8,128)(2,1)S(1)} %get-tuple-element.34), channel_id=1, source_target_pairs={{0,10},{2,8},{4,14},{6,12},{8,2},{10,0},{12,6},{14,4},{1,11},{3,9}... | collective-permute-start | bytes 393224 | tf_op jit(solution)/shard_map/ppermute | solution.py:35
  361.8 19.9 %collective-permute-start.53 = (bf16[32,2048]{1,0:T(8,128)(2,1)S(1)}, bf16[32,2048]{1,0:T(8,128)(2,1)S(1)}, u32[]{:S(2)}, u32[]{:S(2)}) collective-permute-start(bf16[32,2048]{1,0:T(8,128)(2,1)S(1)} %get-tuple-element.35), channel_id=1, source_target_pairs={{0,8},{2,10},{4,12},{6,14},{8,0},{10,2},{12,4},{14,6},{1,9},{3,11}... | collective-permute-start | bytes 393224 | tf_op jit(solution)/shard_map/ppermute | solution.py:35
  367.8 25.1 %collective-permute-start.52 = (bf16[32,2048]{1,0:T(8,128)(2,1)}, bf16[32,2048]{1,0:T(8,128)(2,1)S(1)}, u32[]{:S(2)}, u32[]{:S(2)}) collective-permute-start(bf16[32,2048]{1,0:T(8,128)(2,1)} %get-tuple-element.36), channel_id=1, source_target_pairs={{0,14},{2,12},{4,2},{6,0},{8,6},{10,4},{12,10},{14,8},{1,15},{3,13... | collective-permute-start | bytes 393224 | tf_op jit(solution)/shard_map/ppermute | solution.py:35
  370.1 26.8 %collective-permute-start.51 = (bf16[32,2048]{1,0:T(8,128)(2,1)}, bf16[32,2048]{1,0:T(8,128)(2,1)S(1)}, u32[]{:S(2)}, u32[]{:S(2)}) collective-permute-start(bf16[32,2048]{1,0:T(8,128)(2,1)} %get-tuple-element.37), channel_id=1, source_target_pairs={{0,12},{2,14},{4,0},{6,2},{8,4},{10,6},{12,8},{14,10},{1,13},{3,15... | collective-permute-start | bytes 393224 | tf_op jit(solution)/shard_map/ppermute | solution.py:35
  370.1 27.4 %collective-permute-start.50 = (bf16[32,2048]{1,0:T(8,128)(2,1)}, bf16[32,2048]{1,0:T(8,128)(2,1)}, u32[]{:S(2)}, u32[]{:S(2)}) collective-permute-start(bf16[32,2048]{1,0:T(8,128)(2,1)} %get-tuple-element.38), channel_id=1, source_target_pairs={{0,2},{2,0},{4,6},{6,4},{8,10},{10,8},{12,14},{14,12},{1,3},{3,1},... | collective-permute-start | bytes 393224 | tf_op jit(solution)/shard_map/ppermute | solution.py:35
  373.8 26.5 %collective-permute-start.8 = (bf16[32,4096]{1,0:T(8,128)(2,1)S(1)}, bf16[32,4096]{1,0:T(8,128)(2,1)S(1)}, u32[]{:S(2)}, u32[]{:S(2)}) collective-permute-start(bf16[32,4096]{1,0:T(8,128)(2,1)S(1)} %get-tuple-element.79), channel_id=1, source_target_pairs={{0,6},{2,4},{4,10},{6,8},{8,14},{10,12},{12,2},{14,0},{1,7},{3,5},... | collective-permute-start | bytes 786440 | tf_op jit(solution)/shard_map/ppermute | solution.py:35
  381.7 20.5 %collective-permute-start.7 = (bf16[32,4096]{1,0:T(8,128)(2,1)S(1)}, bf16[32,4096]{1,0:T(8,128)(2,1)S(1)}, u32[]{:S(2)}, u32[]{:S(2)}) collective-permute-start(bf16[32,4096]{1,0:T(8,128)(2,1)S(1)} %get-tuple-element.80), channel_id=1, source_target_pairs={{0,4},{2,6},{4,8},{6,10},{8,12},{10,14},{12,0},{14,2},{1,5},{3,7},... | collective-permute-start | bytes 786440 | tf_op jit(solution)/shard_map/ppermute | solution.py:35
  392.9 19.6 %collective-permute-start.6 = (bf16[32,4096]{1,0:T(8,128)(2,1)S(1)}, bf16[32,4096]{1,0:T(8,128)(2,1)S(1)}, u32[]{:S(2)}, u32[]{:S(2)}) collective-permute-start(bf16[32,4096]{1,0:T(8,128)(2,1)S(1)} %get-tuple-element.81), channel_id=1, source_target_pairs={{0,10},{2,8},{4,14},{6,12},{8,2},{10,0},{12,6},{14,4},{1,11},{3,9}... | collective-permute-start | bytes 786440 | tf_op jit(solution)/shard_map/ppermute | solution.py:35
  397.5 20.1 %collective-permute-start.5 = (bf16[32,4096]{1,0:T(8,128)(2,1)S(1)}, bf16[32,4096]{1,0:T(8,128)(2,1)S(1)}, u32[]{:S(2)}, u32[]{:S(2)}) collective-permute-start(bf16[32,4096]{1,0:T(8,128)(2,1)S(1)} %get-tuple-element.82), channel_id=1, source_target_pairs={{0,8},{2,10},{4,12},{6,14},{8,0},{10,2},{12,4},{14,6},{1,9},{3,11}... | collective-permute-start | bytes 786440 | tf_op jit(solution)/shard_map/ppermute | solution.py:35
  397.5 20.1 %collective-permute-start.4 = (bf16[32,4096]{1,0:T(8,128)(2,1)S(1)}, bf16[32,4096]{1,0:T(8,128)(2,1)S(1)}, u32[]{:S(2)}, u32[]{:S(2)}) collective-permute-start(bf16[32,4096]{1,0:T(8,128)(2,1)S(1)} %get-tuple-element.83), channel_id=1, source_target_pairs={{0,14},{2,12},{4,2},{6,0},{8,6},{10,4},{12,10},{14,8},{1,15},{3,13... | collective-permute-start | bytes 786440 | tf_op jit(solution)/shard_map/ppermute | solution.py:35
  400.3 32.7 %collective-permute-start.3 = (bf16[32,4096]{1,0:T(8,128)(2,1)S(1)}, bf16[32,4096]{1,0:T(8,128)(2,1)S(1)}, u32[]{:S(2)}, u32[]{:S(2)}) collective-permute-start(bf16[32,4096]{1,0:T(8,128)(2,1)S(1)} %get-tuple-element.84), channel_id=1, source_target_pairs={{0,12},{2,14},{4,0},{6,2},{8,4},{10,6},{12,8},{14,10},{1,13},{3,15... | collective-permute-start | bytes 786440 | tf_op jit(solution)/shard_map/ppermute | solution.py:35
  402.3 30.8 %collective-permute-start.2 = (bf16[32,4096]{1,0:T(8,128)(2,1)S(1)}, bf16[32,4096]{1,0:T(8,128)(2,1)S(1)}, u32[]{:S(2)}, u32[]{:S(2)}) collective-permute-start(bf16[32,4096]{1,0:T(8,128)(2,1)S(1)} %get-tuple-element.85), channel_id=1, source_target_pairs={{0,2},{2,0},{4,6},{6,4},{8,10},{10,8},{12,14},{14,12},{1,3},{3,1},... | collective-permute-start | bytes 786440 | tf_op jit(solution)/shard_map/ppermute | solution.py:35
  412.5 29.9 %collective-permute-start.47 = (bf16[32,1024]{1,0:T(8,128)(2,1)S(1)}, bf16[32,1024]{1,0:T(8,128)(2,1)S(1)}, u32[]{:S(2)}, u32[]{:S(2)}) collective-permute-start(bf16[32,1024]{1,0:T(8,128)(2,1)S(1)} %copy-done.47), channel_id=1, source_target_pairs={{0,10},{2,8},{4,14},{6,12},{8,2},{10,0},{12,6},{14,4},{1,11},{3,9}... | collective-permute-start | bytes 196616 | tf_op jit(solution)/shard_map/ppermute | solution.py:35
  417.6 26.9 %collective-permute-start.46 = (bf16[32,1024]{1,0:T(8,128)(2,1)S(1)}, bf16[32,1024]{1,0:T(8,128)(2,1)S(1)}, u32[]{:S(2)}, u32[]{:S(2)}) collective-permute-start(bf16[32,1024]{1,0:T(8,128)(2,1)S(1)} %copy-done.46), channel_id=1, source_target_pairs={{0,8},{2,10},{4,12},{6,14},{8,0},{10,2},{12,4},{14,6},{1,9},{3,11}... | collective-permute-start | bytes 196616 | tf_op jit(solution)/shard_map/ppermute | solution.py:35
  417.7 29.8 %collective-permute-start.45 = (bf16[32,1024]{1,0:T(8,128)(2,1)S(1)}, bf16[32,1024]{1,0:T(8,128)(2,1)S(1)}, u32[]{:S(2)}, u32[]{:S(2)}) collective-permute-start(bf16[32,1024]{1,0:T(8,128)(2,1)S(1)} %copy-done.45), channel_id=1, source_target_pairs={{0,14},{2,12},{4,2},{6,0},{8,6},{10,4},{12,10},{14,8},{1,15},{3,13... | collective-permute-start | bytes 196616 | tf_op jit(solution)/shard_map/ppermute | solution.py:35
  433.0 14.5 %collective-permute-start.44 = (bf16[32,1024]{1,0:T(8,128)(2,1)S(1)}, bf16[32,1024]{1,0:T(8,128)(2,1)S(1)}, u32[]{:S(2)}, u32[]{:S(2)}) collective-permute-start(bf16[32,1024]{1,0:T(8,128)(2,1)S(1)} %copy-done.44), channel_id=1, source_target_pairs={{0,12},{2,14},{4,0},{6,2},{8,4},{10,6},{12,8},{14,10},{1,13},{3,15... | collective-permute-start | bytes 196616 | tf_op jit(solution)/shard_map/ppermute | solution.py:35
  433.1 15.5 %collective-permute-start.43 = (bf16[32,1024]{1,0:T(8,128)(2,1)S(1)}, bf16[32,1024]{1,0:T(8,128)(2,1)S(1)}, u32[]{:S(2)}, u32[]{:S(2)}) collective-permute-start(bf16[32,1024]{1,0:T(8,128)(2,1)S(1)} %copy-done.43), channel_id=1, source_target_pairs={{0,2},{2,0},{4,6},{6,4},{8,10},{10,8},{12,14},{14,12},{1,3},{3,1},... | collective-permute-start | bytes 196616 | tf_op jit(solution)/shard_map/ppermute | solution.py:35
  442.5 14.1 %collective-permute-start.21 = (bf16[32,1024]{1,0:T(8,128)(2,1)S(1)}, bf16[32,1024]{1,0:T(8,128)(2,1)S(1)}, u32[]{:S(2)}, u32[]{:S(2)}) collective-permute-start(bf16[32,1024]{1,0:T(8,128)(2,1)S(1)} %copy-done.41), channel_id=1, source_target_pairs={{0,8},{2,10},{4,12},{6,14},{8,0},{10,2},{12,4},{14,6},{1,9},{3,11}... | collective-permute-start | bytes 196616 | tf_op jit(solution)/shard_map/ppermute | solution.py:35
  444.5 12.1 %collective-permute-start.20 = (bf16[32,1024]{1,0:T(8,128)(2,1)S(1)}, bf16[32,1024]{1,0:T(8,128)(2,1)S(1)}, u32[]{:S(2)}, u32[]{:S(2)}) collective-permute-start(bf16[32,1024]{1,0:T(8,128)(2,1)S(1)} %copy-done.40), channel_id=1, source_target_pairs={{0,14},{2,12},{4,2},{6,0},{8,6},{10,4},{12,10},{14,8},{1,15},{3,13... | collective-permute-start | bytes 196616 | tf_op jit(solution)/shard_map/ppermute | solution.py:35
  (66 other events, 892.2 us)

commit v8 on v7

--- a/solution.py
+++ b/solution.py
@@ -173,7 +173,7 @@
 
 def inverse_fourier(pieces, tables, shape, start, levels, current=None, partial=None, dtype=None):
     _, rows_here, lon_count = shape
-    block = level_block(levels, rows_here, 8 if partial is None else levels // 2)
+    block = level_block(levels, rows_here, 8 if partial is None or levels <= 16 else 16)
     width = block * rows_here
     first = start // block
     height = sum(table.shape[0] for table in tables)
@@ -503,11 +503,10 @@
             pieces.append(piece.reshape(2, count, width))
         arrived.append(pieces)
 
-    half, fourth = local_levels // 2, local_levels // 4
-    groups = [(0, half), (half, fourth), (half + fourth, fourth)]
+    most = local_levels // 4 * 3
+    groups = [(0, most), (most, local_levels - most)]
     cuts = {chunk: [(0, local_levels)] for chunk in range(chunks)}
-    cuts[1] = [(0, half), (half, half)]
-    cuts[chunks - 1] = groups
+    cuts[1] = cuts[chunks - 1] = groups
     returned = []
     for chunk in range(chunks):
         is_whole = chunk in WHOLE_SENDS
@@ -566,7 +565,7 @@
             )
         )
     current = None
-    for start, levels in groups:
+    for cut, (start, levels) in enumerate(groups):
         current = inverse_fourier(
             pieces_at(everything[2:], start),
             tables[2:],
@@ -574,7 +573,7 @@
             start,
             levels,
             current=current,
-            partial=(partials[0], 0) if start < half else (partials[1], half),
+            partial=(partials[cut], start),
         )
     return current.reshape(out_shape)
 

time: 464 us -> 477 us (1.028)
  starting transfers between devices: 175 us -> 191 us
    ppermute x56 -> x49, starting transfers between devices: 157 us -> 174 us  [shift_places(): return lax.ppermute(value, EXCHANGE_AXES, pairs)]
    mul x6 -> x5, other arithmetic: 14.3 us -> 11.1 us  [joined(): scale * (other.astype(jnp.float32) + hemi_sign * own.astype(jnp.float32))]
    unnamed x134 -> x128, local copies, waits for them, and re-layouts: 13.5 us -> 10.7 us
    pallas_call x5 -> x4, Pallas kernels: 36.7 us -> 35.7 us  [inverse_fourier(): pl.pallas_call(functools.partial(inverse_kernel, len(pieces), len(tables)...]
    ppermute x56 -> x49, waiting for transfers between devices: 71.4 us -> 71.2 us  [shift_places(): return lax.ppermute(value, EXCHANGE_AXES, pairs)]
  transfers between devices with their start and end apart: 67 -> 60, of which waited for: 16 -> 13; matrix products, arithmetic and copies ran while one was open for 9% -> 8% of each run, Pallas kernels for 30% -> 29%
where the time goes in v8:
time: 477 us; the launch traced here: 476 us
  starting transfers between devices  191 us (40%)
  Pallas kernels  156 us (33%)
  waiting for transfers between devices  85.9 us (18%)
  other arithmetic  24.9 us (5%)
  local copies, waits for them, and re-layouts  17 us (4%)
    ppermute x49, starting transfers between devices, shift_places(): return lax.ppermute(value, EXCHANGE_AXES, pairs)  174 us
    pallas_call x4, Pallas kernels, columns_fused(): pl.pallas_call(functools.partial(column_kernel, sizes), out_shape=jax.Sha...  78.7 us
    ppermute x49, waiting for transfers between devices, shift_places(): return lax.ppermute(value, EXCHANGE_AXES, pairs)  71.2 us
    pallas_call x4, Pallas kernels, fourier(): pl.pallas_call(functools.partial(fourier_kernel, sizes), out_shape=[jax.S...  41.3 us
    pallas_call x4, Pallas kernels, inverse_fourier(): pl.pallas_call(functools.partial(inverse_kernel, len(pieces), len(tables)...  35.7 us
    all_to_all x3, starting transfers between devices, exchange(): lax.all_to_all(value, EXCHANGE_AXES, split_axis=0, concat_axis=0, tiled=T...  15.6 us
    all_to_all x3, waiting for transfers between devices, exchange(): lax.all_to_all(value, EXCHANGE_AXES, split_axis=0, concat_axis=0, tiled=T...  14.7 us
    mul x5, other arithmetic, joined(): scale * (other.astype(jnp.float32) + hemi_sign * own.astype(jnp.float32))  11.1 us
  transfers between devices with their start and end apart: 60, of which 13 were waited for; matrix products, arithmetic and copies ran while one was open for 8% of the time, Pallas kernels for 29%

profile of v8, /device:TPU:0, one launch (start us, length us, event | category | flops | bytes accessed | tf_op | source)
XLA Modules:
  0.0 475.5 jit_solution(11344306971447363983)
XLA Ops:
  0.6 10.3 %shard_map.77 = (bf16[256,4096]{1,0:T(8,128)(2,1)}, bf16[256,1536]{1,0:T(8,128)(2,1)}) custom-call(s32[3]{0:T(128)} %pad_add_fusion.1.place_ref, bf16[64,64,1536]{2,1,0:T(8,128)(2,1)} %bitcast.136, s32[1,512]{1,0:T(1,128)} %bitcast.176, s32[1,256]{1,0:T(1,128)} %bitcast.180), custom_call_target="tpu_custom_call" | custom-call | flops 3221225472 | bytes 15466496 | tf_op jit(solution)/shard_map/pallas_call | solution.py:119
  10.8 7.3 %all-to-all-start.1 = ((bf16[8,2,16,4096]{3,2,1,0:T(8,128)(2,1)}), bf16[8,2,16,4096]{3,2,1,0:T(8,128)(2,1)S(1)}, u32[]{:S(2)}, u32[]{:S(2)}) async-start(bf16[8,2,16,4096]{3,2,1,0:T(8,128)(2,1)} %bitcast.156), calls=%async_computation.1 | async-start | bytes 4194304 | tf_op jit(solution)/shard_map/all_to_all | solution.py:438
  18.1 10.4 %shard_map.79 = (bf16[256,4096]{1,0:T(8,128)(2,1)}, bf16[256,1536]{1,0:T(8,128)(2,1)}) custom-call(s32[3]{0:T(128)} %pad_add_fusion.1.place_ref, bf16[64,64,1536]{2,1,0:T(8,128)(2,1)} %bitcast.137, s32[1,512]{1,0:T(1,128)} %bitcast.177, s32[1,256]{1,0:T(1,128)} %bitcast.181), custom_call_target="tpu_custom_call" | custom-call | flops 3221225472 | bytes 15466496 | tf_op jit(solution)/shard_map/pallas_call | solution.py:119
  28.6 10.4 %shard_map.75 = (bf16[256,4096]{1,0:T(8,128)(2,1)}, bf16[256,1536]{1,0:T(8,128)(2,1)}) custom-call(s32[3]{0:T(128)} %pad_add_fusion.1.place_ref, bf16[64,64,1536]{2,1,0:T(8,128)(2,1)} %bitcast.138, s32[1,512]{1,0:T(1,128)} %bitcast.178, s32[1,256]{1,0:T(1,128)} %bitcast.182), custom_call_target="tpu_custom_call" | custom-call | flops 3221225472 | bytes 15466496 | tf_op jit(solution)/shard_map/pallas_call | solution.py:119
  41.4 10.2 %shard_map.73 = (bf16[256,4096]{1,0:T(8,128)(2,1)}, bf16[256,1536]{1,0:T(8,128)(2,1)}) custom-call(s32[3]{0:T(128)} %pad_add_fusion.1.place_ref, bf16[64,64,1536]{2,1,0:T(8,128)(2,1)} %bitcast.139, s32[1,512]{1,0:T(1,128)} %bitcast.179, s32[1,256]{1,0:T(1,128)} %bitcast.183), custom_call_target="tpu_custom_call" | custom-call | flops 3221225472 | bytes 15466496 | tf_op jit(solution)/shard_map/pallas_call | solution.py:119
  51.6 14.7 %all-to-all-done.1.refs_0_ = bf16[8,2,16,4096]{3,2,1,0:T(8,128)(2,1)S(1)} async-done(((bf16[8,2,16,4096]{3,2,1,0:T(8,128)(2,1)}), bf16[8,2,16,4096]{3,2,1,0:T(8,128)(2,1)S(1)}, u32[]{:S(2)}, u32[]{:S(2)}) %all-to-all-start.1) | async-done | bytes 2097184 | tf_op jit(solution)/shard_map/all_to_all | solution.py:438
  66.4 4.7 all-to-all-start
  78.8 3.6 add_convert_fusion
  82.4 4.3 collective-permute-start.34
  87.3 20.4 %shard_map.78 = bf16[8,2,16,4096]{3,2,1,0:T(8,128)(2,1)} custom-call(s32[64]{0:T(128)} %dynamic_slice.77.waves, s32[5]{0:T(128)} %pad_add_fusion.scalars, f32[128,1]{1,0:T(8,128)} %copy.11.eig_ref, bf16[128,128]{1,0:T(8,128)(2,1)} %select_bitcast_fusion.1.modes_in, bf16[128,128]{1,0:T(8,128)(2,1)} %broadcast_select_fusion.1.modes_out, ...), custom_call_target="tpu_custom_call" | custom-call | flops 1610612736 | bytes 6291456 | tf_op jit(solution)/shard_map/pallas_call | solution.py:357
  107.7 3.0 collective-permute-start.31
  110.7 1.5 collective-permute-done.34
  112.2 32.2 %collective-permute-start.30 = (bf16[32,4096]{1,0:T(8,128)(2,1)S(1)}, bf16[32,4096]{1,0:T(8,128)(2,1)}, u32[]{:S(2)}, u32[]{:S(2)}) collective-permute-start(bf16[32,4096]{1,0:T(8,128)(2,1)S(1)} %get-tuple-element.51), channel_id=1, source_target_pairs={{0,6},{2,4},{4,10},{6,8},{8,14},{10,12},{12,2},{14,0},{1,7},{3,5},... | collective-permute-start | bytes 786440 | tf_op jit(solution)/shard_map/ppermute | solution.py:35
  144.4 10.3 %collective-permute-start.29 = (bf16[32,4096]{1,0:T(8,128)(2,1)S(1)}, bf16[32,4096]{1,0:T(8,128)(2,1)}, u32[]{:S(2)}, u32[]{:S(2)}) collective-permute-start(bf16[32,4096]{1,0:T(8,128)(2,1)S(1)} %get-tuple-element.52), channel_id=1, source_target_pairs={{0,4},{2,6},{4,8},{6,10},{8,12},{10,14},{12,0},{14,2},{1,5},{3,7},... | collective-permute-start | bytes 786440 | tf_op jit(solution)/shard_map/ppermute | solution.py:35
  154.7 5.0 %collective-permute-done.32 = bf16[32,4096]{1,0:T(8,128)(2,1)S(1)} collective-permute-done((bf16[32,4096]{1,0:T(8,128)(2,1)S(1)}, bf16[32,4096]{1,0:T(8,128)(2,1)S(1)}, u32[]{:S(2)}, u32[]{:S(2)}) %collective-permute-start.32) | collective-permute-done | bytes 262176 | tf_op jit(solution)/shard_map/ppermute | solution.py:35
  159.8 1.5 collective-permute-start.28
  161.3 3.2 add_convert_fusion.8
  166.8 3.4 collective-permute-start.14
  171.1 3.6 collective-permute-done.16
  175.5 5.2 %collective-permute-done.15 = bf16[32,4096]{1,0:T(8,128)(2,1)S(1)} collective-permute-done((bf16[32,4096]{1,0:T(8,128)(2,1)}, bf16[32,4096]{1,0:T(8,128)(2,1)S(1)}, u32[]{:S(2)}, u32[]{:S(2)}) %collective-permute-start.15) | collective-permute-done | bytes 262176 | tf_op jit(solution)/shard_map/ppermute | solution.py:35
  180.7 14.4 %collective-permute-start.12 = (bf16[32,4096]{1,0:T(8,128)(2,1)}, bf16[32,4096]{1,0:T(8,128)(2,1)S(1)}, u32[]{:S(2)}, u32[]{:S(2)}) collective-permute-start(bf16[32,4096]{1,0:T(8,128)(2,1)} %get-tuple-element.67), channel_id=1, source_target_pairs={{0,6},{2,4},{4,10},{6,8},{8,14},{10,12},{12,2},{14,0},{1,7},{3,5},... | collective-permute-start | bytes 786440 | tf_op jit(solution)/shard_map/ppermute | solution.py:35
  195.1 5.2 %collective-permute-done.14 = bf16[32,4096]{1,0:T(8,128)(2,1)} collective-permute-done((bf16[32,4096]{1,0:T(8,128)(2,1)}, bf16[32,4096]{1,0:T(8,128)(2,1)}, u32[]{:S(2)}, u32[]{:S(2)}) %collective-permute-start.14) | collective-permute-done | bytes 262176 | tf_op jit(solution)/shard_map/ppermute | solution.py:35
  200.3 5.5 %collective-permute-done.13 = bf16[32,4096]{1,0:T(8,128)(2,1)} collective-permute-done((bf16[32,4096]{1,0:T(8,128)(2,1)}, bf16[32,4096]{1,0:T(8,128)(2,1)}, u32[]{:S(2)}, u32[]{:S(2)}) %collective-permute-start.13) | collective-permute-done | bytes 262176 | tf_op jit(solution)/shard_map/ppermute | solution.py:35
  205.9 4.6 collective-permute-start.10
  211.1 18.9 %shard_map.80 = bf16[8,2,16,4096]{3,2,1,0:T(8,128)(2,1)} custom-call(s32[64]{0:T(128)} %dynamic_slice.77.waves, s32[5]{0:T(128)} %pad_add_fusion.2.scalars, f32[128,1]{1,0:T(8,128)} %copy.11.eig_ref, bf16[128,128]{1,0:T(8,128)(2,1)} %select_bitcast_fusion.modes_in, bf16[128,128]{1,0:T(8,128)(2,1)} %broadcast_select_fusion.modes_out, ...), custom_call_target="tpu_custom_call" | custom-call | flops 1610612736 | bytes 6291456 | tf_op jit(solution)/shard_map/pallas_call | solution.py:357
  230.9 19.0 %shard_map.76 = bf16[8,2,16,4096]{3,2,1,0:T(8,128)(2,1)} custom-call(s32[64]{0:T(128)} %dynamic_slice.77.waves, s32[5]{0:T(128)} %pad_add_fusion.2.scalars, f32[128,1]{1,0:T(8,128)} %copy.11.eig_ref, bf16[128,128]{1,0:T(8,128)(2,1)} %select_bitcast_fusion.modes_in, bf16[128,128]{1,0:T(8,128)(2,1)} %broadcast_select_fusion.modes_out, ...), custom_call_target="tpu_custom_call" | custom-call | flops 1610612736 | bytes 6291456 | tf_op jit(solution)/shard_map/pallas_call | solution.py:357
  250.4 2.3 multiply_convert_fusion
  252.8 3.6 all-to-all-start.2
  258.2 20.4 %shard_map.74 = bf16[8,2,16,4096]{3,2,1,0:T(8,128)(2,1)} custom-call(s32[64]{0:T(128)} %dynamic_slice.77.waves, s32[5]{0:T(128)} %pad_add_fusion.scalars, f32[128,1]{1,0:T(8,128)} %copy.11.eig_ref, bf16[128,128]{1,0:T(8,128)(2,1)} %select_bitcast_fusion.1.modes_in, bf16[128,128]{1,0:T(8,128)(2,1)} %broadcast_select_fusion.1.modes_out, ...), custom_call_target="tpu_custom_call" | custom-call | flops 1610612736 | bytes 6291456 | tf_op jit(solution)/shard_map/pallas_call | solution.py:357
  280.4 1.9 fusion.39
  282.3 2.8 collective-permute-start.42
  285.2 1.5 collective-permute-start.41
  287.6 2.7 fusion.23
  290.3 1.9 collective-permute-start.39
  292.2 5.8 %collective-permute-done.42.refs_8_ = bf16[32,1024]{1,0:T(8,128)(2,1)S(1)} collective-permute-done((bf16[32,1024]{1,0:T(8,128)(2,1)S(1)}, bf16[32,1024]{1,0:T(8,128)(2,1)S(1)}, u32[]{:S(2)}, u32[]{:S(2)}) %collective-permute-start.42) | collective-permute-done | bytes 65568 | tf_op jit(solution)/shard_map/ppermute | solution.py:35
  298.1 10.7 %collective-permute-start.56 = (bf16[32,3072]{1,0:T(8,128)(2,1)S(1)}, bf16[32,3072]{1,0:T(8,128)(2,1)S(1)}, u32[]{:S(2)}, u32[]{:S(2)}) collective-permute-start(bf16[32,3072]{1,0:T(8,128)(2,1)S(1)} %get-tuple-element.23), channel_id=1, source_target_pairs={{0,6},{2,4},{4,10},{6,8},{8,14},{10,12},{12,2},{14,0},{1,7},{3,5},... | collective-permute-start | bytes 589832 | tf_op jit(solution)/shard_map/ppermute | solution.py:35
  308.8 3.3 collective-permute-start.55
  312.1 18.3 %collective-permute-done.40.refs_6_ = bf16[32,1024]{1,0:T(8,128)(2,1)S(1)} collective-permute-done((bf16[32,1024]{1,0:T(8,128)(2,1)S(1)}, bf16[32,1024]{1,0:T(8,128)(2,1)S(1)}, u32[]{:S(2)}, u32[]{:S(2)}) %collective-permute-start.40) | collective-permute-done | bytes 65568 | tf_op jit(solution)/shard_map/ppermute | solution.py:35
  331.1 2.8 fusion.15
  334.0 2.8 collective-permute-start.53
  336.8 2.4 collective-permute-start.51
  339.3 1.5 collective-permute-done.54.refs_6_
  341.3 1.7 fusion.7
  343.0 1.7 collective-permute-done.53.refs_5_
  345.3 8.4 %collective-permute-done.52.refs_4_ = bf16[32,3072]{1,0:T(8,128)(2,1)S(1)} collective-permute-done((bf16[32,3072]{1,0:T(8,128)(2,1)S(1)}, bf16[32,3072]{1,0:T(8,128)(2,1)S(1)}, u32[]{:S(2)}, u32[]{:S(2)}) %collective-permute-start.52) | collective-permute-done | bytes 196640 | tf_op jit(solution)/shard_map/ppermute | solution.py:35
  353.7 5.6 %collective-permute-start.47 = (bf16[32,3072]{1,0:T(8,128)(2,1)S(1)}, bf16[32,3072]{1,0:T(8,128)(2,1)S(1)}, u32[]{:S(2)}, u32[]{:S(2)}) collective-permute-start(bf16[32,3072]{1,0:T(8,128)(2,1)S(1)} %get-tuple-element.33), channel_id=1, source_target_pairs={{0,10},{2,8},{4,14},{6,12},{8,2},{10,0},{12,6},{14,4},{1,11},{3,9}... | collective-permute-start | bytes 589832 | tf_op jit(solution)/shard_map/ppermute | solution.py:35
  359.2 3.5 collective-permute-start.46
  362.7 11.7 %collective-permute-start.8 = (bf16[32,4096]{1,0:T(8,128)(2,1)S(1)}, bf16[32,4096]{1,0:T(8,128)(2,1)S(1)}, u32[]{:S(2)}, u32[]{:S(2)}) collective-permute-start(bf16[32,4096]{1,0:T(8,128)(2,1)S(1)} %get-tuple-element.71), channel_id=1, source_target_pairs={{0,6},{2,4},{4,10},{6,8},{8,14},{10,12},{12,2},{14,0},{1,7},{3,5},... | collective-permute-start | bytes 786440 | tf_op jit(solution)/shard_map/ppermute | solution.py:35
  375.4 4.1 collective-permute-start.45
  380.1 9.3 %collective-permute-done.46.refs_12_ = bf16[32,3072]{1,0:T(8,128)(2,1)S(1)} collective-permute-done((bf16[32,3072]{1,0:T(8,128)(2,1)S(1)}, bf16[32,3072]{1,0:T(8,128)(2,1)S(1)}, u32[]{:S(2)}, u32[]{:S(2)}) %collective-permute-start.46) | collective-permute-done | bytes 196640 | tf_op jit(solution)/shard_map/ppermute | solution.py:35
  390.5 1.9 fusion.31
  393.7 12.1 %collective-permute-start.5 = (bf16[32,4096]{1,0:T(8,128)(2,1)}, bf16[32,4096]{1,0:T(8,128)(2,1)}, u32[]{:S(2)}, u32[]{:S(2)}) collective-permute-start(bf16[32,4096]{1,0:T(8,128)(2,1)} %get-tuple-element.74), channel_id=1, source_target_pairs={{0,8},{2,10},{4,12},{6,14},{8,0},{10,2},{12,4},{14,6},{1,9},{3,11}... | collective-permute-start | bytes 786440 | tf_op jit(solution)/shard_map/ppermute | solution.py:35
  405.8 3.9 collective-permute-start.4
  412.3 11.7 %shard_map.82.refs_18_ = bf16[48,64,1536]{2,1,0:T(8,128)(2,1)} custom-call(bf16[256,4096]{1,0:T(8,128)(2,1)} %bitcast.150, bf16[32,3072]{1,0:T(8,128)(2,1)} %get-tuple-element.30.refs_1_, bf16[32,3072]{1,0:T(8,128)(2,1)} %copy-done.59, bf16[32,3072]{1,0:T(8,128)(2,1)} %copy-done.58, bf16[32,3072]{1,0:T(8,128)(2,1)} %copy-done.57, ...), custom_call_target="tpu_custom_call" | custom-call | flops 4831838208 | bytes 12582912 | tf_op jit(solution)/shard_map/pallas_call | solution.py:203
  424.1 4.4 collective-permute-start.38
  428.5 8.8 %collective-permute-start.37 = (bf16[32,1024]{1,0:T(8,128)(2,1)S(1)}, bf16[32,1024]{1,0:T(8,128)(2,1)S(1)}, u32[]{:S(2)}, u32[]{:S(2)}) collective-permute-start(bf16[32,1024]{1,0:T(8,128)(2,1)S(1)} %copy-done.43), channel_id=1, source_target_pairs={{0,12},{2,14},{4,0},{6,2},{8,4},{10,6},{12,8},{14,10},{1,13},{3,15... | collective-permute-start | bytes 196616 | tf_op jit(solution)/shard_map/ppermute | solution.py:35
  437.3 1.8 collective-permute-start.36
  439.3 12.8 %shard_map.83.refs_19_ = bf16[64,64,1536]{2,1,0:T(8,128)(2,1)} custom-call(bf16[32,4096]{1,0:T(8,128)(2,1)} %get-tuple-element.78.refs_0_, bf16[32,4096]{1,0:T(8,128)(2,1)} %collective-permute-done.2.refs_1_, bf16[32,4096]{1,0:T(8,128)(2,1)} %collective-permute-done.3.refs_2_, bf16[32,4096]{1,0:T(8,128)(2,1)} %collective-permute-done.4.refs_3_, ...), custom_call_target="tpu_custom_call" | custom-call | flops 4831838208 | bytes 12582912 | tf_op jit(solution)/shard_map/pallas_call | solution.py:203
  452.1 5.3 %collective-permute-start.22 = (bf16[32,1024]{1,0:T(8,128)(2,1)S(1)}, bf16[32,1024]{1,0:T(8,128)(2,1)S(1)}, u32[]{:S(2)}, u32[]{:S(2)}) collective-permute-start(bf16[32,1024]{1,0:T(8,128)(2,1)S(1)} %copy-done.48), channel_id=1, source_target_pairs={{0,10},{2,8},{4,14},{6,12},{8,2},{10,0},{12,6},{14,4},{1,11},{3,9}... | collective-permute-start | bytes 196616 | tf_op jit(solution)/shard_map/ppermute | solution.py:35
  457.5 2.4 collective-permute-start.20
  459.9 1.7 collective-permute-start.19
  461.6 1.8 collective-permute-start.18
  463.4 5.8 %shard_map.81.refs_18_ = bf16[16,64,1536]{2,1,0:T(8,128)(2,1)} custom-call(bf16[256,4096]{1,0:T(8,128)(2,1)} %bitcast.151, bf16[32,1024]{1,0:T(8,128)(2,1)} %get-tuple-element.46.refs_1_, bf16[32,1024]{1,0:T(8,128)(2,1)} %copy-done.36, bf16[32,1024]{1,0:T(8,128)(2,1)} %copy-done.35, bf16[32,1024]{1,0:T(8,128)(2,1)} %copy-done.34, ...), custom_call_target="tpu_custom_call" | custom-call | flops 1610612736 | bytes 4194304 | tf_op jit(solution)/shard_map/pallas_call | solution.py:203
  469.9 5.4 %shard_map.84 = bf16[64,64,1536]{2,1,0:T(8,128)(2,1)} custom-call(bf16[32,4096]{1,0:T(8,128)(2,1)} %get-tuple-element.78.refs_0_, bf16[32,4096]{1,0:T(8,128)(2,1)} %collective-permute-done.2.refs_1_, bf16[32,4096]{1,0:T(8,128)(2,1)} %collective-permute-done.3.refs_2_, ...), custom_call_target="tpu_custom_call", output_to_operand_aliasing={{}: (19, {})} | custom-call | flops 1610612736 | bytes 4194304 | tf_op jit(solution)/shard_map/pallas_call | solution.py:203
  (233 shorter events, 30.7 us)
Async XLA Ops:
  0.0 73.3 %copy-start = (bf16[128,128]{1,0:T(8,128)(2,1)S(1)}, bf16[128,128]{1,0:T(8,128)(2,1)}, u32[]{:S(2)}) copy-start(bf16[128,128]{1,0:T(8,128)(2,1)} %param.17) | copy-start | bytes 98308
  10.8 55.5 %all-to-all-start.1 = ((bf16[8,2,16,4096]{3,2,1,0:T(8,128)(2,1)}), bf16[8,2,16,4096]{3,2,1,0:T(8,128)(2,1)S(1)}, u32[]{:S(2)}, u32[]{:S(2)}) async-start(bf16[8,2,16,4096]{3,2,1,0:T(8,128)(2,1)} %bitcast.156), calls=%async_computation.1 | async-start | bytes 4194304 | tf_op jit(solution)/shard_map/all_to_all | solution.py:438
  28.6 50.3 %collective-permute-start.27 = (bf16[256,4096]{1,0:T(8,128)(2,1)}, bf16[256,4096]{1,0:T(8,128)(2,1)}, u32[]{:S(2)}, u32[]{:S(2)}) collective-permute-start(bf16[256,4096]{1,0:T(8,128)(2,1)} %get-tuple-element.20), channel_id=1, source_target_pairs={{0,1},{1,0},{2,3},{3,2},{4,5},{5,4},{6,7},{7,6},{8,9},{9,8},{10,11... | collective-permute-start | bytes 6291464 | tf_op jit(solution)/shard_map/ppermute | solution.py:23
  39.1 68.7 %collective-permute-start.9 = (bf16[256,4096]{1,0:T(8,128)(2,1)}, bf16[256,4096]{1,0:T(8,128)(2,1)}, u32[]{:S(2)}, u32[]{:S(2)}) collective-permute-start(bf16[256,4096]{1,0:T(8,128)(2,1)} %get-tuple-element.16), channel_id=1, source_target_pairs={{0,1},{1,0},{2,3},{3,2},{4,5},{5,4},{6,7},{7,6},{8,9},{9,8},{10,11... | collective-permute-start | bytes 6291464 | tf_op jit(solution)/shard_map/ppermute | solution.py:23
  66.4 108.4 %all-to-all-start = ((bf16[8,2,16,4096]{3,2,1,0:T(8,128)(2,1)}), bf16[8,2,16,4096]{3,2,1,0:T(8,128)(2,1)}, u32[]{:S(2)}, u32[]{:S(2)}) async-start(bf16[8,2,16,4096]{3,2,1,0:T(8,128)(2,1)} %bitcast.155), calls=%async_computation | async-start | bytes 4194304 | tf_op jit(solution)/shard_map/all_to_all | solution.py:438
  71.1 16.3 %collective-permute-start.25 = (bf16[8,2,16,4096]{3,2,1,0:T(8,128)(2,1)S(1)}, bf16[8,2,16,4096]{3,2,1,0:T(8,128)(2,1)}, u32[]{:S(2)}, u32[]{:S(2)}) collective-permute-start(bf16[8,2,16,4096]{3,2,1,0:T(8,128)(2,1)S(1)} %all-to-all-done.1.refs_0_), channel_id=1, source_target_pairs={{0,1},{1,0},{2,3},{3,2},{4,5},{5,4},{6,7},{7,6},{8,9},{9,8},{10,11... | collective-permute-start | bytes 6291464 | tf_op jit(solution)/shard_map/ppermute | solution.py:23
  82.4 29.8 %collective-permute-start.34 = (bf16[32,4096]{1,0:T(8,128)(2,1)S(1)}, bf16[32,4096]{1,0:T(8,128)(2,1)S(1)}, u32[]{:S(2)}, u32[]{:S(2)}) collective-permute-start(bf16[32,4096]{1,0:T(8,128)(2,1)S(1)} %get-tuple-element.47), channel_id=1, source_target_pairs={{0,14},{2,12},{4,2},{6,0},{8,6},{10,4},{12,10},{14,8},{1,15},{3,13... | collective-permute-start | bytes 786440 | tf_op jit(solution)/shard_map/ppermute | solution.py:35
  86.8 57.6 %collective-permute-start.33 = (bf16[32,4096]{1,0:T(8,128)(2,1)S(1)}, bf16[32,4096]{1,0:T(8,128)(2,1)S(1)}, u32[]{:S(2)}, u32[]{:S(2)}) collective-permute-start(bf16[32,4096]{1,0:T(8,128)(2,1)S(1)} %get-tuple-element.48), channel_id=1, source_target_pairs={{0,12},{2,14},{4,0},{6,2},{8,4},{10,6},{12,8},{14,10},{1,13},{3,15... | collective-permute-start | bytes 786440 | tf_op jit(solution)/shard_map/ppermute | solution.py:35
  87.3 72.4 %collective-permute-start.32 = (bf16[32,4096]{1,0:T(8,128)(2,1)S(1)}, bf16[32,4096]{1,0:T(8,128)(2,1)S(1)}, u32[]{:S(2)}, u32[]{:S(2)}) collective-permute-start(bf16[32,4096]{1,0:T(8,128)(2,1)S(1)} %get-tuple-element.49), channel_id=1, source_target_pairs={{0,10},{2,8},{4,14},{6,12},{8,2},{10,0},{12,6},{14,4},{1,11},{3,9}... | collective-permute-start | bytes 786440 | tf_op jit(solution)/shard_map/ppermute | solution.py:35
  87.3 73.9 %copy-start.9 = (bf16[256,4096]{1,0:T(8,128)(2,1)S(1)}, bf16[256,4096]{1,0:T(8,128)(2,1)}, u32[]{:S(2)}) copy-start(bf16[256,4096]{1,0:T(8,128)(2,1)} %get-tuple-element.16) | copy-start | bytes 6291460
  107.7 142.7 %collective-permute-start.26 = (bf16[8,32,4096]{2,1,0:T(8,128)(2,1)}, bf16[8,32,4096]{2,1,0:T(8,128)(2,1)S(1)}, u32[]{:S(2)}, u32[]{:S(2)}) collective-permute-start(bf16[8,32,4096]{2,1,0:T(8,128)(2,1)} %bitcast.152), channel_id=1, source_target_pairs={{0,1},{1,0},{2,3},{3,2},{4,5},{5,4},{6,7},{7,6},{8,9},{9,8},{10,11... | collective-permute-start | bytes 6291464 | tf_op jit(solution)/shard_map/ppermute | solution.py:23
  107.7 56.8 %collective-permute-start.31 = (bf16[32,4096]{1,0:T(8,128)(2,1)S(1)}, bf16[32,4096]{1,0:T(8,128)(2,1)S(1)}, u32[]{:S(2)}, u32[]{:S(2)}) collective-permute-start(bf16[32,4096]{1,0:T(8,128)(2,1)S(1)} %get-tuple-element.50), channel_id=1, source_target_pairs={{0,8},{2,10},{4,12},{6,14},{8,0},{10,2},{12,4},{14,6},{1,9},{3,11}... | collective-permute-start | bytes 786440 | tf_op jit(solution)/shard_map/ppermute | solution.py:35
  112.2 53.6 %collective-permute-start.30 = (bf16[32,4096]{1,0:T(8,128)(2,1)S(1)}, bf16[32,4096]{1,0:T(8,128)(2,1)}, u32[]{:S(2)}, u32[]{:S(2)}) collective-permute-start(bf16[32,4096]{1,0:T(8,128)(2,1)S(1)} %get-tuple-element.51), channel_id=1, source_target_pairs={{0,6},{2,4},{4,10},{6,8},{8,14},{10,12},{12,2},{14,0},{1,7},{3,5},... | collective-permute-start | bytes 786440 | tf_op jit(solution)/shard_map/ppermute | solution.py:35
  144.4 22.4 %collective-permute-start.29 = (bf16[32,4096]{1,0:T(8,128)(2,1)S(1)}, bf16[32,4096]{1,0:T(8,128)(2,1)}, u32[]{:S(2)}, u32[]{:S(2)}) collective-permute-start(bf16[32,4096]{1,0:T(8,128)(2,1)S(1)} %get-tuple-element.52), channel_id=1, source_target_pairs={{0,4},{2,6},{4,8},{6,10},{8,12},{10,14},{12,0},{14,2},{1,5},{3,7},... | collective-permute-start | bytes 786440 | tf_op jit(solution)/shard_map/ppermute | solution.py:35
  159.8 10.4 %collective-permute-start.28 = (bf16[32,4096]{1,0:T(8,128)(2,1)S(1)}, bf16[32,4096]{1,0:T(8,128)(2,1)}, u32[]{:S(2)}, u32[]{:S(2)}) collective-permute-start(bf16[32,4096]{1,0:T(8,128)(2,1)S(1)} %get-tuple-element.53), channel_id=1, source_target_pairs={{0,2},{2,0},{4,6},{6,4},{8,10},{10,8},{12,14},{14,12},{1,3},{3,1},... | collective-permute-start | bytes 786440 | tf_op jit(solution)/shard_map/ppermute | solution.py:35
  165.2 9.6 %collective-permute-start.16 = (bf16[32,4096]{1,0:T(8,128)(2,1)}, bf16[32,4096]{1,0:T(8,128)(2,1)S(1)}, u32[]{:S(2)}, u32[]{:S(2)}) collective-permute-start(bf16[32,4096]{1,0:T(8,128)(2,1)} %get-tuple-element.63), channel_id=1, source_target_pairs={{0,14},{2,12},{4,2},{6,0},{8,6},{10,4},{12,10},{14,8},{1,15},{3,13... | collective-permute-start | bytes 786440 | tf_op jit(solution)/shard_map/ppermute | solution.py:35
  165.8 14.9 %collective-permute-start.15 = (bf16[32,4096]{1,0:T(8,128)(2,1)}, bf16[32,4096]{1,0:T(8,128)(2,1)S(1)}, u32[]{:S(2)}, u32[]{:S(2)}) collective-permute-start(bf16[32,4096]{1,0:T(8,128)(2,1)} %get-tuple-element.64), channel_id=1, source_target_pairs={{0,12},{2,14},{4,0},{6,2},{8,4},{10,6},{12,8},{14,10},{1,13},{3,15... | collective-permute-start | bytes 786440 | tf_op jit(solution)/shard_map/ppermute | solution.py:35
  166.8 33.5 %collective-permute-start.14 = (bf16[32,4096]{1,0:T(8,128)(2,1)}, bf16[32,4096]{1,0:T(8,128)(2,1)}, u32[]{:S(2)}, u32[]{:S(2)}) collective-permute-start(bf16[32,4096]{1,0:T(8,128)(2,1)} %get-tuple-element.65), channel_id=1, source_target_pairs={{0,10},{2,8},{4,14},{6,12},{8,2},{10,0},{12,6},{14,4},{1,11},{3,9}... | collective-permute-start | bytes 786440 | tf_op jit(solution)/shard_map/ppermute | solution.py:35
  170.2 35.6 %collective-permute-start.13 = (bf16[32,4096]{1,0:T(8,128)(2,1)}, bf16[32,4096]{1,0:T(8,128)(2,1)}, u32[]{:S(2)}, u32[]{:S(2)}) collective-permute-start(bf16[32,4096]{1,0:T(8,128)(2,1)} %get-tuple-element.66), channel_id=1, source_target_pairs={{0,8},{2,10},{4,12},{6,14},{8,0},{10,2},{12,4},{14,6},{1,9},{3,11}... | collective-permute-start | bytes 786440 | tf_op jit(solution)/shard_map/ppermute | solution.py:35
  174.8 83.4 %collective-permute-start = (bf16[8,2,16,4096]{3,2,1,0:T(8,128)(2,1)}, bf16[8,2,16,4096]{3,2,1,0:T(8,128)(2,1)}, u32[]{:S(2)}, u32[]{:S(2)}) collective-permute-start(bf16[8,2,16,4096]{3,2,1,0:T(8,128)(2,1)} %all-to-all-done.refs_0_), channel_id=1, source_target_pairs={{0,1},{1,0},{2,3},{3,2},{4,5},{5,4},{6,7},{7,6},{8,9},{9,8},{10,11... | collective-permute-start | bytes 6291464 | tf_op jit(solution)/shard_map/ppermute | solution.py:23
  180.7 49.3 %collective-permute-start.12 = (bf16[32,4096]{1,0:T(8,128)(2,1)}, bf16[32,4096]{1,0:T(8,128)(2,1)S(1)}, u32[]{:S(2)}, u32[]{:S(2)}) collective-permute-start(bf16[32,4096]{1,0:T(8,128)(2,1)} %get-tuple-element.67), channel_id=1, source_target_pairs={{0,6},{2,4},{4,10},{6,8},{8,14},{10,12},{12,2},{14,0},{1,7},{3,5},... | collective-permute-start | bytes 786440 | tf_op jit(solution)/shard_map/ppermute | solution.py:35
  200.3 29.8 %collective-permute-start.11 = (bf16[32,4096]{1,0:T(8,128)(2,1)}, bf16[32,4096]{1,0:T(8,128)(2,1)S(1)}, u32[]{:S(2)}, u32[]{:S(2)}) collective-permute-start(bf16[32,4096]{1,0:T(8,128)(2,1)} %get-tuple-element.68), channel_id=1, source_target_pairs={{0,4},{2,6},{4,8},{6,10},{8,12},{10,14},{12,0},{14,2},{1,5},{3,7},... | collective-permute-start | bytes 786440 | tf_op jit(solution)/shard_map/ppermute | solution.py:35
  205.9 24.2 %collective-permute-start.10 = (bf16[32,4096]{1,0:T(8,128)(2,1)}, bf16[32,4096]{1,0:T(8,128)(2,1)S(1)}, u32[]{:S(2)}, u32[]{:S(2)}) collective-permute-start(bf16[32,4096]{1,0:T(8,128)(2,1)} %get-tuple-element.69), channel_id=1, source_target_pairs={{0,2},{2,0},{4,6},{6,4},{8,10},{10,8},{12,14},{14,12},{1,3},{3,1},... | collective-permute-start | bytes 786440 | tf_op jit(solution)/shard_map/ppermute | solution.py:35
  230.0 50.4 %collective-permute-start.35 = (bf16[8,32,4096]{2,1,0:T(8,128)(2,1)}, bf16[8,32,4096]{2,1,0:T(8,128)(2,1)}, u32[]{:S(2)}, u32[]{:S(2)}) collective-permute-start(bf16[8,32,4096]{2,1,0:T(8,128)(2,1)} %bitcast.147), channel_id=1, source_target_pairs={{0,1},{1,0},{2,3},{3,2},{4,5},{5,4},{6,7},{7,6},{8,9},{9,8},{10,11... | collective-permute-start | bytes 6291464 | tf_op jit(solution)/shard_map/ppermute | solution.py:23
  249.9 40.4 %collective-permute-start.17 = (bf16[8,32,4096]{2,1,0:T(8,128)(2,1)}, bf16[8,32,4096]{2,1,0:T(8,128)(2,1)}, u32[]{:S(2)}, u32[]{:S(2)}) collective-permute-start(bf16[8,32,4096]{2,1,0:T(8,128)(2,1)} %bitcast.144), channel_id=1, source_target_pairs={{0,1},{1,0},{2,3},{3,2},{4,5},{5,4},{6,7},{7,6},{8,9},{9,8},{10,11... | collective-permute-start | bytes 6291464 | tf_op jit(solution)/shard_map/ppermute | solution.py:23
  252.8 158.1 %all-to-all-start.2 = ((bf16[8,32,4096]{2,1,0:T(8,128)(2,1)}), bf16[8,32,4096]{2,1,0:T(8,128)(2,1)S(1)}, u32[]{:S(2)}, u32[]{:S(2)}) async-start(bf16[8,32,4096]{2,1,0:T(8,128)(2,1)} %multiply_convert_fusion), calls=%async_computation.2 | async-start | bytes 4194304 | tf_op jit(solution)/shard_map/all_to_all | solution.py:438
  278.6 62.6 %collective-permute-start.1 = (bf16[8,32,4096]{2,1,0:T(8,128)(2,1)}, bf16[8,32,4096]{2,1,0:T(8,128)(2,1)S(1)}, u32[]{:S(2)}, u32[]{:S(2)}) collective-permute-start(bf16[8,32,4096]{2,1,0:T(8,128)(2,1)} %bitcast.153), channel_id=1, source_target_pairs={{0,1},{1,0},{2,3},{3,2},{4,5},{5,4},{6,7},{7,6},{8,9},{9,8},{10,11... | collective-permute-start | bytes 6291464 | tf_op jit(solution)/shard_map/ppermute | solution.py:23
  282.3 15.7 %collective-permute-start.42 = (bf16[32,1024]{1,0:T(8,128)(2,1)S(1)}, bf16[32,1024]{1,0:T(8,128)(2,1)S(1)}, u32[]{:S(2)}, u32[]{:S(2)}) collective-permute-start(bf16[32,1024]{1,0:T(8,128)(2,1)S(1)} %get-tuple-element.39), channel_id=1, source_target_pairs={{0,6},{2,4},{4,10},{6,8},{8,14},{10,12},{12,2},{14,0},{1,7},{3,5},... | collective-permute-start | bytes 196616 | tf_op jit(solution)/shard_map/ppermute | solution.py:35
  285.2 23.7 %collective-permute-start.41 = (bf16[32,1024]{1,0:T(8,128)(2,1)S(1)}, bf16[32,1024]{1,0:T(8,128)(2,1)S(1)}, u32[]{:S(2)}, u32[]{:S(2)}) collective-permute-start(bf16[32,1024]{1,0:T(8,128)(2,1)S(1)} %get-tuple-element.40), channel_id=1, source_target_pairs={{0,4},{2,6},{4,8},{6,10},{8,12},{10,14},{12,0},{14,2},{1,5},{3,7},... | collective-permute-start | bytes 196616 | tf_op jit(solution)/shard_map/ppermute | solution.py:35
  286.6 43.8 %collective-permute-start.40 = (bf16[32,1024]{1,0:T(8,128)(2,1)S(1)}, bf16[32,1024]{1,0:T(8,128)(2,1)S(1)}, u32[]{:S(2)}, u32[]{:S(2)}) collective-permute-start(bf16[32,1024]{1,0:T(8,128)(2,1)S(1)} %get-tuple-element.41), channel_id=1, source_target_pairs={{0,10},{2,8},{4,14},{6,12},{8,2},{10,0},{12,6},{14,4},{1,11},{3,9}... | collective-permute-start | bytes 196616 | tf_op jit(solution)/shard_map/ppermute | solution.py:35
  290.3 43.6 %collective-permute-start.39 = (bf16[32,1024]{1,0:T(8,128)(2,1)S(1)}, bf16[32,1024]{1,0:T(8,128)(2,1)S(1)}, u32[]{:S(2)}, u32[]{:S(2)}) collective-permute-start(bf16[32,1024]{1,0:T(8,128)(2,1)S(1)} %get-tuple-element.42), channel_id=1, source_target_pairs={{0,8},{2,10},{4,12},{6,14},{8,0},{10,2},{12,4},{14,6},{1,9},{3,11}... | collective-permute-start | bytes 196616 | tf_op jit(solution)/shard_map/ppermute | solution.py:35
  298.1 38.7 %collective-permute-start.56 = (bf16[32,3072]{1,0:T(8,128)(2,1)S(1)}, bf16[32,3072]{1,0:T(8,128)(2,1)S(1)}, u32[]{:S(2)}, u32[]{:S(2)}) collective-permute-start(bf16[32,3072]{1,0:T(8,128)(2,1)S(1)} %get-tuple-element.23), channel_id=1, source_target_pairs={{0,6},{2,4},{4,10},{6,8},{8,14},{10,12},{12,2},{14,0},{1,7},{3,5},... | collective-permute-start | bytes 589832 | tf_op jit(solution)/shard_map/ppermute | solution.py:35
  308.8 28.0 %collective-permute-start.55 = (bf16[32,3072]{1,0:T(8,128)(2,1)S(1)}, bf16[32,3072]{1,0:T(8,128)(2,1)S(1)}, u32[]{:S(2)}, u32[]{:S(2)}) collective-permute-start(bf16[32,3072]{1,0:T(8,128)(2,1)S(1)} %get-tuple-element.24), channel_id=1, source_target_pairs={{0,4},{2,6},{4,8},{6,10},{8,12},{10,14},{12,0},{14,2},{1,5},{3,7},... | collective-permute-start | bytes 589832 | tf_op jit(solution)/shard_map/ppermute | solution.py:35
  331.1 9.7 %collective-permute-start.54 = (bf16[32,3072]{1,0:T(8,128)(2,1)S(1)}, bf16[32,3072]{1,0:T(8,128)(2,1)S(1)}, u32[]{:S(2)}, u32[]{:S(2)}) collective-permute-start(bf16[32,3072]{1,0:T(8,128)(2,1)S(1)} %get-tuple-element.25), channel_id=1, source_target_pairs={{0,10},{2,8},{4,14},{6,12},{8,2},{10,0},{12,6},{14,4},{1,11},{3,9}... | collective-permute-start | bytes 589832 | tf_op jit(solution)/shard_map/ppermute | solution.py:35
  334.0 10.7 %collective-permute-start.53 = (bf16[32,3072]{1,0:T(8,128)(2,1)S(1)}, bf16[32,3072]{1,0:T(8,128)(2,1)S(1)}, u32[]{:S(2)}, u32[]{:S(2)}) collective-permute-start(bf16[32,3072]{1,0:T(8,128)(2,1)S(1)} %get-tuple-element.26), channel_id=1, source_target_pairs={{0,8},{2,10},{4,12},{6,14},{8,0},{10,2},{12,4},{14,6},{1,9},{3,11}... | collective-permute-start | bytes 589832 | tf_op jit(solution)/shard_map/ppermute | solution.py:35
  336.8 16.9 %collective-permute-start.52 = (bf16[32,3072]{1,0:T(8,128)(2,1)S(1)}, bf16[32,3072]{1,0:T(8,128)(2,1)S(1)}, u32[]{:S(2)}, u32[]{:S(2)}) collective-permute-start(bf16[32,3072]{1,0:T(8,128)(2,1)S(1)} %get-tuple-element.27), channel_id=1, source_target_pairs={{0,14},{2,12},{4,2},{6,0},{8,6},{10,4},{12,10},{14,8},{1,15},{3,13... | collective-permute-start | bytes 589832 | tf_op jit(solution)/shard_map/ppermute | solution.py:35
  336.8 22.4 %collective-permute-start.51 = (bf16[32,3072]{1,0:T(8,128)(2,1)S(1)}, bf16[32,3072]{1,0:T(8,128)(2,1)S(1)}, u32[]{:S(2)}, u32[]{:S(2)}) collective-permute-start(bf16[32,3072]{1,0:T(8,128)(2,1)S(1)} %get-tuple-element.28), channel_id=1, source_target_pairs={{0,12},{2,14},{4,0},{6,2},{8,4},{10,6},{12,8},{14,10},{1,13},{3,15... | collective-permute-start | bytes 589832 | tf_op jit(solution)/shard_map/ppermute | solution.py:35
  340.8 21.9 %collective-permute-start.50 = (bf16[32,3072]{1,0:T(8,128)(2,1)S(1)}, bf16[32,3072]{1,0:T(8,128)(2,1)S(1)}, u32[]{:S(2)}, u32[]{:S(2)}) collective-permute-start(bf16[32,3072]{1,0:T(8,128)(2,1)S(1)} %get-tuple-element.29), channel_id=1, source_target_pairs={{0,2},{2,0},{4,6},{6,4},{8,10},{10,8},{12,14},{14,12},{1,3},{3,1},... | collective-permute-start | bytes 589832 | tf_op jit(solution)/shard_map/ppermute | solution.py:35
  341.2 33.2 %collective-permute-start.49 = (bf16[32,3072]{1,0:T(8,128)(2,1)S(1)}, bf16[32,3072]{1,0:T(8,128)(2,1)S(1)}, u32[]{:S(2)}, u32[]{:S(2)}) collective-permute-start(bf16[32,3072]{1,0:T(8,128)(2,1)S(1)} %get-tuple-element.31), channel_id=1, source_target_pairs={{0,6},{2,4},{4,10},{6,8},{8,14},{10,12},{12,2},{14,0},{1,7},{3,5},... | collective-permute-start | bytes 589832 | tf_op jit(solution)/shard_map/ppermute | solution.py:35
  344.7 65.1 %copy-start.56 = (bf16[32,3072]{1,0:T(8,128)(2,1)}, bf16[32,3072]{1,0:T(8,128)(2,1)S(1)}, u32[]{:S(2)}) copy-start(bf16[32,3072]{1,0:T(8,128)(2,1)S(1)} %collective-permute-done.53.refs_5_) | copy-start | bytes 589828
  344.7 30.7 %collective-permute-start.48 = (bf16[32,3072]{1,0:T(8,128)(2,1)S(1)}, bf16[32,3072]{1,0:T(8,128)(2,1)S(1)}, u32[]{:S(2)}, u32[]{:S(2)}) collective-permute-start(bf16[32,3072]{1,0:T(8,128)(2,1)S(1)} %get-tuple-element.32), channel_id=1, source_target_pairs={{0,4},{2,6},{4,8},{6,10},{8,12},{10,14},{12,0},{14,2},{1,5},{3,7},... | collective-permute-start | bytes 589832 | tf_op jit(solution)/shard_map/ppermute | solution.py:35
  353.7 56.1 %copy-start.57 = (bf16[32,3072]{1,0:T(8,128)(2,1)}, bf16[32,3072]{1,0:T(8,128)(2,1)S(1)}, u32[]{:S(2)}) copy-start(bf16[32,3072]{1,0:T(8,128)(2,1)S(1)} %collective-permute-done.52.refs_4_) | copy-start | bytes 589828
  353.7 25.8 %collective-permute-start.47 = (bf16[32,3072]{1,0:T(8,128)(2,1)S(1)}, bf16[32,3072]{1,0:T(8,128)(2,1)S(1)}, u32[]{:S(2)}, u32[]{:S(2)}) collective-permute-start(bf16[32,3072]{1,0:T(8,128)(2,1)S(1)} %get-tuple-element.33), channel_id=1, source_target_pairs={{0,10},{2,8},{4,14},{6,12},{8,2},{10,0},{12,6},{14,4},{1,11},{3,9}... | collective-permute-start | bytes 589832 | tf_op jit(solution)/shard_map/ppermute | solution.py:35
  359.2 30.2 %collective-permute-start.46 = (bf16[32,3072]{1,0:T(8,128)(2,1)S(1)}, bf16[32,3072]{1,0:T(8,128)(2,1)S(1)}, u32[]{:S(2)}, u32[]{:S(2)}) collective-permute-start(bf16[32,3072]{1,0:T(8,128)(2,1)S(1)} %get-tuple-element.34), channel_id=1, source_target_pairs={{0,8},{2,10},{4,12},{6,14},{8,0},{10,2},{12,4},{14,6},{1,9},{3,11}... | collective-permute-start | bytes 589832 | tf_op jit(solution)/shard_map/ppermute | solution.py:35
  362.7 47.0 %collective-permute-start.8 = (bf16[32,4096]{1,0:T(8,128)(2,1)S(1)}, bf16[32,4096]{1,0:T(8,128)(2,1)S(1)}, u32[]{:S(2)}, u32[]{:S(2)}) collective-permute-start(bf16[32,4096]{1,0:T(8,128)(2,1)S(1)} %get-tuple-element.71), channel_id=1, source_target_pairs={{0,6},{2,4},{4,10},{6,8},{8,14},{10,12},{12,2},{14,0},{1,7},{3,5},... | collective-permute-start | bytes 786440 | tf_op jit(solution)/shard_map/ppermute | solution.py:35
  374.4 35.3 %collective-permute-start.7 = (bf16[32,4096]{1,0:T(8,128)(2,1)S(1)}, bf16[32,4096]{1,0:T(8,128)(2,1)S(1)}, u32[]{:S(2)}, u32[]{:S(2)}) collective-permute-start(bf16[32,4096]{1,0:T(8,128)(2,1)S(1)} %get-tuple-element.72), channel_id=1, source_target_pairs={{0,4},{2,6},{4,8},{6,10},{8,12},{10,14},{12,0},{14,2},{1,5},{3,7},... | collective-permute-start | bytes 786440 | tf_op jit(solution)/shard_map/ppermute | solution.py:35
  375.4 17.1 %collective-permute-start.45 = (bf16[32,3072]{1,0:T(8,128)(2,1)S(1)}, bf16[32,3072]{1,0:T(8,128)(2,1)S(1)}, u32[]{:S(2)}, u32[]{:S(2)}) collective-permute-start(bf16[32,3072]{1,0:T(8,128)(2,1)S(1)} %get-tuple-element.35), channel_id=1, source_target_pairs={{0,14},{2,12},{4,2},{6,0},{8,6},{10,4},{12,10},{14,8},{1,15},{3,13... | collective-permute-start | bytes 589832 | tf_op jit(solution)/shard_map/ppermute | solution.py:35
  379.5 14.2 %collective-permute-start.44 = (bf16[32,3072]{1,0:T(8,128)(2,1)S(1)}, bf16[32,3072]{1,0:T(8,128)(2,1)S(1)}, u32[]{:S(2)}, u32[]{:S(2)}) collective-permute-start(bf16[32,3072]{1,0:T(8,128)(2,1)S(1)} %get-tuple-element.36), channel_id=1, source_target_pairs={{0,12},{2,14},{4,0},{6,2},{8,4},{10,6},{12,8},{14,10},{1,13},{3,15... | collective-permute-start | bytes 589832 | tf_op jit(solution)/shard_map/ppermute | solution.py:35
  389.4 16.4 %collective-permute-start.43 = (bf16[32,3072]{1,0:T(8,128)(2,1)S(1)}, bf16[32,3072]{1,0:T(8,128)(2,1)S(1)}, u32[]{:S(2)}, u32[]{:S(2)}) collective-permute-start(bf16[32,3072]{1,0:T(8,128)(2,1)S(1)} %get-tuple-element.37), channel_id=1, source_target_pairs={{0,2},{2,0},{4,6},{6,4},{8,10},{10,8},{12,14},{14,12},{1,3},{3,1},... | collective-permute-start | bytes 589832 | tf_op jit(solution)/shard_map/ppermute | solution.py:35
  392.5 31.6 %collective-permute-start.6 = (bf16[32,4096]{1,0:T(8,128)(2,1)}, bf16[32,4096]{1,0:T(8,128)(2,1)}, u32[]{:S(2)}, u32[]{:S(2)}) collective-permute-start(bf16[32,4096]{1,0:T(8,128)(2,1)} %get-tuple-element.73), channel_id=1, source_target_pairs={{0,10},{2,8},{4,14},{6,12},{8,2},{10,0},{12,6},{14,4},{1,11},{3,9}... | collective-permute-start | bytes 786440 | tf_op jit(solution)/shard_map/ppermute | solution.py:35
  393.7 34.8 %collective-permute-start.5 = (bf16[32,4096]{1,0:T(8,128)(2,1)}, bf16[32,4096]{1,0:T(8,128)(2,1)}, u32[]{:S(2)}, u32[]{:S(2)}) collective-permute-start(bf16[32,4096]{1,0:T(8,128)(2,1)} %get-tuple-element.74), channel_id=1, source_target_pairs={{0,8},{2,10},{4,12},{6,14},{8,0},{10,2},{12,4},{14,6},{1,9},{3,11}... | collective-permute-start | bytes 786440 | tf_op jit(solution)/shard_map/ppermute | solution.py:35
  405.8 31.5 %collective-permute-start.4 = (bf16[32,4096]{1,0:T(8,128)(2,1)}, bf16[32,4096]{1,0:T(8,128)(2,1)}, u32[]{:S(2)}, u32[]{:S(2)}) collective-permute-start(bf16[32,4096]{1,0:T(8,128)(2,1)} %get-tuple-element.75), channel_id=1, source_target_pairs={{0,14},{2,12},{4,2},{6,0},{8,6},{10,4},{12,10},{14,8},{1,15},{3,13... | collective-permute-start | bytes 786440 | tf_op jit(solution)/shard_map/ppermute | solution.py:35
  409.7 29.4 %collective-permute-start.3 = (bf16[32,4096]{1,0:T(8,128)(2,1)}, bf16[32,4096]{1,0:T(8,128)(2,1)}, u32[]{:S(2)}, u32[]{:S(2)}) collective-permute-start(bf16[32,4096]{1,0:T(8,128)(2,1)} %get-tuple-element.76), channel_id=1, source_target_pairs={{0,12},{2,14},{4,0},{6,2},{8,4},{10,6},{12,8},{14,10},{1,13},{3,15... | collective-permute-start | bytes 786440 | tf_op jit(solution)/shard_map/ppermute | solution.py:35
  409.9 29.3 %collective-permute-start.2 = (bf16[32,4096]{1,0:T(8,128)(2,1)}, bf16[32,4096]{1,0:T(8,128)(2,1)}, u32[]{:S(2)}, u32[]{:S(2)}) collective-permute-start(bf16[32,4096]{1,0:T(8,128)(2,1)} %get-tuple-element.77), channel_id=1, source_target_pairs={{0,2},{2,0},{4,6},{6,4},{8,10},{10,8},{12,14},{14,12},{1,3},{3,1},... | collective-permute-start | bytes 786440 | tf_op jit(solution)/shard_map/ppermute | solution.py:35
  424.1 28.0 %collective-permute-start.38 = (bf16[32,1024]{1,0:T(8,128)(2,1)S(1)}, bf16[32,1024]{1,0:T(8,128)(2,1)S(1)}, u32[]{:S(2)}, u32[]{:S(2)}) collective-permute-start(bf16[32,1024]{1,0:T(8,128)(2,1)S(1)} %copy-done.44), channel_id=1, source_target_pairs={{0,14},{2,12},{4,2},{6,0},{8,6},{10,4},{12,10},{14,8},{1,15},{3,13... | collective-permute-start | bytes 196616 | tf_op jit(solution)/shard_map/ppermute | solution.py:35
  428.5 28.9 %collective-permute-start.37 = (bf16[32,1024]{1,0:T(8,128)(2,1)S(1)}, bf16[32,1024]{1,0:T(8,128)(2,1)S(1)}, u32[]{:S(2)}, u32[]{:S(2)}) collective-permute-start(bf16[32,1024]{1,0:T(8,128)(2,1)S(1)} %copy-done.43), channel_id=1, source_target_pairs={{0,12},{2,14},{4,0},{6,2},{8,4},{10,6},{12,8},{14,10},{1,13},{3,15... | collective-permute-start | bytes 196616 | tf_op jit(solution)/shard_map/ppermute | solution.py:35
  437.3 20.1 %collective-permute-start.36 = (bf16[32,1024]{1,0:T(8,128)(2,1)S(1)}, bf16[32,1024]{1,0:T(8,128)(2,1)S(1)}, u32[]{:S(2)}, u32[]{:S(2)}) collective-permute-start(bf16[32,1024]{1,0:T(8,128)(2,1)S(1)} %copy-done.42), channel_id=1, source_target_pairs={{0,2},{2,0},{4,6},{6,4},{8,10},{10,8},{12,14},{14,12},{1,3},{3,1},... | collective-permute-start | bytes 196616 | tf_op jit(solution)/shard_map/ppermute | solution.py:35
  439.1 20.8 %collective-permute-start.24 = (bf16[32,1024]{1,0:T(8,128)(2,1)S(1)}, bf16[32,1024]{1,0:T(8,128)(2,1)S(1)}, u32[]{:S(2)}, u32[]{:S(2)}) collective-permute-start(bf16[32,1024]{1,0:T(8,128)(2,1)S(1)} %copy-done.50), channel_id=1, source_target_pairs={{0,6},{2,4},{4,10},{6,8},{8,14},{10,12},{12,2},{14,0},{1,7},{3,5},... | collective-permute-start | bytes 196616 | tf_op jit(solution)/shard_map/ppermute | solution.py:35
  439.2 22.4 %collective-permute-start.23 = (bf16[32,1024]{1,0:T(8,128)(2,1)S(1)}, bf16[32,1024]{1,0:T(8,128)(2,1)S(1)}, u32[]{:S(2)}, u32[]{:S(2)}) collective-permute-start(bf16[32,1024]{1,0:T(8,128)(2,1)S(1)} %copy-done.49), channel_id=1, source_target_pairs={{0,4},{2,6},{4,8},{6,10},{8,12},{10,14},{12,0},{14,2},{1,5},{3,7},... | collective-permute-start | bytes 196616 | tf_op jit(solution)/shard_map/ppermute | solution.py:35
  452.1 17.1 %collective-permute-start.22 = (bf16[32,1024]{1,0:T(8,128)(2,1)S(1)}, bf16[32,1024]{1,0:T(8,128)(2,1)S(1)}, u32[]{:S(2)}, u32[]{:S(2)}) collective-permute-start(bf16[32,1024]{1,0:T(8,128)(2,1)S(1)} %copy-done.48), channel_id=1, source_target_pairs={{0,10},{2,8},{4,14},{6,12},{8,2},{10,0},{12,6},{14,4},{1,11},{3,9}... | collective-permute-start | bytes 196616 | tf_op jit(solution)/shard_map/ppermute | solution.py:35
  457.4 11.8 %collective-permute-start.21 = (bf16[32,1024]{1,0:T(8,128)(2,1)S(1)}, bf16[32,1024]{1,0:T(8,128)(2,1)S(1)}, u32[]{:S(2)}, u32[]{:S(2)}) collective-permute-start(bf16[32,1024]{1,0:T(8,128)(2,1)S(1)} %copy-done.47), channel_id=1, source_target_pairs={{0,8},{2,10},{4,12},{6,14},{8,0},{10,2},{12,4},{14,6},{1,9},{3,11}... | collective-permute-start | bytes 196616 | tf_op jit(solution)/shard_map/ppermute | solution.py:35
  457.5 11.7 %collective-permute-start.20 = (bf16[32,1024]{1,0:T(8,128)(2,1)S(1)}, bf16[32,1024]{1,0:T(8,128)(2,1)S(1)}, u32[]{:S(2)}, u32[]{:S(2)}) collective-permute-start(bf16[32,1024]{1,0:T(8,128)(2,1)S(1)} %copy-done.46), channel_id=1, source_target_pairs={{0,14},{2,12},{4,2},{6,0},{8,6},{10,4},{12,10},{14,8},{1,15},{3,13... | collective-permute-start | bytes 196616 | tf_op jit(solution)/shard_map/ppermute | solution.py:35
  459.9 9.3 %collective-permute-start.19 = (bf16[32,1024]{1,0:T(8,128)(2,1)S(1)}, bf16[32,1024]{1,0:T(8,128)(2,1)S(1)}, u32[]{:S(2)}, u32[]{:S(2)}) collective-permute-start(bf16[32,1024]{1,0:T(8,128)(2,1)S(1)} %copy-done.45), channel_id=1, source_target_pairs={{0,12},{2,14},{4,0},{6,2},{8,4},{10,6},{12,8},{14,10},{1,13},{3,15... | collective-permute-start | bytes 196616 | tf_op jit(solution)/shard_map/ppermute | solution.py:35
  461.6 7.7 %collective-permute-start.18 = (bf16[32,1024]{1,0:T(8,128)(2,1)S(1)}, bf16[32,1024]{1,0:T(8,128)(2,1)S(1)}, u32[]{:S(2)}, u32[]{:S(2)}) collective-permute-start(bf16[32,1024]{1,0:T(8,128)(2,1)S(1)} %get-tuple-element.61), channel_id=1, source_target_pairs={{0,2},{2,0},{4,6},{6,4},{8,10},{10,8},{12,14},{14,12},{1,3},{3,1},... | collective-permute-start | bytes 196616 | tf_op jit(solution)/shard_map/ppermute | solution.py:35
  (56 other events, 944.5 us)

commit v9 on v8

--- a/solution.py
+++ b/solution.py
@@ -173,7 +173,7 @@
 
 def inverse_fourier(pieces, tables, shape, start, levels, current=None, partial=None, dtype=None):
     _, rows_here, lon_count = shape
-    block = level_block(levels, rows_here, 8 if partial is None or levels <= 16 else 16)
+    block = level_block(levels, rows_here, 8 if partial is None else levels // 2)
     width = block * rows_here
     first = start // block
     height = sum(table.shape[0] for table in tables)
@@ -352,7 +352,7 @@
     width = tiles * LANES
     levels = modes[0].shape[0]
     whole = lambda shape: pl.BlockSpec(shape, lambda i: (0,) * len(shape))
-    scratch = pltpu.VMEM((places * 2 * group * tiles, LANES), jnp.float32)
+    scratch = pltpu.VMEM((places * 2 * group * tiles + 8, LANES), jnp.float32)
     values = places * 2 * group * width
     return pl.pallas_call(
         functools.partial(column_kernel, sizes),
@@ -503,8 +503,8 @@
             pieces.append(piece.reshape(2, count, width))
         arrived.append(pieces)
 
-    most = local_levels // 4 * 3
-    groups = [(0, most), (most, local_levels - most)]
+    half = local_levels // 2
+    groups = [(0, half), (half, half)]
     cuts = {chunk: [(0, local_levels)] for chunk in range(chunks)}
     cuts[1] = cuts[chunks - 1] = groups
     returned = []

time: 477 us -> 459 us (0.962)
  starting transfers between devices: 191 us -> 149 us
  waiting for transfers between devices: 85.9 us -> 108 us
    ppermute x49, starting transfers between devices: 174 us -> 132 us  [shift_places(): return lax.ppermute(value, EXCHANGE_AXES, pairs)]
    ppermute x49, waiting for transfers between devices: 71.2 us -> 96.4 us  [shift_places(): return lax.ppermute(value, EXCHANGE_AXES, pairs)]
    unnamed x128 -> x122, local copies, waits for them, and re-layouts: 10.7 us -> 12.6 us
  transfers between devices with their start and end apart: 60 -> 60, of which waited for: 13 -> 18; matrix products, arithmetic and copies ran while one was open for 8% -> 9% of each run, Pallas kernels for 29% -> 30%
where the time goes in v9:
time: 459 us; the launch traced here: 457 us
  Pallas kernels  154 us (34%)
  starting transfers between devices  149 us (32%)
  waiting for transfers between devices  108 us (24%)
  other arithmetic  27.1 us (6%)
  local copies, waits for them, and re-layouts  18.8 us (4%)
    ppermute x49, starting transfers between devices, shift_places(): return lax.ppermute(value, EXCHANGE_AXES, pairs)  132 us
    ppermute x49, waiting for transfers between devices, shift_places(): return lax.ppermute(value, EXCHANGE_AXES, pairs)  96.4 us
    pallas_call x4, Pallas kernels, columns_fused(): pl.pallas_call(functools.partial(column_kernel, sizes), out_shape=jax.Sha...  79.2 us
    pallas_call x4, Pallas kernels, fourier(): pl.pallas_call(functools.partial(fourier_kernel, sizes), out_shape=[jax.S...  41.3 us
    pallas_call x4, Pallas kernels, inverse_fourier(): pl.pallas_call(functools.partial(inverse_kernel, len(pieces), len(tables)...  33.9 us
    all_to_all x3, starting transfers between devices, exchange(): lax.all_to_all(value, EXCHANGE_AXES, split_axis=0, concat_axis=0, tiled=T...  15.5 us
    unnamed x122, local copies, waits for them, and re-layouts  12.6 us
    convert_element_type x3, other arithmetic, joined(): return both.astype(jnp.bfloat16)  11.6 us
  transfers between devices with their start and end apart: 60, of which 18 were waited for; matrix products, arithmetic and copies ran while one was open for 9% of the time, Pallas kernels for 30%

profile of v9, /device:TPU:0, one launch (start us, length us, event | category | flops | bytes accessed | tf_op | source)
XLA Modules:
  0.0 457.4 jit_solution(5705416777052840089)
XLA Ops:
  0.6 10.2 %shard_map.77 = (bf16[256,4096]{1,0:T(8,128)(2,1)}, bf16[256,1536]{1,0:T(8,128)(2,1)}) custom-call(s32[3]{0:T(128)} %pad_add_fusion.1.place_ref, bf16[64,64,1536]{2,1,0:T(8,128)(2,1)} %bitcast.136, s32[1,512]{1,0:T(1,128)} %bitcast.171, s32[1,256]{1,0:T(1,128)} %bitcast.175), custom_call_target="tpu_custom_call" | custom-call | flops 3221225472 | bytes 15466496 | tf_op jit(solution)/shard_map/pallas_call | solution.py:119
  10.8 7.3 %all-to-all-start.1 = ((bf16[8,2,16,4096]{3,2,1,0:T(8,128)(2,1)}), bf16[8,2,16,4096]{3,2,1,0:T(8,128)(2,1)}, u32[]{:S(2)}, u32[]{:S(2)}) async-start(bf16[8,2,16,4096]{3,2,1,0:T(8,128)(2,1)} %bitcast.154), calls=%async_computation.1 | async-start | bytes 4194304 | tf_op jit(solution)/shard_map/all_to_all | solution.py:438
  18.1 10.4 %shard_map.79 = (bf16[256,4096]{1,0:T(8,128)(2,1)}, bf16[256,1536]{1,0:T(8,128)(2,1)}) custom-call(s32[3]{0:T(128)} %pad_add_fusion.1.place_ref, bf16[64,64,1536]{2,1,0:T(8,128)(2,1)} %bitcast.137, s32[1,512]{1,0:T(1,128)} %bitcast.172, s32[1,256]{1,0:T(1,128)} %bitcast.176), custom_call_target="tpu_custom_call" | custom-call | flops 3221225472 | bytes 15466496 | tf_op jit(solution)/shard_map/pallas_call | solution.py:119
  28.6 10.5 %shard_map.75 = (bf16[256,4096]{1,0:T(8,128)(2,1)}, bf16[256,1536]{1,0:T(8,128)(2,1)}) custom-call(s32[3]{0:T(128)} %pad_add_fusion.1.place_ref, bf16[64,64,1536]{2,1,0:T(8,128)(2,1)} %bitcast.138, s32[1,512]{1,0:T(1,128)} %bitcast.173, s32[1,256]{1,0:T(1,128)} %bitcast.177), custom_call_target="tpu_custom_call" | custom-call | flops 3221225472 | bytes 15466496 | tf_op jit(solution)/shard_map/pallas_call | solution.py:119
  42.9 1.2 dynamic_slice.77.waves
  45.1 10.2 %shard_map.73 = (bf16[256,4096]{1,0:T(8,128)(2,1)}, bf16[256,1536]{1,0:T(8,128)(2,1)}) custom-call(s32[3]{0:T(128)} %pad_add_fusion.1.place_ref, bf16[64,64,1536]{2,1,0:T(8,128)(2,1)} %bitcast.139, s32[1,512]{1,0:T(1,128)} %bitcast.174, s32[1,256]{1,0:T(1,128)} %bitcast.178), custom_call_target="tpu_custom_call" | custom-call | flops 3221225472 | bytes 15466496 | tf_op jit(solution)/shard_map/pallas_call | solution.py:119
  55.4 11.1 %all-to-all-done.1.refs_0_ = bf16[8,2,16,4096]{3,2,1,0:T(8,128)(2,1)} async-done(((bf16[8,2,16,4096]{3,2,1,0:T(8,128)(2,1)}), bf16[8,2,16,4096]{3,2,1,0:T(8,128)(2,1)}, u32[]{:S(2)}, u32[]{:S(2)}) %all-to-all-start.1) | async-done | bytes 2097184 | tf_op jit(solution)/shard_map/all_to_all | solution.py:438
  66.5 3.8 all-to-all-start
  73.9 3.8 add_convert_fusion
  77.7 4.4 collective-permute-start.34
  82.7 1.3 copy-done.8
  84.0 20.2 %shard_map.78 = bf16[8,2,16,4096]{3,2,1,0:T(8,128)(2,1)} custom-call(s32[64]{0:T(128)} %dynamic_slice.77.waves, s32[5]{0:T(128)} %pad_add_fusion.scalars, f32[128,1]{1,0:T(8,128)} %copy.11.eig_ref, bf16[128,128]{1,0:T(8,128)(2,1)} %select_bitcast_fusion.1.modes_in, bf16[128,128]{1,0:T(8,128)(2,1)} %broadcast_select_fusion.1.modes_out, ...), custom_call_target="tpu_custom_call" | custom-call | flops 1610612736 | bytes 6291456 | tf_op jit(solution)/shard_map/pallas_call | solution.py:357
  105.9 2.9 collective-permute-start.31
  108.8 3.3 collective-permute-done.34
  112.2 31.5 %collective-permute-start.30 = (bf16[32,4096]{1,0:T(8,128)(2,1)}, bf16[32,4096]{1,0:T(8,128)(2,1)}, u32[]{:S(2)}, u32[]{:S(2)}) collective-permute-start(bf16[32,4096]{1,0:T(8,128)(2,1)} %get-tuple-element.52), channel_id=1, source_target_pairs={{0,6},{2,4},{4,10},{6,8},{8,14},{10,12},{12,2},{14,0},{1,7},{3,5},... | collective-permute-start | bytes 786440 | tf_op jit(solution)/shard_map/ppermute | solution.py:35
  143.7 10.3 %collective-permute-start.29 = (bf16[32,4096]{1,0:T(8,128)(2,1)}, bf16[32,4096]{1,0:T(8,128)(2,1)}, u32[]{:S(2)}, u32[]{:S(2)}) collective-permute-start(bf16[32,4096]{1,0:T(8,128)(2,1)} %get-tuple-element.53), channel_id=1, source_target_pairs={{0,4},{2,6},{4,8},{6,10},{8,12},{10,14},{12,0},{14,2},{1,5},{3,7},... | collective-permute-start | bytes 786440 | tf_op jit(solution)/shard_map/ppermute | solution.py:35
  154.1 3.8 add_convert_fusion.8
  157.9 1.8 collective-permute-done.32
  161.3 2.7 collective-permute-done.31
  164.0 1.6 collective-permute-start.15
  165.7 2.7 collective-permute-start.14
  169.3 1.9 collective-permute-done.28
  171.2 3.2 collective-permute-done.16
  174.4 5.2 %collective-permute-done.15 = bf16[32,4096]{1,0:T(8,128)(2,1)S(1)} collective-permute-done((bf16[32,4096]{1,0:T(8,128)(2,1)}, bf16[32,4096]{1,0:T(8,128)(2,1)S(1)}, u32[]{:S(2)}, u32[]{:S(2)}) %collective-permute-start.15) | collective-permute-done | bytes 262176 | tf_op jit(solution)/shard_map/ppermute | solution.py:35
  179.5 25.8 %collective-permute-done.14 = bf16[32,4096]{1,0:T(8,128)(2,1)} collective-permute-done((bf16[32,4096]{1,0:T(8,128)(2,1)}, bf16[32,4096]{1,0:T(8,128)(2,1)}, u32[]{:S(2)}, u32[]{:S(2)}) %collective-permute-start.14) | collective-permute-done | bytes 262176 | tf_op jit(solution)/shard_map/ppermute | solution.py:35
  206.7 18.9 %shard_map.80 = bf16[8,2,16,4096]{3,2,1,0:T(8,128)(2,1)} custom-call(s32[64]{0:T(128)} %dynamic_slice.77.waves, s32[5]{0:T(128)} %pad_add_fusion.2.scalars, f32[128,1]{1,0:T(8,128)} %copy.11.eig_ref, bf16[128,128]{1,0:T(8,128)(2,1)} %select_bitcast_fusion.modes_in, bf16[128,128]{1,0:T(8,128)(2,1)} %broadcast_select_fusion.modes_out, ...), custom_call_target="tpu_custom_call" | custom-call | flops 1610612736 | bytes 6291456 | tf_op jit(solution)/shard_map/pallas_call | solution.py:357
  226.5 19.6 %shard_map.76 = bf16[8,2,16,4096]{3,2,1,0:T(8,128)(2,1)} custom-call(s32[64]{0:T(128)} %dynamic_slice.77.waves, s32[5]{0:T(128)} %pad_add_fusion.2.scalars, f32[128,1]{1,0:T(8,128)} %copy.11.eig_ref, bf16[128,128]{1,0:T(8,128)(2,1)} %select_bitcast_fusion.modes_in, bf16[128,128]{1,0:T(8,128)(2,1)} %broadcast_select_fusion.modes_out, ...), custom_call_target="tpu_custom_call" | custom-call | flops 1610612736 | bytes 6291456 | tf_op jit(solution)/shard_map/pallas_call | solution.py:357
  246.1 3.9 multiply_convert_fusion
  250.0 4.4 all-to-all-start.2
  258.0 20.4 %shard_map.74 = bf16[8,2,16,4096]{3,2,1,0:T(8,128)(2,1)} custom-call(s32[64]{0:T(128)} %dynamic_slice.77.waves, s32[5]{0:T(128)} %pad_add_fusion.scalars, f32[128,1]{1,0:T(8,128)} %copy.11.eig_ref, bf16[128,128]{1,0:T(8,128)(2,1)} %select_bitcast_fusion.1.modes_in, bf16[128,128]{1,0:T(8,128)(2,1)} %broadcast_select_fusion.1.modes_out, ...), custom_call_target="tpu_custom_call" | custom-call | flops 1610612736 | bytes 6291456 | tf_op jit(solution)/shard_map/pallas_call | solution.py:357
  278.9 2.2 fusion.22
  281.2 1.6 collective-permute-start.41
  282.8 3.3 collective-permute-start.40
  286.6 2.4 fusion.39
  289.0 2.2 collective-permute-start.38
  291.2 5.4 %collective-permute-done.41.refs_7_ = bf16[32,2048]{1,0:T(8,128)(2,1)S(1)} collective-permute-done((bf16[32,2048]{1,0:T(8,128)(2,1)S(1)}, bf16[32,2048]{1,0:T(8,128)(2,1)S(1)}, u32[]{:S(2)}, u32[]{:S(2)}) %collective-permute-start.41) | collective-permute-done | bytes 131104 | tf_op jit(solution)/shard_map/ppermute | solution.py:35
  296.6 19.4 %collective-permute-done.40.refs_6_ = bf16[32,2048]{1,0:T(8,128)(2,1)S(1)} collective-permute-done((bf16[32,2048]{1,0:T(8,128)(2,1)S(1)}, bf16[32,2048]{1,0:T(8,128)(2,1)S(1)}, u32[]{:S(2)}, u32[]{:S(2)}) %collective-permute-start.40) | collective-permute-done | bytes 131104 | tf_op jit(solution)/shard_map/ppermute | solution.py:35
  316.7 1.3 collective-permute-done.39.refs_5_
  318.0 4.6 %collective-permute-start.56 = (bf16[32,2048]{1,0:T(8,128)(2,1)S(1)}, bf16[32,2048]{1,0:T(8,128)(2,1)S(1)}, u32[]{:S(2)}, u32[]{:S(2)}) collective-permute-start(bf16[32,2048]{1,0:T(8,128)(2,1)S(1)} %get-tuple-element.23), channel_id=1, source_target_pairs={{0,6},{2,4},{4,10},{6,8},{8,14},{10,12},{12,2},{14,0},{1,7},{3,5},... | collective-permute-start | bytes 393224 | tf_op jit(solution)/shard_map/ppermute | solution.py:35
  323.7 4.3 collective-permute-start.54
  328.0 1.9 collective-permute-done.56.refs_8_
  329.8 2.9 collective-permute-start.52
  332.7 2.3 fusion.14
  335.1 5.5 %collective-permute-done.54.refs_6_ = bf16[32,2048]{1,0:T(8,128)(2,1)S(1)} collective-permute-done((bf16[32,2048]{1,0:T(8,128)(2,1)S(1)}, bf16[32,2048]{1,0:T(8,128)(2,1)S(1)}, u32[]{:S(2)}, u32[]{:S(2)}) %collective-permute-start.54) | collective-permute-done | bytes 131104 | tf_op jit(solution)/shard_map/ppermute | solution.py:35
  340.6 1.3 collective-permute-start.50
  341.9 1.3 collective-permute-done.53.refs_5_
  343.3 5.4 %collective-permute-start.42 = (bf16[32,2048]{1,0:T(8,128)(2,1)S(1)}, bf16[32,2048]{1,0:T(8,128)(2,1)S(1)}, u32[]{:S(2)}, u32[]{:S(2)}) collective-permute-start(bf16[32,2048]{1,0:T(8,128)(2,1)S(1)} %get-tuple-element.31), channel_id=1, source_target_pairs={{0,6},{2,4},{4,10},{6,8},{8,14},{10,12},{12,2},{14,0},{1,7},{3,5},... | collective-permute-start | bytes 393224 | tf_op jit(solution)/shard_map/ppermute | solution.py:35
  348.7 2.5 fusion.31
  351.3 4.0 collective-permute-start.22
  355.4 1.3 collective-permute-start.49
  356.7 4.0 collective-permute-start.47
  360.8 1.5 fusion.7
  362.3 11.5 %collective-permute-done.22.refs_13_ = bf16[32,2048]{1,0:T(8,128)(2,1)S(1)} collective-permute-done((bf16[32,2048]{1,0:T(8,128)(2,1)S(1)}, bf16[32,2048]{1,0:T(8,128)(2,1)S(1)}, u32[]{:S(2)}, u32[]{:S(2)}) %collective-permute-start.22) | collective-permute-done | bytes 131104 | tf_op jit(solution)/shard_map/ppermute | solution.py:35
  377.3 4.5 collective-permute-start.8
  382.4 2.9 collective-permute-start.7
  385.3 8.7 %shard_map.82.refs_18_ = bf16[32,64,1536]{2,1,0:T(8,128)(2,1)} custom-call(bf16[256,4096]{1,0:T(8,128)(2,1)} %bitcast.48.refs_0_, bf16[32,2048]{1,0:T(8,128)(2,1)} %get-tuple-element.30.refs_1_, bf16[32,2048]{1,0:T(8,128)(2,1)} %copy-done.56, bf16[32,2048]{1,0:T(8,128)(2,1)} %copy-done.55, bf16[32,2048]{1,0:T(8,128)(2,1)} %copy-done.54, ...), custom_call_target="tpu_custom_call" | custom-call | flops 3221225472 | bytes 8388608 | tf_op jit(solution)/shard_map/pallas_call | solution.py:203
  394.0 3.3 collective-permute-start.6
  398.8 4.5 collective-permute-start.4
  404.5 8.8 %shard_map.81.refs_18_ = bf16[32,64,1536]{2,1,0:T(8,128)(2,1)} custom-call(bf16[256,4096]{1,0:T(8,128)(2,1)} %bitcast.48.refs_0_, bf16[32,2048]{1,0:T(8,128)(2,1)} %get-tuple-element.47.refs_1_, bf16[32,2048]{1,0:T(8,128)(2,1)} %copy-done.48, bf16[32,2048]{1,0:T(8,128)(2,1)} %copy-done.47, bf16[32,2048]{1,0:T(8,128)(2,1)} %copy-done.46, ...), custom_call_target="tpu_custom_call" | custom-call | flops 3221225472 | bytes 8388608 | tf_op jit(solution)/shard_map/pallas_call | solution.py:203
  413.6 4.6 %collective-permute-done.5.refs_4_ = bf16[32,4096]{1,0:T(8,128)(2,1)S(1)} collective-permute-done((bf16[32,4096]{1,0:T(8,128)(2,1)S(1)}, bf16[32,4096]{1,0:T(8,128)(2,1)S(1)}, u32[]{:S(2)}, u32[]{:S(2)}) %collective-permute-start.5) | collective-permute-done | bytes 262176 | tf_op jit(solution)/shard_map/ppermute | solution.py:35
  418.3 18.0 %collective-permute-start.20 = (bf16[32,2048]{1,0:T(8,128)(2,1)S(1)}, bf16[32,2048]{1,0:T(8,128)(2,1)S(1)}, u32[]{:S(2)}, u32[]{:S(2)}) collective-permute-start(bf16[32,2048]{1,0:T(8,128)(2,1)S(1)} %copy-done.38), channel_id=1, source_target_pairs={{0,14},{2,12},{4,2},{6,0},{8,6},{10,4},{12,10},{14,8},{1,15},{3,13... | collective-permute-start | bytes 393224 | tf_op jit(solution)/shard_map/ppermute | solution.py:35
  437.5 2.4 collective-permute-start.24
  439.9 8.2 %shard_map.83.refs_19_ = bf16[64,64,1536]{2,1,0:T(8,128)(2,1)} custom-call(bf16[32,4096]{1,0:T(8,128)(2,1)} %get-tuple-element.78.refs_0_, bf16[32,4096]{1,0:T(8,128)(2,1)} %copy-done.15, bf16[32,4096]{1,0:T(8,128)(2,1)} %copy-done.14, bf16[32,4096]{1,0:T(8,128)(2,1)} %copy-done.13, bf16[32,4096]{1,0:T(8,128)(2,1)} %copy-done.12, ...), custom_call_target="tpu_custom_call" | custom-call | flops 3221225472 | bytes 8388608 | tf_op jit(solution)/shard_map/pallas_call | solution.py:203
  449.0 8.2 %shard_map.84 = bf16[64,64,1536]{2,1,0:T(8,128)(2,1)} custom-call(bf16[32,4096]{1,0:T(8,128)(2,1)} %get-tuple-element.78.refs_0_, bf16[32,4096]{1,0:T(8,128)(2,1)} %copy-done.15, bf16[32,4096]{1,0:T(8,128)(2,1)} %copy-done.14, bf16[32,4096]{1,0:T(8,128)(2,1)} %copy-done.13, bf16[32,4096]{1,0:T(8,128)(2,1)} %copy-done.12, ...), custom_call_target="tpu_custom_call", output_to_operand_aliasing={{}: (19, {})} | custom-call | flops 3221225472 | bytes 8388608 | tf_op jit(solution)/shard_map/pallas_call | solution.py:203
  (227 shorter events, 31.4 us)
Async XLA Ops:
  10.8 55.6 %all-to-all-start.1 = ((bf16[8,2,16,4096]{3,2,1,0:T(8,128)(2,1)}), bf16[8,2,16,4096]{3,2,1,0:T(8,128)(2,1)}, u32[]{:S(2)}, u32[]{:S(2)}) async-start(bf16[8,2,16,4096]{3,2,1,0:T(8,128)(2,1)} %bitcast.154), calls=%async_computation.1 | async-start | bytes 4194304 | tf_op jit(solution)/shard_map/all_to_all | solution.py:438
  28.5 45.3 %collective-permute-start.27 = (bf16[256,4096]{1,0:T(8,128)(2,1)}, bf16[256,4096]{1,0:T(8,128)(2,1)}, u32[]{:S(2)}, u32[]{:S(2)}) collective-permute-start(bf16[256,4096]{1,0:T(8,128)(2,1)} %get-tuple-element.20), channel_id=1, source_target_pairs={{0,1},{1,0},{2,3},{3,2},{4,5},{5,4},{6,7},{7,6},{8,9},{9,8},{10,11... | collective-permute-start | bytes 6291464 | tf_op jit(solution)/shard_map/ppermute | solution.py:23
  39.1 66.8 %collective-permute-start.9 = (bf16[256,4096]{1,0:T(8,128)(2,1)}, bf16[256,4096]{1,0:T(8,128)(2,1)}, u32[]{:S(2)}, u32[]{:S(2)}) collective-permute-start(bf16[256,4096]{1,0:T(8,128)(2,1)} %get-tuple-element.16), channel_id=1, source_target_pairs={{0,1},{1,0},{2,3},{3,2},{4,5},{5,4},{6,7},{7,6},{8,9},{9,8},{10,11... | collective-permute-start | bytes 6291464 | tf_op jit(solution)/shard_map/ppermute | solution.py:23
  66.5 159.9 %all-to-all-start = ((bf16[8,2,16,4096]{3,2,1,0:T(8,128)(2,1)}), bf16[8,2,16,4096]{3,2,1,0:T(8,128)(2,1)S(1)}, u32[]{:S(2)}, u32[]{:S(2)}) async-start(bf16[8,2,16,4096]{3,2,1,0:T(8,128)(2,1)} %bitcast.153), calls=%async_computation | async-start | bytes 4194304 | tf_op jit(solution)/shard_map/all_to_all | solution.py:438
  70.3 12.4 %collective-permute-start.25 = (bf16[8,2,16,4096]{3,2,1,0:T(8,128)(2,1)}, bf16[8,2,16,4096]{3,2,1,0:T(8,128)(2,1)S(1)}, u32[]{:S(2)}, u32[]{:S(2)}) collective-permute-start(bf16[8,2,16,4096]{3,2,1,0:T(8,128)(2,1)} %all-to-all-done.1.refs_0_), channel_id=1, source_target_pairs={{0,1},{1,0},{2,3},{3,2},{4,5},{5,4},{6,7},{7,6},{8,9},{9,8},{10,11... | collective-permute-start | bytes 6291464 | tf_op jit(solution)/shard_map/ppermute | solution.py:23
  77.7 34.5 %collective-permute-start.34 = (bf16[32,4096]{1,0:T(8,128)(2,1)}, bf16[32,4096]{1,0:T(8,128)(2,1)S(1)}, u32[]{:S(2)}, u32[]{:S(2)}) collective-permute-start(bf16[32,4096]{1,0:T(8,128)(2,1)} %get-tuple-element.48), channel_id=1, source_target_pairs={{0,14},{2,12},{4,2},{6,0},{8,6},{10,4},{12,10},{14,8},{1,15},{3,13... | collective-permute-start | bytes 786440 | tf_op jit(solution)/shard_map/ppermute | solution.py:35
  82.2 61.6 %collective-permute-start.33 = (bf16[32,4096]{1,0:T(8,128)(2,1)}, bf16[32,4096]{1,0:T(8,128)(2,1)S(1)}, u32[]{:S(2)}, u32[]{:S(2)}) collective-permute-start(bf16[32,4096]{1,0:T(8,128)(2,1)} %get-tuple-element.49), channel_id=1, source_target_pairs={{0,12},{2,14},{4,0},{6,2},{8,4},{10,6},{12,8},{14,10},{1,13},{3,15... | collective-permute-start | bytes 786440 | tf_op jit(solution)/shard_map/ppermute | solution.py:35
  104.3 141.8 %collective-permute-start.26 = (bf16[8,32,4096]{2,1,0:T(8,128)(2,1)}, bf16[8,32,4096]{2,1,0:T(8,128)(2,1)}, u32[]{:S(2)}, u32[]{:S(2)}) collective-permute-start(bf16[8,32,4096]{2,1,0:T(8,128)(2,1)} %bitcast.150), channel_id=1, source_target_pairs={{0,1},{1,0},{2,3},{3,2},{4,5},{5,4},{6,7},{7,6},{8,9},{9,8},{10,11... | collective-permute-start | bytes 6291464 | tf_op jit(solution)/shard_map/ppermute | solution.py:23
  105.9 53.9 %collective-permute-start.32 = (bf16[32,4096]{1,0:T(8,128)(2,1)}, bf16[32,4096]{1,0:T(8,128)(2,1)S(1)}, u32[]{:S(2)}, u32[]{:S(2)}) collective-permute-start(bf16[32,4096]{1,0:T(8,128)(2,1)} %get-tuple-element.50), channel_id=1, source_target_pairs={{0,10},{2,8},{4,14},{6,12},{8,2},{10,0},{12,6},{14,4},{1,11},{3,9}... | collective-permute-start | bytes 786440 | tf_op jit(solution)/shard_map/ppermute | solution.py:35
  105.9 58.1 %collective-permute-start.31 = (bf16[32,4096]{1,0:T(8,128)(2,1)}, bf16[32,4096]{1,0:T(8,128)(2,1)}, u32[]{:S(2)}, u32[]{:S(2)}) collective-permute-start(bf16[32,4096]{1,0:T(8,128)(2,1)} %get-tuple-element.51), channel_id=1, source_target_pairs={{0,8},{2,10},{4,12},{6,14},{8,0},{10,2},{12,4},{14,6},{1,9},{3,11}... | collective-permute-start | bytes 786440 | tf_op jit(solution)/shard_map/ppermute | solution.py:35
  112.2 51.8 %collective-permute-start.30 = (bf16[32,4096]{1,0:T(8,128)(2,1)}, bf16[32,4096]{1,0:T(8,128)(2,1)}, u32[]{:S(2)}, u32[]{:S(2)}) collective-permute-start(bf16[32,4096]{1,0:T(8,128)(2,1)} %get-tuple-element.52), channel_id=1, source_target_pairs={{0,6},{2,4},{4,10},{6,8},{8,14},{10,12},{12,2},{14,0},{1,7},{3,5},... | collective-permute-start | bytes 786440 | tf_op jit(solution)/shard_map/ppermute | solution.py:35
  143.7 21.9 %collective-permute-start.29 = (bf16[32,4096]{1,0:T(8,128)(2,1)}, bf16[32,4096]{1,0:T(8,128)(2,1)}, u32[]{:S(2)}, u32[]{:S(2)}) collective-permute-start(bf16[32,4096]{1,0:T(8,128)(2,1)} %get-tuple-element.53), channel_id=1, source_target_pairs={{0,4},{2,6},{4,8},{6,10},{8,12},{10,14},{12,0},{14,2},{1,5},{3,7},... | collective-permute-start | bytes 786440 | tf_op jit(solution)/shard_map/ppermute | solution.py:35
  160.5 10.7 %collective-permute-start.28 = (bf16[32,4096]{1,0:T(8,128)(2,1)}, bf16[32,4096]{1,0:T(8,128)(2,1)}, u32[]{:S(2)}, u32[]{:S(2)}) collective-permute-start(bf16[32,4096]{1,0:T(8,128)(2,1)} %get-tuple-element.54), channel_id=1, source_target_pairs={{0,2},{2,0},{4,6},{6,4},{8,10},{10,8},{12,14},{14,12},{1,3},{3,1},... | collective-permute-start | bytes 786440 | tf_op jit(solution)/shard_map/ppermute | solution.py:35
  164.0 10.4 %collective-permute-start.16 = (bf16[32,4096]{1,0:T(8,128)(2,1)}, bf16[32,4096]{1,0:T(8,128)(2,1)S(1)}, u32[]{:S(2)}, u32[]{:S(2)}) collective-permute-start(bf16[32,4096]{1,0:T(8,128)(2,1)} %get-tuple-element.63), channel_id=1, source_target_pairs={{0,14},{2,12},{4,2},{6,0},{8,6},{10,4},{12,10},{14,8},{1,15},{3,13... | collective-permute-start | bytes 786440 | tf_op jit(solution)/shard_map/ppermute | solution.py:35
  164.0 15.5 %collective-permute-start.15 = (bf16[32,4096]{1,0:T(8,128)(2,1)}, bf16[32,4096]{1,0:T(8,128)(2,1)S(1)}, u32[]{:S(2)}, u32[]{:S(2)}) collective-permute-start(bf16[32,4096]{1,0:T(8,128)(2,1)} %get-tuple-element.64), channel_id=1, source_target_pairs={{0,12},{2,14},{4,0},{6,2},{8,4},{10,6},{12,8},{14,10},{1,13},{3,15... | collective-permute-start | bytes 786440 | tf_op jit(solution)/shard_map/ppermute | solution.py:35
  165.7 39.7 %collective-permute-start.14 = (bf16[32,4096]{1,0:T(8,128)(2,1)}, bf16[32,4096]{1,0:T(8,128)(2,1)}, u32[]{:S(2)}, u32[]{:S(2)}) collective-permute-start(bf16[32,4096]{1,0:T(8,128)(2,1)} %get-tuple-element.65), channel_id=1, source_target_pairs={{0,10},{2,8},{4,14},{6,12},{8,2},{10,0},{12,6},{14,4},{1,11},{3,9}... | collective-permute-start | bytes 786440 | tf_op jit(solution)/shard_map/ppermute | solution.py:35
  171.2 54.5 %collective-permute-start.13 = (bf16[32,4096]{1,0:T(8,128)(2,1)}, bf16[32,4096]{1,0:T(8,128)(2,1)S(1)}, u32[]{:S(2)}, u32[]{:S(2)}) collective-permute-start(bf16[32,4096]{1,0:T(8,128)(2,1)} %get-tuple-element.66), channel_id=1, source_target_pairs={{0,8},{2,10},{4,12},{6,14},{8,0},{10,2},{12,4},{14,6},{1,9},{3,11}... | collective-permute-start | bytes 786440 | tf_op jit(solution)/shard_map/ppermute | solution.py:35
  174.4 51.3 %copy-start.19 = (bf16[32,4096]{1,0:T(8,128)(2,1)}, bf16[32,4096]{1,0:T(8,128)(2,1)S(1)}, u32[]{:S(2)}) copy-start(bf16[32,4096]{1,0:T(8,128)(2,1)S(1)} %collective-permute-done.16) | copy-start | bytes 786436
  174.4 52.0 %collective-permute-start.12 = (bf16[32,4096]{1,0:T(8,128)(2,1)}, bf16[32,4096]{1,0:T(8,128)(2,1)}, u32[]{:S(2)}, u32[]{:S(2)}) collective-permute-start(bf16[32,4096]{1,0:T(8,128)(2,1)} %get-tuple-element.67), channel_id=1, source_target_pairs={{0,6},{2,4},{4,10},{6,8},{8,14},{10,12},{12,2},{14,0},{1,7},{3,5},... | collective-permute-start | bytes 786440 | tf_op jit(solution)/shard_map/ppermute | solution.py:35
  179.5 46.1 %copy-start.20 = (bf16[32,4096]{1,0:T(8,128)(2,1)}, bf16[32,4096]{1,0:T(8,128)(2,1)S(1)}, u32[]{:S(2)}) copy-start(bf16[32,4096]{1,0:T(8,128)(2,1)S(1)} %collective-permute-done.15) | copy-start | bytes 786436
  179.5 46.9 %collective-permute-start.11 = (bf16[32,4096]{1,0:T(8,128)(2,1)}, bf16[32,4096]{1,0:T(8,128)(2,1)}, u32[]{:S(2)}, u32[]{:S(2)}) collective-permute-start(bf16[32,4096]{1,0:T(8,128)(2,1)} %get-tuple-element.68), channel_id=1, source_target_pairs={{0,4},{2,6},{4,8},{6,10},{8,12},{10,14},{12,0},{14,2},{1,5},{3,7},... | collective-permute-start | bytes 786440 | tf_op jit(solution)/shard_map/ppermute | solution.py:35
  205.4 21.1 %collective-permute-start.10 = (bf16[32,4096]{1,0:T(8,128)(2,1)}, bf16[32,4096]{1,0:T(8,128)(2,1)}, u32[]{:S(2)}, u32[]{:S(2)}) collective-permute-start(bf16[32,4096]{1,0:T(8,128)(2,1)} %get-tuple-element.69), channel_id=1, source_target_pairs={{0,2},{2,0},{4,6},{6,4},{8,10},{10,8},{12,14},{14,12},{1,3},{3,1},... | collective-permute-start | bytes 786440 | tf_op jit(solution)/shard_map/ppermute | solution.py:35
  225.7 53.3 %collective-permute-start.35 = (bf16[8,32,4096]{2,1,0:T(8,128)(2,1)}, bf16[8,32,4096]{2,1,0:T(8,128)(2,1)}, u32[]{:S(2)}, u32[]{:S(2)}) collective-permute-start(bf16[8,32,4096]{2,1,0:T(8,128)(2,1)} %bitcast.147), channel_id=1, source_target_pairs={{0,1},{1,0},{2,3},{3,2},{4,5},{5,4},{6,7},{7,6},{8,9},{9,8},{10,11... | collective-permute-start | bytes 6291464 | tf_op jit(solution)/shard_map/ppermute | solution.py:23
  226.4 31.7 %collective-permute-start = (bf16[8,2,16,4096]{3,2,1,0:T(8,128)(2,1)S(1)}, bf16[8,2,16,4096]{3,2,1,0:T(8,128)(2,1)}, u32[]{:S(2)}, u32[]{:S(2)}) collective-permute-start(bf16[8,2,16,4096]{3,2,1,0:T(8,128)(2,1)S(1)} %all-to-all-done.refs_0_), channel_id=1, source_target_pairs={{0,1},{1,0},{2,3},{3,2},{4,5},{5,4},{6,7},{7,6},{8,9},{9,8},{10,11... | collective-permute-start | bytes 6291464 | tf_op jit(solution)/shard_map/ppermute | solution.py:23
  246.1 43.0 %collective-permute-start.17 = (bf16[8,32,4096]{2,1,0:T(8,128)(2,1)}, bf16[8,32,4096]{2,1,0:T(8,128)(2,1)}, u32[]{:S(2)}, u32[]{:S(2)}) collective-permute-start(bf16[8,32,4096]{2,1,0:T(8,128)(2,1)} %bitcast.144), channel_id=1, source_target_pairs={{0,1},{1,0},{2,3},{3,2},{4,5},{5,4},{6,7},{7,6},{8,9},{9,8},{10,11... | collective-permute-start | bytes 6291464 | tf_op jit(solution)/shard_map/ppermute | solution.py:23
  250.0 135.3 %all-to-all-start.2 = ((bf16[8,32,4096]{2,1,0:T(8,128)(2,1)}), bf16[8,32,4096]{2,1,0:T(8,128)(2,1)}, u32[]{:S(2)}, u32[]{:S(2)}) async-start(bf16[8,32,4096]{2,1,0:T(8,128)(2,1)} %multiply_convert_fusion), calls=%async_computation.2 | async-start | bytes 4194304 | tf_op jit(solution)/shard_map/all_to_all | solution.py:438
  278.4 82.2 %collective-permute-start.1 = (bf16[8,32,4096]{2,1,0:T(8,128)(2,1)}, bf16[8,32,4096]{2,1,0:T(8,128)(2,1)S(1)}, u32[]{:S(2)}, u32[]{:S(2)}) collective-permute-start(bf16[8,32,4096]{2,1,0:T(8,128)(2,1)} %bitcast.151), channel_id=1, source_target_pairs={{0,1},{1,0},{2,3},{3,2},{4,5},{5,4},{6,7},{7,6},{8,9},{9,8},{10,11... | collective-permute-start | bytes 6291464 | tf_op jit(solution)/shard_map/ppermute | solution.py:23
  281.2 51.6 %copy-start.2 = (bf16[8,2,16,4096]{3,2,1,0:T(8,128)(2,1)S(1)}, bf16[8,2,16,4096]{3,2,1,0:T(8,128)(2,1)}, u32[]{:S(2)}) copy-start(bf16[8,2,16,4096]{3,2,1,0:T(8,128)(2,1)} %shard_map.76) | copy-start | bytes 6291460
  281.2 15.5 %collective-permute-start.41 = (bf16[32,2048]{1,0:T(8,128)(2,1)S(1)}, bf16[32,2048]{1,0:T(8,128)(2,1)S(1)}, u32[]{:S(2)}, u32[]{:S(2)}) collective-permute-start(bf16[32,2048]{1,0:T(8,128)(2,1)S(1)} %get-tuple-element.41), channel_id=1, source_target_pairs={{0,4},{2,6},{4,8},{6,10},{8,12},{10,14},{12,0},{14,2},{1,5},{3,7},... | collective-permute-start | bytes 393224 | tf_op jit(solution)/shard_map/ppermute | solution.py:35
  282.8 33.3 %collective-permute-start.40 = (bf16[32,2048]{1,0:T(8,128)(2,1)S(1)}, bf16[32,2048]{1,0:T(8,128)(2,1)S(1)}, u32[]{:S(2)}, u32[]{:S(2)}) collective-permute-start(bf16[32,2048]{1,0:T(8,128)(2,1)S(1)} %get-tuple-element.42), channel_id=1, source_target_pairs={{0,10},{2,8},{4,14},{6,12},{8,2},{10,0},{12,6},{14,4},{1,11},{3,9}... | collective-permute-start | bytes 393224 | tf_op jit(solution)/shard_map/ppermute | solution.py:35
  286.1 32.0 %collective-permute-start.39 = (bf16[32,2048]{1,0:T(8,128)(2,1)S(1)}, bf16[32,2048]{1,0:T(8,128)(2,1)S(1)}, u32[]{:S(2)}, u32[]{:S(2)}) collective-permute-start(bf16[32,2048]{1,0:T(8,128)(2,1)S(1)} %get-tuple-element.43), channel_id=1, source_target_pairs={{0,8},{2,10},{4,12},{6,14},{8,0},{10,2},{12,4},{14,6},{1,9},{3,11}... | collective-permute-start | bytes 393224 | tf_op jit(solution)/shard_map/ppermute | solution.py:35
  289.0 34.5 %collective-permute-start.38 = (bf16[32,2048]{1,0:T(8,128)(2,1)S(1)}, bf16[32,2048]{1,0:T(8,128)(2,1)S(1)}, u32[]{:S(2)}, u32[]{:S(2)}) collective-permute-start(bf16[32,2048]{1,0:T(8,128)(2,1)S(1)} %get-tuple-element.44), channel_id=1, source_target_pairs={{0,14},{2,12},{4,2},{6,0},{8,6},{10,4},{12,10},{14,8},{1,15},{3,13... | collective-permute-start | bytes 393224 | tf_op jit(solution)/shard_map/ppermute | solution.py:35
  296.6 54.6 %copy-start.43 = (bf16[32,2048]{1,0:T(8,128)(2,1)}, bf16[32,2048]{1,0:T(8,128)(2,1)S(1)}, u32[]{:S(2)}) copy-start(bf16[32,2048]{1,0:T(8,128)(2,1)S(1)} %collective-permute-done.41.refs_7_) | copy-start | bytes 393220
  296.6 27.0 %collective-permute-start.37 = (bf16[32,2048]{1,0:T(8,128)(2,1)S(1)}, bf16[32,2048]{1,0:T(8,128)(2,1)S(1)}, u32[]{:S(2)}, u32[]{:S(2)}) collective-permute-start(bf16[32,2048]{1,0:T(8,128)(2,1)S(1)} %get-tuple-element.45), channel_id=1, source_target_pairs={{0,12},{2,14},{4,0},{6,2},{8,4},{10,6},{12,8},{14,10},{1,13},{3,15... | collective-permute-start | bytes 393224 | tf_op jit(solution)/shard_map/ppermute | solution.py:35
  316.1 11.9 %collective-permute-start.36 = (bf16[32,2048]{1,0:T(8,128)(2,1)S(1)}, bf16[32,2048]{1,0:T(8,128)(2,1)S(1)}, u32[]{:S(2)}, u32[]{:S(2)}) collective-permute-start(bf16[32,2048]{1,0:T(8,128)(2,1)S(1)} %get-tuple-element.46), channel_id=1, source_target_pairs={{0,2},{2,0},{4,6},{6,4},{8,10},{10,8},{12,14},{14,12},{1,3},{3,1},... | collective-permute-start | bytes 393224 | tf_op jit(solution)/shard_map/ppermute | solution.py:35
  318.0 11.8 %collective-permute-start.56 = (bf16[32,2048]{1,0:T(8,128)(2,1)S(1)}, bf16[32,2048]{1,0:T(8,128)(2,1)S(1)}, u32[]{:S(2)}, u32[]{:S(2)}) collective-permute-start(bf16[32,2048]{1,0:T(8,128)(2,1)S(1)} %get-tuple-element.23), channel_id=1, source_target_pairs={{0,6},{2,4},{4,10},{6,8},{8,14},{10,12},{12,2},{14,0},{1,7},{3,5},... | collective-permute-start | bytes 393224 | tf_op jit(solution)/shard_map/ppermute | solution.py:35
  323.6 11.4 %collective-permute-start.55 = (bf16[32,2048]{1,0:T(8,128)(2,1)S(1)}, bf16[32,2048]{1,0:T(8,128)(2,1)S(1)}, u32[]{:S(2)}, u32[]{:S(2)}) collective-permute-start(bf16[32,2048]{1,0:T(8,128)(2,1)S(1)} %get-tuple-element.24), channel_id=1, source_target_pairs={{0,4},{2,6},{4,8},{6,10},{8,12},{10,14},{12,0},{14,2},{1,5},{3,7},... | collective-permute-start | bytes 393224 | tf_op jit(solution)/shard_map/ppermute | solution.py:35
  323.7 16.9 %collective-permute-start.54 = (bf16[32,2048]{1,0:T(8,128)(2,1)S(1)}, bf16[32,2048]{1,0:T(8,128)(2,1)S(1)}, u32[]{:S(2)}, u32[]{:S(2)}) collective-permute-start(bf16[32,2048]{1,0:T(8,128)(2,1)S(1)} %get-tuple-element.25), channel_id=1, source_target_pairs={{0,10},{2,8},{4,14},{6,12},{8,2},{10,0},{12,6},{14,4},{1,11},{3,9}... | collective-permute-start | bytes 393224 | tf_op jit(solution)/shard_map/ppermute | solution.py:35
  328.0 15.3 %collective-permute-start.53 = (bf16[32,2048]{1,0:T(8,128)(2,1)S(1)}, bf16[32,2048]{1,0:T(8,128)(2,1)S(1)}, u32[]{:S(2)}, u32[]{:S(2)}) collective-permute-start(bf16[32,2048]{1,0:T(8,128)(2,1)S(1)} %get-tuple-element.26), channel_id=1, source_target_pairs={{0,8},{2,10},{4,12},{6,14},{8,0},{10,2},{12,4},{14,6},{1,9},{3,11}... | collective-permute-start | bytes 393224 | tf_op jit(solution)/shard_map/ppermute | solution.py:35
  329.8 18.8 %collective-permute-start.52 = (bf16[32,2048]{1,0:T(8,128)(2,1)S(1)}, bf16[32,2048]{1,0:T(8,128)(2,1)S(1)}, u32[]{:S(2)}, u32[]{:S(2)}) collective-permute-start(bf16[32,2048]{1,0:T(8,128)(2,1)S(1)} %get-tuple-element.27), channel_id=1, source_target_pairs={{0,14},{2,12},{4,2},{6,0},{8,6},{10,4},{12,10},{14,8},{1,15},{3,13... | collective-permute-start | bytes 393224 | tf_op jit(solution)/shard_map/ppermute | solution.py:35
  335.1 16.2 %collective-permute-start.51 = (bf16[32,2048]{1,0:T(8,128)(2,1)S(1)}, bf16[32,2048]{1,0:T(8,128)(2,1)S(1)}, u32[]{:S(2)}, u32[]{:S(2)}) collective-permute-start(bf16[32,2048]{1,0:T(8,128)(2,1)S(1)} %get-tuple-element.28), channel_id=1, source_target_pairs={{0,12},{2,14},{4,0},{6,2},{8,4},{10,6},{12,8},{14,10},{1,13},{3,15... | collective-permute-start | bytes 393224 | tf_op jit(solution)/shard_map/ppermute | solution.py:35
  340.6 14.7 %collective-permute-start.50 = (bf16[32,2048]{1,0:T(8,128)(2,1)S(1)}, bf16[32,2048]{1,0:T(8,128)(2,1)S(1)}, u32[]{:S(2)}, u32[]{:S(2)}) collective-permute-start(bf16[32,2048]{1,0:T(8,128)(2,1)S(1)} %get-tuple-element.29), channel_id=1, source_target_pairs={{0,2},{2,0},{4,6},{6,4},{8,10},{10,8},{12,14},{14,12},{1,3},{3,1},... | collective-permute-start | bytes 393224 | tf_op jit(solution)/shard_map/ppermute | solution.py:35
  343.3 13.4 %collective-permute-start.42 = (bf16[32,2048]{1,0:T(8,128)(2,1)S(1)}, bf16[32,2048]{1,0:T(8,128)(2,1)S(1)}, u32[]{:S(2)}, u32[]{:S(2)}) collective-permute-start(bf16[32,2048]{1,0:T(8,128)(2,1)S(1)} %get-tuple-element.31), channel_id=1, source_target_pairs={{0,6},{2,4},{4,10},{6,8},{8,14},{10,12},{12,2},{14,0},{1,7},{3,5},... | collective-permute-start | bytes 393224 | tf_op jit(solution)/shard_map/ppermute | solution.py:35
  348.7 8.0 %collective-permute-start.23 = (bf16[32,2048]{1,0:T(8,128)(2,1)S(1)}, bf16[32,2048]{1,0:T(8,128)(2,1)S(1)}, u32[]{:S(2)}, u32[]{:S(2)}) collective-permute-start(bf16[32,2048]{1,0:T(8,128)(2,1)S(1)} %get-tuple-element.56), channel_id=1, source_target_pairs={{0,4},{2,6},{4,8},{6,10},{8,12},{10,14},{12,0},{14,2},{1,5},{3,7},... | collective-permute-start | bytes 393224 | tf_op jit(solution)/shard_map/ppermute | solution.py:35
  351.3 22.4 %collective-permute-start.22 = (bf16[32,2048]{1,0:T(8,128)(2,1)S(1)}, bf16[32,2048]{1,0:T(8,128)(2,1)S(1)}, u32[]{:S(2)}, u32[]{:S(2)}) collective-permute-start(bf16[32,2048]{1,0:T(8,128)(2,1)S(1)} %get-tuple-element.57), channel_id=1, source_target_pairs={{0,10},{2,8},{4,14},{6,12},{8,2},{10,0},{12,6},{14,4},{1,11},{3,9}... | collective-permute-start | bytes 393224 | tf_op jit(solution)/shard_map/ppermute | solution.py:35
  355.4 18.4 %collective-permute-start.49 = (bf16[32,2048]{1,0:T(8,128)(2,1)S(1)}, bf16[32,2048]{1,0:T(8,128)(2,1)S(1)}, u32[]{:S(2)}, u32[]{:S(2)}) collective-permute-start(bf16[32,2048]{1,0:T(8,128)(2,1)S(1)} %get-tuple-element.32), channel_id=1, source_target_pairs={{0,6},{2,4},{4,10},{6,8},{8,14},{10,12},{12,2},{14,0},{1,7},{3,5},... | collective-permute-start | bytes 393224 | tf_op jit(solution)/shard_map/ppermute | solution.py:35
  356.7 18.1 %collective-permute-start.48 = (bf16[32,2048]{1,0:T(8,128)(2,1)S(1)}, bf16[32,2048]{1,0:T(8,128)(2,1)S(1)}, u32[]{:S(2)}, u32[]{:S(2)}) collective-permute-start(bf16[32,2048]{1,0:T(8,128)(2,1)S(1)} %get-tuple-element.33), channel_id=1, source_target_pairs={{0,4},{2,6},{4,8},{6,10},{8,12},{10,14},{12,0},{14,2},{1,5},{3,7},... | collective-permute-start | bytes 393224 | tf_op jit(solution)/shard_map/ppermute | solution.py:35
  356.7 19.9 %collective-permute-start.47 = (bf16[32,2048]{1,0:T(8,128)(2,1)S(1)}, bf16[32,2048]{1,0:T(8,128)(2,1)S(1)}, u32[]{:S(2)}, u32[]{:S(2)}) collective-permute-start(bf16[32,2048]{1,0:T(8,128)(2,1)S(1)} %get-tuple-element.34), channel_id=1, source_target_pairs={{0,10},{2,8},{4,14},{6,12},{8,2},{10,0},{12,6},{14,4},{1,11},{3,9}... | collective-permute-start | bytes 393224 | tf_op jit(solution)/shard_map/ppermute | solution.py:35
  360.7 21.0 %collective-permute-start.46 = (bf16[32,2048]{1,0:T(8,128)(2,1)S(1)}, bf16[32,2048]{1,0:T(8,128)(2,1)S(1)}, u32[]{:S(2)}, u32[]{:S(2)}) collective-permute-start(bf16[32,2048]{1,0:T(8,128)(2,1)S(1)} %get-tuple-element.35), channel_id=1, source_target_pairs={{0,8},{2,10},{4,12},{6,14},{8,0},{10,2},{12,4},{14,6},{1,9},{3,11}... | collective-permute-start | bytes 393224 | tf_op jit(solution)/shard_map/ppermute | solution.py:35
  373.7 20.3 %collective-permute-start.45 = (bf16[32,2048]{1,0:T(8,128)(2,1)}, bf16[32,2048]{1,0:T(8,128)(2,1)S(1)}, u32[]{:S(2)}, u32[]{:S(2)}) collective-permute-start(bf16[32,2048]{1,0:T(8,128)(2,1)} %get-tuple-element.36), channel_id=1, source_target_pairs={{0,14},{2,12},{4,2},{6,0},{8,6},{10,4},{12,10},{14,8},{1,15},{3,13... | collective-permute-start | bytes 393224 | tf_op jit(solution)/shard_map/ppermute | solution.py:35
  373.8 23.5 %collective-permute-start.44 = (bf16[32,2048]{1,0:T(8,128)(2,1)}, bf16[32,2048]{1,0:T(8,128)(2,1)S(1)}, u32[]{:S(2)}, u32[]{:S(2)}) collective-permute-start(bf16[32,2048]{1,0:T(8,128)(2,1)} %get-tuple-element.37), channel_id=1, source_target_pairs={{0,12},{2,14},{4,0},{6,2},{8,4},{10,6},{12,8},{14,10},{1,13},{3,15... | collective-permute-start | bytes 393224 | tf_op jit(solution)/shard_map/ppermute | solution.py:35
  374.8 23.4 %collective-permute-start.43 = (bf16[32,2048]{1,0:T(8,128)(2,1)}, bf16[32,2048]{1,0:T(8,128)(2,1)S(1)}, u32[]{:S(2)}, u32[]{:S(2)}) collective-permute-start(bf16[32,2048]{1,0:T(8,128)(2,1)} %get-tuple-element.38), channel_id=1, source_target_pairs={{0,2},{2,0},{4,6},{6,4},{8,10},{10,8},{12,14},{14,12},{1,3},{3,1},... | collective-permute-start | bytes 393224 | tf_op jit(solution)/shard_map/ppermute | solution.py:35
  377.3 26.1 %collective-permute-start.8 = (bf16[32,4096]{1,0:T(8,128)(2,1)S(1)}, bf16[32,4096]{1,0:T(8,128)(2,1)S(1)}, u32[]{:S(2)}, u32[]{:S(2)}) collective-permute-start(bf16[32,4096]{1,0:T(8,128)(2,1)S(1)} %get-tuple-element.71), channel_id=1, source_target_pairs={{0,6},{2,4},{4,10},{6,8},{8,14},{10,12},{12,2},{14,0},{1,7},{3,5},... | collective-permute-start | bytes 786440 | tf_op jit(solution)/shard_map/ppermute | solution.py:35
  382.4 21.7 %collective-permute-start.7 = (bf16[32,4096]{1,0:T(8,128)(2,1)S(1)}, bf16[32,4096]{1,0:T(8,128)(2,1)S(1)}, u32[]{:S(2)}, u32[]{:S(2)}) collective-permute-start(bf16[32,4096]{1,0:T(8,128)(2,1)S(1)} %get-tuple-element.72), channel_id=1, source_target_pairs={{0,4},{2,6},{4,8},{6,10},{8,12},{10,14},{12,0},{14,2},{1,5},{3,7},... | collective-permute-start | bytes 786440 | tf_op jit(solution)/shard_map/ppermute | solution.py:35
  394.0 19.6 %collective-permute-start.6 = (bf16[32,4096]{1,0:T(8,128)(2,1)S(1)}, bf16[32,4096]{1,0:T(8,128)(2,1)S(1)}, u32[]{:S(2)}, u32[]{:S(2)}) collective-permute-start(bf16[32,4096]{1,0:T(8,128)(2,1)S(1)} %get-tuple-element.73), channel_id=1, source_target_pairs={{0,10},{2,8},{4,14},{6,12},{8,2},{10,0},{12,6},{14,4},{1,11},{3,9}... | collective-permute-start | bytes 786440 | tf_op jit(solution)/shard_map/ppermute | solution.py:35
  398.0 20.3 %collective-permute-start.5 = (bf16[32,4096]{1,0:T(8,128)(2,1)S(1)}, bf16[32,4096]{1,0:T(8,128)(2,1)S(1)}, u32[]{:S(2)}, u32[]{:S(2)}) collective-permute-start(bf16[32,4096]{1,0:T(8,128)(2,1)S(1)} %get-tuple-element.74), channel_id=1, source_target_pairs={{0,8},{2,10},{4,12},{6,14},{8,0},{10,2},{12,4},{14,6},{1,9},{3,11}... | collective-permute-start | bytes 786440 | tf_op jit(solution)/shard_map/ppermute | solution.py:35
  398.8 37.4 %collective-permute-start.4 = (bf16[32,4096]{1,0:T(8,128)(2,1)S(1)}, bf16[32,4096]{1,0:T(8,128)(2,1)S(1)}, u32[]{:S(2)}, u32[]{:S(2)}) collective-permute-start(bf16[32,4096]{1,0:T(8,128)(2,1)S(1)} %get-tuple-element.75), channel_id=1, source_target_pairs={{0,14},{2,12},{4,2},{6,0},{8,6},{10,4},{12,10},{14,8},{1,15},{3,13... | collective-permute-start | bytes 786440 | tf_op jit(solution)/shard_map/ppermute | solution.py:35
  403.3 32.9 %collective-permute-start.3 = (bf16[32,4096]{1,0:T(8,128)(2,1)S(1)}, bf16[32,4096]{1,0:T(8,128)(2,1)S(1)}, u32[]{:S(2)}, u32[]{:S(2)}) collective-permute-start(bf16[32,4096]{1,0:T(8,128)(2,1)S(1)} %get-tuple-element.76), channel_id=1, source_target_pairs={{0,12},{2,14},{4,0},{6,2},{8,4},{10,6},{12,8},{14,10},{1,13},{3,15... | collective-permute-start | bytes 786440 | tf_op jit(solution)/shard_map/ppermute | solution.py:35
  404.1 33.4 %collective-permute-start.2 = (bf16[32,4096]{1,0:T(8,128)(2,1)S(1)}, bf16[32,4096]{1,0:T(8,128)(2,1)S(1)}, u32[]{:S(2)}, u32[]{:S(2)}) collective-permute-start(bf16[32,4096]{1,0:T(8,128)(2,1)S(1)} %get-tuple-element.77), channel_id=1, source_target_pairs={{0,2},{2,0},{4,6},{6,4},{8,10},{10,8},{12,14},{14,12},{1,3},{3,1},... | collective-permute-start | bytes 786440 | tf_op jit(solution)/shard_map/ppermute | solution.py:35
  413.6 34.5 %collective-permute-start.21 = (bf16[32,2048]{1,0:T(8,128)(2,1)S(1)}, bf16[32,2048]{1,0:T(8,128)(2,1)S(1)}, u32[]{:S(2)}, u32[]{:S(2)}) collective-permute-start(bf16[32,2048]{1,0:T(8,128)(2,1)S(1)} %copy-done.39), channel_id=1, source_target_pairs={{0,8},{2,10},{4,12},{6,14},{8,0},{10,2},{12,4},{14,6},{1,9},{3,11}... | collective-permute-start | bytes 393224 | tf_op jit(solution)/shard_map/ppermute | solution.py:35
  418.3 29.9 %collective-permute-start.20 = (bf16[32,2048]{1,0:T(8,128)(2,1)S(1)}, bf16[32,2048]{1,0:T(8,128)(2,1)S(1)}, u32[]{:S(2)}, u32[]{:S(2)}) collective-permute-start(bf16[32,2048]{1,0:T(8,128)(2,1)S(1)} %copy-done.38), channel_id=1, source_target_pairs={{0,14},{2,12},{4,2},{6,0},{8,6},{10,4},{12,10},{14,8},{1,15},{3,13... | collective-permute-start | bytes 393224 | tf_op jit(solution)/shard_map/ppermute | solution.py:35
  436.2 11.9 %collective-permute-start.19 = (bf16[32,2048]{1,0:T(8,128)(2,1)S(1)}, bf16[32,2048]{1,0:T(8,128)(2,1)S(1)}, u32[]{:S(2)}, u32[]{:S(2)}) collective-permute-start(bf16[32,2048]{1,0:T(8,128)(2,1)S(1)} %copy-done.37), channel_id=1, source_target_pairs={{0,12},{2,14},{4,0},{6,2},{8,4},{10,6},{12,8},{14,10},{1,13},{3,15... | collective-permute-start | bytes 393224 | tf_op jit(solution)/shard_map/ppermute | solution.py:35
  436.3 11.8 %collective-permute-start.18 = (bf16[32,2048]{1,0:T(8,128)(2,1)S(1)}, bf16[32,2048]{1,0:T(8,128)(2,1)S(1)}, u32[]{:S(2)}, u32[]{:S(2)}) collective-permute-start(bf16[32,2048]{1,0:T(8,128)(2,1)S(1)} %copy-done.36), channel_id=1, source_target_pairs={{0,2},{2,0},{4,6},{6,4},{8,10},{10,8},{12,14},{14,12},{1,3},{3,1},... | collective-permute-start | bytes 393224 | tf_op jit(solution)/shard_map/ppermute | solution.py:35
  437.5 10.7 %collective-permute-start.24 = (bf16[32,2048]{1,0:T(8,128)(2,1)S(1)}, bf16[32,2048]{1,0:T(8,128)(2,1)S(1)}, u32[]{:S(2)}, u32[]{:S(2)}) collective-permute-start(bf16[32,2048]{1,0:T(8,128)(2,1)S(1)} %copy-done.40), channel_id=1, source_target_pairs={{0,6},{2,4},{4,10},{6,8},{8,14},{10,12},{12,2},{14,0},{1,7},{3,5},... | collective-permute-start | bytes 393224 | tf_op jit(solution)/shard_map/ppermute | solution.py:35
  (53 other events, 716.9 us)
